TPU v7x, 32 devices: a whole 2x2x4 slice. The times are simulated.
32 devices in a mesh: groups: 2 (over y), reach: 4 (over z), day: 2 (over x), head: 2 (over core).
Axes of the slice: x: 2, y: 2, z: 4, core: 2. Of those that a mesh axis runs over, the one named last changes fastest.
Arguments:
- inputs: bfloat16 [4, 8192, 256], P(('groups', 'day'), 'reach'), parts along dimension 0, may hold values from -8 to 8
- upstream: bfloat16 [4, 8192, 256], P(('groups', 'day'), 'reach'), parts along dimension 0, may hold values from -6 to 6
- query_weight: bfloat16 [256, 256], P(None, 'head'), may hold values from -0.375 to 0.375
- key_weight: bfloat16 [256, 256], P(None, 'head'), may hold values from -0.375 to 0.375
- value_weight: bfloat16 [256, 256], P(None, 'head'), may hold values from -0.375 to 0.375
- output_weight: bfloat16 [256, 256], P('head'), may hold values from -0.375 to 0.375
- partner: int32 [128], P('groups'), parts along dimension 0, may hold values from 0 to 63, as said below
- counts: int32 [128], P('groups'), parts along dimension 0, may hold values from 32 to 128, as said below
Outputs:
- delta_inputs: bfloat16 [4, 8192, 256], P(('groups', 'day'), 'reach', 'head'), parts along dimension 0
- delta_query_weight: float32 [512, 256], P('groups', 'head'), parts along dimension 0
- delta_key_weight: float32 [512, 256], P('groups', 'head'), parts along dimension 0
- delta_value_weight: float32 [512, 256], P('groups', 'head'), parts along dimension 0
- delta_output_weight: float32 [512, 256], P(('groups', 'head')), parts along dimension 0
There are 2 independent parts, one for each index of `groups`. A program takes and returns all parts, laid end to end along the dimension named above; an argument that names none is the same for every part. Nothing has to cross between parts.
Inputs may be any that keep to these rules, and one draw needn't show every extreme that they name: Each block is the partner of exactly one block. Block b is held by reach index b // 16; at most 8 of the blocks held by one reach index have their partners held by one reach index. Reaches 0 to counts - 1 of a block are valid.
All inputs are finite; a program needn't handle non-finite values.
Results may differ from a plain program's by a relative error of at most 0.012.
The roundings to bfloat16 on the way count: a program that leaves them out, or rounds other values in their place, can miss the bound.
Values may be sent and summed in bfloat16 or wider, within the bound.
No kernel may reach another device: no remote copies, remote signals or barrier semaphores. Data moves between devices by JAX's collectives and lax.ppermute only.
A program may use at most 64 MiB of HBM per device.

v0:
```python
import math

import jax
import jax.numpy as jnp
from jax import lax
from jax.sharding import PartitionSpec as P

HD = 32
BLOCK = 128


def shifted(value, axis, steps):
    count = lax.axis_size(axis)
    first, last = (max(0, -steps), min(count, count - steps))
    return lax.ppermute(value, axis, [(source, source + steps) for source in range(first, last)])


def scores_of(queries, keys, values, valid, heads):
    item_count, block_rows, head_cols = queries.shape
    head_size = head_cols // heads
    factor = head_size ** (-0.5)
    query_heads = queries.reshape(item_count, block_rows, heads, head_size)
    key_heads = keys.reshape(item_count, -1, heads, head_size)
    value_heads = values.reshape(item_count, -1, heads, head_size)
    logits = (
        jnp.einsum("gqhd,gkhd->ghqk", query_heads, key_heads, preferred_element_type=jnp.float32)
        * factor
    )
    logits = jnp.where(valid[:, None, None, :], logits, -1e30)
    highest = jnp.max(logits, axis=-1, keepdims=True)
    raised = jnp.exp(logits - highest)
    weights = raised / jnp.sum(raised, axis=-1, keepdims=True)
    return (weights, weights.astype(jnp.bfloat16), query_heads, key_heads, value_heads, factor)


def attn_output(weights_low, value_heads, out_shape):
    result = jnp.einsum(
        "ghqk,gkhd->gqhd", weights_low, value_heads, preferred_element_type=jnp.float32
    )
    return result.astype(jnp.bfloat16).reshape(out_shape)


def attn_back(weights, weights_low, query_heads, key_heads, value_heads, factor, back_out):
    item_count, block_rows, head_cols = back_out.shape
    back_heads = back_out.reshape(query_heads.shape)
    back_weights = jnp.einsum(
        "gqhd,gkhd->ghqk", back_heads, value_heads, preferred_element_type=jnp.float32
    )
    centered = back_weights - jnp.sum(weights * back_weights, axis=-1, keepdims=True)
    back_logits = (weights * centered * factor).astype(jnp.bfloat16)
    back_query = jnp.einsum(
        "ghqk,gkhd->gqhd", back_logits, key_heads, preferred_element_type=jnp.float32
    )
    back_key = jnp.einsum(
        "ghqk,gqhd->gkhd", back_logits, query_heads, preferred_element_type=jnp.float32
    )
    back_value = jnp.einsum(
        "ghqk,gqhd->gkhd", weights_low, back_heads, preferred_element_type=jnp.float32
    )
    return (
        back_query.astype(jnp.bfloat16).reshape(item_count, block_rows, head_cols),
        back_key.reshape(item_count, -1, head_cols),
        back_value.reshape(item_count, -1, head_cols),
    )


def split_terms(terms, block_rows):
    return (
        terms[:, :block_rows],
        terms[:, block_rows : 2 * block_rows].astype(jnp.bfloat16),
        terms[:, 2 * block_rows :].astype(jnp.bfloat16),
    )


def tables(partner, counts, blocks_dev, reach_total, reach_pos):
    block_total = partner.shape[0]
    slot_count = 2 * blocks_dev // reach_total
    all_blocks = jnp.arange(block_total, dtype=jnp.int32)
    own_blocks = reach_pos * blocks_dev + jnp.arange(blocks_dev, dtype=jnp.int32)
    wanted = lax.dynamic_slice_in_dim(partner, reach_pos * blocks_dev, blocks_dev)
    sources = wanted // blocks_dev
    local_index = wanted % blocks_dev
    same_source = sources[:, None] == sources[None, :]
    recv_rank = jnp.sum(same_source & (local_index[None, :] < local_index[:, None]), axis=1)
    peer_ids = jnp.arange(reach_total, dtype=jnp.int32)
    slot_ids = jnp.arange(slot_count, dtype=jnp.int32)
    recv_select = (
        (sources[:, None, None] == peer_ids[None, :, None])
        & (recv_rank[:, None, None] == slot_ids[None, None, :])
    ).astype(jnp.bfloat16)
    askers = jnp.sum(
        jnp.where(partner[None, :] == own_blocks[:, None], all_blocks[None, :], 0), axis=1
    )
    targets = askers // blocks_dev
    positions = jnp.arange(blocks_dev, dtype=jnp.int32)
    send_rank = jnp.sum(
        (targets[:, None] == targets[None, :]) & (positions[None, :] < positions[:, None]), axis=1
    )
    send_select = (
        (targets[None, None, :] == peer_ids[:, None, None])
        & (send_rank[None, None, :] == slot_ids[None, :, None])
    ).astype(jnp.bfloat16)
    count_own = lax.dynamic_slice_in_dim(counts, reach_pos * blocks_dev, blocks_dev)
    count_wanted = jnp.sum(
        jnp.where(wanted[:, None] == all_blocks[None, :], counts[None, :], 0), axis=1
    )
    return (recv_select, send_select, count_own, count_wanted)


def fetch_keys(key_blocks, value_blocks, recv_select, send_select):
    days_dev, blocks_dev, block_rows, head_cols = key_blocks.shape
    outgoing_keys = jnp.einsum(
        "dcj,tjbh->dctbh", send_select, key_blocks, preferred_element_type=jnp.float32
    ).astype(jnp.bfloat16)
    outgoing_values = jnp.einsum(
        "dcj,tjbh->dctbh", send_select, value_blocks, preferred_element_type=jnp.float32
    ).astype(jnp.bfloat16)
    incoming_keys, incoming_values = (
        lax.all_to_all(outgoing_keys, "reach", split_axis=0, concat_axis=0, tiled=True),
        lax.all_to_all(outgoing_values, "reach", split_axis=0, concat_axis=0, tiled=True),
    )
    shifted_keys, shifted_values = shifted((key_blocks, value_blocks), "day", 1)
    partner_keys = jnp.einsum(
        "isc,sctbh->tibh", recv_select, incoming_keys, preferred_element_type=jnp.float32
    ).astype(jnp.bfloat16)
    partner_values = jnp.einsum(
        "isc,sctbh->tibh", recv_select, incoming_values, preferred_element_type=jnp.float32
    ).astype(jnp.bfloat16)
    prior_keys = jnp.concatenate([shifted_keys, key_blocks[:-1]], 0)
    prior_values = jnp.concatenate([shifted_values, value_blocks[:-1]], 0)
    all_keys = jnp.concatenate([key_blocks, partner_keys, prior_keys], 2).reshape(
        -1, 3 * block_rows, head_cols
    )
    all_values = jnp.concatenate([value_blocks, partner_values, prior_values], 2).reshape(
        -1, 3 * block_rows, head_cols
    )
    return (all_keys, all_values)


def contract_rows(left, right):
    return lax.dot_general(
        left, right, (((0,), (0,)), ((), ())), preferred_element_type=jnp.float32
    )


def contract_cols(left, right):
    return lax.dot_general(
        left, right, (((1,), (1,)), ((), ())), preferred_element_type=jnp.float32
    )


def on_device(
    inputs, upstream, query_weight, key_weight, value_weight, output_weight, partner, counts
):
    days_dev, rows_dev, width = inputs.shape
    head_cols = query_weight.shape[1]
    heads_dev = head_cols // HD
    block_rows = BLOCK
    blocks_dev = rows_dev // block_rows
    reach_total = lax.axis_size("reach")
    reach_pos = lax.axis_index("reach")
    day_pos = lax.axis_index("day")
    flat_in = inputs.reshape(-1, width)
    flat_up = upstream.reshape(-1, width)
    queries = jnp.dot(flat_in, query_weight, preferred_element_type=jnp.float32).astype(
        jnp.bfloat16
    )
    keys = jnp.dot(flat_in, key_weight, preferred_element_type=jnp.float32).astype(jnp.bfloat16)
    values = jnp.dot(flat_in, value_weight, preferred_element_type=jnp.float32).astype(jnp.bfloat16)
    back_out = contract_cols(flat_up, output_weight).astype(jnp.bfloat16)
    recv_select, send_select, count_own, count_wanted = tables(
        partner, counts, blocks_dev, reach_total, reach_pos
    )
    item_shape = (days_dev, blocks_dev, block_rows, head_cols)
    key_blocks = keys.reshape(item_shape)
    value_blocks = values.reshape(item_shape)
    positions = jnp.arange(block_rows, dtype=jnp.int32)
    own_valid = positions[None, :] < count_own[:, None]
    partner_valid = positions[None, :] < count_wanted[:, None]
    day_index = day_pos * days_dev + jnp.arange(days_dev, dtype=jnp.int32)
    mask_shape = (days_dev, blocks_dev, block_rows)
    valid = jnp.concatenate(
        [own_valid[None], partner_valid[None], own_valid[None] & (day_index > 0)[:, None, None]],
        axis=-1,
    ).reshape(-1, 3 * block_rows)
    item_count = days_dev * blocks_dev
    per_group = math.gcd(item_count, max(1, 512 // block_rows))
    query_items = queries.reshape(item_count, block_rows, head_cols)
    back_items = back_out.reshape(item_count, block_rows, head_cols)

    def grouped(array):
        return array.reshape((item_count // per_group, per_group) + array.shape[1:])

    all_keys, all_values = fetch_keys(key_blocks, value_blocks, recv_select, send_select)

    def both_passes(pieces):
        query_g, key_g, value_g, valid_g, back_g = pieces
        weights, weights_low, query_heads, key_heads, value_heads, factor = scores_of(
            query_g, key_g, value_g, valid_g, heads_dev
        )
        outputs = attn_output(weights_low, value_heads, query_g.shape)
        back_query, back_key, back_value = attn_back(
            weights, weights_low, query_heads, key_heads, value_heads, factor, back_g
        )
        return (
            (outputs, back_query)
            + split_terms(back_key, block_rows)
            + split_terms(back_value, block_rows)
        )

    results = lax.map(
        both_passes,
        (
            grouped(query_items),
            grouped(all_keys),
            grouped(all_values),
            grouped(valid),
            grouped(back_items),
        ),
    )
    outputs = results[0].reshape(-1, head_cols)
    back_query = results[1].reshape(-1, head_cols)
    own_key, partner_key, prior_key = [piece.reshape(item_shape) for piece in results[2:5]]
    own_value, partner_value, prior_value = [piece.reshape(item_shape) for piece in results[5:8]]
    return_keys = jnp.einsum(
        "isc,tibh->sctbh", recv_select, partner_key, preferred_element_type=jnp.float32
    ).astype(jnp.bfloat16)
    return_values = jnp.einsum(
        "isc,tibh->sctbh", recv_select, partner_value, preferred_element_type=jnp.float32
    ).astype(jnp.bfloat16)
    home_keys, home_values = (
        lax.all_to_all(return_keys, "reach", split_axis=0, concat_axis=0, tiled=True),
        lax.all_to_all(return_values, "reach", split_axis=0, concat_axis=0, tiled=True),
    )
    from_partner_key = jnp.einsum(
        "dcj,dctbh->tjbh", send_select, home_keys, preferred_element_type=jnp.float32
    )
    from_partner_value = jnp.einsum(
        "dcj,dctbh->tjbh", send_select, home_values, preferred_element_type=jnp.float32
    )
    sent_key, sent_value = shifted((prior_key, prior_value), "day", -1)
    next_key = jnp.concatenate([prior_key[1:], sent_key], 0)
    next_value = jnp.concatenate([prior_value[1:], sent_value], 0)
    back_key = (
        (own_key + from_partner_key + next_key.astype(jnp.float32))
        .astype(jnp.bfloat16)
        .reshape(-1, head_cols)
    )
    back_value = (
        (own_value + from_partner_value + next_value.astype(jnp.float32))
        .astype(jnp.bfloat16)
        .reshape(-1, head_cols)
    )
    partial_sum = (
        contract_cols(back_query, query_weight)
        + contract_cols(back_key, key_weight)
        + contract_cols(back_value, value_weight)
    )
    summed = lax.psum_scatter(
        partial_sum.reshape(days_dev, rows_dev, width), "head", scatter_dimension=2, tiled=True
    )
    delta_inputs = summed.astype(jnp.bfloat16)
    weight_terms = (
        contract_rows(flat_in, back_query),
        contract_rows(flat_in, back_key),
        contract_rows(flat_in, back_value),
        contract_rows(outputs, flat_up),
    )
    delta_query_weight, delta_key_weight, delta_value_weight, delta_output_weight = lax.psum(
        (weight_terms[0], weight_terms[1], weight_terms[2], weight_terms[3]), ("reach", "day")
    )
    return (
        delta_inputs,
        delta_query_weight,
        delta_key_weight,
        delta_value_weight,
        delta_output_weight,
    )


def solution(mesh):
    placed = (
        P(("groups", "day"), "reach", None),
        P(("groups", "day"), "reach", None),
        P(None, "head"),
        P(None, "head"),
        P(None, "head"),
        P("head", None),
        P("groups"),
        P("groups"),
    )
    return jax.shard_map(
        on_device,
        mesh=mesh,
        in_specs=placed,
        out_specs=(
            P(("groups", "day"), "reach", "head"),
            P("groups", "head"),
            P("groups", "head"),
            P("groups", "head"),
            P(("groups", "head"), None),
        ),
        check_vma=False,
    )
```

profile of v0, /device:TPU:0, one launch (start us, length us, event | category | flops | bytes accessed | tf_op | source)
XLA Modules:
  0.0 448.1 jit_solution(13401154131591608003)
XLA Ops:
  12.0 6.3 %all-to-all-start = ((bf16[4,8,1,128,128]{4,1,3,2,0:T(8,128)(2,1)}), bf16[4,8,1,128,128]{4,1,3,2,0:T(8,128)(2,1)S(1)}, u32[]{:S(2)}, u32[]{:S(2)}) async-start(bf16[4,8,1,128,128]{4,1,3,2,0:T(8,128)(2,1)} %fusion.34), calls=%async_computation | async-start | bytes 2097152 | tf_op jit(solution)/shard_map/all_to_all | solution.py:120
  18.3 4.2 collective-permute-start
  22.9 2.2 collective-permute-start.1
  29.4 14.7 %all-to-all-done = bf16[4,8,1,128,128]{4,1,3,2,0:T(8,128)(2,1)S(1)} async-done(((bf16[4,8,1,128,128]{4,1,3,2,0:T(8,128)(2,1)}), bf16[4,8,1,128,128]{4,1,3,2,0:T(8,128)(2,1)S(1)}, u32[]{:S(2)}, u32[]{:S(2)}) %all-to-all-start) | async-done | bytes 1048608 | tf_op jit(solution)/shard_map/all_to_all | solution.py:120
  44.1 4.4 all-to-all-start.1
  50.0 2.5 convolution_convert_fusion.1
  52.4 2.0 copy.92
  54.5 2.1 copy.97
  57.8 2.3 copy.94
  60.1 13.5 %all-to-all-done.1 = bf16[4,8,1,128,128]{4,1,3,2,0:T(8,128)(2,1)} async-done(((bf16[4,8,1,128,128]{4,1,3,2,0:T(8,128)(2,1)}), bf16[4,8,1,128,128]{4,1,3,2,0:T(8,128)(2,1)}, u32[]{:S(2)}, u32[]{:S(2)}) %all-to-all-start.1) | async-done | bytes 1048608 | tf_op jit(solution)/shard_map/all_to_all | solution.py:119
  73.6 2.4 fusion.41
  76.0 2.2 copy.99
  78.2 3.4 pad_maximum_fusion
  81.6 209.8 %while.24 = (s32[]{:T(128)}, bf16[4,4,128,128]{3,2,1,0:T(8,128)(2,1)}, bf16[4,4,128,128]{3,2,1,0:T(8,128)(2,1)}, f32[4,4,128,128]{3,1,0,2:T(4,128)}, bf16[4,4,12...) while((s32[]{:T(128)}, ...), condition=%wide.region_8.9_spmd, body=%wide.region_4.8_spmd.sunk | while | flops 319820928 | bytes 40415928 | solution.py:211
  85.8 2.3 fusion.159
  88.1 2.8 fusion.160
  90.9 2.6 convolution_convert_fusion.10
  93.5 15.9 %fusion.161 = bf16[4,4,32,128]{3,2,1,0:T(8,128)(2,1)S(1)} fusion(bf16[4,384,4,32]{1,3,2,0:T(8,128)(2,1)S(1)} %bitcast.267, f32[4,4,128,384]{3,2,1,0:T(8,128)} %fusion.159, f32[4,4,128,384]{3,2,1,0:T(8,128)} %get-tuple-element.311, f32[4,4,128]{2,1,0:T(4,128)S(1)} %get-tuple-element.312), kind=kOutput, calls=%fused_computation.16.clone.1 | convolution fusion | flops 55904640 | bytes 6823936 | tf_op jit(solution)/shard_map/while/body/eval_jaxpr/ghqk,gkhd->gqhd/dot_general | solution.py:51
  109.4 15.8 %fusion.163 = f32[4,4,32,384]{3,2,1,0:T(8,128)S(1)} fusion(bf16[4,128,4,32]{1,3,2,0:T(8,128)(2,1)S(1)} %bitcast.279, f32[4,4,128,384]{3,2,1,0:T(8,128)} %fusion.159, f32[4,4,128,384]{3,2,1,0:T(8,128)} %get-tuple-element.311, f32[4,4,128]{2,1,0:T(4,128)S(1)} %get-tuple-element.312), kind=kOutput, calls=%fused_computation.8.clone.1 | convolution fusion | flops 55839104 | bytes 7217152 | tf_op jit(solution)/shard_map/while/body/eval_jaxpr/ghqk,gqhd->gkhd/dot_general | solution.py:54
  125.2 2.4 fusion.162
  138.3 2.3 fusion.159
  140.5 2.8 fusion.160
  143.3 2.6 convolution_convert_fusion.10
  146.0 15.9 %fusion.161 = bf16[4,4,32,128]{3,2,1,0:T(8,128)(2,1)S(1)} fusion(bf16[4,384,4,32]{1,3,2,0:T(8,128)(2,1)S(1)} %bitcast.267, f32[4,4,128,384]{3,2,1,0:T(8,128)} %fusion.159, f32[4,4,128,384]{3,2,1,0:T(8,128)} %get-tuple-element.311, f32[4,4,128]{2,1,0:T(4,128)S(1)} %get-tuple-element.312), kind=kOutput, calls=%fused_computation.16.clone.1 | convolution fusion | flops 55904640 | bytes 6823936 | tf_op jit(solution)/shard_map/while/body/eval_jaxpr/ghqk,gkhd->gqhd/dot_general | solution.py:51
  161.9 15.8 %fusion.163 = f32[4,4,32,384]{3,2,1,0:T(8,128)S(1)} fusion(bf16[4,128,4,32]{1,3,2,0:T(8,128)(2,1)S(1)} %bitcast.279, f32[4,4,128,384]{3,2,1,0:T(8,128)} %fusion.159, f32[4,4,128,384]{3,2,1,0:T(8,128)} %get-tuple-element.311, f32[4,4,128]{2,1,0:T(4,128)S(1)} %get-tuple-element.312), kind=kOutput, calls=%fused_computation.8.clone.1 | convolution fusion | flops 55839104 | bytes 7217152 | tf_op jit(solution)/shard_map/while/body/eval_jaxpr/ghqk,gqhd->gkhd/dot_general | solution.py:54
  177.6 2.4 fusion.162
  190.7 2.3 fusion.159
  193.0 2.8 fusion.160
  195.8 2.6 convolution_convert_fusion.10
  198.4 15.9 %fusion.161 = bf16[4,4,32,128]{3,2,1,0:T(8,128)(2,1)S(1)} fusion(bf16[4,384,4,32]{1,3,2,0:T(8,128)(2,1)S(1)} %bitcast.267, f32[4,4,128,384]{3,2,1,0:T(8,128)} %fusion.159, f32[4,4,128,384]{3,2,1,0:T(8,128)} %get-tuple-element.311, f32[4,4,128]{2,1,0:T(4,128)S(1)} %get-tuple-element.312), kind=kOutput, calls=%fused_computation.16.clone.1 | convolution fusion | flops 55904640 | bytes 6823936 | tf_op jit(solution)/shard_map/while/body/eval_jaxpr/ghqk,gkhd->gqhd/dot_general | solution.py:51
  214.3 15.8 %fusion.163 = f32[4,4,32,384]{3,2,1,0:T(8,128)S(1)} fusion(bf16[4,128,4,32]{1,3,2,0:T(8,128)(2,1)S(1)} %bitcast.279, f32[4,4,128,384]{3,2,1,0:T(8,128)} %fusion.159, f32[4,4,128,384]{3,2,1,0:T(8,128)} %get-tuple-element.311, f32[4,4,128]{2,1,0:T(4,128)S(1)} %get-tuple-element.312), kind=kOutput, calls=%fused_computation.8.clone.1 | convolution fusion | flops 55839104 | bytes 7217152 | tf_op jit(solution)/shard_map/while/body/eval_jaxpr/ghqk,gqhd->gkhd/dot_general | solution.py:54
  230.1 2.4 fusion.162
  243.2 2.3 fusion.159
  245.5 2.8 fusion.160
  248.3 2.6 convolution_convert_fusion.10
  250.9 15.9 %fusion.161 = bf16[4,4,32,128]{3,2,1,0:T(8,128)(2,1)S(1)} fusion(bf16[4,384,4,32]{1,3,2,0:T(8,128)(2,1)S(1)} %bitcast.267, f32[4,4,128,384]{3,2,1,0:T(8,128)} %fusion.159, f32[4,4,128,384]{3,2,1,0:T(8,128)} %get-tuple-element.311, f32[4,4,128]{2,1,0:T(4,128)S(1)} %get-tuple-element.312), kind=kOutput, calls=%fused_computation.16.clone.1 | convolution fusion | flops 55904640 | bytes 6823936 | tf_op jit(solution)/shard_map/while/body/eval_jaxpr/ghqk,gkhd->gqhd/dot_general | solution.py:51
  266.8 15.8 %fusion.163 = f32[4,4,32,384]{3,2,1,0:T(8,128)S(1)} fusion(bf16[4,128,4,32]{1,3,2,0:T(8,128)(2,1)S(1)} %bitcast.279, f32[4,4,128,384]{3,2,1,0:T(8,128)} %fusion.159, f32[4,4,128,384]{3,2,1,0:T(8,128)} %get-tuple-element.311, f32[4,4,128]{2,1,0:T(4,128)S(1)} %get-tuple-element.312), kind=kOutput, calls=%fused_computation.8.clone.1 | convolution fusion | flops 55839104 | bytes 7217152 | tf_op jit(solution)/shard_map/while/body/eval_jaxpr/ghqk,gqhd->gkhd/dot_general | solution.py:54
  282.6 2.4 fusion.162
  295.0 3.9 all-to-all-start.3
  298.8 2.3 copy.104
  301.1 2.4 fusion.36
  303.5 20.3 %all-to-all-done.3 = bf16[4,8,1,128,128]{4,1,3,2,0:T(8,128)(2,1)S(1)} async-done(((bf16[4,8,1,128,128]{4,1,3,2,0:T(8,128)(2,1)}), bf16[4,8,1,128,128]{4,1,3,2,0:T(8,128)(2,1)S(1)}, u32[]{:S(2)}, u32[]{:S(2)}) %all-to-all-start.3) | async-done | bytes 1048608 | tf_op jit(solution)/shard_map/all_to_all | solution.py:233
  323.8 4.2 all-to-all-start.2
  335.4 9.8 %collective-permute-done.3 = bf16[1,16,128,128]{3,1,2,0:T(8,128)(2,1)S(1)} collective-permute-done((bf16[1,16,128,128]{3,1,2,0:T(8,128)(2,1)}, bf16[1,16,128,128]{3,1,2,0:T(8,128)(2,1)S(1)}, u32[]{:S(2)}, u32[]{:S(2)}) %collective-permute-start.3) | collective-permute-done | bytes 524320 | tf_op jit(solution)/shard_map/ppermute | solution.py:15
  347.6 7.0 %collective-permute-done.2 = bf16[1,16,128,128]{3,1,2,0:T(8,128)(2,1)} collective-permute-done((bf16[1,16,128,128]{3,1,2,0:T(8,128)(2,1)}, bf16[1,16,128,128]{3,1,2,0:T(8,128)(2,1)}, u32[]{:S(2)}, u32[]{:S(2)}) %collective-permute-start.2) | collective-permute-done | bytes 524320 | tf_op jit(solution)/shard_map/ppermute | solution.py:15
  354.6 2.1 add_convert_fusion.1
  362.1 69.9 %all-reduce.3.cloned.1.call-done = (f32[256,128]{0,1:T(8,128)}, f32[256,128]{0,1:T(8,128)}, f32[256,128]{0,1:T(8,128)}, f32[128,256]{1,0:T(8,128)}) async-done(((f32[256,128]{0,1:T(8,128)}, f32[256,128]{0,1:T(8,128)}, f32[256,128]{0,1:T(8,128)}, f32[128,256]{1,0:T(8,128)}), (f32[256,128]{0,1:T(8,128)}, f32[256,128]{0,1:T(8,128)}, f32[256,128]{0,1:T(8,128)}, ...) | async-done | bytes 524304 | tf_op jit(solution)/shard_map/psum | solution.py:269
  437.0 2.1 convert_element_type.123
  (202 shorter events, 78.6 us)
Async XLA Ops:
  8.0 1.2 copy-start
  8.0 14.5 %copy-start.13 = (bf16[256,128]{1,0:T(8,128)(2,1)S(1)}, bf16[256,128]{1,0:T(8,128)(2,1)}, u32[]{:S(2)}) copy-start(bf16[256,128]{1,0:T(8,128)(2,1)} %param.13) | copy-start | bytes 196612
  9.0 18.9 %copy-start.21 = (pred[4,16]{1,0:T(4,128)(4,1)}, pred[4,16]{1,0:T(4,128)(4,1)S(1)}, u32[]{:S(2)}) copy-start(pred[4,16]{1,0:T(4,128)(4,1)S(1)} %iota_compare_fusion.7) | copy-start | bytes 196
  9.2 15.9 %copy-start.24 = (s32[64]{0:T(128)S(1)}, s32[64]{0:T(128)}, u32[]{:S(2)}) copy-start(s32[64]{0:T(128)} %param.17) | copy-start | bytes 772
  9.2 16.0 %copy-start.23 = (s32[64]{0:T(128)S(1)}, s32[64]{0:T(128)}, u32[]{:S(2)}) copy-start(s32[64]{0:T(128)} %param.16) | copy-start | bytes 772
  12.0 32.0 %all-to-all-start = ((bf16[4,8,1,128,128]{4,1,3,2,0:T(8,128)(2,1)}), bf16[4,8,1,128,128]{4,1,3,2,0:T(8,128)(2,1)S(1)}, u32[]{:S(2)}, u32[]{:S(2)}) async-start(bf16[4,8,1,128,128]{4,1,3,2,0:T(8,128)(2,1)} %fusion.34), calls=%async_computation | async-start | bytes 2097152 | tf_op jit(solution)/shard_map/all_to_all | solution.py:120
  18.3 34.1 %collective-permute-start = (bf16[1,16,128,128]{3,2,1,0:T(8,128)(2,1)S(1)}, bf16[1,16,128,128]{3,2,1,0:T(8,128)(2,1)}, u32[]{:S(2)}, u32[]{:S(2)}) collective-permute-start(bf16[1,16,128,128]{3,2,1,0:T(8,128)(2,1)S(1)} %bitcast.269), channel_id=1, source_target_pairs={{0,2},{1,3},{4,6},{5,7},{8,10},{9,11},{12,14},{13,15},{16,18},{17,... | collective-permute-start | bytes 1572872 | tf_op jit(solution)/shard_map/ppermute | solution.py:15
  22.9 25.8 %copy-start.16 = (bf16[256,128]{1,0:T(8,128)(2,1)S(1)}, bf16[256,128]{1,0:T(8,128)(2,1)}, u32[]{:S(2)}) copy-start(bf16[256,128]{1,0:T(8,128)(2,1)} %param.12) | copy-start | bytes 196612
  22.9 31.5 %collective-permute-start.1 = (bf16[1,16,128,128]{3,2,1,0:T(8,128)(2,1)S(1)}, bf16[1,16,128,128]{3,2,1,0:T(8,128)(2,1)}, u32[]{:S(2)}, u32[]{:S(2)}) collective-permute-start(bf16[1,16,128,128]{3,2,1,0:T(8,128)(2,1)S(1)} %bitcast.271), channel_id=1, source_target_pairs={{0,2},{1,3},{4,6},{5,7},{8,10},{9,11},{12,14},{13,15},{16,18},{17,... | collective-permute-start | bytes 1572872 | tf_op jit(solution)/shard_map/ppermute | solution.py:15
  26.7 23.2 %copy-start.18 = (bf16[128,256]{1,0:T(8,128)(2,1)S(1)}, bf16[128,256]{1,0:T(8,128)(2,1)}, u32[]{:S(2)}) copy-start(bf16[128,256]{1,0:T(8,128)(2,1)} %param.15) | copy-start | bytes 196612
  44.1 29.6 %all-to-all-start.1 = ((bf16[4,8,1,128,128]{4,1,3,2,0:T(8,128)(2,1)}), bf16[4,8,1,128,128]{4,1,3,2,0:T(8,128)(2,1)}, u32[]{:S(2)}, u32[]{:S(2)}) async-start(bf16[4,8,1,128,128]{4,1,3,2,0:T(8,128)(2,1)} %fusion.35), calls=%async_computation.1 | async-start | bytes 2097152 | tf_op jit(solution)/shard_map/all_to_all | solution.py:119
  48.7 24.9 %copy-start.19 = (pred[16,4]{0,1:T(4,128)(4,1)}, pred[16,4]{0,1:T(4,128)(4,1)S(1)}, u32[]{:S(2)}) copy-start(pred[16,4]{0,1:T(4,128)(4,1)S(1)} %iota_compare_fusion.6) | copy-start | bytes 196
  54.5 23.7 %copy-start.7 = (bf16[4,4,128,128]{2,3,1,0:T(8,128)(2,1)S(1)}, bf16[4,4,128,128]{2,3,1,0:T(8,128)(2,1)}, u32[]{:S(2)}) copy-start(bf16[4,4,128,128]{2,3,1,0:T(8,128)(2,1)} %copy.93) | copy-start | bytes 1572868
  54.5 23.7 %copy-start.8 = (bf16[4,4,128,128]{2,3,1,0:T(8,128)(2,1)S(1)}, bf16[4,4,128,128]{2,3,1,0:T(8,128)(2,1)}, u32[]{:S(2)}) copy-start(bf16[4,4,128,128]{2,3,1,0:T(8,128)(2,1)} %copy.98) | copy-start | bytes 1572868
  57.8 20.4 %copy-start.9 = (bf16[1,16,128,128]{2,3,1,0:T(8,128)(2,1)S(1)}, bf16[1,16,128,128]{2,3,1,0:T(8,128)(2,1)}, u32[]{:S(2)}) copy-start(bf16[1,16,128,128]{2,3,1,0:T(8,128)(2,1)} %copy.92) | copy-start | bytes 1572868
  57.8 20.4 %copy-start.10 = (bf16[1,16,128,128]{2,3,1,0:T(8,128)(2,1)S(1)}, bf16[1,16,128,128]{2,3,1,0:T(8,128)(2,1)}, u32[]{:S(2)}) copy-start(bf16[1,16,128,128]{2,3,1,0:T(8,128)(2,1)} %copy.97) | copy-start | bytes 1572868
  291.4 9.7 %copy-start.20 = (pred[16,4]{0,1:T(4,128)(4,1)S(1)}, pred[16,4]{0,1:T(4,128)(4,1)}, u32[]{:S(2)}) copy-start(pred[16,4]{0,1:T(4,128)(4,1)} %copy-done.19) | copy-start | bytes 196
  295.0 35.9 %copy-start.6 = (bf16[1,2048,256]{2,1,0:T(8,128)(2,1)S(1)}, bf16[1,2048,256]{2,1,0:T(8,128)(2,1)}, u32[]{:S(2)}) copy-start(bf16[1,2048,256]{2,1,0:T(8,128)(2,1)} %param.11) | copy-start | bytes 3145732
  295.0 28.8 %all-to-all-start.3 = ((bf16[4,8,1,128,128]{4,1,3,2,0:T(8,128)(2,1)}), bf16[4,8,1,128,128]{4,1,3,2,0:T(8,128)(2,1)S(1)}, u32[]{:S(2)}, u32[]{:S(2)}) async-start(bf16[4,8,1,128,128]{4,1,3,2,0:T(8,128)(2,1)} %fusion.37), calls=%async_computation.3 | async-start | bytes 2097152 | tf_op jit(solution)/shard_map/all_to_all | solution.py:233
  303.5 31.4 %copy-start.17 = (bf16[256,128]{1,0:T(8,128)(2,1)S(1)}, bf16[256,128]{1,0:T(8,128)(2,1)}, u32[]{:S(2)}) copy-start(bf16[256,128]{1,0:T(8,128)(2,1)} %param.12) | copy-start | bytes 196612
  323.8 9.1 %copy-start.4 = (bf16[4,8,1,128,128]{4,1,3,2,0:T(8,128)(2,1)}, bf16[4,8,1,128,128]{4,1,3,2,0:T(8,128)(2,1)S(1)}, u32[]{:S(2)}) copy-start(bf16[4,8,1,128,128]{4,1,3,2,0:T(8,128)(2,1)S(1)} %all-to-all-done.3) | copy-start | bytes 3145732
  323.8 30.8 %all-to-all-start.2 = ((bf16[4,8,1,128,128]{4,1,3,2,0:T(8,128)(2,1)}), bf16[4,8,1,128,128]{4,1,3,2,0:T(8,128)(2,1)}, u32[]{:S(2)}, u32[]{:S(2)}) async-start(bf16[4,8,1,128,128]{4,1,3,2,0:T(8,128)(2,1)} %fusion.36), calls=%async_computation.2 | async-start | bytes 2097152 | tf_op jit(solution)/shard_map/all_to_all | solution.py:232
  328.1 17.2 %copy-start.22 = (pred[4,16]{1,0:T(4,128)(4,1)S(1)}, pred[4,16]{1,0:T(4,128)(4,1)}, u32[]{:S(2)}) copy-start(pred[4,16]{1,0:T(4,128)(4,1)} %copy-done.21) | copy-start | bytes 196
  328.1 103.9 %all-reduce.3.cloned.1.call-start = ((), (), s32[]{:S(2)}) async-start(), calls=%async_computation.6 | async-start | bytes 1048576 | tf_op jit(solution)/shard_map/psum | solution.py:269
  328.1 6.9 %copy-start.11 = (bf16[4,4,128,128]{3,2,1,0:T(8,128)(2,1)S(1)}, bf16[4,4,128,128]{3,2,1,0:T(8,128)(2,1)}, u32[]{:S(2)}) copy-start(bf16[4,4,128,128]{3,2,1,0:T(8,128)(2,1)} %get-tuple-element.84) | copy-start | bytes 1572868
  328.1 17.1 %copy-start.12 = (f32[4,4,128,128]{3,1,0,2:T(4,128)S(1)}, f32[4,4,128,128]{3,1,0,2:T(4,128)}, u32[]{:S(2)}) copy-start(f32[4,4,128,128]{3,1,0,2:T(4,128)} %get-tuple-element.88) | copy-start | bytes 3145732
  328.1 17.1 %collective-permute-start.3 = (bf16[1,16,128,128]{3,1,2,0:T(8,128)(2,1)}, bf16[1,16,128,128]{3,1,2,0:T(8,128)(2,1)S(1)}, u32[]{:S(2)}, u32[]{:S(2)}) collective-permute-start(bf16[1,16,128,128]{3,1,2,0:T(8,128)(2,1)} %bitcast.293), channel_id=1, source_target_pairs={{2,0},{3,1},{6,4},{7,5},{10,8},{11,9},{14,12},{15,13},{18,16},{19,... | collective-permute-start | bytes 1572872 | tf_op jit(solution)/shard_map/ppermute | solution.py:15
  329.6 25.0 %collective-permute-start.2 = (bf16[1,16,128,128]{3,1,2,0:T(8,128)(2,1)}, bf16[1,16,128,128]{3,1,2,0:T(8,128)(2,1)}, u32[]{:S(2)}, u32[]{:S(2)}) collective-permute-start(bf16[1,16,128,128]{3,1,2,0:T(8,128)(2,1)} %bitcast.294), channel_id=1, source_target_pairs={{2,0},{3,1},{6,4},{7,5},{10,8},{11,9},{14,12},{15,13},{18,16},{19,... | collective-permute-start | bytes 1572872 | tf_op jit(solution)/shard_map/ppermute | solution.py:15
  335.0 10.3 %copy-start.5 = (bf16[4,8,1,128,128]{4,1,3,2,0:T(8,128)(2,1)S(1)}, bf16[4,8,1,128,128]{4,1,3,2,0:T(8,128)(2,1)}, u32[]{:S(2)}) copy-start(bf16[4,8,1,128,128]{4,1,3,2,0:T(8,128)(2,1)} %copy-done.4) | copy-start | bytes 3145732
  345.8 0.8 copy-start.1
  354.6 4.1 copy-start.14
  356.8 0.8 copy-start.3
  357.6 2.6 copy-start.15
  358.7 78.3 %reduce-scatter.2.cloned.1.call-start = ((), (), s32[]{:S(2)}) async-start(), calls=%async_computation.5 | async-start | bytes 3145728 | tf_op jit(solution)/shard_map/reduce_scatter | solution.py:259
  358.7 1.6 copy-start.2
Sparse Core Ops, SparseCore 0:
  358.8 73.1 all-reduce.2
Sparse Core Ops, SparseCore 1:
  362.2 9.7 reduce-scatter.1
where the time goes:
time: 450 us; the launch traced here: 448 us
  matrix products  196 us (44%)
  waiting for transfers between devices  135 us (30%)
  local copies, waits for them, and re-layouts  65.4 us (15%)
  starting transfers between devices  28.1 us (6%)
  between operations  15.8 us (4%)
  other arithmetic  7.58 us (2%)
    psum x1, waiting for transfers between devices, on_device(): lax.psum((weight_terms[0], weight_terms[1], weight_terms[2], weight_terms...  69.9 us
    dot_general x4, matrix products, attn_back(): jnp.einsum('ghqk,gkhd->gqhd', back_logits, key_heads, preferred_element_t...  63.6 us
    dot_general x4, matrix products, attn_back(): jnp.einsum('ghqk,gqhd->gkhd', back_logits, query_heads, preferred_element...  63.1 us
    dynamic_update_slice x40, local copies, waits for them, and re-layouts, on_device(): lax.map(both_passes, (grouped(query_items), grouped(all_keys), grouped(al...  25 us
    all_to_all x1, waiting for transfers between devices, on_device(): lax.all_to_all(return_values, 'reach', split_axis=0, concat_axis=0, tiled...  20.3 us
    ppermute x4, waiting for transfers between devices, shifted(): lax.ppermute(value, axis, [(source, source + steps) for source in range(f...  16.8 us
    dynamic_slice x24, local copies, waits for them, and re-layouts, on_device(): lax.map(both_passes, (grouped(query_items), grouped(all_keys), grouped(al...  16.7 us
    all_to_all x1, waiting for transfers between devices, fetch_keys(): lax.all_to_all(outgoing_values, 'reach', split_axis=0, concat_axis=0, til...  14.7 us
  transfers between devices with their start and end apart: 10, of which 6 were waited for; matrix products, arithmetic and copies ran while one was open for 8% of the time, Pallas kernels for 0%

commit v1 on v0

v1 whole, which is shorter than its diff:
```python
import jax
import jax.numpy as jnp
from jax import lax
from jax.experimental import pallas as pl
from jax.experimental.pallas import tpu as pltpu
from jax.sharding import PartitionSpec as P

HD = 32
BLOCK = 128
GROUP = 128
CORES = 2
F32 = jnp.float32
BF16 = jnp.bfloat16
LOG2E = 1.4426950408889634


class Layout:
    def __init__(self, blocks_dev, reach_total):
        self.blocks = blocks_dev
        self.items = blocks_dev // CORES
        self.reach = reach_total
        self.slots = max(1, blocks_dev // reach_total)
        self.block_of = 0
        self.recv_of = self.items
        self.count_own = 2 * self.items
        self.count_partner = 3 * self.items
        self.owner_of = 4 * self.items
        self.item_of = self.owner_of + blocks_dev
        self.home_of = self.item_of + blocks_dev
        self.core = self.home_of + blocks_dev
        self.later_day = self.core + 1
        self.size = -(-(self.core + 2) // 128) * 128


def prepare_kernel(lay, partner, counts, where, inputs, sent, prior, tab, start, used, picks, sems):
    bd, slots = lay.blocks, lay.slots
    reach_pos, core = where[0], where[1]

    def clear(index, carry):
        used[index] = 0
        start[index] = 0
        return carry

    lax.fori_loop(0, lay.reach, clear, 0, unroll=True)

    def count(index, carry):
        source = lax.div(partner[reach_pos * bd + index], bd)
        start[source] = start[source] + 1
        return carry

    lax.fori_loop(0, bd, count, 0)

    def prefix(index, total):
        here = start[index]
        start[index] = total
        return total + here

    lax.fori_loop(0, lay.reach, prefix, jnp.int32(0))

    def assign(index, carry):
        wanted = partner[reach_pos * bd + index]
        source = lax.div(wanted, bd)
        rank = used[source]
        used[source] = rank + 1
        place = start[source] + rank
        owner = lax.bitwise_and(place, 1)
        item = lax.div(place, 2)
        slot = jnp.minimum(lax.div(rank, 2), slots - 1)
        tab[lay.owner_of + index] = owner
        tab[lay.item_of + index] = item

        @pl.when(owner == core)
        def _():
            tab[lay.block_of + item] = index
            tab[lay.recv_of + item] = source * slots + slot
            tab[lay.count_own + item] = counts[reach_pos * bd + index]
            tab[lay.count_partner + item] = counts[wanted]

        return carry

    lax.fori_loop(0, bd, assign, 0)
    tab[lay.core] = core
    tab[lay.later_day] = where[2]

    def clear_picks(index, carry):
        picks[index] = 0
        return carry

    lax.fori_loop(0, lay.reach * slots, clear_picks, 0)

    def one_reach(peer, carry):
        def before(index, total):
            source = lax.div(partner[peer * bd + index], bd)
            return total + jnp.where(source < reach_pos, 1, 0)

        base = lax.fori_loop(0, bd, before, jnp.int32(0), unroll=True)

        def serve(index, rank):
            wanted = partner[peer * bd + index]
            hit = lax.div(wanted, bd) == reach_pos

            @pl.when(hit)
            def _():
                owner = lax.bitwise_and(base + rank, 1)
                slot = jnp.minimum(lax.div(rank, 2), slots - 1)
                local = lax.rem(wanted, bd)
                tab[lay.home_of + local] = (peer * CORES + owner) * slots + slot

                @pl.when(owner == core)
                def _():
                    picks[peer * slots + slot] = local

            return rank + jnp.where(hit, 1, 0)

        lax.fori_loop(0, bd, serve, jnp.int32(0))
        return carry

    lax.fori_loop(0, lay.reach, one_reach, 0)

    copies = []
    for place in range(lay.reach * slots):
        copies.append(
            pltpu.make_async_copy(inputs.at[picks[place]], sent.at[place], sems.at[place])
        )
    for item in range(lay.items):
        copies.append(
            pltpu.make_async_copy(
                inputs.at[tab[lay.block_of + item]],
                prior.at[item],
                sems.at[lay.reach * slots + item],
            )
        )
    for copy in copies:
        copy.start()
    for copy in copies:
        copy.wait()


def dot(left, right):
    return lax.dot_general(left, right, (((1,), (0,)), ((), ())), preferred_element_type=F32)


def dot_t(left, right):
    return lax.dot_general(left, right, (((1,), (1,)), ((), ())), preferred_element_type=F32)


def attention_kernel(
    lay,
    tab,
    own_ref,
    up_ref,
    partner_ref,
    prior_ref,
    mine_ref,
    other_ref,
    keep_ref,
    swap_ref,
    same_ref,
    cross_ref,
    home_ref,
    grad_mine_ref,
    grad_other_ref,
):
    item = pl.program_id(0)
    core = tab[lay.core]
    factor = HD ** (-0.5)
    own, up = own_ref[0], up_ref[0]
    key_inputs = jnp.concatenate([own, partner_ref[0], prior_ref[0]], axis=0)
    width = own.shape[1]

    @pl.when(item == 0)
    def _():
        grad_mine_ref[...] = jnp.zeros_like(grad_mine_ref)
        grad_other_ref[...] = jnp.zeros_like(grad_other_ref)

    def eye(size):
        rows = lax.broadcasted_iota(jnp.int32, (size, size), 0)
        cols = lax.broadcasted_iota(jnp.int32, (size, size), 1)
        return jnp.where(rows == cols, 1.0, 0.0).astype(BF16)

    query_t = jnp.concatenate([mine_ref[256:384, :], other_ref[256:384, :]], axis=0)
    output_w = jnp.concatenate([mine_ref[384:512, :], other_ref[384:512, :]], axis=0)
    queries = dot_t(own, query_t)
    back_out = dot_t(up, output_w)
    key_inputs_t = dot_t(eye(width), key_inputs).astype(BF16)

    count_own = tab[lay.count_own + item]
    count_partner = tab[lay.count_partner + item]
    count_prior = count_own * tab[lay.later_day]
    rows = lax.broadcasted_iota(jnp.int32, (BLOCK, 2 * BLOCK), 0)
    valid = jnp.concatenate([rows < count_own, rows < count_partner, rows < count_prior], axis=0)
    lane_head = lax.broadcasted_iota(jnp.int32, (BLOCK, GROUP), 1) // HD

    back_inputs = None
    outputs_t, back_query_t = [], []
    for group, (weights_ref, grad_ref) in enumerate(
        ((mine_ref, grad_mine_ref), (other_ref, grad_other_ref))
    ):
        kv_t = weights_ref[0:256, :]
        kv = dot_t(key_inputs, kv_t).astype(BF16)
        kv_cols = dot_t(kv_t, key_inputs).astype(BF16)
        keys, values = kv[:, :GROUP], kv[:, GROUP:]
        group_queries = queries[:, group * GROUP : (group + 1) * GROUP]
        group_back = back_out[:, group * GROUP : (group + 1) * GROUP]
        back_keys = back_values = None
        for pair in range(GROUP // HD // 2):
            heads = (2 * pair, 2 * pair + 1)
            query_pair = jnp.concatenate(
                [jnp.where(lane_head == h, group_queries, 0.0) for h in heads], axis=0
            ).astype(BF16)
            back_pair = jnp.concatenate(
                [jnp.where(lane_head == h, group_back, 0.0) for h in heads], axis=0
            ).astype(BF16)
            logits = jnp.where(valid, dot_t(keys, query_pair), -1e30)
            highest = jnp.max(logits, axis=0, keepdims=True)
            raised = jnp.exp2((logits - highest) * (factor * LOG2E))
            scale = 1.0 / jnp.sum(raised, axis=0, keepdims=True)
            weights = raised * scale
            weights_low = weights.astype(BF16)
            back_weights = dot_t(values, back_pair)
            center = jnp.sum(weights * back_weights, axis=0, keepdims=True)
            back_logits = (weights * ((back_weights - center) * factor)).astype(BF16)
            pair_values = dot(weights_low, back_pair)
            pair_keys = dot(back_logits, query_pair)
            back_values = pair_values if back_values is None else back_values + pair_values
            back_keys = pair_keys if back_keys is None else back_keys + pair_keys
            first = 2 * pair * HD
            out_t = dot(kv_cols[GROUP + first : GROUP + first + 2 * HD, :], weights_low)
            query_grad_t = dot(kv_cols[first : first + 2 * HD, :], back_logits)
            for h in range(2):
                lanes = slice(h * BLOCK, (h + 1) * BLOCK)
                outputs_t.append(out_t[h * HD : (h + 1) * HD, lanes])
                back_query_t.append(query_grad_t[h * HD : (h + 1) * HD, lanes])
        back_kv = jnp.concatenate([back_keys, back_values], axis=1).astype(BF16)
        term = dot(back_kv, kv_t)
        back_inputs = term if back_inputs is None else back_inputs + term
        grad_ref[0:256, :] += dot(key_inputs_t, back_kv)

    outputs_t = jnp.concatenate(outputs_t, axis=0).astype(BF16)
    back_query_t = jnp.concatenate(back_query_t, axis=0).astype(BF16)
    query_grad = dot(back_query_t, own)
    output_grad = dot(outputs_t, up)
    grad_mine_ref[256:384, :] += query_grad[:GROUP]
    grad_other_ref[256:384, :] += query_grad[GROUP:]
    grad_mine_ref[384:512, :] += output_grad[:GROUP]
    grad_other_ref[384:512, :] += output_grad[GROUP:]
    back_query = dot_t(eye(BLOCK), back_query_t).astype(BF16)
    own_term = back_inputs[:BLOCK] + dot(back_query, query_t)
    partner_term = back_inputs[BLOCK : 2 * BLOCK].astype(BF16)
    prior_term = back_inputs[2 * BLOCK :]
    half = width // 2
    first_core = core == 0
    keep_ref[0] = jnp.where(first_core, own_term[:, :half], own_term[:, half:])
    swap_ref[0] = jnp.where(first_core, own_term[:, half:], own_term[:, :half])
    same_ref[0] = jnp.where(first_core, prior_term[:, :half], prior_term[:, half:]).astype(BF16)
    cross_ref[0] = jnp.where(first_core, prior_term[:, half:], prior_term[:, :half]).astype(BF16)
    home_ref[0, 0, 0] = partner_term[:, :half]
    home_ref[0, 1, 0] = partner_term[:, half:]


def gather_kernel(lay, tab, keep, swapped, same, cross, home, out):
    core = tab[lay.core]

    def one(block, carry):
        item = tab[lay.item_of + block]
        mine = tab[lay.owner_of + block] == core
        total = jnp.where(mine, keep[item], swapped[item])
        total += jnp.where(mine, same[item].astype(F32), cross[item].astype(F32))
        total += home[tab[lay.home_of + block]].astype(F32)
        out[block] = total.astype(BF16)
        return carry

    lax.fori_loop(0, lay.blocks, one, 0)


def on_device(
    inputs, upstream, query_weight, key_weight, value_weight, output_weight, partner, counts
):
    days_dev, rows_dev, width = inputs.shape
    assert days_dev == 1 and width == 2 * GROUP
    blocks_dev = rows_dev // BLOCK
    reach_total = lax.axis_size("reach")
    day_total = lax.axis_size("day")
    assert lax.axis_size("head") == CORES
    lay = Layout(blocks_dev, reach_total)
    half = width // 2
    in_blocks = inputs.reshape(blocks_dev, BLOCK, width)
    up_blocks = upstream.reshape(blocks_dev, BLOCK, width)
    where = jnp.stack(
        [
            lax.axis_index("reach"),
            lax.axis_index("head"),
            (lax.axis_index("day") > 0).astype(jnp.int32),
        ]
    )
    pack = jnp.concatenate([key_weight.T, value_weight.T, query_weight.T, output_weight], axis=0)
    swap_cores = [(0, 1), (1, 0)]
    pack_other = lax.ppermute(pack, "head", swap_cores)

    smem = pl.BlockSpec(memory_space=pltpu.SMEM)
    anywhere = pl.BlockSpec(memory_space=pl.ANY)
    in_vmem = pl.BlockSpec(memory_space=pltpu.VMEM)
    send_count = lay.reach * lay.slots
    sent, prior, tab = pl.pallas_call(
        lambda *refs: prepare_kernel(lay, *refs),
        out_shape=(
            jax.ShapeDtypeStruct((send_count, BLOCK, width), BF16),
            jax.ShapeDtypeStruct((lay.items, BLOCK, width), BF16),
            jax.ShapeDtypeStruct((lay.size,), jnp.int32),
        ),
        in_specs=[smem, smem, smem, anywhere],
        out_specs=(anywhere, anywhere, smem),
        scratch_shapes=[
            pltpu.SMEM((lay.reach,), jnp.int32),
            pltpu.SMEM((lay.reach,), jnp.int32),
            pltpu.SMEM((send_count,), jnp.int32),
            pltpu.SemaphoreType.DMA((send_count + lay.items,)),
        ],
        name="prepare",
    )(partner, counts, where, in_blocks)

    received = lax.all_to_all(
        sent.reshape(lay.reach, lay.slots * BLOCK, width), "reach", 0, 0, tiled=True
    ).reshape(send_count, BLOCK, width)
    prior_inputs = lax.ppermute(prior, "day", [(d, d + 1) for d in range(day_total - 1)])

    def at_item(item, tab):
        return (item, 0, 0)

    def at_block(item, tab):
        return (tab[lay.block_of + item], 0, 0)

    def at_recv(item, tab):
        return (tab[lay.recv_of + item], 0, 0)

    def at_home(item, tab):
        place = tab[lay.recv_of + item]
        return (lax.div(place, lay.slots), 0, lax.rem(place, lay.slots), 0, 0)

    def fixed(item, tab):
        return (0, 0)

    full_block = (1, BLOCK, width)
    half_block = (1, BLOCK, half)
    weights_block = (4 * GROUP, width)
    flops = 2 * lay.items * (23 * BLOCK * width * width + 24 * BLOCK * 3 * BLOCK * 512)
    keep, swap, same, cross, home, grad_mine, grad_other = pl.pallas_call(
        lambda *refs: attention_kernel(lay, *refs),
        grid_spec=pltpu.PrefetchScalarGridSpec(
            num_scalar_prefetch=1,
            grid=(lay.items,),
            in_specs=[
                pl.BlockSpec(full_block, at_block),
                pl.BlockSpec(full_block, at_block),
                pl.BlockSpec(full_block, at_recv),
                pl.BlockSpec(full_block, at_item),
                pl.BlockSpec(weights_block, fixed),
                pl.BlockSpec(weights_block, fixed),
            ],
            out_specs=(
                pl.BlockSpec(half_block, at_item),
                pl.BlockSpec(half_block, at_item),
                pl.BlockSpec(half_block, at_item),
                pl.BlockSpec(half_block, at_item),
                pl.BlockSpec((1, CORES, 1, BLOCK, half), at_home),
                pl.BlockSpec(weights_block, fixed),
                pl.BlockSpec(weights_block, fixed),
            ),
        ),
        out_shape=(
            jax.ShapeDtypeStruct((lay.items, BLOCK, half), F32),
            jax.ShapeDtypeStruct((lay.items, BLOCK, half), F32),
            jax.ShapeDtypeStruct((lay.items, BLOCK, half), BF16),
            jax.ShapeDtypeStruct((lay.items, BLOCK, half), BF16),
            jax.ShapeDtypeStruct((lay.reach, CORES, lay.slots, BLOCK, half), BF16),
            jax.ShapeDtypeStruct(weights_block, F32),
            jax.ShapeDtypeStruct(weights_block, F32),
        ),
        compiler_params=pltpu.CompilerParams(vmem_limit_bytes=32 << 20),
        cost_estimate=pl.CostEstimate(
            flops=flops, bytes_accessed=8 << 20, transcendentals=lay.items * 8 * BLOCK * 3 * BLOCK
        ),
        name="attention",
    )(tab, in_blocks, up_blocks, received, prior_inputs, pack, pack_other)

    came_home = lax.all_to_all(
        home.reshape(lay.reach * CORES, lay.slots * BLOCK, half),
        ("reach", "head"),
        0,
        0,
        tiled=True,
    ).reshape(lay.reach * CORES * lay.slots, BLOCK, half)
    grad_swapped = lax.ppermute(grad_other, "head", swap_cores)
    swapped = lax.ppermute(swap, "head", swap_cores)
    same_came = lax.ppermute(
        same, "day", [(d + 1, d) for d in range(day_total - 1)]
    )
    cross_came = lax.ppermute(
        cross,
        ("day", "head"),
        [
            ((d + 1) * CORES + c, d * CORES + 1 - c)
            for d in range(day_total - 1)
            for c in range(CORES)
        ],
    )
    parts = lay.reach * day_total
    grad_rows = 4 * GROUP
    shares = (grad_mine + grad_swapped).astype(BF16).reshape(parts, grad_rows // parts, width)
    shares = lax.all_to_all(shares, ("reach", "day"), 0, 0, tiled=True)
    share = jnp.sum(shares.astype(F32), axis=0)
    grads = lax.all_gather(share, ("reach", "day"), axis=0, tiled=True)

    back_blocks = pl.pallas_call(
        lambda *refs: gather_kernel(lay, *refs),
        out_shape=jax.ShapeDtypeStruct((blocks_dev, BLOCK, half), BF16),
        in_specs=[smem] + [in_vmem] * 5,
        out_specs=in_vmem,
        compiler_params=pltpu.CompilerParams(vmem_limit_bytes=16 << 20),
        name="assemble",
    )(tab, keep, swapped, same_came, cross_came, came_home)
    return (
        back_blocks.reshape(1, rows_dev, half),
        grads[256:384].T,
        grads[0:256, :GROUP],
        grads[0:256, GROUP:],
        grads[384:512],
    )


def solution(mesh):
    placed = (
        P(("groups", "day"), "reach", None),
        P(("groups", "day"), "reach", None),
        P(None, "head"),
        P(None, "head"),
        P(None, "head"),
        P("head", None),
        P("groups"),
        P("groups"),
    )
    return jax.shard_map(
        on_device,
        mesh=mesh,
        in_specs=placed,
        out_specs=(
            P(("groups", "day"), "reach", "head"),
            P("groups", "head"),
            P("groups", "head"),
            P("groups", "head"),
            P(("groups", "head"), None),
        ),
        check_vma=False,
    )
```

time: 450 us -> 190 us (0.42)
  matrix products: 196 us -> 0 us
  waiting for transfers between devices: 135 us -> 20.7 us
  Pallas kernels: 0 us -> 81.7 us
  blocking collectives: 0 us -> 56.8 us
  local copies, waits for them, and re-layouts: 65.4 us -> 11 us
  between operations: 15.8 us -> 0.8 us
  starting transfers between devices: 28.1 us -> 16.8 us
  other arithmetic: 7.58 us -> 1.67 us
    dot_general x39 -> x0, matrix products: 184 us -> none  [the longest x4 63.6 us: attn_back(): jnp.einsum('ghqk,gkhd->gqhd', back_logits, key_heads, preferred_element_t...]
    pallas_call x0 -> x3, Pallas kernels: none -> 81.7 us  [the longest x1 52.1 us: on_device(): pl.pallas_call(lambda *refs: prepare_kernel(lay, *refs), out_shape=(jax.S...]
    psum x1 -> x0, waiting for transfers between devices: 69.9 us -> none  [on_device(): lax.psum((weight_terms[0], weight_terms[1], weight_terms[2], weight_terms...]
    all_gather x0 -> x1, blocking collectives: none -> 44 us  [on_device(): grads = lax.all_gather(share, ('reach', 'day'), axis=0, tiled=True)]
    all_to_all x4 -> x2, waiting for transfers between devices: 48.5 us -> 10.2 us  [the longest x1 10.2 us: on_device(): lax.all_to_all(sent.reshape(lay.reach, lay.slots * BLOCK, width), 'reach'...]
    dynamic_update_slice x40 -> x0, local copies, waits for them, and re-layouts: 25 us -> none  [on_device(): lax.map(both_passes, (grouped(query_items), grouped(all_keys), grouped(al...]
    dynamic_slice x25 -> x0, local copies, waits for them, and re-layouts: 16.8 us -> none  [the longest x24 16.7 us: on_device(): lax.map(both_passes, (grouped(query_items), grouped(all_keys), grouped(al...]
    all_to_all x0 -> x1, blocking collectives: none -> 12.8 us  [on_device(): shares = lax.all_to_all(shares, ('reach', 'day'), 0, 0, tiled=True)]
  transfers between devices with their start and end apart: 10 -> 8, of which waited for: 6 -> 4; matrix products, arithmetic and copies ran while one was open for 8% -> 2% of each run, Pallas kernels for 0% -> 0%
where the time goes in v1:
time: 190 us; the launch traced here: 189 us
  Pallas kernels  81.7 us (43%)
  blocking collectives  56.8 us (30%)
  waiting for transfers between devices  20.7 us (11%)
  starting transfers between devices  16.8 us (9%)
  local copies, waits for them, and re-layouts  11 us (6%)
    pallas_call x1, Pallas kernels, on_device(): pl.pallas_call(lambda *refs: prepare_kernel(lay, *refs), out_shape=(jax.S...  52.1 us
    all_gather x1, blocking collectives, on_device(): grads = lax.all_gather(share, ('reach', 'day'), axis=0, tiled=True)  44 us
    pallas_call x1, Pallas kernels, on_device(): pl.pallas_call(lambda *refs: attention_kernel(lay, *refs), grid_spec=pltp...  27.9 us
    all_to_all x1, blocking collectives, on_device(): shares = lax.all_to_all(shares, ('reach', 'day'), 0, 0, tiled=True)  12.8 us
    all_to_all x1, waiting for transfers between devices, on_device(): lax.all_to_all(sent.reshape(lay.reach, lay.slots * BLOCK, width), 'reach'...  10.2 us
    unnamed x32, local copies, waits for them, and re-layouts  8.69 us
    ppermute x1, waiting for transfers between devices, on_device(): lax.ppermute(prior, 'day', [(d, d + 1) for d in range(day_total - 1)])  7.03 us
    all_to_all x1, starting transfers between devices, on_device(): lax.all_to_all(sent.reshape(lay.reach, lay.slots * BLOCK, width), 'reach'...  6.46 us
  transfers between devices with their start and end apart: 8, of which 4 were waited for; matrix products, arithmetic and copies ran while one was open for 2% of the time, Pallas kernels for 0%

profile of v1, /device:TPU:0, one launch (start us, length us, event | category | flops | bytes accessed | tf_op | source)
XLA Modules:
  0.0 189.4 jit_solution(7905983948406979334)
XLA Ops:
  0.6 0.6 pad_add_fusion.refs_2_
  1.2 52.1 %prepare.1 = (bf16[16,128,256]{2,1,0:T(8,128)(2,1)}, bf16[8,128,256]{2,1,0:T(8,128)(2,1)}, s32[128]{0:T(128)}) custom-call(s32[64]{0:T(128)} %refs_0_.1, s32[64]{0:T(128)} %refs_1_.1, s32[3]{0:T(128)} %pad_add_fusion.refs_2_, bf16[16,128,256]{2,1,0:T(8,128)(2,1)} %bitcast.17), custom_call_target="tpu_custom_call" | custom-call | tf_op jit(solution)/shard_map/prepare/pallas_call | solution.py:304
  53.3 0.0 copy-start.10
  53.3 0.0 copy-start
  53.3 6.5 %all-to-all-start = ((bf16[4,512,256]{2,1,0:T(8,128)(2,1)}), bf16[4,512,256]{2,1,0:T(8,128)(2,1)S(1)}, u32[]{:S(2)}, u32[]{:S(2)}) async-start(bf16[4,512,256]{2,1,0:T(8,128)(2,1)} %bitcast.22), calls=%async_computation | async-start | bytes 2097152 | tf_op jit(solution)/shard_map/all_to_all | solution.py:322
  59.8 0.0 copy-start.11
  59.8 3.5 %collective-permute-start = (bf16[8,128,256]{2,1,0:T(8,128)(2,1)}, bf16[8,128,256]{2,1,0:T(8,128)(2,1)S(1)}, u32[]{:S(2)}, u32[]{:S(2)}) collective-permute-start(bf16[8,128,256]{2,1,0:T(8,128)(2,1)} %get-tuple-element.17), channel_id=1, source_target_pairs={{0,2},{1,3},{4,6},{5,7},{8,10},{9,11},{12,14},{13,15},{16,18},{17,... | collective-permute-start | bytes 1572872 | tf_op jit(solution)/shard_map/ppermute | solution.py:325
  63.3 0.0 copy-done.10
  63.3 0.1 copy.15
  63.5 0.0 copy-done.11
  63.5 0.0 copy-start.12
  63.5 0.1 copy.13
  63.6 0.7 copy-done.12
  64.3 0.1 copy.14
  64.4 0.7 copy-done.13
  65.2 0.1 collective-permute-start.1
  65.2 1.5 collective-permute-done.1.refs_6_
  66.8 0.7 copy-done.7
  67.5 7.0 %collective-permute-done.refs_4_ = bf16[8,128,256]{2,1,0:T(8,128)(2,1)S(1)} collective-permute-done((bf16[8,128,256]{2,1,0:T(8,128)(2,1)}, bf16[8,128,256]{2,1,0:T(8,128)(2,1)S(1)}, u32[]{:S(2)}, u32[]{:S(2)}) %collective-permute-start) | collective-permute-done | bytes 524320 | tf_op jit(solution)/shard_map/ppermute | solution.py:325
  74.5 0.8 copy-done.3
  75.3 10.2 %all-to-all-done = bf16[4,512,256]{2,1,0:T(8,128)(2,1)S(1)} async-done(((bf16[4,512,256]{2,1,0:T(8,128)(2,1)}), bf16[4,512,256]{2,1,0:T(8,128)(2,1)S(1)}, u32[]{:S(2)}, u32[]{:S(2)}) %all-to-all-start) | async-done | bytes 1048608 | tf_op jit(solution)/shard_map/all_to_all | solution.py:322
  85.5 0.0 copy-done
  85.5 0.7 copy-done.1
  86.2 1.2 copy-done.2
  87.4 1.0 copy-done.4
  88.4 0.9 copy-done.8
  89.4 27.9 %attention.1 = (f32[8,128,128]{2,1,0:T(8,128)S(1)}, f32[8,128,128]{2,1,0:T(8,128)S(1)}, bf16[8,128,128]{2,1,0:T(8,128)(2,1)}, bf16[8,128,128]{2,1,0:T(8,128)(2,1...) custom-call(s32[128]{0:T(128)S(1)} %copy-done.1, ...), custom_call_target="tpu_custom_call" | custom-call | flops 12750684160 | bytes 8388608 | tf_op jit(solution)/shard_map/attention/pallas_call | solution.py:347
  117.2 0.0 collective-permute-start.5
  117.2 1.9 %collective-permute-done.5 = f32[512,256]{1,0:T(8,128)S(1)} collective-permute-done((f32[512,256]{1,0:T(8,128)S(1)}, f32[512,256]{1,0:T(8,128)S(1)}, u32[]{:S(2)}, u32[]{:S(2)}) %collective-permute-start.5) | collective-permute-done | bytes 524320 | tf_op jit(solution)/shard_map/ppermute | solution.py:393
  119.1 0.1 add_convert_fusion
  119.2 0.0 copy-done.5
  119.2 12.8 %all_to_all.15 = bf16[8,64,256]{2,1,0:T(8,128)(2,1)} all-to-all(bf16[8,64,256]{2,1,0:T(8,128)(2,1)S(1)} %bitcast.21), channel_id=1, replica_groups=mesh['groups'=2,'reach'=4,'day'=2,'head'=2] {'reach','day'}, dimensions={0} | all-to-all | bytes 524288 | tf_op jit(solution)/shard_map/all_to_all | solution.py:410
  132.0 3.7 %all-to-all-start.1 = ((bf16[8,512,128]{2,1,0:T(8,128)(2,1)}), bf16[8,512,128]{2,1,0:T(8,128)(2,1)S(1)}, u32[]{:S(2)}, u32[]{:S(2)}) async-start(bf16[8,512,128]{2,1,0:T(8,128)(2,1)} %bitcast.10), calls=%async_computation.1 | async-start | bytes 2097152 | tf_op jit(solution)/shard_map/all_to_all | solution.py:386
  135.7 1.3 collective-permute-start.3
  137.0 0.0 copy-done.6
  137.0 1.3 collective-permute-start.4
  138.3 0.5 collective-permute-start.2
  138.8 1.0 convert_reduce_fusion
  139.8 44.0 %all_gather.3 = f32[512,256]{1,0:T(8,128)S(1)} all-gather(f32[64,256]{1,0:T(8,128)S(1)} %convert_reduce_fusion), channel_id=1, replica_groups=mesh['groups'=2,'reach'=4,'day'=2,'head'=2] {'reach','day'}, dimensions={0}, use_global_device_ids=true | all-gather | bytes 589824 | tf_op jit(solution)/shard_map/all_gather | solution.py:412
  183.8 0.8 copy-done.9
  184.5 0.7 fusion
  185.2 0.8 copy.16
  186.0 1.7 fusion.1
  187.7 0.0 collective-permute-done.3.refs_3_
  187.7 0.0 collective-permute-done.4.refs_4_
  187.7 0.0 collective-permute-done.2.refs_2_
  187.7 0.0 all-to-all-done.1
  187.7 1.8 assemble.1
  (11 shorter events, 0.0 us)
Async XLA Ops:
  53.3 10.0 %copy-start.10 = (bf16[256,128]{1,0:T(8,128)(2,1)S(1)}, bf16[256,128]{1,0:T(8,128)(2,1)}, u32[]{:S(2)}) copy-start(bf16[256,128]{1,0:T(8,128)(2,1)} %param.10) | copy-start | bytes 196612
  53.3 32.2 %copy-start = (bf16[1,2048,256]{2,1,0:T(8,128)(2,1)S(1)}, bf16[1,2048,256]{2,1,0:T(8,128)(2,1)}, u32[]{:S(2)}) copy-start(bf16[1,2048,256]{2,1,0:T(8,128)(2,1)} %param.8) | copy-start | bytes 3145732
  53.3 32.2 %all-to-all-start = ((bf16[4,512,256]{2,1,0:T(8,128)(2,1)}), bf16[4,512,256]{2,1,0:T(8,128)(2,1)S(1)}, u32[]{:S(2)}, u32[]{:S(2)}) async-start(bf16[4,512,256]{2,1,0:T(8,128)(2,1)} %bitcast.22), calls=%async_computation | async-start | bytes 2097152 | tf_op jit(solution)/shard_map/all_to_all | solution.py:322
  59.8 3.7 %copy-start.11 = (bf16[256,128]{1,0:T(8,128)(2,1)S(1)}, bf16[256,128]{1,0:T(8,128)(2,1)}, u32[]{:S(2)}) copy-start(bf16[256,128]{1,0:T(8,128)(2,1)} %param.11) | copy-start | bytes 196612
  59.8 14.7 %collective-permute-start = (bf16[8,128,256]{2,1,0:T(8,128)(2,1)}, bf16[8,128,256]{2,1,0:T(8,128)(2,1)S(1)}, u32[]{:S(2)}, u32[]{:S(2)}) collective-permute-start(bf16[8,128,256]{2,1,0:T(8,128)(2,1)} %get-tuple-element.17), channel_id=1, source_target_pairs={{0,2},{1,3},{4,6},{5,7},{8,10},{9,11},{12,14},{13,15},{16,18},{17,... | collective-permute-start | bytes 1572872 | tf_op jit(solution)/shard_map/ppermute | solution.py:325
  63.5 0.8 copy-start.12
  64.3 0.8 copy-start.13
  65.2 1.6 collective-permute-start.1
  66.8 0.7 copy-start.7
  74.5 0.8 copy-start.3
  85.5 0.7 copy-start.1
  86.2 1.2 copy-start.2
  87.4 1.0 copy-start.4
  88.4 0.9 copy-start.8
  117.2 2.0 %copy-start.5 = (bf16[8,128,128]{2,1,0:T(8,128)(2,1)}, bf16[8,128,128]{2,1,0:T(8,128)(2,1)S(1)}, u32[]{:S(2)}) copy-start(bf16[8,128,128]{2,1,0:T(8,128)(2,1)S(1)} %get-tuple-element.21) | copy-start | bytes 786436
  117.2 1.9 %collective-permute-start.5 = (f32[512,256]{1,0:T(8,128)S(1)}, f32[512,256]{1,0:T(8,128)S(1)}, u32[]{:S(2)}, u32[]{:S(2)}) collective-permute-start(f32[512,256]{1,0:T(8,128)S(1)} %get-tuple-element.24), channel_id=1, source_target_pairs={{0,1},{1,0},{2,3},{3,2},{4,5},{5,4},{6,7},{7,6},{8,9},{9,8},{10,11... | collective-permute-start | bytes 1572872 | tf_op jit(solution)/shard_map/ppermute | solution.py:393
  132.0 5.0 %copy-start.6 = (bf16[8,128,128]{2,1,0:T(8,128)(2,1)S(1)}, bf16[8,128,128]{2,1,0:T(8,128)(2,1)}, u32[]{:S(2)}) copy-start(bf16[8,128,128]{2,1,0:T(8,128)(2,1)} %copy-done.5) | copy-start | bytes 786436
  132.0 55.7 %all-to-all-start.1 = ((bf16[8,512,128]{2,1,0:T(8,128)(2,1)}), bf16[8,512,128]{2,1,0:T(8,128)(2,1)S(1)}, u32[]{:S(2)}, u32[]{:S(2)}) async-start(bf16[8,512,128]{2,1,0:T(8,128)(2,1)} %bitcast.10), calls=%async_computation.1 | async-start | bytes 2097152 | tf_op jit(solution)/shard_map/all_to_all | solution.py:386
  135.7 51.9 %collective-permute-start.3 = (bf16[8,128,128]{2,1,0:T(8,128)(2,1)}, bf16[8,128,128]{2,1,0:T(8,128)(2,1)S(1)}, u32[]{:S(2)}, u32[]{:S(2)}) collective-permute-start(bf16[8,128,128]{2,1,0:T(8,128)(2,1)} %get-tuple-element.20), channel_id=1, source_target_pairs={{2,0},{3,1},{6,4},{7,5},{10,8},{11,9},{14,12},{15,13},{18,16},{19,... | collective-permute-start | bytes 786440 | tf_op jit(solution)/shard_map/ppermute | solution.py:395
  137.0 50.6 %collective-permute-start.4 = (bf16[8,128,128]{2,1,0:T(8,128)(2,1)S(1)}, bf16[8,128,128]{2,1,0:T(8,128)(2,1)S(1)}, u32[]{:S(2)}, u32[]{:S(2)}) collective-permute-start(bf16[8,128,128]{2,1,0:T(8,128)(2,1)S(1)} %copy-done.6), channel_id=1, source_target_pairs={{2,1},{3,0},{6,5},{7,4},{10,9},{11,8},{14,13},{15,12},{18,17},{19,... | collective-permute-start | bytes 786440 | tf_op jit(solution)/shard_map/ppermute | solution.py:398
  138.3 49.3 %collective-permute-start.2 = (f32[8,128,128]{2,1,0:T(8,128)S(1)}, f32[8,128,128]{2,1,0:T(8,128)S(1)}, u32[]{:S(2)}, u32[]{:S(2)}) collective-permute-start(f32[8,128,128]{2,1,0:T(8,128)S(1)} %get-tuple-element.19), channel_id=1, source_target_pairs={{0,1},{1,0},{2,3},{3,2},{4,5},{5,4},{6,7},{7,6},{8,9},{9,8},{10,11... | collective-permute-start | bytes 1572872 | tf_op jit(solution)/shard_map/ppermute | solution.py:394
  183.8 0.8 copy-start.9

commit v2 on v1

--- a/solution.py
+++ b/solution.py
@@ -9,6 +9,8 @@
 BLOCK = 128
 GROUP = 128
 CORES = 2
+CHUNKS = 2
+WORKERS = CORES * CHUNKS
 F32 = jnp.float32
 BF16 = jnp.bfloat16
 LOG2E = 1.4426950408889634
@@ -18,8 +20,10 @@
     def __init__(self, blocks_dev, reach_total):
         self.blocks = blocks_dev
         self.items = blocks_dev // CORES
+        self.chunk_items = self.items // CHUNKS
         self.reach = reach_total
-        self.slots = max(1, blocks_dev // reach_total)
+        self.slots = max(1, 2 * blocks_dev // reach_total // WORKERS)
+        self.places = reach_total * self.slots
         self.block_of = 0
         self.recv_of = self.items
         self.count_own = 2 * self.items
@@ -27,12 +31,13 @@
         self.owner_of = 4 * self.items
         self.item_of = self.owner_of + blocks_dev
         self.home_of = self.item_of + blocks_dev
-        self.core = self.home_of + blocks_dev
+        self.chunk_of = self.home_of + blocks_dev
+        self.core = self.chunk_of + blocks_dev
         self.later_day = self.core + 1
         self.size = -(-(self.core + 2) // 128) * 128
 
 
-def prepare_kernel(lay, partner, counts, where, inputs, sent, prior, tab, start, used, picks, sems):
+def prepare_kernel(lay, partner, counts, where, inputs, sent_a, sent_b, prior, tab, start, used, picks):
     bd, slots = lay.blocks, lay.slots
     reach_pos, core = where[0], where[1]
 
@@ -63,11 +68,12 @@
         rank = used[source]
         used[source] = rank + 1
         place = start[source] + rank
-        owner = lax.bitwise_and(place, 1)
-        item = lax.div(place, 2)
-        slot = jnp.minimum(lax.div(rank, 2), slots - 1)
+        owner = lax.rem(place, CORES)
+        chunk = lax.rem(lax.div(place, CORES), CHUNKS)
+        item = chunk * lay.chunk_items + lax.div(place, WORKERS)
+        slot = jnp.minimum(lax.div(rank, WORKERS), slots - 1)
         tab[lay.owner_of + index] = owner
-        tab[lay.item_of + index] = item
+        tab[lay.item_of + index] = lax.div(place, WORKERS) * CHUNKS + chunk
 
         @pl.when(owner == core)
         def _():
@@ -86,7 +92,7 @@
         picks[index] = 0
         return carry
 
-    lax.fori_loop(0, lay.reach * slots, clear_picks, 0)
+    lax.fori_loop(0, CHUNKS * lay.places, clear_picks, 0)
 
     def one_reach(peer, carry):
         def before(index, total):
@@ -101,14 +107,17 @@
 
             @pl.when(hit)
             def _():
-                owner = lax.bitwise_and(base + rank, 1)
-                slot = jnp.minimum(lax.div(rank, 2), slots - 1)
+                place = base + rank
+                owner = lax.rem(place, CORES)
+                chunk = lax.rem(lax.div(place, CORES), CHUNKS)
+                slot = jnp.minimum(lax.div(rank, WORKERS), slots - 1)
                 local = lax.rem(wanted, bd)
                 tab[lay.home_of + local] = (peer * CORES + owner) * slots + slot
+                tab[lay.chunk_of + local] = chunk
 
                 @pl.when(owner == core)
                 def _():
-                    picks[peer * slots + slot] = local
+                    picks[chunk * lay.places + peer * slots + slot] = local
 
             return rank + jnp.where(hit, 1, 0)
 
@@ -117,23 +126,21 @@
 
     lax.fori_loop(0, lay.reach, one_reach, 0)
 
-    copies = []
-    for place in range(lay.reach * slots):
-        copies.append(
-            pltpu.make_async_copy(inputs.at[picks[place]], sent.at[place], sems.at[place])
-        )
-    for item in range(lay.items):
-        copies.append(
-            pltpu.make_async_copy(
-                inputs.at[tab[lay.block_of + item]],
-                prior.at[item],
-                sems.at[lay.reach * slots + item],
-            )
-        )
-    for copy in copies:
-        copy.start()
-    for copy in copies:
-        copy.wait()
+    def pick_a(place, carry):
+        sent_a[place] = inputs[picks[place]]
+        return carry
+
+    def pick_b(place, carry):
+        sent_b[place] = inputs[picks[lay.places + place]]
+        return carry
+
+    def pick_prior(item, carry):
+        prior[item] = inputs[tab[lay.block_of + item]]
+        return carry
+
+    lax.fori_loop(0, lay.places, pick_a, 0)
+    lax.fori_loop(0, lay.places, pick_b, 0)
+    lax.fori_loop(0, lay.items, pick_prior, 0)
 
 
 def dot(left, right):
@@ -146,6 +153,7 @@
 
 def attention_kernel(
     lay,
+    chunk,
     tab,
     own_ref,
     up_ref,
@@ -153,25 +161,29 @@
     prior_ref,
     mine_ref,
     other_ref,
-    keep_ref,
-    swap_ref,
-    same_ref,
-    cross_ref,
-    home_ref,
-    grad_mine_ref,
-    grad_other_ref,
+    *refs,
 ):
-    item = pl.program_id(0)
+    if chunk:
+        start_mine_ref, start_other_ref = refs[0], refs[1]
+        carried_refs = refs[2:6]
+        refs = refs[6:]
+    keep_ref, swap_ref, same_ref, cross_ref, home_ref, grad_mine_ref, grad_other_ref = refs
+    step = pl.program_id(0)
+    item = step + chunk * lay.chunk_items
     core = tab[lay.core]
     factor = HD ** (-0.5)
     own, up = own_ref[0], up_ref[0]
     key_inputs = jnp.concatenate([own, partner_ref[0], prior_ref[0]], axis=0)
     width = own.shape[1]
 
-    @pl.when(item == 0)
+    @pl.when(step == 0)
     def _():
-        grad_mine_ref[...] = jnp.zeros_like(grad_mine_ref)
-        grad_other_ref[...] = jnp.zeros_like(grad_other_ref)
+        if chunk:
+            grad_mine_ref[...] = start_mine_ref[...]
+            grad_other_ref[...] = start_other_ref[...]
+        else:
+            grad_mine_ref[...] = jnp.zeros_like(grad_mine_ref)
+            grad_other_ref[...] = jnp.zeros_like(grad_other_ref)
 
     def eye(size):
         rows = lax.broadcasted_iota(jnp.int32, (size, size), 0)
@@ -250,27 +262,137 @@
     prior_term = back_inputs[2 * BLOCK :]
     half = width // 2
     first_core = core == 0
-    keep_ref[0] = jnp.where(first_core, own_term[:, :half], own_term[:, half:])
-    swap_ref[0] = jnp.where(first_core, own_term[:, half:], own_term[:, :half])
-    same_ref[0] = jnp.where(first_core, prior_term[:, :half], prior_term[:, half:]).astype(BF16)
-    cross_ref[0] = jnp.where(first_core, prior_term[:, half:], prior_term[:, :half]).astype(BF16)
+    terms = (
+        jnp.where(first_core, own_term[:, :half], own_term[:, half:]),
+        jnp.where(first_core, own_term[:, half:], own_term[:, :half]),
+        jnp.where(first_core, prior_term[:, :half], prior_term[:, half:]).astype(BF16),
+        jnp.where(first_core, prior_term[:, half:], prior_term[:, :half]).astype(BF16),
+    )
+    for place, (term_ref, term) in enumerate(zip((keep_ref, swap_ref, same_ref, cross_ref), terms)):
+        if chunk:
+            term_ref[0, 0] = carried_refs[place][0]
+            term_ref[0, 1] = term
+        else:
+            term_ref[0] = term
     home_ref[0, 0, 0] = partner_term[:, :half]
     home_ref[0, 1, 0] = partner_term[:, half:]
 
 
-def gather_kernel(lay, tab, keep, swapped, same, cross, home, out):
+def gather_kernel(lay, tab, keep, swapped, same, cross, home_a, home_b, out):
     core = tab[lay.core]
 
     def one(block, carry):
         item = tab[lay.item_of + block]
         mine = tab[lay.owner_of + block] == core
+        place = tab[lay.home_of + block]
+        first = tab[lay.chunk_of + block] == 0
         total = jnp.where(mine, keep[item], swapped[item])
         total += jnp.where(mine, same[item].astype(F32), cross[item].astype(F32))
-        total += home[tab[lay.home_of + block]].astype(F32)
+        total += jnp.where(first, home_a[place].astype(F32), home_b[place].astype(F32))
         out[block] = total.astype(BF16)
         return carry
 
     lax.fori_loop(0, lay.blocks, one, 0)
+
+
+def attend(lay, chunk, tab, in_blocks, up_blocks, received, prior_inputs, pack, pack_other, carried):
+    width = in_blocks.shape[-1]
+    half = width // 2
+    offset = chunk * lay.chunk_items
+
+    def at_item(step, tab):
+        return (offset + step, 0, 0)
+
+    def at_block(step, tab):
+        return (tab[lay.block_of + offset + step], 0, 0)
+
+    def at_recv(step, tab):
+        return (tab[lay.recv_of + offset + step], 0, 0)
+
+    def at_home(step, tab):
+        place = tab[lay.recv_of + offset + step]
+        return (lax.div(place, lay.slots), 0, lax.rem(place, lay.slots), 0, 0)
+
+    def fixed(step, tab):
+        return (0, 0)
+
+    full_block = (1, BLOCK, width)
+    half_block = (1, BLOCK, half)
+    weights_block = (4 * GROUP, width)
+    in_specs = [
+        pl.BlockSpec(full_block, at_block),
+        pl.BlockSpec(full_block, at_block),
+        pl.BlockSpec(full_block, at_recv),
+        pl.BlockSpec(full_block, at_item),
+        pl.BlockSpec(weights_block, fixed),
+        pl.BlockSpec(weights_block, fixed),
+    ]
+    operands = [in_blocks, up_blocks, received, prior_inputs, pack, pack_other]
+    term_shape = (lay.chunk_items, BLOCK, half)
+    term_spec = pl.BlockSpec(half_block, lambda step, tab: (step, 0, 0))
+    if chunk:
+        in_specs += [pl.BlockSpec(weights_block, fixed)] * 2 + [term_spec] * 4
+        operands += [carried[5], carried[6]] + list(carried[:4])
+        term_shape = (lay.chunk_items, CHUNKS, BLOCK, half)
+        term_spec = pl.BlockSpec((1, CHUNKS, BLOCK, half), lambda step, tab: (step, 0, 0, 0))
+    pieces = lay.chunk_items
+    flops = 2 * pieces * (23 * BLOCK * width * width + 24 * BLOCK * 3 * BLOCK * 512)
+    return pl.pallas_call(
+        lambda *refs: attention_kernel(lay, chunk, *refs),
+        grid_spec=pltpu.PrefetchScalarGridSpec(
+            num_scalar_prefetch=1,
+            grid=(pieces,),
+            in_specs=in_specs,
+            out_specs=(
+                *[term_spec] * 4,
+                pl.BlockSpec((1, CORES, 1, BLOCK, half), at_home),
+                pl.BlockSpec(weights_block, fixed),
+                pl.BlockSpec(weights_block, fixed),
+            ),
+        ),
+        out_shape=(
+            jax.ShapeDtypeStruct(term_shape, F32),
+            jax.ShapeDtypeStruct(term_shape, F32),
+            jax.ShapeDtypeStruct(term_shape, BF16),
+            jax.ShapeDtypeStruct(term_shape, BF16),
+            jax.ShapeDtypeStruct((lay.reach, CORES, lay.slots, BLOCK, half), BF16),
+            jax.ShapeDtypeStruct(weights_block, F32),
+            jax.ShapeDtypeStruct(weights_block, F32),
+        ),
+        compiler_params=pltpu.CompilerParams(vmem_limit_bytes=32 << 20),
+        cost_estimate=pl.CostEstimate(
+            flops=flops, bytes_accessed=5 << 20, transcendentals=pieces * 8 * BLOCK * 3 * BLOCK
+        ),
+        name=f"attention_{chunk}",
+    )(tab, *operands)
+
+
+def exchanged(value, axis, bit):
+    count = lax.axis_size(axis)
+    return lax.ppermute(value, axis, [(place, place ^ bit) for place in range(count)])
+
+
+def summed_over(value, axis, bit):
+    while bit < lax.axis_size(axis):
+        low = value.astype(BF16)
+        value = low.astype(F32) + exchanged(low, axis, bit).astype(F32)
+        bit *= 2
+    return value
+
+
+def sum_gradients(total):
+    half = total.shape[0] // 2
+    low = total.astype(BF16)
+    first = lax.rem(lax.axis_index("day"), 2) == 0
+    kept = jnp.where(first, low[:half], low[half:])
+    given = jnp.where(first, low[half:], low[:half])
+    part = kept.astype(F32) + exchanged(given, "day", 1).astype(F32)
+    part = summed_over(part, "day", 2)
+    part = summed_over(part, "reach", 1).astype(BF16)
+    other = exchanged(part, "day", 1)
+    upper = jnp.where(first, part, other).astype(F32)
+    lower = jnp.where(first, other, part).astype(F32)
+    return upper, lower
 
 
 def on_device(
@@ -294,107 +416,61 @@
         ]
     )
     pack = jnp.concatenate([key_weight.T, value_weight.T, query_weight.T, output_weight], axis=0)
-    swap_cores = [(0, 1), (1, 0)]
-    pack_other = lax.ppermute(pack, "head", swap_cores)
+    pack_other = exchanged(pack, "head", 1)
 
     smem = pl.BlockSpec(memory_space=pltpu.SMEM)
-    anywhere = pl.BlockSpec(memory_space=pl.ANY)
     in_vmem = pl.BlockSpec(memory_space=pltpu.VMEM)
-    send_count = lay.reach * lay.slots
-    sent, prior, tab = pl.pallas_call(
+    sent_shape = jax.ShapeDtypeStruct((lay.places, BLOCK, width), BF16)
+    sent_a, sent_b, prior, tab = pl.pallas_call(
         lambda *refs: prepare_kernel(lay, *refs),
         out_shape=(
-            jax.ShapeDtypeStruct((send_count, BLOCK, width), BF16),
+            sent_shape,
+            sent_shape,
             jax.ShapeDtypeStruct((lay.items, BLOCK, width), BF16),
             jax.ShapeDtypeStruct((lay.size,), jnp.int32),
         ),
-        in_specs=[smem, smem, smem, anywhere],
-        out_specs=(anywhere, anywhere, smem),
+        in_specs=[smem, smem, smem, in_vmem],
+        out_specs=(in_vmem, in_vmem, in_vmem, smem),
         scratch_shapes=[
             pltpu.SMEM((lay.reach,), jnp.int32),
             pltpu.SMEM((lay.reach,), jnp.int32),
-            pltpu.SMEM((send_count,), jnp.int32),
-            pltpu.SemaphoreType.DMA((send_count + lay.items,)),
+            pltpu.SMEM((CHUNKS * lay.places,), jnp.int32),
         ],
+        compiler_params=pltpu.CompilerParams(vmem_limit_bytes=16 << 20),
         name="prepare",
     )(partner, counts, where, in_blocks)
 
-    received = lax.all_to_all(
-        sent.reshape(lay.reach, lay.slots * BLOCK, width), "reach", 0, 0, tiled=True
-    ).reshape(send_count, BLOCK, width)
+    def outward(sent):
+        return lax.all_to_all(
+            sent.reshape(lay.reach, lay.slots * BLOCK, width), "reach", 0, 0, tiled=True
+        ).reshape(lay.places, BLOCK, width)
+
+    def homeward(home):
+        return lax.all_to_all(
+            home.reshape(lay.reach * CORES, lay.slots * BLOCK, half),
+            ("reach", "head"),
+            0,
+            0,
+            tiled=True,
+        ).reshape(lay.reach * CORES * lay.slots, BLOCK, half)
+
+    received_a = outward(sent_a)
     prior_inputs = lax.ppermute(prior, "day", [(d, d + 1) for d in range(day_total - 1)])
-
-    def at_item(item, tab):
-        return (item, 0, 0)
-
-    def at_block(item, tab):
-        return (tab[lay.block_of + item], 0, 0)
-
-    def at_recv(item, tab):
-        return (tab[lay.recv_of + item], 0, 0)
-
-    def at_home(item, tab):
-        place = tab[lay.recv_of + item]
-        return (lax.div(place, lay.slots), 0, lax.rem(place, lay.slots), 0, 0)
-
-    def fixed(item, tab):
-        return (0, 0)
-
-    full_block = (1, BLOCK, width)
-    half_block = (1, BLOCK, half)
-    weights_block = (4 * GROUP, width)
-    flops = 2 * lay.items * (23 * BLOCK * width * width + 24 * BLOCK * 3 * BLOCK * 512)
-    keep, swap, same, cross, home, grad_mine, grad_other = pl.pallas_call(
-        lambda *refs: attention_kernel(lay, *refs),
-        grid_spec=pltpu.PrefetchScalarGridSpec(
-            num_scalar_prefetch=1,
-            grid=(lay.items,),
-            in_specs=[
-                pl.BlockSpec(full_block, at_block),
-                pl.BlockSpec(full_block, at_block),
-                pl.BlockSpec(full_block, at_recv),
-                pl.BlockSpec(full_block, at_item),
-                pl.BlockSpec(weights_block, fixed),
-                pl.BlockSpec(weights_block, fixed),
-            ],
-            out_specs=(
-                pl.BlockSpec(half_block, at_item),
-                pl.BlockSpec(half_block, at_item),
-                pl.BlockSpec(half_block, at_item),
-                pl.BlockSpec(half_block, at_item),
-                pl.BlockSpec((1, CORES, 1, BLOCK, half), at_home),
-                pl.BlockSpec(weights_block, fixed),
-                pl.BlockSpec(weights_block, fixed),
-            ),
-        ),
-        out_shape=(
-            jax.ShapeDtypeStruct((lay.items, BLOCK, half), F32),
-            jax.ShapeDtypeStruct((lay.items, BLOCK, half), F32),
-            jax.ShapeDtypeStruct((lay.items, BLOCK, half), BF16),
-            jax.ShapeDtypeStruct((lay.items, BLOCK, half), BF16),
-            jax.ShapeDtypeStruct((lay.reach, CORES, lay.slots, BLOCK, half), BF16),
-            jax.ShapeDtypeStruct(weights_block, F32),
-            jax.ShapeDtypeStruct(weights_block, F32),
-        ),
-        compiler_params=pltpu.CompilerParams(vmem_limit_bytes=32 << 20),
-        cost_estimate=pl.CostEstimate(
-            flops=flops, bytes_accessed=8 << 20, transcendentals=lay.items * 8 * BLOCK * 3 * BLOCK
-        ),
-        name="attention",
-    )(tab, in_blocks, up_blocks, received, prior_inputs, pack, pack_other)
-
-    came_home = lax.all_to_all(
-        home.reshape(lay.reach * CORES, lay.slots * BLOCK, half),
-        ("reach", "head"),
-        0,
-        0,
-        tiled=True,
-    ).reshape(lay.reach * CORES * lay.slots, BLOCK, half)
-    grad_swapped = lax.ppermute(grad_other, "head", swap_cores)
-    swapped = lax.ppermute(swap, "head", swap_cores)
-    same_came = lax.ppermute(
-        same, "day", [(d + 1, d) for d in range(day_total - 1)]
-    )
+    received_b = outward(sent_b)
+    shared = (prior_inputs, pack, pack_other)
+    first = attend(lay, 0, tab, in_blocks, up_blocks, received_a, *shared, None)
+    home_a = homeward(first[4])
+    keep, swap, same, cross, home, grad_mine, grad_other = attend(
+        lay, 1, tab, in_blocks, up_blocks, received_b, *shared, first
+    )
+    home_a, home, grad_other = lax.optimization_barrier((home_a, home, grad_other))
+    keep, swap, same, cross = (
+        term.reshape(lay.items, BLOCK, half) for term in (keep, swap, same, cross)
+    )
+    home_b = homeward(home)
+    grad_swapped = exchanged(grad_other, "head", 1)
+    swapped = exchanged(swap, "head", 1)
+    same_came = lax.ppermute(same, "day", [(d + 1, d) for d in range(day_total - 1)])
     cross_came = lax.ppermute(
         cross,
         ("day", "head"),
@@ -404,27 +480,22 @@
             for c in range(CORES)
         ],
     )
-    parts = lay.reach * day_total
-    grad_rows = 4 * GROUP
-    shares = (grad_mine + grad_swapped).astype(BF16).reshape(parts, grad_rows // parts, width)
-    shares = lax.all_to_all(shares, ("reach", "day"), 0, 0, tiled=True)
-    share = jnp.sum(shares.astype(F32), axis=0)
-    grads = lax.all_gather(share, ("reach", "day"), axis=0, tiled=True)
+    upper, lower = sum_gradients(grad_mine + grad_swapped)
 
     back_blocks = pl.pallas_call(
         lambda *refs: gather_kernel(lay, *refs),
         out_shape=jax.ShapeDtypeStruct((blocks_dev, BLOCK, half), BF16),
-        in_specs=[smem] + [in_vmem] * 5,
+        in_specs=[smem] + [in_vmem] * 6,
         out_specs=in_vmem,
         compiler_params=pltpu.CompilerParams(vmem_limit_bytes=16 << 20),
         name="assemble",
-    )(tab, keep, swapped, same_came, cross_came, came_home)
+    )(tab, keep, swapped, same_came, cross_came, home_a, home_b)
     return (
         back_blocks.reshape(1, rows_dev, half),
-        grads[256:384].T,
-        grads[0:256, :GROUP],
-        grads[0:256, GROUP:],
-        grads[384:512],
+        lower[:GROUP].T,
+        upper[:, :GROUP],
+        upper[:, GROUP:],
+        lower[GROUP:],
     )
 
 

time: 190 us -> 130 us (0.68)
  blocking collectives: 56.8 us -> 0 us
  Pallas kernels: 81.7 us -> 36.7 us
  starting transfers between devices: 16.8 us -> 35.2 us
  waiting for transfers between devices: 20.7 us -> 35.8 us
  local copies, waits for them, and re-layouts: 11 us -> 19 us
    pallas_call x2 -> x3, Pallas kernels: 79.9 us -> 34.9 us  [the longest x2 31 us: attend(): pl.pallas_call(lambda *refs: attention_kernel(lay, chunk, *refs), grid_sp...]
    all_gather x1 -> x0, blocking collectives: 44 us -> none  [on_device(): grads = lax.all_gather(share, ('reach', 'day'), axis=0, tiled=True)]
    ppermute x3 -> x7, waiting for transfers between devices: 3.43 us -> 18.5 us  [exchanged(): lax.ppermute(value, axis, [(place, place ^ bit) for place in range(count)])]
    all_to_all x1 -> x0, blocking collectives: 12.8 us -> none  [on_device(): shares = lax.all_to_all(shares, ('reach', 'day'), 0, 0, tiled=True)]
    all_to_all x2 -> x4, starting transfers between devices: 10.2 us -> 19.9 us  [the longest x2 10 us: homeward(): lax.all_to_all(home.reshape(lay.reach * CORES, lay.slots * BLOCK, half),...]
    unnamed x32 -> x58, local copies, waits for them, and re-layouts: 8.69 us -> 17.6 us
    ppermute x3 -> x7, starting transfers between devices: 0.53 us -> 9.12 us  [exchanged(): lax.ppermute(value, axis, [(place, place ^ bit) for place in range(count)])]
    ppermute x1, waiting for transfers between devices: 7.03 us -> 0.01 us  [on_device(): lax.ppermute(prior, 'day', [(d, d + 1) for d in range(day_total - 1)])]
  transfers between devices with their start and end apart: 8 -> 14, of which waited for: 4 -> 7; matrix products, arithmetic and copies ran while one was open for 2% -> 0% of each run, Pallas kernels for 0% -> 25%
where the time goes in v2:
time: 130 us; the launch traced here: 129 us
  Pallas kernels  36.7 us (28%)
  waiting for transfers between devices  35.8 us (28%)
  starting transfers between devices  35.2 us (27%)
  local copies, waits for them, and re-layouts  19 us (15%)
    pallas_call x2, Pallas kernels, attend(): pl.pallas_call(lambda *refs: attention_kernel(lay, chunk, *refs), grid_sp...  31 us
    ppermute x7, waiting for transfers between devices, exchanged(): lax.ppermute(value, axis, [(place, place ^ bit) for place in range(count)])  18.5 us
    unnamed x58, local copies, waits for them, and re-layouts  17.6 us
    all_to_all x2, waiting for transfers between devices, outward(): lax.all_to_all(sent.reshape(lay.reach, lay.slots * BLOCK, width), 'reach'...  10.4 us
    all_to_all x2, starting transfers between devices, homeward(): lax.all_to_all(home.reshape(lay.reach * CORES, lay.slots * BLOCK, half),...  10 us
    all_to_all x2, starting transfers between devices, outward(): lax.all_to_all(sent.reshape(lay.reach, lay.slots * BLOCK, width), 'reach'...  9.93 us
    ppermute x7, starting transfers between devices, exchanged(): lax.ppermute(value, axis, [(place, place ^ bit) for place in range(count)])  9.12 us
    ppermute x1, waiting for transfers between devices, on_device(): lax.ppermute(same, 'day', [(d + 1, d) for d in range(day_total - 1)])  4.59 us
  transfers between devices with their start and end apart: 14, of which 7 were waited for; matrix products, arithmetic and copies ran while one was open for 0% of the time, Pallas kernels for 25%

profile of v2, /device:TPU:0, one launch (start us, length us, event | category | flops | bytes accessed | tf_op | source)
XLA Modules:
  0.0 128.9 jit_solution(15658852769856816638)
XLA Ops:
  0.7 0.7 copy-done.2
  1.4 1.2 copy-done
  2.6 3.9 %prepare.1 = (bf16[8,128,256]{2,1,0:T(8,128)(2,1)}, bf16[8,128,256]{2,1,0:T(8,128)(2,1)}, bf16[8,128,256]{2,1,0:T(8,128)(2,1)S(1)}, s32[128]{0:T(128)S(1)}) custom-call(s32[64]{0:T(128)S(1)} %copy-done.2, s32[64]{0:T(128)S(1)} %copy-done.3, s32[3]{0:T(128)S(1)} %pad_add_fusion.refs_2_, bf16[16,128,256]{2,1,0:T(8,128)(2,1)S(1)} %bitcast.25), custom_call_target="tpu_custom_call" | custom-call | tf_op jit(solution)/shard_map/prepare/pallas_call | solution.py:424
  6.6 6.5 %all-to-all-start.1 = ((bf16[4,256,256]{2,1,0:T(8,128)(2,1)}), bf16[4,256,256]{2,1,0:T(8,128)(2,1)S(1)}, u32[]{:S(2)}, u32[]{:S(2)}) async-start(bf16[4,256,256]{2,1,0:T(8,128)(2,1)} %bitcast.10), calls=%async_computation.1 | async-start | bytes 1048576 | tf_op jit(solution)/shard_map/all_to_all | solution.py:444
  13.1 3.5 %collective-permute-start = (bf16[8,128,256]{2,1,0:T(8,128)(2,1)S(1)}, bf16[8,128,256]{2,1,0:T(8,128)(2,1)S(1)}, u32[]{:S(2)}, u32[]{:S(2)}) collective-permute-start(bf16[8,128,256]{2,1,0:T(8,128)(2,1)S(1)} %get-tuple-element.28), channel_id=1, source_target_pairs={{0,2},{1,3},{4,6},{5,7},{8,10},{9,11},{12,14},{13,15},{16,18},{17,... | collective-permute-start | bytes 1572872 | tf_op jit(solution)/shard_map/ppermute | solution.py:458
  16.6 0.1 copy.15
  16.8 0.1 copy.13
  16.9 0.1 copy.14
  17.1 10.4 %all-to-all-done.1 = bf16[4,256,256]{2,1,0:T(8,128)(2,1)S(1)} async-done(((bf16[4,256,256]{2,1,0:T(8,128)(2,1)}), bf16[4,256,256]{2,1,0:T(8,128)(2,1)S(1)}, u32[]{:S(2)}, u32[]{:S(2)}) %all-to-all-start.1) | async-done | bytes 524320 | tf_op jit(solution)/shard_map/all_to_all | solution.py:444
  27.5 3.5 %all-to-all-start = ((bf16[4,256,256]{2,1,0:T(8,128)(2,1)}), bf16[4,256,256]{2,1,0:T(8,128)(2,1)S(1)}, u32[]{:S(2)}, u32[]{:S(2)}) async-start(bf16[4,256,256]{2,1,0:T(8,128)(2,1)} %bitcast.5), calls=%async_computation | async-start | bytes 1048576 | tf_op jit(solution)/shard_map/all_to_all | solution.py:444
  31.1 1.4 %copy-done.4 = bf16[1,2048,256]{2,1,0:T(8,128)(2,1)S(1)} copy-done((bf16[1,2048,256]{2,1,0:T(8,128)(2,1)S(1)}, bf16[1,2048,256]{2,1,0:T(8,128)(2,1)}, u32[]{:S(2)}) %copy-start.4) | copy-done | bytes 1048600
  32.5 15.4 %attention_0.1 = (f32[4,128,128]{2,1,0:T(8,128)S(1)}, f32[4,128,128]{2,1,0:T(8,128)S(1)}, bf16[4,128,128]{2,1,0:T(8,128)(2,1)S(1)}, bf16[4,128,128]{2,1,0:T(8,12...) custom-call(s32[128]{0:T(128)S(1)} %get-tuple-element.26.refs_0_, ...), custom_call_target="tpu_custom_call" | custom-call | flops 6375342080 | bytes 5242880 | tf_op jit(solution)/shard_map/attention_0/pallas_call | solution.py:340
  47.9 0.8 copy-done.13
  48.7 0.7 copy-done.17
  49.4 0.7 copy-done.19
  50.2 0.7 copy-done.21
  50.8 0.8 copy-done.15
  51.6 5.1 %all-to-all-start.2 = ((bf16[8,256,128]{2,1,0:T(8,128)(2,1)}), bf16[8,256,128]{2,1,0:T(8,128)(2,1)S(1)}, u32[]{:S(2)}, u32[]{:S(2)}) async-start(bf16[8,256,128]{2,1,0:T(8,128)(2,1)} %bitcast.16), calls=%async_computation.2 | async-start | bytes 1048576 | tf_op jit(solution)/shard_map/all_to_all | solution.py:449
  56.7 1.2 copy-done.5
  57.9 1.0 copy-done.9
  58.9 1.0 copy-done.14
  60.0 1.0 copy-done.16
  61.0 0.9 copy-done.18
  62.0 0.9 copy-done.20
  62.9 0.9 copy-done.22
  63.8 15.5 %attention_1.1 = (f32[4,2,128,128]{3,2,1,0:T(8,128)S(1)}, f32[4,2,128,128]{3,2,1,0:T(8,128)S(1)}, bf16[4,2,128,128]{3,2,1,0:T(8,128)(2,1)}, bf16[4,2,128,128]{3,...) custom-call(s32[128]{0:T(128)S(1)} %get-tuple-element.26.refs_0_, ...), custom_call_target="tpu_custom_call" | custom-call | flops 6375342080 | bytes 5242880 | tf_op jit(solution)/shard_map/attention_1/pallas_call | solution.py:340
  79.4 0.8 copy-done.6
  80.2 0.8 copy-done.10
  81.0 0.7 copy-done.11
  81.7 0.5 collective-permute-start.5
  82.2 1.7 %collective-permute-done.5 = f32[512,256]{1,0:T(8,128)S(1)} collective-permute-done((f32[512,256]{1,0:T(8,128)}, f32[512,256]{1,0:T(8,128)S(1)}, u32[]{:S(2)}, u32[]{:S(2)}) %collective-permute-start.5) | collective-permute-done | bytes 524320 | tf_op jit(solution)/shard_map/ppermute | solution.py:372
  84.1 1.6 %collective-permute-start.6 = (bf16[256,256]{1,0:T(8,128)(2,1)S(1)}, bf16[256,256]{1,0:T(8,128)(2,1)S(1)}, u32[]{:S(2)}, u32[]{:S(2)}) collective-permute-start(bf16[256,256]{1,0:T(8,128)(2,1)S(1)} %broadcast_select_fusion), channel_id=1, source_target_pairs={{0,2},{2,0},{1,3},{3,1},{4,6},{6,4},{5,7},{7,5},{8,10},{10,8},{9,1... | collective-permute-start | bytes 393224 | tf_op jit(solution)/shard_map/ppermute | solution.py:372
  85.6 4.9 %all-to-all-start.3 = ((bf16[8,256,128]{2,1,0:T(8,128)(2,1)}), bf16[8,256,128]{2,1,0:T(8,128)(2,1)S(1)}, u32[]{:S(2)}, u32[]{:S(2)}) async-start(bf16[8,256,128]{2,1,0:T(8,128)(2,1)} %bitcast.18), calls=%async_computation.3 | async-start | bytes 1048576 | tf_op jit(solution)/shard_map/all_to_all | solution.py:449
  90.7 2.1 %collective-permute-start.7 = (bf16[256,256]{1,0:T(8,128)(2,1)S(1)}, bf16[256,256]{1,0:T(8,128)(2,1)S(1)}, u32[]{:S(2)}, u32[]{:S(2)}) collective-permute-start(bf16[256,256]{1,0:T(8,128)(2,1)S(1)} %add_convert_fusion.3), channel_id=1, source_target_pairs={{0,4},{4,0},{8,12},{12,8},{1,5},{5,1},{9,13},{13,9},{2,6},{6,2},{1... | collective-permute-start | bytes 393224 | tf_op jit(solution)/shard_map/ppermute | solution.py:372
  92.8 10.5 %collective-permute-done.7 = bf16[256,256]{1,0:T(8,128)(2,1)S(1)} collective-permute-done((bf16[256,256]{1,0:T(8,128)(2,1)S(1)}, bf16[256,256]{1,0:T(8,128)(2,1)S(1)}, u32[]{:S(2)}, u32[]{:S(2)}) %collective-permute-start.7) | collective-permute-done | bytes 131104 | tf_op jit(solution)/shard_map/ppermute | solution.py:372
  103.3 4.3 %collective-permute-start.8 = (bf16[256,256]{1,0:T(8,128)(2,1)S(1)}, bf16[256,256]{1,0:T(8,128)(2,1)S(1)}, u32[]{:S(2)}, u32[]{:S(2)}) collective-permute-start(bf16[256,256]{1,0:T(8,128)(2,1)S(1)} %add_convert_fusion.2), channel_id=1, source_target_pairs={{0,8},{4,12},{8,0},{12,4},{1,9},{5,13},{9,1},{13,5},{2,10},{6,14},... | collective-permute-start | bytes 393224 | tf_op jit(solution)/shard_map/ppermute | solution.py:372
  107.6 1.3 collective-permute-start.3
  108.9 1.3 %collective-permute-start.4 = (bf16[8,128,128]{2,1,0:T(8,128)(2,1)S(1)}, bf16[8,128,128]{2,1,0:T(8,128)(2,1)S(1)}, u32[]{:S(2)}, u32[]{:S(2)}) collective-permute-start(bf16[8,128,128]{2,1,0:T(8,128)(2,1)S(1)} %bitcast.34), channel_id=1, source_target_pairs={{2,1},{3,0},{6,5},{7,4},{10,9},{11,8},{14,13},{15,12},{18,17},{19,... | collective-permute-start | bytes 786440 | tf_op jit(solution)/shard_map/ppermute | solution.py:474
  110.2 3.5 %collective-permute-done.8 = bf16[256,256]{1,0:T(8,128)(2,1)S(1)} collective-permute-done((bf16[256,256]{1,0:T(8,128)(2,1)S(1)}, bf16[256,256]{1,0:T(8,128)(2,1)S(1)}, u32[]{:S(2)}, u32[]{:S(2)}) %collective-permute-start.8) | collective-permute-done | bytes 131104 | tf_op jit(solution)/shard_map/ppermute | solution.py:372
  113.7 0.6 collective-permute-start.9
  114.3 4.6 %collective-permute-done.3.refs_3_ = bf16[8,128,128]{2,1,0:T(8,128)(2,1)S(1)} collective-permute-done((bf16[8,128,128]{2,1,0:T(8,128)(2,1)}, bf16[8,128,128]{2,1,0:T(8,128)(2,1)S(1)}, u32[]{:S(2)}, u32[]{:S(2)}) %collective-permute-start.3) | collective-permute-done | bytes 262176 | tf_op jit(solution)/shard_map/ppermute | solution.py:473
  118.9 2.3 %collective-permute-done.4.refs_4_ = bf16[8,128,128]{2,1,0:T(8,128)(2,1)S(1)} collective-permute-done((bf16[8,128,128]{2,1,0:T(8,128)(2,1)S(1)}, bf16[8,128,128]{2,1,0:T(8,128)(2,1)S(1)}, u32[]{:S(2)}, u32[]{:S(2)}) %collective-permute-start.4) | collective-permute-done | bytes 262176 | tf_op jit(solution)/shard_map/ppermute | solution.py:474
  121.2 1.8 %assemble.1 = bf16[16,128,128]{2,1,0:T(8,128)(2,1)} custom-call(s32[128]{0:T(128)S(1)} %get-tuple-element.26.refs_0_, f32[8,128,128]{2,1,0:T(8,128)S(1)} %bitcast.30, f32[8,128,128]{2,1,0:T(8,128)S(1)} %collective-permute-done.2.refs_2_, bf16[8,128,128]{2,1,0:T(8,128)(2,1)S(1)} %collective-permute-done.3.refs_3_, ...), custom_call_target="tpu_custom_call" | custom-call | tf_op jit(solution)/shard_map/assemble/pallas_call | solution.py:485
  123.0 2.8 %collective-permute-done.9 = bf16[256,256]{1,0:T(8,128)(2,1)} collective-permute-done((bf16[256,256]{1,0:T(8,128)(2,1)S(1)}, bf16[256,256]{1,0:T(8,128)(2,1)}, u32[]{:S(2)}, u32[]{:S(2)}) %collective-permute-start.9) | collective-permute-done | bytes 131104 | tf_op jit(solution)/shard_map/ppermute | solution.py:372
  125.8 0.9 select_convert_fusion
  126.7 0.7 fusion.1
  127.4 0.7 fusion
  128.1 0.8 copy.16
  (52 shorter events, 0.5 us)
Async XLA Ops:
  0.7 0.7 copy-start.2
  0.7 0.7 copy-start.3
  1.4 1.2 copy-start
  6.5 10.1 %copy-start.23 = (bf16[256,128]{1,0:T(8,128)(2,1)S(1)}, bf16[256,128]{1,0:T(8,128)(2,1)}, u32[]{:S(2)}) copy-start(bf16[256,128]{1,0:T(8,128)(2,1)} %param.10) | copy-start | bytes 196612
  6.6 10.2 %copy-start.24 = (bf16[256,128]{1,0:T(8,128)(2,1)S(1)}, bf16[256,128]{1,0:T(8,128)(2,1)}, u32[]{:S(2)}) copy-start(bf16[256,128]{1,0:T(8,128)(2,1)} %param.11) | copy-start | bytes 196612
  6.6 10.3 %copy-start.25 = (bf16[256,128]{1,0:T(8,128)(2,1)S(1)}, bf16[256,128]{1,0:T(8,128)(2,1)}, u32[]{:S(2)}) copy-start(bf16[256,128]{1,0:T(8,128)(2,1)} %param.12) | copy-start | bytes 196612
  6.6 10.4 %copy-start.26 = (bf16[128,256]{1,0:T(8,128)(2,1)S(1)}, bf16[128,256]{1,0:T(8,128)(2,1)}, u32[]{:S(2)}) copy-start(bf16[128,256]{1,0:T(8,128)(2,1)} %param.13) | copy-start | bytes 196612
  6.6 21.0 %all-to-all-start.1 = ((bf16[4,256,256]{2,1,0:T(8,128)(2,1)}), bf16[4,256,256]{2,1,0:T(8,128)(2,1)S(1)}, u32[]{:S(2)}, u32[]{:S(2)}) async-start(bf16[4,256,256]{2,1,0:T(8,128)(2,1)} %bitcast.10), calls=%async_computation.1 | async-start | bytes 1048576 | tf_op jit(solution)/shard_map/all_to_all | solution.py:444
  13.1 18.0 %copy-start.1 = (bf16[1,2048,256]{2,1,0:T(8,128)(2,1)S(1)}, bf16[1,2048,256]{2,1,0:T(8,128)(2,1)}, u32[]{:S(2)}) copy-start(bf16[1,2048,256]{2,1,0:T(8,128)(2,1)} %param.8) | copy-start | bytes 3145732
  13.1 18.0 %collective-permute-start = (bf16[8,128,256]{2,1,0:T(8,128)(2,1)S(1)}, bf16[8,128,256]{2,1,0:T(8,128)(2,1)S(1)}, u32[]{:S(2)}, u32[]{:S(2)}) collective-permute-start(bf16[8,128,256]{2,1,0:T(8,128)(2,1)S(1)} %get-tuple-element.28), channel_id=1, source_target_pairs={{0,2},{1,3},{4,6},{5,7},{8,10},{9,11},{12,14},{13,15},{16,18},{17,... | collective-permute-start | bytes 1572872 | tf_op jit(solution)/shard_map/ppermute | solution.py:458
  17.0 14.0 %collective-permute-start.1 = (bf16[512,256]{1,0:T(8,128)(2,1)S(1)}, bf16[512,256]{1,0:T(8,128)(2,1)}, u32[]{:S(2)}, u32[]{:S(2)}) collective-permute-start(bf16[512,256]{1,0:T(8,128)(2,1)S(1)} %pad_maximum_fusion.refs_5_), channel_id=1, source_target_pairs={{0,1},{1,0},{2,3},{3,2},{4,5},{5,4},{6,7},{7,6},{8,9},{9,8},{10,11... | collective-permute-start | bytes 786440 | tf_op jit(solution)/shard_map/ppermute | solution.py:372
  27.5 23.3 %all-to-all-start = ((bf16[4,256,256]{2,1,0:T(8,128)(2,1)}), bf16[4,256,256]{2,1,0:T(8,128)(2,1)S(1)}, u32[]{:S(2)}, u32[]{:S(2)}) async-start(bf16[4,256,256]{2,1,0:T(8,128)(2,1)} %bitcast.5), calls=%async_computation | async-start | bytes 1048576 | tf_op jit(solution)/shard_map/all_to_all | solution.py:444
  31.0 16.9 %copy-start.8 = (bf16[8,128,256]{2,1,0:T(8,128)(2,1)}, bf16[8,128,256]{2,1,0:T(8,128)(2,1)S(1)}, u32[]{:S(2)}) copy-start(bf16[8,128,256]{2,1,0:T(8,128)(2,1)S(1)} %collective-permute-done.refs_4_) | copy-start | bytes 1572868
  31.1 1.4 %copy-start.4 = (bf16[1,2048,256]{2,1,0:T(8,128)(2,1)S(1)}, bf16[1,2048,256]{2,1,0:T(8,128)(2,1)}, u32[]{:S(2)}) copy-start(bf16[1,2048,256]{2,1,0:T(8,128)(2,1)} %param.9) | copy-start | bytes 3145732
  47.9 0.8 copy-start.13
  48.7 0.7 copy-start.17
  49.4 0.7 copy-start.19
  50.1 0.7 copy-start.21
  50.8 0.8 copy-start.15
  51.6 30.1 %all-to-all-start.2 = ((bf16[8,256,128]{2,1,0:T(8,128)(2,1)}), bf16[8,256,128]{2,1,0:T(8,128)(2,1)S(1)}, u32[]{:S(2)}, u32[]{:S(2)}) async-start(bf16[8,256,128]{2,1,0:T(8,128)(2,1)} %bitcast.16), calls=%async_computation.2 | async-start | bytes 1048576 | tf_op jit(solution)/shard_map/all_to_all | solution.py:449
  56.7 1.2 copy-start.5
  57.9 1.0 copy-start.9
  58.9 1.0 copy-start.14
  60.0 1.0 copy-start.16
  61.0 0.9 copy-start.18
  62.0 0.9 copy-start.20
  62.9 0.9 copy-start.22
  79.4 0.8 copy-start.6
  80.2 0.8 copy-start.10
  81.0 0.7 copy-start.11
  81.7 2.3 %collective-permute-start.5 = (f32[512,256]{1,0:T(8,128)}, f32[512,256]{1,0:T(8,128)S(1)}, u32[]{:S(2)}, u32[]{:S(2)}) collective-permute-start(f32[512,256]{1,0:T(8,128)} %copy-done.10), channel_id=1, source_target_pairs={{0,1},{1,0},{2,3},{3,2},{4,5},{5,4},{6,7},{7,6},{8,9},{9,8},{10,11... | collective-permute-start | bytes 1572872 | tf_op jit(solution)/shard_map/ppermute | solution.py:372
  84.1 6.5 %collective-permute-start.6 = (bf16[256,256]{1,0:T(8,128)(2,1)S(1)}, bf16[256,256]{1,0:T(8,128)(2,1)S(1)}, u32[]{:S(2)}, u32[]{:S(2)}) collective-permute-start(bf16[256,256]{1,0:T(8,128)(2,1)S(1)} %broadcast_select_fusion), channel_id=1, source_target_pairs={{0,2},{2,0},{1,3},{3,1},{4,6},{6,4},{5,7},{7,5},{8,10},{10,8},{9,1... | collective-permute-start | bytes 393224 | tf_op jit(solution)/shard_map/ppermute | solution.py:372
  85.6 35.6 %all-to-all-start.3 = ((bf16[8,256,128]{2,1,0:T(8,128)(2,1)}), bf16[8,256,128]{2,1,0:T(8,128)(2,1)S(1)}, u32[]{:S(2)}, u32[]{:S(2)}) async-start(bf16[8,256,128]{2,1,0:T(8,128)(2,1)} %bitcast.18), calls=%async_computation.3 | async-start | bytes 1048576 | tf_op jit(solution)/shard_map/all_to_all | solution.py:449
  90.6 2.2 %copy-start.7 = (f32[4,2,128,128]{3,2,1,0:T(8,128)S(1)}, f32[4,2,128,128]{3,2,1,0:T(8,128)}, u32[]{:S(2)}) copy-start(f32[4,2,128,128]{3,2,1,0:T(8,128)} %copy-done.6) | copy-start | bytes 1572868
  90.7 18.2 %copy-start.12 = (bf16[4,2,128,128]{3,2,1,0:T(8,128)(2,1)S(1)}, bf16[4,2,128,128]{3,2,1,0:T(8,128)(2,1)}, u32[]{:S(2)}) copy-start(bf16[4,2,128,128]{3,2,1,0:T(8,128)(2,1)} %copy-done.11) | copy-start | bytes 786436
  90.7 12.6 %collective-permute-start.7 = (bf16[256,256]{1,0:T(8,128)(2,1)S(1)}, bf16[256,256]{1,0:T(8,128)(2,1)S(1)}, u32[]{:S(2)}, u32[]{:S(2)}) collective-permute-start(bf16[256,256]{1,0:T(8,128)(2,1)S(1)} %add_convert_fusion.3), channel_id=1, source_target_pairs={{0,4},{4,0},{8,12},{12,8},{1,5},{5,1},{9,13},{13,9},{2,6},{6,2},{1... | collective-permute-start | bytes 393224 | tf_op jit(solution)/shard_map/ppermute | solution.py:372
  92.8 28.4 %collective-permute-start.2 = (f32[8,128,128]{2,1,0:T(8,128)S(1)}, f32[8,128,128]{2,1,0:T(8,128)S(1)}, u32[]{:S(2)}, u32[]{:S(2)}) collective-permute-start(f32[8,128,128]{2,1,0:T(8,128)S(1)} %bitcast.33), channel_id=1, source_target_pairs={{0,1},{1,0},{2,3},{3,2},{4,5},{5,4},{6,7},{7,6},{8,9},{9,8},{10,11... | collective-permute-start | bytes 1572872 | tf_op jit(solution)/shard_map/ppermute | solution.py:372
  103.3 10.4 %collective-permute-start.8 = (bf16[256,256]{1,0:T(8,128)(2,1)S(1)}, bf16[256,256]{1,0:T(8,128)(2,1)S(1)}, u32[]{:S(2)}, u32[]{:S(2)}) collective-permute-start(bf16[256,256]{1,0:T(8,128)(2,1)S(1)} %add_convert_fusion.2), channel_id=1, source_target_pairs={{0,8},{4,12},{8,0},{12,4},{1,9},{5,13},{9,1},{13,5},{2,10},{6,14},... | collective-permute-start | bytes 393224 | tf_op jit(solution)/shard_map/ppermute | solution.py:372
  107.6 11.3 %collective-permute-start.3 = (bf16[8,128,128]{2,1,0:T(8,128)(2,1)}, bf16[8,128,128]{2,1,0:T(8,128)(2,1)S(1)}, u32[]{:S(2)}, u32[]{:S(2)}) collective-permute-start(bf16[8,128,128]{2,1,0:T(8,128)(2,1)} %bitcast.14), channel_id=1, source_target_pairs={{2,0},{3,1},{6,4},{7,5},{10,8},{11,9},{14,12},{15,13},{18,16},{19,... | collective-permute-start | bytes 786440 | tf_op jit(solution)/shard_map/ppermute | solution.py:473
  108.9 12.3 %collective-permute-start.4 = (bf16[8,128,128]{2,1,0:T(8,128)(2,1)S(1)}, bf16[8,128,128]{2,1,0:T(8,128)(2,1)S(1)}, u32[]{:S(2)}, u32[]{:S(2)}) collective-permute-start(bf16[8,128,128]{2,1,0:T(8,128)(2,1)S(1)} %bitcast.34), channel_id=1, source_target_pairs={{2,1},{3,0},{6,5},{7,4},{10,9},{11,8},{14,13},{15,12},{18,17},{19,... | collective-permute-start | bytes 786440 | tf_op jit(solution)/shard_map/ppermute | solution.py:474
  113.7 12.0 %collective-permute-start.9 = (bf16[256,256]{1,0:T(8,128)(2,1)S(1)}, bf16[256,256]{1,0:T(8,128)(2,1)}, u32[]{:S(2)}, u32[]{:S(2)}) collective-permute-start(bf16[256,256]{1,0:T(8,128)(2,1)S(1)} %add_convert_fusion.1), channel_id=1, source_target_pairs={{0,2},{2,0},{1,3},{3,1},{4,6},{6,4},{5,7},{7,5},{8,10},{10,8},{9,1... | collective-permute-start | bytes 393224 | tf_op jit(solution)/shard_map/ppermute | solution.py:372

commit v3 on v2

--- a/solution.py
+++ b/solution.py
@@ -351,20 +351,28 @@
             ),
         ),
         out_shape=(
-            jax.ShapeDtypeStruct(term_shape, F32),
-            jax.ShapeDtypeStruct(term_shape, F32),
-            jax.ShapeDtypeStruct(term_shape, BF16),
-            jax.ShapeDtypeStruct(term_shape, BF16),
-            jax.ShapeDtypeStruct((lay.reach, CORES, lay.slots, BLOCK, half), BF16),
-            jax.ShapeDtypeStruct(weights_block, F32),
-            jax.ShapeDtypeStruct(weights_block, F32),
+            pltpu.HBM(term_shape, F32),
+            pltpu.HBM(term_shape, F32),
+            pltpu.HBM(term_shape, BF16),
+            pltpu.HBM(term_shape, BF16),
+            pltpu.HBM((lay.reach, CORES, lay.slots, BLOCK, half), BF16),
+            pltpu.HBM(weights_block, F32),
+            pltpu.HBM(weights_block, F32),
         ),
         compiler_params=pltpu.CompilerParams(vmem_limit_bytes=32 << 20),
         cost_estimate=pl.CostEstimate(
             flops=flops, bytes_accessed=5 << 20, transcendentals=pieces * 8 * BLOCK * 3 * BLOCK
         ),
         name=f"attention_{chunk}",
-    )(tab, *operands)
+    )(
+        tab,
+        *[
+            value
+            if place == 2
+            else pltpu.with_memory_space_constraint(value, pltpu.HBM)
+            for place, value in enumerate(operands)
+        ],
+    )
 
 
 def exchanged(value, axis, bit):
@@ -380,19 +388,19 @@
     return value
 
 
-def sum_gradients(total):
+def sum_gradients(total, settled):
     half = total.shape[0] // 2
-    low = total.astype(BF16)
     first = lax.rem(lax.axis_index("day"), 2) == 0
-    kept = jnp.where(first, low[:half], low[half:])
-    given = jnp.where(first, low[half:], low[:half])
-    part = kept.astype(F32) + exchanged(given, "day", 1).astype(F32)
+    kept = jnp.where(first, total[:half], total[half:])
+    given = jnp.where(first, total[half:], total[:half])
+    part = kept + exchanged(given, "day", 1)
     part = summed_over(part, "day", 2)
-    part = summed_over(part, "reach", 1).astype(BF16)
+    part, *settled = lax.optimization_barrier((part, *settled))
+    part = summed_over(part, "reach", 1)
     other = exchanged(part, "day", 1)
-    upper = jnp.where(first, part, other).astype(F32)
-    lower = jnp.where(first, other, part).astype(F32)
-    return upper, lower
+    upper = jnp.where(first, part, other)
+    lower = jnp.where(first, other, part)
+    return upper, lower, settled
 
 
 def on_device(
@@ -480,7 +488,9 @@
             for c in range(CORES)
         ],
     )
-    upper, lower = sum_gradients(grad_mine + grad_swapped)
+    upper, lower, (swapped, same_came, cross_came) = sum_gradients(
+        grad_mine + grad_swapped, (swapped, same_came, cross_came)
+    )
 
     back_blocks = pl.pallas_call(
         lambda *refs: gather_kernel(lay, *refs),

time: 130 us -> 130 us (level)
  waiting for transfers between devices: 35.8 us -> 49.8 us
  local copies, waits for them, and re-layouts: 19 us -> 6.68 us
  starting transfers between devices: 35.2 us -> 31.5 us
  Pallas kernels: 36.7 us -> 39 us
    unnamed x58 -> x30, local copies, waits for them, and re-layouts: 17.6 us -> 5.29 us
    ppermute x7, waiting for transfers between devices: 18.5 us -> 30.7 us  [exchanged(): lax.ppermute(value, axis, [(place, place ^ bit) for place in range(count)])]
    ppermute x7, starting transfers between devices: 9.12 us -> 6.77 us  [exchanged(): lax.ppermute(value, axis, [(place, place ^ bit) for place in range(count)])]
    pallas_call x2, Pallas kernels: 31 us -> 33.3 us  [attend(): pl.pallas_call(lambda *refs: attention_kernel(lay, chunk, *refs), grid_sp...]
    ppermute x1, waiting for transfers between devices: 2.27 us -> 4.5 us  [on_device(): lax.ppermute(cross, ('day', 'head'), [((d + 1) * CORES + c, d * CORES + 1...]
    all_to_all x2, waiting for transfers between devices: 10.4 us -> 9.01 us  [outward(): lax.all_to_all(sent.reshape(lay.reach, lay.slots * BLOCK, width), 'reach'...]
  transfers between devices with their start and end apart: 14 -> 14, of which waited for: 7 -> 8; matrix products, arithmetic and copies ran while one was open for 0% -> 1% of each run, Pallas kernels for 25% -> 27%
where the time goes in v3:
time: 130 us; the launch traced here: 129 us
  waiting for transfers between devices  49.8 us (38%)
  Pallas kernels  39 us (30%)
  starting transfers between devices  31.5 us (24%)
  local copies, waits for them, and re-layouts  6.68 us (5%)
  other arithmetic  1.4 us (1%)
    pallas_call x2, Pallas kernels, attend(): pl.pallas_call(lambda *refs: attention_kernel(lay, chunk, *refs), grid_sp...  33.3 us
    ppermute x7, waiting for transfers between devices, exchanged(): lax.ppermute(value, axis, [(place, place ^ bit) for place in range(count)])  30.7 us
    all_to_all x2, starting transfers between devices, outward(): lax.all_to_all(sent.reshape(lay.reach, lay.slots * BLOCK, width), 'reach'...  9.93 us
    all_to_all x2, waiting for transfers between devices, outward(): lax.all_to_all(sent.reshape(lay.reach, lay.slots * BLOCK, width), 'reach'...  9.01 us
    all_to_all x2, starting transfers between devices, homeward(): lax.all_to_all(home.reshape(lay.reach * CORES, lay.slots * BLOCK, half),...  8.73 us
    ppermute x7, starting transfers between devices, exchanged(): lax.ppermute(value, axis, [(place, place ^ bit) for place in range(count)])  6.77 us
    ppermute x1, waiting for transfers between devices, on_device(): lax.ppermute(same, 'day', [(d + 1, d) for d in range(day_total - 1)])  5.56 us
    unnamed x30, local copies, waits for them, and re-layouts  5.29 us
  transfers between devices with their start and end apart: 14, of which 8 were waited for; matrix products, arithmetic and copies ran while one was open for 1% of the time, Pallas kernels for 27%

profile of v3, /device:TPU:0, one launch (start us, length us, event | category | flops | bytes accessed | tf_op | source)
XLA Modules:
  0.0 129.3 jit_solution(872414711437361541)
XLA Ops:
  0.6 0.1 pad_add_fusion.refs_2_
  0.7 0.7 copy-done.2
  1.4 0.0 copy-done.3
  1.4 1.2 copy-done
  2.6 3.9 %prepare.1 = (bf16[8,128,256]{2,1,0:T(8,128)(2,1)}, bf16[8,128,256]{2,1,0:T(8,128)(2,1)}, bf16[8,128,256]{2,1,0:T(8,128)(2,1)S(1)}, s32[128]{0:T(128)S(1)}) custom-call(s32[64]{0:T(128)S(1)} %copy-done.2, s32[64]{0:T(128)S(1)} %copy-done.3, s32[3]{0:T(128)S(1)} %pad_add_fusion.refs_2_, bf16[16,128,256]{2,1,0:T(8,128)(2,1)S(1)} %bitcast.27), custom_call_target="tpu_custom_call" | custom-call | tf_op jit(solution)/shard_map/prepare/pallas_call | solution.py:432
  6.5 0.0 copy-start.5
  6.5 6.5 %all-to-all-start.1 = ((bf16[4,256,256]{2,1,0:T(8,128)(2,1)}), bf16[4,256,256]{2,1,0:T(8,128)(2,1)S(1)}, u32[]{:S(2)}, u32[]{:S(2)}) async-start(bf16[4,256,256]{2,1,0:T(8,128)(2,1)} %bitcast.10), calls=%async_computation.1 | async-start | bytes 1048576 | tf_op jit(solution)/shard_map/all_to_all | solution.py:452
  13.0 3.5 %collective-permute-start = (bf16[8,128,256]{2,1,0:T(8,128)(2,1)S(1)}, bf16[8,128,256]{2,1,0:T(8,128)(2,1)S(1)}, u32[]{:S(2)}, u32[]{:S(2)}) collective-permute-start(bf16[8,128,256]{2,1,0:T(8,128)(2,1)S(1)} %get-tuple-element.32), channel_id=1, source_target_pairs={{0,2},{1,3},{4,6},{5,7},{8,10},{9,11},{12,14},{13,15},{16,18},{17,... | collective-permute-start | bytes 1572872 | tf_op jit(solution)/shard_map/ppermute | solution.py:466
  16.6 0.1 copy.15
  16.7 0.0 copy-start.7
  16.7 0.1 copy.13
  16.8 0.7 copy-done.7
  17.5 0.1 copy.14
  17.6 0.7 copy-done.8
  18.4 0.1 collective-permute-start.1
  18.5 9.0 %all-to-all-done.1 = bf16[4,256,256]{2,1,0:T(8,128)(2,1)S(1)} async-done(((bf16[4,256,256]{2,1,0:T(8,128)(2,1)}), bf16[4,256,256]{2,1,0:T(8,128)(2,1)S(1)}, u32[]{:S(2)}, u32[]{:S(2)}) %all-to-all-start.1) | async-done | bytes 524320 | tf_op jit(solution)/shard_map/all_to_all | solution.py:452
  27.5 3.5 %all-to-all-start = ((bf16[4,256,256]{2,1,0:T(8,128)(2,1)}), bf16[4,256,256]{2,1,0:T(8,128)(2,1)S(1)}, u32[]{:S(2)}, u32[]{:S(2)}) async-start(bf16[4,256,256]{2,1,0:T(8,128)(2,1)} %bitcast.5), calls=%async_computation | async-start | bytes 1048576 | tf_op jit(solution)/shard_map/all_to_all | solution.py:452
  31.0 0.0 collective-permute-done.1.refs_6_
  31.0 0.0 collective-permute-done.refs_4_
  31.0 0.0 copy-start.9
  31.0 0.7 copy-done.12
  31.7 0.2 copy-done.9
  31.9 16.3 %attention_0.1 = (f32[4,128,128]{2,1,0:T(8,128)}, f32[4,128,128]{2,1,0:T(8,128)}, bf16[4,128,128]{2,1,0:T(8,128)(2,1)}, bf16[4,128,128]{2,1,0:T(8,128)(2,1)}, bf...) custom-call(s32[128]{0:T(128)S(1)} %get-tuple-element.30.refs_0_, ...), custom_call_target="tpu_custom_call" | custom-call | flops 6375342080 | bytes 5242880 | tf_op jit(solution)/shard_map/attention_0/pallas_call | solution.py:340
  48.2 0.0 all-to-all-done
  48.2 5.1 %all-to-all-start.2 = ((bf16[8,256,128]{2,1,0:T(8,128)(2,1)}), bf16[8,256,128]{2,1,0:T(8,128)(2,1)S(1)}, u32[]{:S(2)}, u32[]{:S(2)}) async-start(bf16[8,256,128]{2,1,0:T(8,128)(2,1)} %bitcast.31), calls=%async_computation.2 | async-start | bytes 1048576 | tf_op jit(solution)/shard_map/all_to_all | solution.py:457
  53.2 17.0 %attention_1.1 = (f32[4,2,128,128]{3,2,1,0:T(8,128)}, f32[4,2,128,128]{3,2,1,0:T(8,128)}, bf16[4,2,128,128]{3,2,1,0:T(8,128)(2,1)}, bf16[4,2,128,128]{3,2,1,0:T(...) custom-call(s32[128]{0:T(128)S(1)} %get-tuple-element.30.refs_0_, ...), custom_call_target="tpu_custom_call" | custom-call | flops 6375342080 | bytes 5242880 | tf_op jit(solution)/shard_map/attention_1/pallas_call | solution.py:340
  70.2 0.6 collective-permute-start.2
  70.8 0.1 collective-permute-start.4
  70.9 1.7 %collective-permute-done.2 = f32[512,256]{1,0:T(8,128)S(1)} collective-permute-done((f32[512,256]{1,0:T(8,128)}, f32[512,256]{1,0:T(8,128)S(1)}, u32[]{:S(2)}, u32[]{:S(2)}) %collective-permute-start.2) | collective-permute-done | bytes 524320 | tf_op jit(solution)/shard_map/ppermute | solution.py:380
  72.6 1.1 add.12
  73.7 1.6 %collective-permute-start.3 = (f32[256,256]{1,0:T(8,128)S(1)}, f32[256,256]{1,0:T(8,128)S(1)}, u32[]{:S(2)}, u32[]{:S(2)}) collective-permute-start(f32[256,256]{1,0:T(8,128)S(1)} %slice_select_fusion), channel_id=1, source_target_pairs={{0,2},{2,0},{1,3},{3,1},{4,6},{6,4},{5,7},{7,5},{8,10},{10,8},{9,1... | collective-permute-start | bytes 786440 | tf_op jit(solution)/shard_map/ppermute | solution.py:380
  75.3 1.3 collective-permute-start.5
  76.6 1.3 collective-permute-start.6
  77.9 5.0 %collective-permute-done.3 = f32[256,256]{1,0:T(8,128)S(1)} collective-permute-done((f32[256,256]{1,0:T(8,128)S(1)}, f32[256,256]{1,0:T(8,128)S(1)}, u32[]{:S(2)}, u32[]{:S(2)}) %collective-permute-start.3) | collective-permute-done | bytes 262176 | tf_op jit(solution)/shard_map/ppermute | solution.py:380
  82.9 0.1 select_add_fusion
  83.0 5.6 %collective-permute-done.5.refs_3_ = bf16[8,128,128]{2,1,0:T(8,128)(2,1)S(1)} collective-permute-done((bf16[8,128,128]{2,1,0:T(8,128)(2,1)S(1)}, bf16[8,128,128]{2,1,0:T(8,128)(2,1)S(1)}, u32[]{:S(2)}, u32[]{:S(2)}) %collective-permute-start.5) | collective-permute-done | bytes 262176 | tf_op jit(solution)/shard_map/ppermute | solution.py:481
  88.6 4.5 %collective-permute-done.6.refs_4_ = bf16[8,128,128]{2,1,0:T(8,128)(2,1)S(1)} collective-permute-done((bf16[8,128,128]{2,1,0:T(8,128)(2,1)S(1)}, bf16[8,128,128]{2,1,0:T(8,128)(2,1)S(1)}, u32[]{:S(2)}, u32[]{:S(2)}) %collective-permute-start.6) | collective-permute-done | bytes 262176 | tf_op jit(solution)/shard_map/ppermute | solution.py:482
  93.1 1.4 %collective-permute-start.7 = (bf16[256,256]{1,0:T(8,128)(2,1)S(1)}, bf16[256,256]{1,0:T(8,128)(2,1)S(1)}, u32[]{:S(2)}, u32[]{:S(2)}) collective-permute-start(bf16[256,256]{1,0:T(8,128)(2,1)S(1)} %select_add_fusion), channel_id=1, source_target_pairs={{0,4},{4,0},{8,12},{12,8},{1,5},{5,1},{9,13},{13,9},{2,6},{6,2},{1... | collective-permute-start | bytes 393224 | tf_op jit(solution)/shard_map/ppermute | solution.py:380
  94.5 3.7 %all-to-all-start.3 = ((bf16[8,256,128]{2,1,0:T(8,128)(2,1)}), bf16[8,256,128]{2,1,0:T(8,128)(2,1)S(1)}, u32[]{:S(2)}, u32[]{:S(2)}) async-start(bf16[8,256,128]{2,1,0:T(8,128)(2,1)} %bitcast.18), calls=%async_computation.3 | async-start | bytes 1048576 | tf_op jit(solution)/shard_map/all_to_all | solution.py:457
  98.2 0.7 collective-permute-done.7
  98.9 2.6 %collective-permute-start.8 = (bf16[256,256]{1,0:T(8,128)(2,1)S(1)}, bf16[256,256]{1,0:T(8,128)(2,1)S(1)}, u32[]{:S(2)}, u32[]{:S(2)}) collective-permute-start(bf16[256,256]{1,0:T(8,128)(2,1)S(1)} %add_convert_fusion), channel_id=1, source_target_pairs={{0,8},{4,12},{8,0},{12,4},{1,9},{5,13},{9,1},{13,5},{2,10},{6,14},... | collective-permute-start | bytes 393224 | tf_op jit(solution)/shard_map/ppermute | solution.py:380
  101.5 17.6 %collective-permute-done.8 = bf16[256,256]{1,0:T(8,128)(2,1)S(1)} collective-permute-done((bf16[256,256]{1,0:T(8,128)(2,1)S(1)}, bf16[256,256]{1,0:T(8,128)(2,1)S(1)}, u32[]{:S(2)}, u32[]{:S(2)}) %collective-permute-start.8) | collective-permute-done | bytes 131104 | tf_op jit(solution)/shard_map/ppermute | solution.py:380
  119.2 0.4 collective-permute-start.9
  119.6 1.8 %assemble.1 = bf16[16,128,128]{2,1,0:T(8,128)(2,1)} custom-call(s32[128]{0:T(128)S(1)} %get-tuple-element.30.refs_0_, f32[8,128,128]{2,1,0:T(8,128)S(1)} %bitcast.30, f32[8,128,128]{2,1,0:T(8,128)S(1)} %collective-permute-done.4.refs_2_, bf16[8,128,128]{2,1,0:T(8,128)(2,1)S(1)} %collective-permute-done.5.refs_3_, ...), custom_call_target="tpu_custom_call" | custom-call | tf_op jit(solution)/shard_map/assemble/pallas_call | solution.py:495
  121.4 5.7 %collective-permute-done.9 = f32[256,256]{1,0:T(8,128)S(1)} collective-permute-done((f32[256,256]{1,0:T(8,128)S(1)}, f32[256,256]{1,0:T(8,128)S(1)}, u32[]{:S(2)}, u32[]{:S(2)}) %collective-permute-start.9) | collective-permute-done | bytes 262176 | tf_op jit(solution)/shard_map/ppermute | solution.py:380
  127.1 0.7 fusion.1
  127.8 0.7 fusion
  128.5 0.8 copy.16
  (24 shorter events, 0.2 us)
Async XLA Ops:
  0.7 0.7 copy-start.2
  0.7 0.7 copy-start.3
  1.4 1.2 copy-start
  6.5 10.0 %copy-start.5 = (bf16[256,128]{1,0:T(8,128)(2,1)S(1)}, bf16[256,128]{1,0:T(8,128)(2,1)}, u32[]{:S(2)}) copy-start(bf16[256,128]{1,0:T(8,128)(2,1)} %param.10) | copy-start | bytes 196612
  6.5 21.0 %all-to-all-start.1 = ((bf16[4,256,256]{2,1,0:T(8,128)(2,1)}), bf16[4,256,256]{2,1,0:T(8,128)(2,1)S(1)}, u32[]{:S(2)}, u32[]{:S(2)}) async-start(bf16[4,256,256]{2,1,0:T(8,128)(2,1)} %bitcast.10), calls=%async_computation.1 | async-start | bytes 1048576 | tf_op jit(solution)/shard_map/all_to_all | solution.py:452
  13.0 3.7 %copy-start.6 = (bf16[256,128]{1,0:T(8,128)(2,1)S(1)}, bf16[256,128]{1,0:T(8,128)(2,1)}, u32[]{:S(2)}) copy-start(bf16[256,128]{1,0:T(8,128)(2,1)} %param.11) | copy-start | bytes 196612
  13.0 18.0 %collective-permute-start = (bf16[8,128,256]{2,1,0:T(8,128)(2,1)S(1)}, bf16[8,128,256]{2,1,0:T(8,128)(2,1)S(1)}, u32[]{:S(2)}, u32[]{:S(2)}) collective-permute-start(bf16[8,128,256]{2,1,0:T(8,128)(2,1)S(1)} %get-tuple-element.32), channel_id=1, source_target_pairs={{0,2},{1,3},{4,6},{5,7},{8,10},{9,11},{12,14},{13,15},{16,18},{17,... | collective-permute-start | bytes 1572872 | tf_op jit(solution)/shard_map/ppermute | solution.py:466
  16.7 0.8 copy-start.7
  17.5 0.8 copy-start.8
  18.4 9.1 %copy-start.4 = (bf16[512,256]{1,0:T(8,128)(2,1)}, bf16[512,256]{1,0:T(8,128)(2,1)S(1)}, u32[]{:S(2)}) copy-start(bf16[512,256]{1,0:T(8,128)(2,1)S(1)} %pad_maximum_fusion.refs_5_) | copy-start | bytes 786436
  18.4 12.6 %collective-permute-start.1 = (bf16[512,256]{1,0:T(8,128)(2,1)S(1)}, bf16[512,256]{1,0:T(8,128)(2,1)S(1)}, u32[]{:S(2)}, u32[]{:S(2)}) collective-permute-start(bf16[512,256]{1,0:T(8,128)(2,1)S(1)} %pad_maximum_fusion.refs_5_), channel_id=1, source_target_pairs={{0,1},{1,0},{2,3},{3,2},{4,5},{5,4},{6,7},{7,6},{8,9},{9,8},{10,11... | collective-permute-start | bytes 786440 | tf_op jit(solution)/shard_map/ppermute | solution.py:380
  27.5 20.7 %all-to-all-start = ((bf16[4,256,256]{2,1,0:T(8,128)(2,1)}), bf16[4,256,256]{2,1,0:T(8,128)(2,1)S(1)}, u32[]{:S(2)}, u32[]{:S(2)}) async-start(bf16[4,256,256]{2,1,0:T(8,128)(2,1)} %bitcast.5), calls=%async_computation | async-start | bytes 1048576 | tf_op jit(solution)/shard_map/all_to_all | solution.py:452
  31.0 0.7 copy-start.12
  31.0 0.9 copy-start.9
  48.2 22.1 %all-to-all-start.2 = ((bf16[8,256,128]{2,1,0:T(8,128)(2,1)}), bf16[8,256,128]{2,1,0:T(8,128)(2,1)S(1)}, u32[]{:S(2)}, u32[]{:S(2)}) async-start(bf16[8,256,128]{2,1,0:T(8,128)(2,1)} %bitcast.31), calls=%async_computation.2 | async-start | bytes 1048576 | tf_op jit(solution)/shard_map/all_to_all | solution.py:457
  70.2 2.3 %collective-permute-start.2 = (f32[512,256]{1,0:T(8,128)}, f32[512,256]{1,0:T(8,128)S(1)}, u32[]{:S(2)}, u32[]{:S(2)}) collective-permute-start(f32[512,256]{1,0:T(8,128)} %get-tuple-element.45), channel_id=1, source_target_pairs={{0,1},{1,0},{2,3},{3,2},{4,5},{5,4},{6,7},{7,6},{8,9},{9,8},{10,11... | collective-permute-start | bytes 1572872 | tf_op jit(solution)/shard_map/ppermute | solution.py:380
  70.8 22.3 %collective-permute-start.4 = (f32[8,128,128]{2,1,0:T(8,128)}, f32[8,128,128]{2,1,0:T(8,128)S(1)}, u32[]{:S(2)}, u32[]{:S(2)}) collective-permute-start(f32[8,128,128]{2,1,0:T(8,128)} %bitcast.38), channel_id=1, source_target_pairs={{0,1},{1,0},{2,3},{3,2},{4,5},{5,4},{6,7},{7,6},{8,9},{9,8},{10,11... | collective-permute-start | bytes 1572872 | tf_op jit(solution)/shard_map/ppermute | solution.py:380
  73.7 1.6 %copy-start.11 = (bf16[4,2,128,128]{3,2,1,0:T(8,128)(2,1)S(1)}, bf16[4,2,128,128]{3,2,1,0:T(8,128)(2,1)}, u32[]{:S(2)}) copy-start(bf16[4,2,128,128]{3,2,1,0:T(8,128)(2,1)} %get-tuple-element.47) | copy-start | bytes 786436
  73.7 2.9 %copy-start.10 = (bf16[4,2,128,128]{3,2,1,0:T(8,128)(2,1)S(1)}, bf16[4,2,128,128]{3,2,1,0:T(8,128)(2,1)}, u32[]{:S(2)}) copy-start(bf16[4,2,128,128]{3,2,1,0:T(8,128)(2,1)} %get-tuple-element.48) | copy-start | bytes 786436
  73.7 9.2 %collective-permute-start.3 = (f32[256,256]{1,0:T(8,128)S(1)}, f32[256,256]{1,0:T(8,128)S(1)}, u32[]{:S(2)}, u32[]{:S(2)}) collective-permute-start(f32[256,256]{1,0:T(8,128)S(1)} %slice_select_fusion), channel_id=1, source_target_pairs={{0,2},{2,0},{1,3},{3,1},{4,6},{6,4},{5,7},{7,5},{8,10},{10,8},{9,1... | collective-permute-start | bytes 786440 | tf_op jit(solution)/shard_map/ppermute | solution.py:380
  75.3 13.3 %collective-permute-start.5 = (bf16[8,128,128]{2,1,0:T(8,128)(2,1)S(1)}, bf16[8,128,128]{2,1,0:T(8,128)(2,1)S(1)}, u32[]{:S(2)}, u32[]{:S(2)}) collective-permute-start(bf16[8,128,128]{2,1,0:T(8,128)(2,1)S(1)} %bitcast.40), channel_id=1, source_target_pairs={{2,0},{3,1},{6,4},{7,5},{10,8},{11,9},{14,12},{15,13},{18,16},{19,... | collective-permute-start | bytes 786440 | tf_op jit(solution)/shard_map/ppermute | solution.py:481
  76.6 16.5 %collective-permute-start.6 = (bf16[8,128,128]{2,1,0:T(8,128)(2,1)S(1)}, bf16[8,128,128]{2,1,0:T(8,128)(2,1)S(1)}, u32[]{:S(2)}, u32[]{:S(2)}) collective-permute-start(bf16[8,128,128]{2,1,0:T(8,128)(2,1)S(1)} %bitcast.39), channel_id=1, source_target_pairs={{2,1},{3,0},{6,5},{7,4},{10,9},{11,8},{14,13},{15,12},{18,17},{19,... | collective-permute-start | bytes 786440 | tf_op jit(solution)/shard_map/ppermute | solution.py:482
  93.1 5.8 %collective-permute-start.7 = (bf16[256,256]{1,0:T(8,128)(2,1)S(1)}, bf16[256,256]{1,0:T(8,128)(2,1)S(1)}, u32[]{:S(2)}, u32[]{:S(2)}) collective-permute-start(bf16[256,256]{1,0:T(8,128)(2,1)S(1)} %select_add_fusion), channel_id=1, source_target_pairs={{0,4},{4,0},{8,12},{12,8},{1,5},{5,1},{9,13},{13,9},{2,6},{6,2},{1... | collective-permute-start | bytes 393224 | tf_op jit(solution)/shard_map/ppermute | solution.py:380
  94.5 25.1 %all-to-all-start.3 = ((bf16[8,256,128]{2,1,0:T(8,128)(2,1)}), bf16[8,256,128]{2,1,0:T(8,128)(2,1)S(1)}, u32[]{:S(2)}, u32[]{:S(2)}) async-start(bf16[8,256,128]{2,1,0:T(8,128)(2,1)} %bitcast.18), calls=%async_computation.3 | async-start | bytes 1048576 | tf_op jit(solution)/shard_map/all_to_all | solution.py:457
  98.2 21.4 %copy-start.1 = (f32[4,2,128,128]{3,2,1,0:T(8,128)S(1)}, f32[4,2,128,128]{3,2,1,0:T(8,128)}, u32[]{:S(2)}) copy-start(f32[4,2,128,128]{3,2,1,0:T(8,128)} %get-tuple-element.40) | copy-start | bytes 1572868
  98.9 20.2 %collective-permute-start.8 = (bf16[256,256]{1,0:T(8,128)(2,1)S(1)}, bf16[256,256]{1,0:T(8,128)(2,1)S(1)}, u32[]{:S(2)}, u32[]{:S(2)}) collective-permute-start(bf16[256,256]{1,0:T(8,128)(2,1)S(1)} %add_convert_fusion), channel_id=1, source_target_pairs={{0,8},{4,12},{8,0},{12,4},{1,9},{5,13},{9,1},{13,5},{2,10},{6,14},... | collective-permute-start | bytes 393224 | tf_op jit(solution)/shard_map/ppermute | solution.py:380
  119.2 7.9 %collective-permute-start.9 = (f32[256,256]{1,0:T(8,128)S(1)}, f32[256,256]{1,0:T(8,128)S(1)}, u32[]{:S(2)}, u32[]{:S(2)}) collective-permute-start(f32[256,256]{1,0:T(8,128)S(1)} %convert_add_fusion), channel_id=1, source_target_pairs={{0,2},{2,0},{1,3},{3,1},{4,6},{6,4},{5,7},{7,5},{8,10},{10,8},{9,1... | collective-permute-start | bytes 786440 | tf_op jit(solution)/shard_map/ppermute | solution.py:380

commit v4 on v3

--- a/solution.py
+++ b/solution.py
@@ -381,26 +381,38 @@
 
 
 def summed_over(value, axis, bit):
-    while bit < lax.axis_size(axis):
-        low = value.astype(BF16)
-        value = low.astype(F32) + exchanged(low, axis, bit).astype(F32)
-        bit *= 2
-    return value
-
-
-def sum_gradients(total, settled):
+    low = value.astype(BF16)
+    return low.astype(F32) + exchanged(low, axis, bit).astype(F32)
+
+
+def sum_gradients(total, early, late):
     half = total.shape[0] // 2
     first = lax.rem(lax.axis_index("day"), 2) == 0
     kept = jnp.where(first, total[:half], total[half:])
     given = jnp.where(first, total[half:], total[:half])
     part = kept + exchanged(given, "day", 1)
-    part = summed_over(part, "day", 2)
-    part, *settled = lax.optimization_barrier((part, *settled))
-    part = summed_over(part, "reach", 1)
-    other = exchanged(part, "day", 1)
-    upper = jnp.where(first, part, other)
-    lower = jnp.where(first, other, part)
-    return upper, lower, settled
+    bit = 2
+    while bit < lax.axis_size("day"):
+        part = summed_over(part, "day", bit)
+        bit *= 2
+    part, *early = lax.optimization_barrier((part, *early))
+    bit = 1
+    while bit < lax.axis_size("reach"):
+        part = summed_over(part, "reach", bit)
+        if bit == 1:
+            part, *late = lax.optimization_barrier((part, *late))
+        bit *= 2
+    return part, exchanged(part, "day", 1), (*early, *late)
+
+
+def split_kernel(where, part, other, query_out, key_out, value_out, output_out):
+    first = lax.rem(where[3], 2) == 0
+    upper = jnp.where(first, part[...], other[...])
+    lower = jnp.where(first, other[...], part[...])
+    key_out[...] = upper[:, :GROUP]
+    value_out[...] = upper[:, GROUP:]
+    query_out[...] = lower[:GROUP].T
+    output_out[...] = lower[GROUP:]
 
 
 def on_device(
@@ -421,6 +433,7 @@
             lax.axis_index("reach"),
             lax.axis_index("head"),
             (lax.axis_index("day") > 0).astype(jnp.int32),
+            lax.axis_index("day"),
         ]
     )
     pack = jnp.concatenate([key_weight.T, value_weight.T, query_weight.T, output_weight], axis=0)
@@ -488,9 +501,21 @@
             for c in range(CORES)
         ],
     )
-    upper, lower, (swapped, same_came, cross_came) = sum_gradients(
-        grad_mine + grad_swapped, (swapped, same_came, cross_came)
-    )
+    part, other, (home_b, swapped, same_came, cross_came) = sum_gradients(
+        grad_mine + grad_swapped, (home_b, swapped, same_came), (cross_came,)
+    )
+    weight_grads = pl.pallas_call(
+        split_kernel,
+        out_shape=(
+            jax.ShapeDtypeStruct((width, half), F32),
+            jax.ShapeDtypeStruct((width, half), F32),
+            jax.ShapeDtypeStruct((width, half), F32),
+            jax.ShapeDtypeStruct((half, width), F32),
+        ),
+        in_specs=[smem] + [in_vmem] * 2,
+        out_specs=[in_vmem] * 4,
+        name="split",
+    )(where, part, other)
 
     back_blocks = pl.pallas_call(
         lambda *refs: gather_kernel(lay, *refs),
@@ -500,13 +525,7 @@
         compiler_params=pltpu.CompilerParams(vmem_limit_bytes=16 << 20),
         name="assemble",
     )(tab, keep, swapped, same_came, cross_came, home_a, home_b)
-    return (
-        back_blocks.reshape(1, rows_dev, half),
-        lower[:GROUP].T,
-        upper[:, :GROUP],
-        upper[:, GROUP:],
-        lower[GROUP:],
-    )
+    return (back_blocks.reshape(1, rows_dev, half), *weight_grads)
 
 
 def solution(mesh):

time: 130 us -> 122 us (0.938)
  waiting for transfers between devices: 49.8 us -> 41.5 us
  Pallas kernels: 39 us -> 40.9 us
  local copies, waits for them, and re-layouts: 6.68 us -> 5.25 us
    ppermute x7, waiting for transfers between devices: 30.7 us -> 21 us  [exchanged(): lax.ppermute(value, axis, [(place, place ^ bit) for place in range(count)])]
    pallas_call x0 -> x1, Pallas kernels: none -> 1.86 us  [on_device(): pl.pallas_call(split_kernel, out_shape=(jax.ShapeDtypeStruct((width, half...]
    ppermute x1, waiting for transfers between devices: 4.5 us -> 6.06 us  [on_device(): lax.ppermute(cross, ('day', 'head'), [((d + 1) * CORES + c, d * CORES + 1...]
    slice x2 -> x0, local copies, waits for them, and re-layouts: 1.39 us -> none  [the longest x1 0.72 us: on_device(): upper[:, GROUP:]]
    unnamed x30 -> x39, local copies, waits for them, and re-layouts: 5.29 us -> 5.25 us
  transfers between devices with their start and end apart: 14 -> 14, of which waited for: 8 -> 8; matrix products, arithmetic and copies ran while one was open for 1% -> 0% of each run, Pallas kernels for 27% -> 29%
where the time goes in v4:
time: 122 us; the launch traced here: 121 us
  waiting for transfers between devices  41.5 us (34%)
  Pallas kernels  40.9 us (34%)
  starting transfers between devices  32.5 us (27%)
  local copies, waits for them, and re-layouts  5.25 us (4%)
    pallas_call x2, Pallas kernels, attend(): pl.pallas_call(lambda *refs: attention_kernel(lay, chunk, *refs), grid_sp...  33.3 us
    ppermute x7, waiting for transfers between devices, exchanged(): lax.ppermute(value, axis, [(place, place ^ bit) for place in range(count)])  21 us
    all_to_all x2, starting transfers between devices, homeward(): lax.all_to_all(home.reshape(lay.reach * CORES, lay.slots * BLOCK, half),...  9.94 us
    all_to_all x2, starting transfers between devices, outward(): lax.all_to_all(sent.reshape(lay.reach, lay.slots * BLOCK, width), 'reach'...  9.93 us
    all_to_all x2, waiting for transfers between devices, outward(): lax.all_to_all(sent.reshape(lay.reach, lay.slots * BLOCK, width), 'reach'...  9.01 us
    ppermute x7, starting transfers between devices, exchanged(): lax.ppermute(value, axis, [(place, place ^ bit) for place in range(count)])  6.37 us
    ppermute x1, waiting for transfers between devices, on_device(): lax.ppermute(cross, ('day', 'head'), [((d + 1) * CORES + c, d * CORES + 1...  6.06 us
    unnamed x39, local copies, waits for them, and re-layouts  5.25 us
  transfers between devices with their start and end apart: 14, of which 8 were waited for; matrix products, arithmetic and copies ran while one was open for 0% of the time, Pallas kernels for 29%

profile of v4, /device:TPU:0, one launch (start us, length us, event | category | flops | bytes accessed | tf_op | source)
XLA Modules:
  0.0 121.3 jit_solution(11833101386749945313)
XLA Ops:
  0.6 0.1 pad_add_fusion.refs_2_.where
  0.7 0.5 copy-done.2
  1.2 0.2 copy-done.3
  1.4 0.0 copy-done.4
  1.4 1.2 %copy-done = bf16[1,2048,256]{2,1,0:T(8,128)(2,1)S(1)} copy-done((bf16[1,2048,256]{2,1,0:T(8,128)(2,1)S(1)}, bf16[1,2048,256]{2,1,0:T(8,128)(2,1)}, u32[]{:S(2)}) %copy-start) | copy-done | bytes 1048600
  2.6 3.9 %prepare.1 = (bf16[8,128,256]{2,1,0:T(8,128)(2,1)}, bf16[8,128,256]{2,1,0:T(8,128)(2,1)}, bf16[8,128,256]{2,1,0:T(8,128)(2,1)S(1)}, s32[128]{0:T(128)S(1)}) custom-call(s32[64]{0:T(128)S(1)} %copy-done.3, s32[64]{0:T(128)S(1)} %copy-done.4, s32[4]{0:T(128)S(1)} %pad_add_fusion.refs_2_.where, bf16[16,128,256]{2,1,0:T(8,128)(2,1)S(1)} %bitcast.26), custom_call_target="tpu_custom_call" | custom-call | tf_op jit(solution)/shard_map/prepare/pallas_call | solution.py:445
  6.5 0.0 copy-start.9
  6.5 6.5 %all-to-all-start.1 = ((bf16[4,256,256]{2,1,0:T(8,128)(2,1)}), bf16[4,256,256]{2,1,0:T(8,128)(2,1)S(1)}, u32[]{:S(2)}, u32[]{:S(2)}) async-start(bf16[4,256,256]{2,1,0:T(8,128)(2,1)} %bitcast.11), calls=%async_computation.1 | async-start | bytes 1048576 | tf_op jit(solution)/shard_map/all_to_all | solution.py:465
  13.0 3.5 %collective-permute-start = (bf16[8,128,256]{2,1,0:T(8,128)(2,1)S(1)}, bf16[8,128,256]{2,1,0:T(8,128)(2,1)S(1)}, u32[]{:S(2)}, u32[]{:S(2)}) collective-permute-start(bf16[8,128,256]{2,1,0:T(8,128)(2,1)S(1)} %get-tuple-element.38), channel_id=1, source_target_pairs={{0,2},{1,3},{4,6},{5,7},{8,10},{9,11},{12,14},{13,15},{16,18},{17,... | collective-permute-start | bytes 1572872 | tf_op jit(solution)/shard_map/ppermute | solution.py:479
  16.6 0.1 copy.15
  16.7 0.0 copy-start.11
  16.7 0.1 copy.13
  16.8 0.7 copy-done.11
  17.5 0.1 copy.14
  17.7 0.7 copy-done.12
  18.4 0.1 collective-permute-start.1
  18.5 9.0 %all-to-all-done.1 = bf16[4,256,256]{2,1,0:T(8,128)(2,1)S(1)} async-done(((bf16[4,256,256]{2,1,0:T(8,128)(2,1)}), bf16[4,256,256]{2,1,0:T(8,128)(2,1)S(1)}, u32[]{:S(2)}, u32[]{:S(2)}) %all-to-all-start.1) | async-done | bytes 524320 | tf_op jit(solution)/shard_map/all_to_all | solution.py:465
  27.5 3.5 %all-to-all-start = ((bf16[4,256,256]{2,1,0:T(8,128)(2,1)}), bf16[4,256,256]{2,1,0:T(8,128)(2,1)S(1)}, u32[]{:S(2)}, u32[]{:S(2)}) async-start(bf16[4,256,256]{2,1,0:T(8,128)(2,1)} %bitcast.6), calls=%async_computation | async-start | bytes 1048576 | tf_op jit(solution)/shard_map/all_to_all | solution.py:465
  31.0 0.0 copy-start.14
  31.0 0.7 copy-done.17
  31.7 0.2 copy-done.14
  31.9 16.3 %attention_0.1 = (f32[4,128,128]{2,1,0:T(8,128)}, f32[4,128,128]{2,1,0:T(8,128)}, bf16[4,128,128]{2,1,0:T(8,128)(2,1)}, bf16[4,128,128]{2,1,0:T(8,128)(2,1)}, bf...) custom-call(s32[128]{0:T(128)S(1)} %get-tuple-element.36.refs_0_, ...), custom_call_target="tpu_custom_call" | custom-call | flops 6375342080 | bytes 5242880 | tf_op jit(solution)/shard_map/attention_0/pallas_call | solution.py:340
  48.2 0.0 all-to-all-done
  48.2 5.1 %all-to-all-start.2 = ((bf16[8,256,128]{2,1,0:T(8,128)(2,1)}), bf16[8,256,128]{2,1,0:T(8,128)(2,1)S(1)}, u32[]{:S(2)}, u32[]{:S(2)}) async-start(bf16[8,256,128]{2,1,0:T(8,128)(2,1)} %bitcast.31), calls=%async_computation.2 | async-start | bytes 1048576 | tf_op jit(solution)/shard_map/all_to_all | solution.py:470
  53.3 17.0 %attention_1.1 = (f32[4,2,128,128]{3,2,1,0:T(8,128)}, f32[4,2,128,128]{3,2,1,0:T(8,128)}, bf16[4,2,128,128]{3,2,1,0:T(8,128)(2,1)}, bf16[4,2,128,128]{3,2,1,0:T(...) custom-call(s32[128]{0:T(128)S(1)} %get-tuple-element.36.refs_0_, ...), custom_call_target="tpu_custom_call" | custom-call | flops 6375342080 | bytes 5242880 | tf_op jit(solution)/shard_map/attention_1/pallas_call | solution.py:340
  70.3 0.6 collective-permute-start.2
  70.8 4.9 %all-to-all-start.3 = ((bf16[8,256,128]{2,1,0:T(8,128)(2,1)}), bf16[8,256,128]{2,1,0:T(8,128)(2,1)S(1)}, u32[]{:S(2)}, u32[]{:S(2)}) async-start(bf16[8,256,128]{2,1,0:T(8,128)(2,1)} %bitcast.30), calls=%async_computation.3 | async-start | bytes 1048576 | tf_op jit(solution)/shard_map/all_to_all | solution.py:470
  75.7 0.5 collective-permute-start.4
  76.2 0.0 collective-permute-done.2
  76.2 0.1 add.12
  76.4 1.5 %collective-permute-start.3 = (f32[256,256]{1,0:T(8,128)S(1)}, f32[256,256]{1,0:T(8,128)S(1)}, u32[]{:S(2)}, u32[]{:S(2)}) collective-permute-start(f32[256,256]{1,0:T(8,128)S(1)} %slice_select_fusion), channel_id=1, source_target_pairs={{0,2},{2,0},{1,3},{3,1},{4,6},{6,4},{5,7},{7,5},{8,10},{10,8},{9,1... | collective-permute-start | bytes 786440 | tf_op jit(solution)/shard_map/ppermute | solution.py:380
  77.9 1.4 %collective-permute-start.5 = (bf16[8,128,128]{2,1,0:T(8,128)(2,1)S(1)}, bf16[8,128,128]{2,1,0:T(8,128)(2,1)S(1)}, u32[]{:S(2)}, u32[]{:S(2)}) collective-permute-start(bf16[8,128,128]{2,1,0:T(8,128)(2,1)S(1)} %bitcast.40), channel_id=1, source_target_pairs={{2,0},{3,1},{6,4},{7,5},{10,8},{11,9},{14,12},{15,13},{18,16},{19,... | collective-permute-start | bytes 786440 | tf_op jit(solution)/shard_map/ppermute | solution.py:494
  79.3 6.3 %collective-permute-done.3 = f32[256,256]{1,0:T(8,128)S(1)} collective-permute-done((f32[256,256]{1,0:T(8,128)S(1)}, f32[256,256]{1,0:T(8,128)S(1)}, u32[]{:S(2)}, u32[]{:S(2)}) %collective-permute-start.3) | collective-permute-done | bytes 262176 | tf_op jit(solution)/shard_map/ppermute | solution.py:380
  85.6 0.1 select_add_fusion
  85.6 4.7 %collective-permute-done.5.refs_3_ = bf16[8,128,128]{2,1,0:T(8,128)(2,1)S(1)} collective-permute-done((bf16[8,128,128]{2,1,0:T(8,128)(2,1)S(1)}, bf16[8,128,128]{2,1,0:T(8,128)(2,1)S(1)}, u32[]{:S(2)}, u32[]{:S(2)}) %collective-permute-start.5) | collective-permute-done | bytes 262176 | tf_op jit(solution)/shard_map/ppermute | solution.py:494
  90.3 0.0 collective-permute-done.4.refs_2_
  90.3 0.8 all-to-all-done.3
  91.1 1.2 collective-permute-start.6
  92.3 1.3 %collective-permute-start.7 = (bf16[8,128,128]{2,1,0:T(8,128)(2,1)S(1)}, bf16[8,128,128]{2,1,0:T(8,128)(2,1)S(1)}, u32[]{:S(2)}, u32[]{:S(2)}) collective-permute-start(bf16[8,128,128]{2,1,0:T(8,128)(2,1)S(1)} %bitcast.39), channel_id=1, source_target_pairs={{2,1},{3,0},{6,5},{7,4},{10,9},{11,8},{14,13},{15,12},{18,17},{19,... | collective-permute-start | bytes 786440 | tf_op jit(solution)/shard_map/ppermute | solution.py:495
  93.6 2.5 %collective-permute-done.6 = bf16[256,256]{1,0:T(8,128)(2,1)S(1)} collective-permute-done((bf16[256,256]{1,0:T(8,128)(2,1)S(1)}, bf16[256,256]{1,0:T(8,128)(2,1)S(1)}, u32[]{:S(2)}, u32[]{:S(2)}) %collective-permute-start.6) | collective-permute-done | bytes 131104 | tf_op jit(solution)/shard_map/ppermute | solution.py:380
  96.2 6.1 %collective-permute-done.7.refs_4_ = bf16[8,128,128]{2,1,0:T(8,128)(2,1)S(1)} collective-permute-done((bf16[8,128,128]{2,1,0:T(8,128)(2,1)S(1)}, bf16[8,128,128]{2,1,0:T(8,128)(2,1)S(1)}, u32[]{:S(2)}, u32[]{:S(2)}) %collective-permute-start.7) | collective-permute-done | bytes 262176 | tf_op jit(solution)/shard_map/ppermute | solution.py:495
  102.2 2.4 %collective-permute-start.8 = (bf16[256,256]{1,0:T(8,128)(2,1)S(1)}, bf16[256,256]{1,0:T(8,128)(2,1)S(1)}, u32[]{:S(2)}, u32[]{:S(2)}) collective-permute-start(bf16[256,256]{1,0:T(8,128)(2,1)S(1)} %convert_add_fusion.1), channel_id=1, source_target_pairs={{0,8},{4,12},{8,0},{12,4},{1,9},{5,13},{9,1},{13,5},{2,10},{6,14},... | collective-permute-start | bytes 393224 | tf_op jit(solution)/shard_map/ppermute | solution.py:380
  104.6 6.4 %collective-permute-done.8 = bf16[256,256]{1,0:T(8,128)(2,1)S(1)} collective-permute-done((bf16[256,256]{1,0:T(8,128)(2,1)S(1)}, bf16[256,256]{1,0:T(8,128)(2,1)S(1)}, u32[]{:S(2)}, u32[]{:S(2)}) %collective-permute-start.8) | collective-permute-done | bytes 131104 | tf_op jit(solution)/shard_map/ppermute | solution.py:380
  111.0 0.1 collective-permute-start.9
  111.1 1.8 %assemble.1 = bf16[16,128,128]{2,1,0:T(8,128)(2,1)} custom-call(s32[128]{0:T(128)S(1)} %get-tuple-element.36.refs_0_, f32[8,128,128]{2,1,0:T(8,128)S(1)} %bitcast.29, f32[8,128,128]{2,1,0:T(8,128)S(1)} %collective-permute-done.4.refs_2_, bf16[8,128,128]{2,1,0:T(8,128)(2,1)S(1)} %collective-permute-done.5.refs_3_, ...), custom_call_target="tpu_custom_call" | custom-call | tf_op jit(solution)/shard_map/assemble/pallas_call | solution.py:520
  112.9 5.9 %collective-permute-done.9.other = f32[256,256]{1,0:T(8,128)S(1)} collective-permute-done((f32[256,256]{1,0:T(8,128)S(1)}, f32[256,256]{1,0:T(8,128)S(1)}, u32[]{:S(2)}, u32[]{:S(2)}) %collective-permute-start.9) | collective-permute-done | bytes 262176 | tf_op jit(solution)/shard_map/ppermute | solution.py:380
  118.8 0.7 copy-done.7
  119.5 1.9 %split.1 = (f32[256,128]{1,0:T(8,128)}, f32[256,128]{1,0:T(8,128)}, f32[256,128]{1,0:T(8,128)}, f32[128,256]{1,0:T(8,128)}) custom-call(s32[4]{0:T(128)} %copy-done.2, f32[256,256]{1,0:T(8,128)} %copy-done.5, f32[256,256]{1,0:T(8,128)} %copy-done.7), custom_call_target="tpu_custom_call" | custom-call | tf_op jit(solution)/shard_map/split/pallas_call | solution.py:507
  (31 shorter events, 0.2 us)
Async XLA Ops:
  0.7 0.5 copy-start.2
  0.7 0.7 copy-start.3
  0.7 0.7 copy-start.4
  1.4 1.2 %copy-start = (bf16[1,2048,256]{2,1,0:T(8,128)(2,1)S(1)}, bf16[1,2048,256]{2,1,0:T(8,128)(2,1)}, u32[]{:S(2)}) copy-start(bf16[1,2048,256]{2,1,0:T(8,128)(2,1)} %param.8) | copy-start | bytes 3145732
  6.5 10.0 %copy-start.9 = (bf16[256,128]{1,0:T(8,128)(2,1)S(1)}, bf16[256,128]{1,0:T(8,128)(2,1)}, u32[]{:S(2)}) copy-start(bf16[256,128]{1,0:T(8,128)(2,1)} %param.10) | copy-start | bytes 196612
  6.5 21.0 %all-to-all-start.1 = ((bf16[4,256,256]{2,1,0:T(8,128)(2,1)}), bf16[4,256,256]{2,1,0:T(8,128)(2,1)S(1)}, u32[]{:S(2)}, u32[]{:S(2)}) async-start(bf16[4,256,256]{2,1,0:T(8,128)(2,1)} %bitcast.11), calls=%async_computation.1 | async-start | bytes 1048576 | tf_op jit(solution)/shard_map/all_to_all | solution.py:465
  13.0 3.7 %copy-start.10 = (bf16[256,128]{1,0:T(8,128)(2,1)S(1)}, bf16[256,128]{1,0:T(8,128)(2,1)}, u32[]{:S(2)}) copy-start(bf16[256,128]{1,0:T(8,128)(2,1)} %param.11) | copy-start | bytes 196612
  13.0 18.0 %collective-permute-start = (bf16[8,128,256]{2,1,0:T(8,128)(2,1)S(1)}, bf16[8,128,256]{2,1,0:T(8,128)(2,1)S(1)}, u32[]{:S(2)}, u32[]{:S(2)}) collective-permute-start(bf16[8,128,256]{2,1,0:T(8,128)(2,1)S(1)} %get-tuple-element.38), channel_id=1, source_target_pairs={{0,2},{1,3},{4,6},{5,7},{8,10},{9,11},{12,14},{13,15},{16,18},{17,... | collective-permute-start | bytes 1572872 | tf_op jit(solution)/shard_map/ppermute | solution.py:479
  16.7 0.8 copy-start.11
  17.5 0.8 copy-start.12
  18.4 9.1 %copy-start.8 = (bf16[512,256]{1,0:T(8,128)(2,1)}, bf16[512,256]{1,0:T(8,128)(2,1)S(1)}, u32[]{:S(2)}) copy-start(bf16[512,256]{1,0:T(8,128)(2,1)S(1)} %pad_maximum_fusion.refs_5_) | copy-start | bytes 786436
  18.4 12.6 %collective-permute-start.1 = (bf16[512,256]{1,0:T(8,128)(2,1)S(1)}, bf16[512,256]{1,0:T(8,128)(2,1)S(1)}, u32[]{:S(2)}, u32[]{:S(2)}) collective-permute-start(bf16[512,256]{1,0:T(8,128)(2,1)S(1)} %pad_maximum_fusion.refs_5_), channel_id=1, source_target_pairs={{0,1},{1,0},{2,3},{3,2},{4,5},{5,4},{6,7},{7,6},{8,9},{9,8},{10,11... | collective-permute-start | bytes 786440 | tf_op jit(solution)/shard_map/ppermute | solution.py:380
  27.5 20.7 %all-to-all-start = ((bf16[4,256,256]{2,1,0:T(8,128)(2,1)}), bf16[4,256,256]{2,1,0:T(8,128)(2,1)S(1)}, u32[]{:S(2)}, u32[]{:S(2)}) async-start(bf16[4,256,256]{2,1,0:T(8,128)(2,1)} %bitcast.6), calls=%async_computation | async-start | bytes 1048576 | tf_op jit(solution)/shard_map/all_to_all | solution.py:465
  31.0 0.7 copy-start.17
  31.0 0.9 copy-start.14
  48.2 22.0 %all-to-all-start.2 = ((bf16[8,256,128]{2,1,0:T(8,128)(2,1)}), bf16[8,256,128]{2,1,0:T(8,128)(2,1)S(1)}, u32[]{:S(2)}, u32[]{:S(2)}) async-start(bf16[8,256,128]{2,1,0:T(8,128)(2,1)} %bitcast.31), calls=%async_computation.2 | async-start | bytes 1048576 | tf_op jit(solution)/shard_map/all_to_all | solution.py:470
  70.3 6.0 %collective-permute-start.2 = (f32[512,256]{1,0:T(8,128)}, f32[512,256]{1,0:T(8,128)S(1)}, u32[]{:S(2)}, u32[]{:S(2)}) collective-permute-start(f32[512,256]{1,0:T(8,128)} %get-tuple-element.51), channel_id=1, source_target_pairs={{0,1},{1,0},{2,3},{3,2},{4,5},{5,4},{6,7},{7,6},{8,9},{9,8},{10,11... | collective-permute-start | bytes 1572872 | tf_op jit(solution)/shard_map/ppermute | solution.py:380
  70.8 4.9 %copy-start.13 = (f32[4,2,128,128]{3,2,1,0:T(8,128)S(1)}, f32[4,2,128,128]{3,2,1,0:T(8,128)}, u32[]{:S(2)}) copy-start(f32[4,2,128,128]{3,2,1,0:T(8,128)} %get-tuple-element.53) | copy-start | bytes 1572868
  70.8 5.4 %copy-start.6 = (f32[512,256]{1,0:T(8,128)S(1)}, f32[512,256]{1,0:T(8,128)}, u32[]{:S(2)}) copy-start(f32[512,256]{1,0:T(8,128)} %get-tuple-element.47) | copy-start | bytes 1572868
  70.8 20.2 %all-to-all-start.3 = ((bf16[8,256,128]{2,1,0:T(8,128)(2,1)}), bf16[8,256,128]{2,1,0:T(8,128)(2,1)S(1)}, u32[]{:S(2)}, u32[]{:S(2)}) async-start(bf16[8,256,128]{2,1,0:T(8,128)(2,1)} %bitcast.30), calls=%async_computation.3 | async-start | bytes 1048576 | tf_op jit(solution)/shard_map/all_to_all | solution.py:470
  75.7 14.6 %collective-permute-start.4 = (f32[8,128,128]{2,1,0:T(8,128)S(1)}, f32[8,128,128]{2,1,0:T(8,128)S(1)}, u32[]{:S(2)}, u32[]{:S(2)}) collective-permute-start(f32[8,128,128]{2,1,0:T(8,128)S(1)} %bitcast.38), channel_id=1, source_target_pairs={{0,1},{1,0},{2,3},{3,2},{4,5},{5,4},{6,7},{7,6},{8,9},{9,8},{10,11... | collective-permute-start | bytes 1572872 | tf_op jit(solution)/shard_map/ppermute | solution.py:380
  76.3 1.6 %copy-start.16 = (bf16[4,2,128,128]{3,2,1,0:T(8,128)(2,1)S(1)}, bf16[4,2,128,128]{3,2,1,0:T(8,128)(2,1)}, u32[]{:S(2)}) copy-start(bf16[4,2,128,128]{3,2,1,0:T(8,128)(2,1)} %get-tuple-element.54) | copy-start | bytes 786436
  76.4 9.2 %collective-permute-start.3 = (f32[256,256]{1,0:T(8,128)S(1)}, f32[256,256]{1,0:T(8,128)S(1)}, u32[]{:S(2)}, u32[]{:S(2)}) collective-permute-start(f32[256,256]{1,0:T(8,128)S(1)} %slice_select_fusion), channel_id=1, source_target_pairs={{0,2},{2,0},{1,3},{3,1},{4,6},{6,4},{5,7},{7,5},{8,10},{10,8},{9,1... | collective-permute-start | bytes 786440 | tf_op jit(solution)/shard_map/ppermute | solution.py:380
  77.9 14.4 %copy-start.15 = (bf16[4,2,128,128]{3,2,1,0:T(8,128)(2,1)S(1)}, bf16[4,2,128,128]{3,2,1,0:T(8,128)(2,1)}, u32[]{:S(2)}) copy-start(bf16[4,2,128,128]{3,2,1,0:T(8,128)(2,1)} %get-tuple-element.58) | copy-start | bytes 786436
  77.9 12.4 %collective-permute-start.5 = (bf16[8,128,128]{2,1,0:T(8,128)(2,1)S(1)}, bf16[8,128,128]{2,1,0:T(8,128)(2,1)S(1)}, u32[]{:S(2)}, u32[]{:S(2)}) collective-permute-start(bf16[8,128,128]{2,1,0:T(8,128)(2,1)S(1)} %bitcast.40), channel_id=1, source_target_pairs={{2,0},{3,1},{6,4},{7,5},{10,8},{11,9},{14,12},{15,13},{18,16},{19,... | collective-permute-start | bytes 786440 | tf_op jit(solution)/shard_map/ppermute | solution.py:494
  85.6 25.5 %copy-start.1 = (f32[4,2,128,128]{3,2,1,0:T(8,128)S(1)}, f32[4,2,128,128]{3,2,1,0:T(8,128)}, u32[]{:S(2)}) copy-start(f32[4,2,128,128]{3,2,1,0:T(8,128)} %get-tuple-element.46) | copy-start | bytes 1572868
  91.1 5.0 %collective-permute-start.6 = (bf16[256,256]{1,0:T(8,128)(2,1)S(1)}, bf16[256,256]{1,0:T(8,128)(2,1)S(1)}, u32[]{:S(2)}, u32[]{:S(2)}) collective-permute-start(bf16[256,256]{1,0:T(8,128)(2,1)S(1)} %select_add_fusion), channel_id=1, source_target_pairs={{0,4},{4,0},{8,12},{12,8},{1,5},{5,1},{9,13},{13,9},{2,6},{6,2},{1... | collective-permute-start | bytes 393224 | tf_op jit(solution)/shard_map/ppermute | solution.py:380
  92.3 9.9 %collective-permute-start.7 = (bf16[8,128,128]{2,1,0:T(8,128)(2,1)S(1)}, bf16[8,128,128]{2,1,0:T(8,128)(2,1)S(1)}, u32[]{:S(2)}, u32[]{:S(2)}) collective-permute-start(bf16[8,128,128]{2,1,0:T(8,128)(2,1)S(1)} %bitcast.39), channel_id=1, source_target_pairs={{2,1},{3,0},{6,5},{7,4},{10,9},{11,8},{14,13},{15,12},{18,17},{19,... | collective-permute-start | bytes 786440 | tf_op jit(solution)/shard_map/ppermute | solution.py:495
  102.2 8.7 %collective-permute-start.8 = (bf16[256,256]{1,0:T(8,128)(2,1)S(1)}, bf16[256,256]{1,0:T(8,128)(2,1)S(1)}, u32[]{:S(2)}, u32[]{:S(2)}) collective-permute-start(bf16[256,256]{1,0:T(8,128)(2,1)S(1)} %convert_add_fusion.1), channel_id=1, source_target_pairs={{0,8},{4,12},{8,0},{12,4},{1,9},{5,13},{9,1},{13,5},{2,10},{6,14},... | collective-permute-start | bytes 393224 | tf_op jit(solution)/shard_map/ppermute | solution.py:380
  111.0 1.9 %copy-start.5 = (f32[256,256]{1,0:T(8,128)}, f32[256,256]{1,0:T(8,128)S(1)}, u32[]{:S(2)}) copy-start(f32[256,256]{1,0:T(8,128)S(1)} %convert_add_fusion.part) | copy-start | bytes 786436
  111.0 7.8 %collective-permute-start.9 = (f32[256,256]{1,0:T(8,128)S(1)}, f32[256,256]{1,0:T(8,128)S(1)}, u32[]{:S(2)}, u32[]{:S(2)}) collective-permute-start(f32[256,256]{1,0:T(8,128)S(1)} %convert_add_fusion.part), channel_id=1, source_target_pairs={{0,2},{2,0},{1,3},{3,1},{4,6},{6,4},{5,7},{7,5},{8,10},{10,8},{9,1... | collective-permute-start | bytes 786440 | tf_op jit(solution)/shard_map/ppermute | solution.py:380
  118.8 0.7 copy-start.7

commit v5 on v4

--- a/solution.py
+++ b/solution.py
@@ -24,6 +24,7 @@
         self.reach = reach_total
         self.slots = max(1, 2 * blocks_dev // reach_total // WORKERS)
         self.places = reach_total * self.slots
+        self.cyclic = reach_total <= 4
         self.block_of = 0
         self.recv_of = self.items
         self.count_own = 2 * self.items
@@ -32,9 +33,14 @@
         self.item_of = self.owner_of + blocks_dev
         self.home_of = self.item_of + blocks_dev
         self.chunk_of = self.home_of + blocks_dev
-        self.core = self.chunk_of + blocks_dev
+        self.asker_of = self.chunk_of + blocks_dev
+        self.core = self.asker_of + blocks_dev
         self.later_day = self.core + 1
         self.size = -(-(self.core + 2) // 128) * 128
+
+
+    def offset(self, high, low):
+        return lax.rem(high - low + self.reach, self.reach)
 
 
 def prepare_kernel(lay, partner, counts, where, inputs, sent_a, sent_b, prior, tab, start, used, picks):
@@ -73,12 +79,13 @@
         item = chunk * lay.chunk_items + lax.div(place, WORKERS)
         slot = jnp.minimum(lax.div(rank, WORKERS), slots - 1)
         tab[lay.owner_of + index] = owner
-        tab[lay.item_of + index] = lax.div(place, WORKERS) * CHUNKS + chunk
+        tab[lay.item_of + index] = item
 
         @pl.when(owner == core)
         def _():
             tab[lay.block_of + item] = index
-            tab[lay.recv_of + item] = source * slots + slot
+            peer = lay.offset(reach_pos, source) if lay.cyclic else source
+            tab[lay.recv_of + item] = peer * slots + slot
             tab[lay.count_own + item] = counts[reach_pos * bd + index]
             tab[lay.count_partner + item] = counts[wanted]
 
@@ -100,6 +107,7 @@
             return total + jnp.where(source < reach_pos, 1, 0)
 
         base = lax.fori_loop(0, bd, before, jnp.int32(0), unroll=True)
+        target = lay.offset(peer, reach_pos) if lay.cyclic else peer
 
         def serve(index, rank):
             wanted = partner[peer * bd + index]
@@ -112,12 +120,13 @@
                 chunk = lax.rem(lax.div(place, CORES), CHUNKS)
                 slot = jnp.minimum(lax.div(rank, WORKERS), slots - 1)
                 local = lax.rem(wanted, bd)
-                tab[lay.home_of + local] = (peer * CORES + owner) * slots + slot
+                tab[lay.home_of + local] = target * slots + slot
                 tab[lay.chunk_of + local] = chunk
+                tab[lay.asker_of + local] = owner
 
                 @pl.when(owner == core)
                 def _():
-                    picks[chunk * lay.places + peer * slots + slot] = local
+                    picks[chunk * lay.places + target * slots + slot] = local
 
             return rank + jnp.where(hit, 1, 0)
 
@@ -164,13 +173,11 @@
     *refs,
 ):
     if chunk:
-        start_mine_ref, start_other_ref = refs[0], refs[1]
-        carried_refs = refs[2:6]
-        refs = refs[6:]
-    keep_ref, swap_ref, same_ref, cross_ref, home_ref, grad_mine_ref, grad_other_ref = refs
+        start_mine_ref, start_other_ref = refs[:2]
+        refs = refs[2:]
+    own_out_ref, day_ref, home_ref, grad_mine_ref, grad_other_ref = refs
     step = pl.program_id(0)
     item = step + chunk * lay.chunk_items
-    core = tab[lay.core]
     factor = HD ** (-0.5)
     own, up = own_ref[0], up_ref[0]
     key_inputs = jnp.concatenate([own, partner_ref[0], prior_ref[0]], axis=0)
@@ -257,47 +264,42 @@
     grad_mine_ref[384:512, :] += output_grad[:GROUP]
     grad_other_ref[384:512, :] += output_grad[GROUP:]
     back_query = dot_t(eye(BLOCK), back_query_t).astype(BF16)
-    own_term = back_inputs[:BLOCK] + dot(back_query, query_t)
-    partner_term = back_inputs[BLOCK : 2 * BLOCK].astype(BF16)
-    prior_term = back_inputs[2 * BLOCK :]
-    half = width // 2
-    first_core = core == 0
-    terms = (
-        jnp.where(first_core, own_term[:, :half], own_term[:, half:]),
-        jnp.where(first_core, own_term[:, half:], own_term[:, :half]),
-        jnp.where(first_core, prior_term[:, :half], prior_term[:, half:]).astype(BF16),
-        jnp.where(first_core, prior_term[:, half:], prior_term[:, :half]).astype(BF16),
-    )
-    for place, (term_ref, term) in enumerate(zip((keep_ref, swap_ref, same_ref, cross_ref), terms)):
-        if chunk:
-            term_ref[0, 0] = carried_refs[place][0]
-            term_ref[0, 1] = term
-        else:
-            term_ref[0] = term
-    home_ref[0, 0, 0] = partner_term[:, :half]
-    home_ref[0, 1, 0] = partner_term[:, half:]
-
-
-def gather_kernel(lay, tab, keep, swapped, same, cross, home_a, home_b, out):
+    own_out_ref[0] = back_inputs[:BLOCK] + dot(back_query, query_t)
+    home_ref[0] = back_inputs[BLOCK : 2 * BLOCK].astype(BF16)
+    day_ref[0] = back_inputs[2 * BLOCK :].astype(BF16)
+
+
+def fold_kernel(lay, tab, own_a, own_b, day_a, day_b, home_a, home_b, keep, give):
     core = tab[lay.core]
+    half = keep.shape[2]
 
     def one(block, carry):
         item = tab[lay.item_of + block]
         mine = tab[lay.owner_of + block] == core
         place = tab[lay.home_of + block]
-        first = tab[lay.chunk_of + block] == 0
-        total = jnp.where(mine, keep[item], swapped[item])
-        total += jnp.where(mine, same[item].astype(F32), cross[item].astype(F32))
-        total += jnp.where(first, home_a[place].astype(F32), home_b[place].astype(F32))
-        out[block] = total.astype(BF16)
+        asked = tab[lay.asker_of + block] == core
+        early = tab[lay.chunk_of + block] == 0
+        in_a = item < lay.chunk_items
+        item_a = jnp.minimum(item, lay.chunk_items - 1)
+        item_b = jnp.maximum(item - lay.chunk_items, 0)
+        own = jnp.where(in_a, own_a[item_a], own_b[item_b])
+        own += jnp.where(in_a, day_a[item_a].astype(F32), day_b[item_b].astype(F32))
+        home = jnp.where(early, home_a[place].astype(F32), home_b[place].astype(F32))
+        total = jnp.where(mine, own, 0.0) + jnp.where(asked, home, 0.0)
+        low, high = total[:, :half], total[:, half:]
+        keep[block] = jnp.where(core == 0, low, high)
+        give[block] = jnp.where(core == 0, high, low)
         return carry
 
     lax.fori_loop(0, lay.blocks, one, 0)
+
+
+def add_kernel(kept, got, out):
+    out[...] = (kept[...] + got[...]).astype(BF16)
 
 
 def attend(lay, chunk, tab, in_blocks, up_blocks, received, prior_inputs, pack, pack_other, carried):
     width = in_blocks.shape[-1]
-    half = width // 2
     offset = chunk * lay.chunk_items
 
     def at_item(step, tab):
@@ -309,15 +311,13 @@
     def at_recv(step, tab):
         return (tab[lay.recv_of + offset + step], 0, 0)
 
-    def at_home(step, tab):
-        place = tab[lay.recv_of + offset + step]
-        return (lax.div(place, lay.slots), 0, lax.rem(place, lay.slots), 0, 0)
+    def at_step(step, tab):
+        return (step, 0, 0)
 
     def fixed(step, tab):
         return (0, 0)
 
     full_block = (1, BLOCK, width)
-    half_block = (1, BLOCK, half)
     weights_block = (4 * GROUP, width)
     in_specs = [
         pl.BlockSpec(full_block, at_block),
@@ -328,13 +328,9 @@
         pl.BlockSpec(weights_block, fixed),
     ]
     operands = [in_blocks, up_blocks, received, prior_inputs, pack, pack_other]
-    term_shape = (lay.chunk_items, BLOCK, half)
-    term_spec = pl.BlockSpec(half_block, lambda step, tab: (step, 0, 0))
     if chunk:
-        in_specs += [pl.BlockSpec(weights_block, fixed)] * 2 + [term_spec] * 4
-        operands += [carried[5], carried[6]] + list(carried[:4])
-        term_shape = (lay.chunk_items, CHUNKS, BLOCK, half)
-        term_spec = pl.BlockSpec((1, CHUNKS, BLOCK, half), lambda step, tab: (step, 0, 0, 0))
+        in_specs += [pl.BlockSpec(weights_block, fixed)] * 2
+        operands += carried
     pieces = lay.chunk_items
     flops = 2 * pieces * (23 * BLOCK * width * width + 24 * BLOCK * 3 * BLOCK * 512)
     return pl.pallas_call(
@@ -344,18 +340,17 @@
             grid=(pieces,),
             in_specs=in_specs,
             out_specs=(
-                *[term_spec] * 4,
-                pl.BlockSpec((1, CORES, 1, BLOCK, half), at_home),
+                pl.BlockSpec(full_block, at_step),
+                pl.BlockSpec(full_block, at_step),
+                pl.BlockSpec(full_block, at_recv),
                 pl.BlockSpec(weights_block, fixed),
                 pl.BlockSpec(weights_block, fixed),
             ),
         ),
         out_shape=(
-            pltpu.HBM(term_shape, F32),
-            pltpu.HBM(term_shape, F32),
-            pltpu.HBM(term_shape, BF16),
-            pltpu.HBM(term_shape, BF16),
-            pltpu.HBM((lay.reach, CORES, lay.slots, BLOCK, half), BF16),
+            pltpu.HBM((pieces, BLOCK, width), F32),
+            pltpu.HBM((pieces, BLOCK, width), BF16),
+            pltpu.HBM((lay.places, BLOCK, width), BF16),
             pltpu.HBM(weights_block, F32),
             pltpu.HBM(weights_block, F32),
         ),
@@ -385,7 +380,7 @@
     return low.astype(F32) + exchanged(low, axis, bit).astype(F32)
 
 
-def sum_gradients(total, early, late):
+def sum_gradients(total, settled):
     half = total.shape[0] // 2
     first = lax.rem(lax.axis_index("day"), 2) == 0
     kept = jnp.where(first, total[:half], total[half:])
@@ -395,14 +390,12 @@
     while bit < lax.axis_size("day"):
         part = summed_over(part, "day", bit)
         bit *= 2
-    part, *early = lax.optimization_barrier((part, *early))
+    part, *settled = lax.optimization_barrier((part, *settled))
     bit = 1
     while bit < lax.axis_size("reach"):
         part = summed_over(part, "reach", bit)
-        if bit == 1:
-            part, *late = lax.optimization_barrier((part, *late))
         bit *= 2
-    return part, exchanged(part, "day", 1), (*early, *late)
+    return part, exchanged(part, "day", 1), settled
 
 
 def split_kernel(where, part, other, query_out, key_out, value_out, output_out):
@@ -461,49 +454,65 @@
         name="prepare",
     )(partner, counts, where, in_blocks)
 
-    def outward(sent):
-        return lax.all_to_all(
-            sent.reshape(lay.reach, lay.slots * BLOCK, width), "reach", 0, 0, tiled=True
-        ).reshape(lay.places, BLOCK, width)
-
-    def homeward(home):
-        return lax.all_to_all(
-            home.reshape(lay.reach * CORES, lay.slots * BLOCK, half),
-            ("reach", "head"),
-            0,
-            0,
-            tiled=True,
-        ).reshape(lay.reach * CORES * lay.slots, BLOCK, half)
-
-    received_a = outward(sent_a)
-    prior_inputs = lax.ppermute(prior, "day", [(d, d + 1) for d in range(day_total - 1)])
-    received_b = outward(sent_b)
+    def ring(value, back):
+        shape = value.shape
+        if not lay.cyclic:
+            value = value.reshape(lay.reach, lay.slots * BLOCK, width)
+            return [lax.all_to_all(value, "reach", 0, 0, tiled=True).reshape(shape)]
+        pieces = [value[: lay.slots]]
+        for shift in range(1, lay.reach):
+            step = -shift if back else shift
+            pieces.append(
+                lax.ppermute(
+                    value[shift * lay.slots : (shift + 1) * lay.slots],
+                    "reach",
+                    [(place, (place + step) % lay.reach) for place in range(lay.reach)],
+                )
+            )
+        return pieces
+
+    next_day = [(d, d + 1) for d in range(day_total - 1)]
+    last_day = [(d + 1, d) for d in range(day_total - 1)]
+    received_a = jnp.concatenate(ring(sent_a, False), axis=0)
+    prior_inputs = lax.ppermute(prior, "day", next_day)
+    received_b = ring(sent_b, False)
     shared = (prior_inputs, pack, pack_other)
-    first = attend(lay, 0, tab, in_blocks, up_blocks, received_a, *shared, None)
-    home_a = homeward(first[4])
-    keep, swap, same, cross, home, grad_mine, grad_other = attend(
-        lay, 1, tab, in_blocks, up_blocks, received_b, *shared, first
-    )
-    home_a, home, grad_other = lax.optimization_barrier((home_a, home, grad_other))
-    keep, swap, same, cross = (
-        term.reshape(lay.items, BLOCK, half) for term in (keep, swap, same, cross)
-    )
-    home_b = homeward(home)
+    own_a, day_a, home_a, *grads = attend(
+        lay, 0, tab, in_blocks, up_blocks, received_a, *shared, None
+    )
+    received_b, grads = lax.optimization_barrier((received_b, grads))
+    received_b = jnp.concatenate(received_b, axis=0)
+    home_a = ring(home_a, True)
+    day_a = lax.ppermute(day_a, "day", last_day)
+    own_b, day_b, home_b, grad_mine, grad_other = attend(
+        lay, 1, tab, in_blocks, up_blocks, received_b, *shared, grads
+    )
+    home_a, day_a, home_b, day_b, grad_other = lax.optimization_barrier(
+        (home_a, day_a, home_b, day_b, grad_other)
+    )
     grad_swapped = exchanged(grad_other, "head", 1)
-    swapped = exchanged(swap, "head", 1)
-    same_came = lax.ppermute(same, "day", [(d + 1, d) for d in range(day_total - 1)])
-    cross_came = lax.ppermute(
-        cross,
-        ("day", "head"),
-        [
-            ((d + 1) * CORES + c, d * CORES + 1 - c)
-            for d in range(day_total - 1)
-            for c in range(CORES)
-        ],
-    )
-    part, other, (home_b, swapped, same_came, cross_came) = sum_gradients(
-        grad_mine + grad_swapped, (home_b, swapped, same_came), (cross_came,)
-    )
+    home_b = ring(home_b, True)
+    day_b = lax.ppermute(day_b, "day", last_day)
+    part, other, (home_b, day_b) = sum_gradients(grad_mine + grad_swapped, (home_b, day_b))
+    home_a, home_b = jnp.concatenate(home_a, axis=0), jnp.concatenate(home_b, axis=0)
+    half_shape = jax.ShapeDtypeStruct((blocks_dev, BLOCK, half), F32)
+    keep, give = pl.pallas_call(
+        lambda *refs: fold_kernel(lay, *refs),
+        out_shape=(half_shape, half_shape),
+        in_specs=[smem] + [in_vmem] * 6,
+        out_specs=[in_vmem] * 2,
+        compiler_params=pltpu.CompilerParams(vmem_limit_bytes=16 << 20),
+        name="fold",
+    )(tab, own_a, own_b, day_a, day_b, home_a, home_b)
+    got = exchanged(give, "head", 1)
+    back_blocks = pl.pallas_call(
+        add_kernel,
+        out_shape=jax.ShapeDtypeStruct((blocks_dev, BLOCK, half), BF16),
+        in_specs=[in_vmem] * 2,
+        out_specs=in_vmem,
+        compiler_params=pltpu.CompilerParams(vmem_limit_bytes=16 << 20),
+        name="add",
+    )(keep, got)
     weight_grads = pl.pallas_call(
         split_kernel,
         out_shape=(
@@ -517,14 +526,6 @@
         name="split",
     )(where, part, other)
 
-    back_blocks = pl.pallas_call(
-        lambda *refs: gather_kernel(lay, *refs),
-        out_shape=jax.ShapeDtypeStruct((blocks_dev, BLOCK, half), BF16),
-        in_specs=[smem] + [in_vmem] * 6,
-        out_specs=in_vmem,
-        compiler_params=pltpu.CompilerParams(vmem_limit_bytes=16 << 20),
-        name="assemble",
-    )(tab, keep, swapped, same_came, cross_came, home_a, home_b)
     return (back_blocks.reshape(1, rows_dev, half), *weight_grads)
 
 

time: 122 us -> 126 us (1.033)
  starting transfers between devices: 32.5 us -> 39.5 us
  waiting for transfers between devices: 41.5 us -> 34.9 us
  local copies, waits for them, and re-layouts: 5.25 us -> 7.75 us
  other arithmetic: 0.32 us -> 1.63 us
    ppermute x3 -> x15, starting transfers between devices: 6.24 us -> 31.3 us  [the longest x12 24.3 us: ring(): lax.ppermute(value[shift * lay.slots:(shift + 1) * lay.slots], 'reach', [...]
    all_to_all x4 -> x0, starting transfers between devices: 19.9 us -> none  [the longest x2 9.94 us: homeward(): lax.all_to_all(home.reshape(lay.reach * CORES, lay.slots * BLOCK, half),...]
    all_to_all x4 -> x0, waiting for transfers between devices: 9.76 us -> none  [the longest x2 9.01 us: outward(): lax.all_to_all(sent.reshape(lay.reach, lay.slots * BLOCK, width), 'reach'...]
    ppermute x7, waiting for transfers between devices: 21 us -> 25.8 us  [exchanged(): lax.ppermute(value, axis, [(place, place ^ bit) for place in range(count)])]
    ppermute x7, starting transfers between devices: 6.37 us -> 8.12 us  [exchanged(): lax.ppermute(value, axis, [(place, place ^ bit) for place in range(count)])]
    ppermute x3 -> x15, waiting for transfers between devices: 10.7 us -> 9.09 us  [the longest x12 9.08 us: ring(): lax.ppermute(value[shift * lay.slots:(shift + 1) * lay.slots], 'reach', [...]
    unnamed x39 -> x31, local copies, waits for them, and re-layouts: 5.25 us -> 6.51 us
  transfers between devices with their start and end apart: 14 -> 22, of which waited for: 8 -> 8; matrix products, arithmetic and copies ran while one was open for 0% -> 2% of each run, Pallas kernels for 29% -> 30%
where the time goes in v5:
time: 126 us; the launch traced here: 125 us
  Pallas kernels  40.4 us (32%)
  starting transfers between devices  39.5 us (31%)
  waiting for transfers between devices  34.9 us (28%)
  local copies, waits for them, and re-layouts  7.75 us (6%)
  other arithmetic  1.63 us (1%)
    pallas_call x2, Pallas kernels, attend(): pl.pallas_call(lambda *refs: attention_kernel(lay, chunk, *refs), grid_sp...  32.5 us
    ppermute x7, waiting for transfers between devices, exchanged(): lax.ppermute(value, axis, [(place, place ^ bit) for place in range(count)])  25.8 us
    ppermute x12, starting transfers between devices, ring(): lax.ppermute(value[shift * lay.slots:(shift + 1) * lay.slots], 'reach', [...  24.3 us
    ppermute x12, waiting for transfers between devices, ring(): lax.ppermute(value[shift * lay.slots:(shift + 1) * lay.slots], 'reach', [...  9.08 us
    ppermute x7, starting transfers between devices, exchanged(): lax.ppermute(value, axis, [(place, place ^ bit) for place in range(count)])  8.12 us
    unnamed x31, local copies, waits for them, and re-layouts  6.51 us
    ppermute x1, starting transfers between devices, on_device(): prior_inputs = lax.ppermute(prior, 'day', next_day)  4.45 us
    pallas_call x1, Pallas kernels, on_device(): pl.pallas_call(lambda *refs: prepare_kernel(lay, *refs), out_shape=(sent_...  3.56 us
  transfers between devices with their start and end apart: 22, of which 8 were waited for; matrix products, arithmetic and copies ran while one was open for 2% of the time, Pallas kernels for 30%

profile of v5, /device:TPU:0, one launch (start us, length us, event | category | flops | bytes accessed | tf_op | source)
XLA Modules:
  0.0 125.0 jit_solution(14970323860078456296)
XLA Ops:
  0.6 1.0 copy.15
  1.6 0.1 copy.13
  1.8 0.7 copy-done.10
  2.5 0.1 copy.14
  2.6 0.7 copy-done.11
  3.3 0.5 collective-permute-start.4
  3.9 0.1 pad_add_fusion.refs_2_.where
  3.9 0.5 copy-done.3
  4.5 0.1 copy-done.4
  4.6 1.2 copy-done
  5.8 3.6 %prepare.1 = (bf16[8,128,256]{2,1,0:T(8,128)(2,1)S(1)}, bf16[8,128,256]{2,1,0:T(8,128)(2,1)S(1)}, bf16[8,128,256]{2,1,0:T(8,128)(2,1)S(1)}, s32[128]{0:T(128)S(1)}) custom-call(s32[64]{0:T(128)S(1)} %copy-done.4, s32[64]{0:T(128)S(1)} %copy-done.5, s32[4]{0:T(128)S(1)} %pad_add_fusion.refs_2_.where, bf16[16,128,256]{2,1,0:T(8,128)(2,1)S(1)} %bitcast.12), custom_call_target="tpu_custom_call" | custom-call | tf_op jit(solution)/shard_map/prepare/pallas_call | solution.py:438
  9.4 4.4 %collective-permute-start.3 = (bf16[8,128,256]{2,1,0:T(8,128)(2,1)S(1)}, bf16[8,128,256]{2,1,0:T(8,128)(2,1)S(1)}, u32[]{:S(2)}, u32[]{:S(2)}) collective-permute-start(bf16[8,128,256]{2,1,0:T(8,128)(2,1)S(1)} %get-tuple-element.47), channel_id=1, source_target_pairs={{0,2},{1,3},{4,6},{5,7},{8,10},{9,11},{12,14},{13,15},{16,18},{17,... | collective-permute-start | bytes 1572872 | tf_op jit(solution)/shard_map/ppermute | solution.py:477
  13.9 3.7 %collective-permute-start.2 = (bf16[2,128,256]{2,1,0:T(8,128)(2,1)S(1)}, bf16[2,128,256]{2,1,0:T(8,128)(2,1)S(1)}, u32[]{:S(2)}, u32[]{:S(2)}) collective-permute-start(bf16[2,128,256]{2,1,0:T(8,128)(2,1)S(1)} %get-tuple-element.98), channel_id=1, source_target_pairs={{0,12},{4,0},{8,4},{12,8},{1,13},{5,1},{9,5},{13,9},{2,14},{6,2},{... | collective-permute-start | bytes 393224 | tf_op jit(solution)/shard_map/ppermute | solution.py:466
  17.6 1.0 collective-permute-start
  18.6 2.9 %collective-permute-done.2 = bf16[2,128,256]{2,1,0:T(8,128)(2,1)S(1)} collective-permute-done((bf16[2,128,256]{2,1,0:T(8,128)(2,1)S(1)}, bf16[2,128,256]{2,1,0:T(8,128)(2,1)S(1)}, u32[]{:S(2)}, u32[]{:S(2)}) %collective-permute-start.2) | collective-permute-done | bytes 131104 | tf_op jit(solution)/shard_map/ppermute | solution.py:466
  21.5 4.3 %collective-permute-start.7 = (bf16[2,128,256]{2,1,0:T(8,128)(2,1)S(1)}, bf16[2,128,256]{2,1,0:T(8,128)(2,1)S(1)}, u32[]{:S(2)}, u32[]{:S(2)}) collective-permute-start(bf16[2,128,256]{2,1,0:T(8,128)(2,1)S(1)} %get-tuple-element.93), channel_id=1, source_target_pairs={{0,12},{4,0},{8,4},{12,8},{1,13},{5,1},{9,5},{13,9},{2,14},{6,2},{... | collective-permute-start | bytes 393224 | tf_op jit(solution)/shard_map/ppermute | solution.py:466
  25.8 4.1 %collective-permute-done.1 = bf16[2,128,256]{2,1,0:T(8,128)(2,1)S(1)} collective-permute-done((bf16[2,128,256]{2,1,0:T(8,128)(2,1)S(1)}, bf16[2,128,256]{2,1,0:T(8,128)(2,1)S(1)}, u32[]{:S(2)}, u32[]{:S(2)}) %collective-permute-start.1) | collective-permute-done | bytes 131104 | tf_op jit(solution)/shard_map/ppermute | solution.py:466
  29.9 6.4 %collective-permute-start.5 = (bf16[2,128,256]{2,1,0:T(8,128)(2,1)S(1)}, bf16[2,128,256]{2,1,0:T(8,128)(2,1)S(1)}, u32[]{:S(2)}, u32[]{:S(2)}) collective-permute-start(bf16[2,128,256]{2,1,0:T(8,128)(2,1)S(1)} %get-tuple-element.95), channel_id=1, source_target_pairs={{0,4},{4,8},{8,12},{12,0},{1,5},{5,9},{9,13},{13,1},{2,6},{6,10},{... | collective-permute-start | bytes 393224 | tf_op jit(solution)/shard_map/ppermute | solution.py:466
  36.5 0.7 copy-done.13
  37.1 0.2 copy-done.12
  37.3 16.1 %attention_0.1 = (f32[4,128,256]{2,1,0:T(8,128)}, bf16[4,128,256]{2,1,0:T(8,128)(2,1)}, bf16[8,128,256]{2,1,0:T(8,128)(2,1)}, f32[512,256]{1,0:T(8,128)}, f32[512,256]{1,0:T(8,128)}) custom-call(s32[128]{0:T(128)S(1)} %get-tuple-element.45.refs_0_, bf16[16,128,256]{2,1,0:T(8,128)(2,1)} %bitcast.10, bf16[16,128,256]{2,1,0:T(8,128)(2,1)} %bitcast.17, ...), custom_call_target="tpu_custom_call" | custom-call | flops 6375342080 | bytes 5242880 | tf_op jit(solution)/shard_map/attention_0/pallas_call | solution.py:336
  53.4 1.3 %collective-permute-start.11 = (bf16[4,128,256]{2,1,0:T(8,128)(2,1)}, bf16[4,128,256]{2,1,0:T(8,128)(2,1)S(1)}, u32[]{:S(2)}, u32[]{:S(2)}) collective-permute-start(bf16[4,128,256]{2,1,0:T(8,128)(2,1)} %get-tuple-element.60), channel_id=1, source_target_pairs={{2,0},{3,1},{6,4},{7,5},{10,8},{11,9},{14,12},{15,13},{18,16},{19,... | collective-permute-start | bytes 786440 | tf_op jit(solution)/shard_map/ppermute | solution.py:486
  54.7 1.1 fusion.1
  55.8 2.5 %collective-permute-start.10 = (bf16[2,128,256]{2,1,0:T(8,128)(2,1)S(1)}, bf16[2,128,256]{2,1,0:T(8,128)(2,1)S(1)}, u32[]{:S(2)}, u32[]{:S(2)}) collective-permute-start(bf16[2,128,256]{2,1,0:T(8,128)(2,1)S(1)} %get-tuple-element.89), channel_id=1, source_target_pairs={{0,4},{4,8},{8,12},{12,0},{1,5},{5,9},{9,13},{13,1},{2,6},{6,10},{... | collective-permute-start | bytes 393224 | tf_op jit(solution)/shard_map/ppermute | solution.py:466
  58.4 2.4 %collective-permute-start.8 = (bf16[2,128,256]{2,1,0:T(8,128)(2,1)S(1)}, bf16[2,128,256]{2,1,0:T(8,128)(2,1)S(1)}, u32[]{:S(2)}, u32[]{:S(2)}) collective-permute-start(bf16[2,128,256]{2,1,0:T(8,128)(2,1)S(1)} %get-tuple-element.91), channel_id=1, source_target_pairs={{0,12},{4,0},{8,4},{12,8},{1,13},{5,1},{9,5},{13,9},{2,14},{6,2},{... | collective-permute-start | bytes 393224 | tf_op jit(solution)/shard_map/ppermute | solution.py:466
  60.9 16.4 %attention_1.1 = (f32[4,128,256]{2,1,0:T(8,128)}, bf16[4,128,256]{2,1,0:T(8,128)(2,1)}, bf16[8,128,256]{2,1,0:T(8,128)(2,1)}, f32[512,256]{1,0:T(8,128)}, f32[512,256]{1,0:T(8,128)}) custom-call(s32[128]{0:T(128)S(1)} %get-tuple-element.45.refs_0_, bf16[16,128,256]{2,1,0:T(8,128)(2,1)} %bitcast.11, bf16[16,128,256]{2,1,0:T(8,128)(2,1)} %bitcast.18, ...), custom_call_target="tpu_custom_call" | custom-call | flops 6375342080 | bytes 5242880 | tf_op jit(solution)/shard_map/attention_1/pallas_call | solution.py:336
  77.4 0.1 collective-permute-start.12
  77.4 1.3 %collective-permute-start.17 = (bf16[4,128,256]{2,1,0:T(8,128)(2,1)}, bf16[4,128,256]{2,1,0:T(8,128)(2,1)S(1)}, u32[]{:S(2)}, u32[]{:S(2)}) collective-permute-start(bf16[4,128,256]{2,1,0:T(8,128)(2,1)} %get-tuple-element.68), channel_id=1, source_target_pairs={{2,0},{3,1},{6,4},{7,5},{10,8},{11,9},{14,12},{15,13},{18,16},{19,... | collective-permute-start | bytes 786440 | tf_op jit(solution)/shard_map/ppermute | solution.py:495
  78.7 0.8 collective-permute-done.12
  79.5 1.1 add.13
  80.7 2.7 %collective-permute-start.13 = (f32[256,256]{1,0:T(8,128)S(1)}, f32[256,256]{1,0:T(8,128)S(1)}, u32[]{:S(2)}, u32[]{:S(2)}) collective-permute-start(f32[256,256]{1,0:T(8,128)S(1)} %slice_select_fusion), channel_id=1, source_target_pairs={{0,2},{2,0},{1,3},{3,1},{4,6},{6,4},{5,7},{7,5},{8,10},{10,8},{9,1... | collective-permute-start | bytes 786440 | tf_op jit(solution)/shard_map/ppermute | solution.py:375
  83.5 2.5 %collective-permute-start.15 = (bf16[2,128,256]{2,1,0:T(8,128)(2,1)S(1)}, bf16[2,128,256]{2,1,0:T(8,128)(2,1)S(1)}, u32[]{:S(2)}, u32[]{:S(2)}) collective-permute-start(bf16[2,128,256]{2,1,0:T(8,128)(2,1)S(1)} %get-tuple-element.86), channel_id=1, source_target_pairs={{0,8},{4,12},{8,0},{12,4},{1,9},{5,13},{9,1},{13,5},{2,10},{6,14},... | collective-permute-start | bytes 393224 | tf_op jit(solution)/shard_map/ppermute | solution.py:466
  86.0 1.3 %collective-permute-start.14 = (bf16[2,128,256]{2,1,0:T(8,128)(2,1)S(1)}, bf16[2,128,256]{2,1,0:T(8,128)(2,1)S(1)}, u32[]{:S(2)}, u32[]{:S(2)}) collective-permute-start(bf16[2,128,256]{2,1,0:T(8,128)(2,1)S(1)} %get-tuple-element.87), channel_id=1, source_target_pairs={{0,12},{4,0},{8,4},{12,8},{1,13},{5,1},{9,5},{13,9},{2,14},{6,2},{... | collective-permute-start | bytes 393224 | tf_op jit(solution)/shard_map/ppermute | solution.py:466
  87.5 6.7 %collective-permute-done.13 = f32[256,256]{1,0:T(8,128)S(1)} collective-permute-done((f32[256,256]{1,0:T(8,128)S(1)}, f32[256,256]{1,0:T(8,128)S(1)}, u32[]{:S(2)}, u32[]{:S(2)}) %collective-permute-start.13) | collective-permute-done | bytes 262176 | tf_op jit(solution)/shard_map/ppermute | solution.py:375
  94.2 2.1 %collective-permute-done.15 = bf16[2,128,256]{2,1,0:T(8,128)(2,1)S(1)} collective-permute-done((bf16[2,128,256]{2,1,0:T(8,128)(2,1)S(1)}, bf16[2,128,256]{2,1,0:T(8,128)(2,1)S(1)}, u32[]{:S(2)}, u32[]{:S(2)}) %collective-permute-start.15) | collective-permute-done | bytes 131104 | tf_op jit(solution)/shard_map/ppermute | solution.py:466
  96.3 0.1 pad_maximum_fusion.3.refs_6_
  96.4 1.0 copy-done.1
  97.4 0.2 copy-done.2
  97.5 1.6 %fold.1 = (f32[16,128,128]{2,1,0:T(8,128)S(1)}, f32[16,128,128]{2,1,0:T(8,128)S(1)}) custom-call(s32[128]{0:T(128)S(1)} %get-tuple-element.45.refs_0_, f32[4,128,256]{2,1,0:T(8,128)S(1)} %copy-done.1, f32[4,128,256]{2,1,0:T(8,128)S(1)} %copy-done.2, bf16[4,128,256]{2,1,0:T(8,128)(2,1)S(1)} %collective-permute-done.11.refs_3_, ...), custom_call_target="tpu_custom_call" | custom-call | tf_op jit(solution)/shard_map/fold/pallas_call | solution.py:499
  99.1 0.1 collective-permute-start.18
  99.2 2.5 %collective-permute-start.19 = (bf16[256,256]{1,0:T(8,128)(2,1)S(1)}, bf16[256,256]{1,0:T(8,128)(2,1)S(1)}, u32[]{:S(2)}, u32[]{:S(2)}) collective-permute-start(bf16[256,256]{1,0:T(8,128)(2,1)S(1)} %select_add_fusion), channel_id=1, source_target_pairs={{0,4},{4,0},{8,12},{12,8},{1,5},{5,1},{9,13},{13,9},{2,6},{6,2},{1... | collective-permute-start | bytes 393224 | tf_op jit(solution)/shard_map/ppermute | solution.py:375
  101.7 4.1 %collective-permute-done.19 = bf16[256,256]{1,0:T(8,128)(2,1)S(1)} collective-permute-done((bf16[256,256]{1,0:T(8,128)(2,1)S(1)}, bf16[256,256]{1,0:T(8,128)(2,1)S(1)}, u32[]{:S(2)}, u32[]{:S(2)}) %collective-permute-start.19) | collective-permute-done | bytes 131104 | tf_op jit(solution)/shard_map/ppermute | solution.py:375
  105.8 0.9 collective-permute-start.20
  106.7 8.1 %collective-permute-done.20 = bf16[256,256]{1,0:T(8,128)(2,1)S(1)} collective-permute-done((bf16[256,256]{1,0:T(8,128)(2,1)S(1)}, bf16[256,256]{1,0:T(8,128)(2,1)S(1)}, u32[]{:S(2)}, u32[]{:S(2)}) %collective-permute-start.20) | collective-permute-done | bytes 131104 | tf_op jit(solution)/shard_map/ppermute | solution.py:375
  114.9 1.3 %collective-permute-start.21 = (f32[256,256]{1,0:T(8,128)S(1)}, f32[256,256]{1,0:T(8,128)}, u32[]{:S(2)}, u32[]{:S(2)}) collective-permute-start(f32[256,256]{1,0:T(8,128)S(1)} %convert_add_fusion.part), channel_id=1, source_target_pairs={{0,2},{2,0},{1,3},{3,1},{4,6},{6,4},{5,7},{7,5},{8,10},{10,8},{9,1... | collective-permute-start | bytes 786440 | tf_op jit(solution)/shard_map/ppermute | solution.py:375
  116.2 6.1 %collective-permute-done.21.other = f32[256,256]{1,0:T(8,128)} collective-permute-done((f32[256,256]{1,0:T(8,128)S(1)}, f32[256,256]{1,0:T(8,128)}, u32[]{:S(2)}, u32[]{:S(2)}) %collective-permute-start.21) | collective-permute-done | bytes 262176 | tf_op jit(solution)/shard_map/ppermute | solution.py:375
  122.3 1.9 %split.1 = (f32[256,128]{1,0:T(8,128)}, f32[256,128]{1,0:T(8,128)}, f32[256,128]{1,0:T(8,128)}, f32[128,256]{1,0:T(8,128)}) custom-call(s32[4]{0:T(128)} %copy-done.3, f32[256,256]{1,0:T(8,128)} %copy-done.6, f32[256,256]{1,0:T(8,128)} %collective-permute-done.21.other), custom_call_target="tpu_custom_call" | custom-call | tf_op jit(solution)/shard_map/split/pallas_call | solution.py:516
  124.1 0.9 add.26
  (48 shorter events, 0.6 us)
Async XLA Ops:
  0.6 1.0 copy-start.9
  1.6 0.8 copy-start.10
  2.5 0.8 copy-start.11
  3.3 10.6 %copy-start.8 = (bf16[512,256]{1,0:T(8,128)(2,1)}, bf16[512,256]{1,0:T(8,128)(2,1)S(1)}, u32[]{:S(2)}) copy-start(bf16[512,256]{1,0:T(8,128)(2,1)S(1)} %pad_maximum_fusion.4.refs_5_) | copy-start | bytes 786436
  3.3 33.1 %collective-permute-start.4 = (bf16[512,256]{1,0:T(8,128)(2,1)S(1)}, bf16[512,256]{1,0:T(8,128)(2,1)S(1)}, u32[]{:S(2)}, u32[]{:S(2)}) collective-permute-start(bf16[512,256]{1,0:T(8,128)(2,1)S(1)} %pad_maximum_fusion.4.refs_5_), channel_id=1, source_target_pairs={{0,1},{1,0},{2,3},{3,2},{4,5},{5,4},{6,7},{7,6},{8,9},{9,8},{10,11... | collective-permute-start | bytes 786440 | tf_op jit(solution)/shard_map/ppermute | solution.py:375
  3.9 0.5 copy-start.3
  3.9 0.7 copy-start.4
  3.9 0.7 copy-start.5
  4.6 1.2 copy-start
  9.4 27.0 %collective-permute-start.3 = (bf16[8,128,256]{2,1,0:T(8,128)(2,1)S(1)}, bf16[8,128,256]{2,1,0:T(8,128)(2,1)S(1)}, u32[]{:S(2)}, u32[]{:S(2)}) collective-permute-start(bf16[8,128,256]{2,1,0:T(8,128)(2,1)S(1)} %get-tuple-element.47), channel_id=1, source_target_pairs={{0,2},{1,3},{4,6},{5,7},{8,10},{9,11},{12,14},{13,15},{16,18},{17,... | collective-permute-start | bytes 1572872 | tf_op jit(solution)/shard_map/ppermute | solution.py:477
  13.9 7.6 %collective-permute-start.2 = (bf16[2,128,256]{2,1,0:T(8,128)(2,1)S(1)}, bf16[2,128,256]{2,1,0:T(8,128)(2,1)S(1)}, u32[]{:S(2)}, u32[]{:S(2)}) collective-permute-start(bf16[2,128,256]{2,1,0:T(8,128)(2,1)S(1)} %get-tuple-element.98), channel_id=1, source_target_pairs={{0,12},{4,0},{8,4},{12,8},{1,13},{5,1},{9,5},{13,9},{2,14},{6,2},{... | collective-permute-start | bytes 393224 | tf_op jit(solution)/shard_map/ppermute | solution.py:466
  17.6 12.4 %collective-permute-start.1 = (bf16[2,128,256]{2,1,0:T(8,128)(2,1)S(1)}, bf16[2,128,256]{2,1,0:T(8,128)(2,1)S(1)}, u32[]{:S(2)}, u32[]{:S(2)}) collective-permute-start(bf16[2,128,256]{2,1,0:T(8,128)(2,1)S(1)} %get-tuple-element.99), channel_id=1, source_target_pairs={{0,8},{4,12},{8,0},{12,4},{1,9},{5,13},{9,1},{13,5},{2,10},{6,14},... | collective-permute-start | bytes 393224 | tf_op jit(solution)/shard_map/ppermute | solution.py:466
  17.6 12.4 %collective-permute-start = (bf16[2,128,256]{2,1,0:T(8,128)(2,1)S(1)}, bf16[2,128,256]{2,1,0:T(8,128)(2,1)S(1)}, u32[]{:S(2)}, u32[]{:S(2)}) collective-permute-start(bf16[2,128,256]{2,1,0:T(8,128)(2,1)S(1)} %get-tuple-element.100), channel_id=1, source_target_pairs={{0,4},{4,8},{8,12},{12,0},{1,5},{5,9},{9,13},{13,1},{2,6},{6,10},{... | collective-permute-start | bytes 393224 | tf_op jit(solution)/shard_map/ppermute | solution.py:466
  21.5 31.9 %collective-permute-start.7 = (bf16[2,128,256]{2,1,0:T(8,128)(2,1)S(1)}, bf16[2,128,256]{2,1,0:T(8,128)(2,1)S(1)}, u32[]{:S(2)}, u32[]{:S(2)}) collective-permute-start(bf16[2,128,256]{2,1,0:T(8,128)(2,1)S(1)} %get-tuple-element.93), channel_id=1, source_target_pairs={{0,12},{4,0},{8,4},{12,8},{1,13},{5,1},{9,5},{13,9},{2,14},{6,2},{... | collective-permute-start | bytes 393224 | tf_op jit(solution)/shard_map/ppermute | solution.py:466
  29.9 23.4 %collective-permute-start.6 = (bf16[2,128,256]{2,1,0:T(8,128)(2,1)S(1)}, bf16[2,128,256]{2,1,0:T(8,128)(2,1)S(1)}, u32[]{:S(2)}, u32[]{:S(2)}) collective-permute-start(bf16[2,128,256]{2,1,0:T(8,128)(2,1)S(1)} %get-tuple-element.94), channel_id=1, source_target_pairs={{0,8},{4,12},{8,0},{12,4},{1,9},{5,13},{9,1},{13,5},{2,10},{6,14},... | collective-permute-start | bytes 393224 | tf_op jit(solution)/shard_map/ppermute | solution.py:466
  29.9 23.5 %collective-permute-start.5 = (bf16[2,128,256]{2,1,0:T(8,128)(2,1)S(1)}, bf16[2,128,256]{2,1,0:T(8,128)(2,1)S(1)}, u32[]{:S(2)}, u32[]{:S(2)}) collective-permute-start(bf16[2,128,256]{2,1,0:T(8,128)(2,1)S(1)} %get-tuple-element.95), channel_id=1, source_target_pairs={{0,4},{4,8},{8,12},{12,0},{1,5},{5,9},{9,13},{13,1},{2,6},{6,10},{... | collective-permute-start | bytes 393224 | tf_op jit(solution)/shard_map/ppermute | solution.py:466
  36.4 0.7 copy-start.13
  36.4 0.9 copy-start.12
  53.4 24.0 %collective-permute-start.11 = (bf16[4,128,256]{2,1,0:T(8,128)(2,1)}, bf16[4,128,256]{2,1,0:T(8,128)(2,1)S(1)}, u32[]{:S(2)}, u32[]{:S(2)}) collective-permute-start(bf16[4,128,256]{2,1,0:T(8,128)(2,1)} %get-tuple-element.60), channel_id=1, source_target_pairs={{2,0},{3,1},{6,4},{7,5},{10,8},{11,9},{14,12},{15,13},{18,16},{19,... | collective-permute-start | bytes 786440 | tf_op jit(solution)/shard_map/ppermute | solution.py:486
  55.8 21.5 %collective-permute-start.10 = (bf16[2,128,256]{2,1,0:T(8,128)(2,1)S(1)}, bf16[2,128,256]{2,1,0:T(8,128)(2,1)S(1)}, u32[]{:S(2)}, u32[]{:S(2)}) collective-permute-start(bf16[2,128,256]{2,1,0:T(8,128)(2,1)S(1)} %get-tuple-element.89), channel_id=1, source_target_pairs={{0,4},{4,8},{8,12},{12,0},{1,5},{5,9},{9,13},{13,1},{2,6},{6,10},{... | collective-permute-start | bytes 393224 | tf_op jit(solution)/shard_map/ppermute | solution.py:466
  58.4 19.0 %collective-permute-start.9 = (bf16[2,128,256]{2,1,0:T(8,128)(2,1)S(1)}, bf16[2,128,256]{2,1,0:T(8,128)(2,1)S(1)}, u32[]{:S(2)}, u32[]{:S(2)}) collective-permute-start(bf16[2,128,256]{2,1,0:T(8,128)(2,1)S(1)} %get-tuple-element.90), channel_id=1, source_target_pairs={{0,8},{4,12},{8,0},{12,4},{1,9},{5,13},{9,1},{13,5},{2,10},{6,14},... | collective-permute-start | bytes 393224 | tf_op jit(solution)/shard_map/ppermute | solution.py:466
  58.4 19.0 %collective-permute-start.8 = (bf16[2,128,256]{2,1,0:T(8,128)(2,1)S(1)}, bf16[2,128,256]{2,1,0:T(8,128)(2,1)S(1)}, u32[]{:S(2)}, u32[]{:S(2)}) collective-permute-start(bf16[2,128,256]{2,1,0:T(8,128)(2,1)S(1)} %get-tuple-element.91), channel_id=1, source_target_pairs={{0,12},{4,0},{8,4},{12,8},{1,13},{5,1},{9,5},{13,9},{2,14},{6,2},{... | collective-permute-start | bytes 393224 | tf_op jit(solution)/shard_map/ppermute | solution.py:466
  77.4 2.2 %collective-permute-start.12 = (f32[512,256]{1,0:T(8,128)}, f32[512,256]{1,0:T(8,128)S(1)}, u32[]{:S(2)}, u32[]{:S(2)}) collective-permute-start(f32[512,256]{1,0:T(8,128)} %get-tuple-element.66), channel_id=1, source_target_pairs={{0,1},{1,0},{2,3},{3,2},{4,5},{5,4},{6,7},{7,6},{8,9},{9,8},{10,11... | collective-permute-start | bytes 1572872 | tf_op jit(solution)/shard_map/ppermute | solution.py:375
  77.4 18.9 %collective-permute-start.17 = (bf16[4,128,256]{2,1,0:T(8,128)(2,1)}, bf16[4,128,256]{2,1,0:T(8,128)(2,1)S(1)}, u32[]{:S(2)}, u32[]{:S(2)}) collective-permute-start(bf16[4,128,256]{2,1,0:T(8,128)(2,1)} %get-tuple-element.68), channel_id=1, source_target_pairs={{2,0},{3,1},{6,4},{7,5},{10,8},{11,9},{14,12},{15,13},{18,16},{19,... | collective-permute-start | bytes 786440 | tf_op jit(solution)/shard_map/ppermute | solution.py:495
  80.7 2.8 %copy-start.7 = (bf16[8,128,256]{2,1,0:T(8,128)(2,1)S(1)}, bf16[8,128,256]{2,1,0:T(8,128)(2,1)}, u32[]{:S(2)}) copy-start(bf16[8,128,256]{2,1,0:T(8,128)(2,1)} %get-tuple-element.67) | copy-start | bytes 1572868
  80.7 13.4 %collective-permute-start.13 = (f32[256,256]{1,0:T(8,128)S(1)}, f32[256,256]{1,0:T(8,128)S(1)}, u32[]{:S(2)}, u32[]{:S(2)}) collective-permute-start(f32[256,256]{1,0:T(8,128)S(1)} %slice_select_fusion), channel_id=1, source_target_pairs={{0,2},{2,0},{1,3},{3,1},{4,6},{6,4},{5,7},{7,5},{8,10},{10,8},{9,1... | collective-permute-start | bytes 786440 | tf_op jit(solution)/shard_map/ppermute | solution.py:375
  83.5 10.7 %collective-permute-start.16 = (bf16[2,128,256]{2,1,0:T(8,128)(2,1)S(1)}, bf16[2,128,256]{2,1,0:T(8,128)(2,1)S(1)}, u32[]{:S(2)}, u32[]{:S(2)}) collective-permute-start(bf16[2,128,256]{2,1,0:T(8,128)(2,1)S(1)} %get-tuple-element.85), channel_id=1, source_target_pairs={{0,4},{4,8},{8,12},{12,0},{1,5},{5,9},{9,13},{13,1},{2,6},{6,10},{... | collective-permute-start | bytes 393224 | tf_op jit(solution)/shard_map/ppermute | solution.py:466
  83.5 12.8 %collective-permute-start.15 = (bf16[2,128,256]{2,1,0:T(8,128)(2,1)S(1)}, bf16[2,128,256]{2,1,0:T(8,128)(2,1)S(1)}, u32[]{:S(2)}, u32[]{:S(2)}) collective-permute-start(bf16[2,128,256]{2,1,0:T(8,128)(2,1)S(1)} %get-tuple-element.86), channel_id=1, source_target_pairs={{0,8},{4,12},{8,0},{12,4},{1,9},{5,13},{9,1},{13,5},{2,10},{6,14},... | collective-permute-start | bytes 393224 | tf_op jit(solution)/shard_map/ppermute | solution.py:466
  86.0 10.3 %collective-permute-start.14 = (bf16[2,128,256]{2,1,0:T(8,128)(2,1)S(1)}, bf16[2,128,256]{2,1,0:T(8,128)(2,1)S(1)}, u32[]{:S(2)}, u32[]{:S(2)}) collective-permute-start(bf16[2,128,256]{2,1,0:T(8,128)(2,1)S(1)} %get-tuple-element.87), channel_id=1, source_target_pairs={{0,12},{4,0},{8,4},{12,8},{1,13},{5,1},{9,5},{13,9},{2,14},{6,2},{... | collective-permute-start | bytes 393224 | tf_op jit(solution)/shard_map/ppermute | solution.py:466
  96.3 1.0 copy-start.1
  96.3 1.2 copy-start.2
  99.1 25.0 %collective-permute-start.18 = (f32[16,128,128]{2,1,0:T(8,128)S(1)}, f32[16,128,128]{2,1,0:T(8,128)S(1)}, u32[]{:S(2)}, u32[]{:S(2)}) collective-permute-start(f32[16,128,128]{2,1,0:T(8,128)S(1)} %get-tuple-element.79), channel_id=1, source_target_pairs={{0,1},{1,0},{2,3},{3,2},{4,5},{5,4},{6,7},{7,6},{8,9},{9,8},{10,11... | collective-permute-start | bytes 3145736 | tf_op jit(solution)/shard_map/ppermute | solution.py:375
  99.2 6.6 %collective-permute-start.19 = (bf16[256,256]{1,0:T(8,128)(2,1)S(1)}, bf16[256,256]{1,0:T(8,128)(2,1)S(1)}, u32[]{:S(2)}, u32[]{:S(2)}) collective-permute-start(bf16[256,256]{1,0:T(8,128)(2,1)S(1)} %select_add_fusion), channel_id=1, source_target_pairs={{0,4},{4,0},{8,12},{12,8},{1,5},{5,1},{9,13},{13,9},{2,6},{6,2},{1... | collective-permute-start | bytes 393224 | tf_op jit(solution)/shard_map/ppermute | solution.py:375
  105.8 9.0 %collective-permute-start.20 = (bf16[256,256]{1,0:T(8,128)(2,1)S(1)}, bf16[256,256]{1,0:T(8,128)(2,1)S(1)}, u32[]{:S(2)}, u32[]{:S(2)}) collective-permute-start(bf16[256,256]{1,0:T(8,128)(2,1)S(1)} %add_convert_fusion), channel_id=1, source_target_pairs={{0,8},{4,12},{8,0},{12,4},{1,9},{5,13},{9,1},{13,5},{2,10},{6,14},... | collective-permute-start | bytes 393224 | tf_op jit(solution)/shard_map/ppermute | solution.py:375
  114.9 7.4 %copy-start.6 = (f32[256,256]{1,0:T(8,128)}, f32[256,256]{1,0:T(8,128)S(1)}, u32[]{:S(2)}) copy-start(f32[256,256]{1,0:T(8,128)S(1)} %convert_add_fusion.part) | copy-start | bytes 786436
  114.9 7.4 %collective-permute-start.21 = (f32[256,256]{1,0:T(8,128)S(1)}, f32[256,256]{1,0:T(8,128)}, u32[]{:S(2)}, u32[]{:S(2)}) collective-permute-start(f32[256,256]{1,0:T(8,128)S(1)} %convert_add_fusion.part), channel_id=1, source_target_pairs={{0,2},{2,0},{1,3},{3,1},{4,6},{6,4},{5,7},{7,5},{8,10},{10,8},{9,1... | collective-permute-start | bytes 786440 | tf_op jit(solution)/shard_map/ppermute | solution.py:375

commit v6 on v5

--- a/solution.py
+++ b/solution.py
@@ -13,6 +13,7 @@
 WORKERS = CORES * CHUNKS
 F32 = jnp.float32
 BF16 = jnp.bfloat16
+PACK = 4
 LOG2E = 1.4426950408889634
 
 
@@ -24,26 +25,76 @@
         self.reach = reach_total
         self.slots = max(1, 2 * blocks_dev // reach_total // WORKERS)
         self.places = reach_total * self.slots
-        self.cyclic = reach_total <= 4
         self.block_of = 0
         self.recv_of = self.items
         self.count_own = 2 * self.items
         self.count_partner = 3 * self.items
         self.owner_of = 4 * self.items
         self.item_of = self.owner_of + blocks_dev
-        self.home_of = self.item_of + blocks_dev
-        self.chunk_of = self.home_of + blocks_dev
-        self.asker_of = self.chunk_of + blocks_dev
-        self.core = self.asker_of + blocks_dev
+        self.core = self.item_of + blocks_dev
         self.later_day = self.core + 1
         self.size = -(-(self.core + 2) // 128) * 128
-
-
-    def offset(self, high, low):
-        return lax.rem(high - low + self.reach, self.reach)
-
-
-def prepare_kernel(lay, partner, counts, where, inputs, sent_a, sent_b, prior, tab, start, used, picks):
+        self.home_of = 0
+        self.chunk_of = blocks_dev
+        self.asker_of = 2 * blocks_dev
+        self.picks = 3 * blocks_dev
+        self.homes_size = -(-(self.picks + CHUNKS * self.places) // 128) * 128
+
+
+def pick_kernel(lay, partner, where, inputs, sent, homes, held, sem):
+    bd, slots = lay.blocks, lay.slots
+    reach_pos, core = where[0], where[1]
+    copy = pltpu.make_async_copy(inputs, held, sem)
+    copy.start()
+
+    def clear_picks(index, carry):
+        homes[lay.picks + index] = 0
+        return carry
+
+    lax.fori_loop(0, CHUNKS * lay.places, clear_picks, 0, unroll=True)
+
+    def one_reach(peer, carry):
+        def before(index, total):
+            source = lax.div(partner[peer * bd + index], bd)
+            return total + jnp.where(source < reach_pos, 1, 0)
+
+        base = lax.fori_loop(0, bd, before, jnp.int32(0), unroll=True)
+
+        def serve(index, rank):
+            wanted = partner[peer * bd + index]
+            hit = lax.div(wanted, bd) == reach_pos
+
+            @pl.when(hit)
+            def _():
+                place = base + rank
+                owner = lax.rem(place, CORES)
+                chunk = lax.rem(lax.div(place, CORES), CHUNKS)
+                slot = peer * slots + jnp.minimum(lax.div(rank, WORKERS), slots - 1)
+                local = lax.rem(wanted, bd)
+                homes[lay.home_of + local] = slot
+                homes[lay.chunk_of + local] = chunk
+                homes[lay.asker_of + local] = owner
+
+                @pl.when(owner == core)
+                def _():
+                    homes[lay.picks + chunk * lay.places + slot] = local
+
+            return rank + jnp.where(hit, 1, 0)
+
+        lax.fori_loop(0, bd, serve, jnp.int32(0))
+        return carry
+
+    lax.fori_loop(0, lay.reach, one_reach, 0)
+    copy.wait()
+
+    def pick(place, carry):
+        sent[place] = held[homes[lay.picks + place]]
+        return carry
+
+    lax.fori_loop(0, lay.places, pick, 0)
+
+
+def deal_kernel(lay, partner, counts, where, homes, inputs, sent, prior, tab, start, used):
     bd, slots = lay.blocks, lay.slots
     reach_pos, core = where[0], where[1]
 
@@ -84,8 +135,7 @@
         @pl.when(owner == core)
         def _():
             tab[lay.block_of + item] = index
-            peer = lay.offset(reach_pos, source) if lay.cyclic else source
-            tab[lay.recv_of + item] = peer * slots + slot
+            tab[lay.recv_of + item] = source * slots + slot
             tab[lay.count_own + item] = counts[reach_pos * bd + index]
             tab[lay.count_partner + item] = counts[wanted]
 
@@ -95,60 +145,15 @@
     tab[lay.core] = core
     tab[lay.later_day] = where[2]
 
-    def clear_picks(index, carry):
-        picks[index] = 0
-        return carry
-
-    lax.fori_loop(0, CHUNKS * lay.places, clear_picks, 0)
-
-    def one_reach(peer, carry):
-        def before(index, total):
-            source = lax.div(partner[peer * bd + index], bd)
-            return total + jnp.where(source < reach_pos, 1, 0)
-
-        base = lax.fori_loop(0, bd, before, jnp.int32(0), unroll=True)
-        target = lay.offset(peer, reach_pos) if lay.cyclic else peer
-
-        def serve(index, rank):
-            wanted = partner[peer * bd + index]
-            hit = lax.div(wanted, bd) == reach_pos
-
-            @pl.when(hit)
-            def _():
-                place = base + rank
-                owner = lax.rem(place, CORES)
-                chunk = lax.rem(lax.div(place, CORES), CHUNKS)
-                slot = jnp.minimum(lax.div(rank, WORKERS), slots - 1)
-                local = lax.rem(wanted, bd)
-                tab[lay.home_of + local] = target * slots + slot
-                tab[lay.chunk_of + local] = chunk
-                tab[lay.asker_of + local] = owner
-
-                @pl.when(owner == core)
-                def _():
-                    picks[chunk * lay.places + target * slots + slot] = local
-
-            return rank + jnp.where(hit, 1, 0)
-
-        lax.fori_loop(0, bd, serve, jnp.int32(0))
-        return carry
-
-    lax.fori_loop(0, lay.reach, one_reach, 0)
-
-    def pick_a(place, carry):
-        sent_a[place] = inputs[picks[place]]
-        return carry
-
-    def pick_b(place, carry):
-        sent_b[place] = inputs[picks[lay.places + place]]
+    def pick(place, carry):
+        sent[place] = inputs[homes[lay.picks + lay.places + place]]
         return carry
 
     def pick_prior(item, carry):
         prior[item] = inputs[tab[lay.block_of + item]]
         return carry
 
-    lax.fori_loop(0, lay.places, pick_a, 0)
-    lax.fori_loop(0, lay.places, pick_b, 0)
+    lax.fori_loop(0, lay.places, pick, 0)
     lax.fori_loop(0, lay.items, pick_prior, 0)
 
 
@@ -201,56 +206,78 @@
     output_w = jnp.concatenate([mine_ref[384:512, :], other_ref[384:512, :]], axis=0)
     queries = dot_t(own, query_t)
     back_out = dot_t(up, output_w)
-    key_inputs_t = dot_t(eye(width), key_inputs).astype(BF16)
+    key_inputs_t = key_inputs.T
 
     count_own = tab[lay.count_own + item]
     count_partner = tab[lay.count_partner + item]
     count_prior = count_own * tab[lay.later_day]
-    rows = lax.broadcasted_iota(jnp.int32, (BLOCK, 2 * BLOCK), 0)
+    rows = lax.broadcasted_iota(jnp.int32, (BLOCK, PACK * BLOCK), 0)
     valid = jnp.concatenate([rows < count_own, rows < count_partner, rows < count_prior], axis=0)
     lane_head = lax.broadcasted_iota(jnp.int32, (BLOCK, GROUP), 1) // HD
 
-    back_inputs = None
-    outputs_t, back_query_t = [], []
+    per_group = GROUP // HD // PACK
+    groups = []
     for group, (weights_ref, grad_ref) in enumerate(
         ((mine_ref, grad_mine_ref), (other_ref, grad_other_ref))
     ):
         kv_t = weights_ref[0:256, :]
         kv = dot_t(key_inputs, kv_t).astype(BF16)
-        kv_cols = dot_t(kv_t, key_inputs).astype(BF16)
-        keys, values = kv[:, :GROUP], kv[:, GROUP:]
-        group_queries = queries[:, group * GROUP : (group + 1) * GROUP]
-        group_back = back_out[:, group * GROUP : (group + 1) * GROUP]
-        back_keys = back_values = None
-        for pair in range(GROUP // HD // 2):
-            heads = (2 * pair, 2 * pair + 1)
-            query_pair = jnp.concatenate(
-                [jnp.where(lane_head == h, group_queries, 0.0) for h in heads], axis=0
-            ).astype(BF16)
-            back_pair = jnp.concatenate(
-                [jnp.where(lane_head == h, group_back, 0.0) for h in heads], axis=0
-            ).astype(BF16)
-            logits = jnp.where(valid, dot_t(keys, query_pair), -1e30)
-            highest = jnp.max(logits, axis=0, keepdims=True)
-            raised = jnp.exp2((logits - highest) * (factor * LOG2E))
-            scale = 1.0 / jnp.sum(raised, axis=0, keepdims=True)
-            weights = raised * scale
-            weights_low = weights.astype(BF16)
-            back_weights = dot_t(values, back_pair)
-            center = jnp.sum(weights * back_weights, axis=0, keepdims=True)
-            back_logits = (weights * ((back_weights - center) * factor)).astype(BF16)
-            pair_values = dot(weights_low, back_pair)
-            pair_keys = dot(back_logits, query_pair)
-            back_values = pair_values if back_values is None else back_values + pair_values
-            back_keys = pair_keys if back_keys is None else back_keys + pair_keys
-            first = 2 * pair * HD
-            out_t = dot(kv_cols[GROUP + first : GROUP + first + 2 * HD, :], weights_low)
-            query_grad_t = dot(kv_cols[first : first + 2 * HD, :], back_logits)
-            for h in range(2):
-                lanes = slice(h * BLOCK, (h + 1) * BLOCK)
-                outputs_t.append(out_t[h * HD : (h + 1) * HD, lanes])
-                back_query_t.append(query_grad_t[h * HD : (h + 1) * HD, lanes])
-        back_kv = jnp.concatenate([back_keys, back_values], axis=1).astype(BF16)
+        kv_cols = kv.T
+        lanes = slice(group * GROUP, (group + 1) * GROUP)
+        groups.append((kv_t, kv, kv_cols, queries[:, lanes], back_out[:, lanes], grad_ref))
+
+    def start(step):
+        kv_t, kv, kv_cols, group_queries, group_back, grad_ref = groups[step // per_group]
+        heads = [step % per_group * PACK + h for h in range(PACK)]
+        query_pack, back_pack = (
+            jnp.concatenate([jnp.where(lane_head == h, rows_of, 0.0) for h in heads], axis=0).astype(BF16)
+            for rows_of in (group_queries, group_back)
+        )
+        return query_pack, back_pack, dot_t(kv[:, :GROUP], query_pack), dot_t(kv[:, GROUP:], back_pack)
+
+    def middle(logits, back_weights):
+        logits = jnp.where(valid, logits, -1e30)
+        highest = jnp.max(logits, axis=0, keepdims=True)
+        raised = jnp.exp2((logits - highest) * (factor * LOG2E))
+        scale = 1.0 / jnp.sum(raised, axis=0, keepdims=True)
+        weights = raised * scale
+        center = jnp.sum(weights * back_weights, axis=0, keepdims=True)
+        back_logits = (weights * ((back_weights - center) * factor)).astype(BF16)
+        return weights.astype(BF16), back_logits
+
+    outputs_t, back_query_t = [], []
+    pair_keys, pair_values = {}, {}
+
+    def finish(step, query_pack, back_pack, weights_low, back_logits):
+        group = step // per_group
+        kv_cols = groups[group][2]
+        pair_values.setdefault(group, []).append(dot(weights_low, back_pack))
+        pair_keys.setdefault(group, []).append(dot(back_logits, query_pack))
+        first = step % per_group * PACK * HD
+        size = PACK * HD
+        out_t = dot(kv_cols[GROUP + first : GROUP + first + size, :], weights_low)
+        query_grad_t = dot(kv_cols[first : first + size, :], back_logits)
+        for h in range(PACK):
+            lanes = slice(h * BLOCK, (h + 1) * BLOCK)
+            outputs_t.append(out_t[h * HD : (h + 1) * HD, lanes])
+            back_query_t.append(query_grad_t[h * HD : (h + 1) * HD, lanes])
+
+    total_steps = 2 * per_group
+    started = start(0)
+    waiting = None
+    for step in range(total_steps):
+        following = start(step + 1) if step + 1 < total_steps else None
+        query_pack, back_pack, logits, back_weights = started
+        if waiting is not None:
+            finish(*waiting)
+        made = middle(logits, back_weights)
+        waiting = (step, query_pack, back_pack, *made)
+        started = following
+    finish(*waiting)
+
+    back_inputs = None
+    for group, (kv_t, _, _, _, _, grad_ref) in enumerate(groups):
+        back_kv = jnp.concatenate([sum(pair_keys[group][1:], pair_keys[group][0]), sum(pair_values[group][1:], pair_values[group][0])], axis=1).astype(BF16)
         term = dot(back_kv, kv_t)
         back_inputs = term if back_inputs is None else back_inputs + term
         grad_ref[0:256, :] += dot(key_inputs_t, back_kv)
@@ -263,22 +290,22 @@
     grad_other_ref[256:384, :] += query_grad[GROUP:]
     grad_mine_ref[384:512, :] += output_grad[:GROUP]
     grad_other_ref[384:512, :] += output_grad[GROUP:]
-    back_query = dot_t(eye(BLOCK), back_query_t).astype(BF16)
+    back_query = back_query_t.T
     own_out_ref[0] = back_inputs[:BLOCK] + dot(back_query, query_t)
     home_ref[0] = back_inputs[BLOCK : 2 * BLOCK].astype(BF16)
     day_ref[0] = back_inputs[2 * BLOCK :].astype(BF16)
 
 
-def fold_kernel(lay, tab, own_a, own_b, day_a, day_b, home_a, home_b, keep, give):
+def fold_kernel(lay, tab, homes, own_a, own_b, day_a, day_b, home_a, home_b, keep, give):
     core = tab[lay.core]
     half = keep.shape[2]
 
     def one(block, carry):
         item = tab[lay.item_of + block]
         mine = tab[lay.owner_of + block] == core
-        place = tab[lay.home_of + block]
-        asked = tab[lay.asker_of + block] == core
-        early = tab[lay.chunk_of + block] == 0
+        place = homes[lay.home_of + block]
+        asked = homes[lay.asker_of + block] == core
+        early = homes[lay.chunk_of + block] == 0
         in_a = item < lay.chunk_items
         item_a = jnp.minimum(item, lay.chunk_items - 1)
         item_b = jnp.maximum(item - lay.chunk_items, 0)
@@ -385,15 +412,16 @@
     first = lax.rem(lax.axis_index("day"), 2) == 0
     kept = jnp.where(first, total[:half], total[half:])
     given = jnp.where(first, total[half:], total[:half])
-    part = kept + exchanged(given, "day", 1)
+    part = kept.astype(BF16).astype(F32) + exchanged(given.astype(BF16), "day", 1).astype(F32)
     bit = 2
     while bit < lax.axis_size("day"):
         part = summed_over(part, "day", bit)
         bit *= 2
-    part, *settled = lax.optimization_barrier((part, *settled))
     bit = 1
     while bit < lax.axis_size("reach"):
         part = summed_over(part, "reach", bit)
+        if bit == 1:
+            part, *settled = lax.optimization_barrier((part, *settled))
         bit *= 2
     return part, exchanged(part, "day", 1), settled
 
@@ -434,55 +462,52 @@
 
     smem = pl.BlockSpec(memory_space=pltpu.SMEM)
     in_vmem = pl.BlockSpec(memory_space=pltpu.VMEM)
+    anywhere = pl.BlockSpec(memory_space=pl.ANY)
     sent_shape = jax.ShapeDtypeStruct((lay.places, BLOCK, width), BF16)
-    sent_a, sent_b, prior, tab = pl.pallas_call(
-        lambda *refs: prepare_kernel(lay, *refs),
+    sent_a, homes = pl.pallas_call(
+        lambda *refs: pick_kernel(lay, *refs),
+        out_shape=(sent_shape, jax.ShapeDtypeStruct((lay.homes_size,), jnp.int32)),
+        in_specs=[smem, smem, anywhere],
+        out_specs=(in_vmem, smem),
+        scratch_shapes=[
+            pltpu.VMEM((blocks_dev, BLOCK, width), BF16),
+            pltpu.SemaphoreType.DMA,
+        ],
+        compiler_params=pltpu.CompilerParams(vmem_limit_bytes=16 << 20),
+        name="pick",
+    )(partner, where, pltpu.with_memory_space_constraint(in_blocks, pltpu.HBM))
+    sent_b, prior, tab = pl.pallas_call(
+        lambda *refs: deal_kernel(lay, *refs),
         out_shape=(
-            sent_shape,
             sent_shape,
             jax.ShapeDtypeStruct((lay.items, BLOCK, width), BF16),
             jax.ShapeDtypeStruct((lay.size,), jnp.int32),
         ),
-        in_specs=[smem, smem, smem, in_vmem],
-        out_specs=(in_vmem, in_vmem, in_vmem, smem),
+        in_specs=[smem, smem, smem, smem, in_vmem],
+        out_specs=(in_vmem, in_vmem, smem),
         scratch_shapes=[
             pltpu.SMEM((lay.reach,), jnp.int32),
             pltpu.SMEM((lay.reach,), jnp.int32),
-            pltpu.SMEM((CHUNKS * lay.places,), jnp.int32),
         ],
         compiler_params=pltpu.CompilerParams(vmem_limit_bytes=16 << 20),
-        name="prepare",
-    )(partner, counts, where, in_blocks)
-
-    def ring(value, back):
+        name="deal",
+    )(partner, counts, where, homes, in_blocks)
+
+    def ring(value):
         shape = value.shape
-        if not lay.cyclic:
-            value = value.reshape(lay.reach, lay.slots * BLOCK, width)
-            return [lax.all_to_all(value, "reach", 0, 0, tiled=True).reshape(shape)]
-        pieces = [value[: lay.slots]]
-        for shift in range(1, lay.reach):
-            step = -shift if back else shift
-            pieces.append(
-                lax.ppermute(
-                    value[shift * lay.slots : (shift + 1) * lay.slots],
-                    "reach",
-                    [(place, (place + step) % lay.reach) for place in range(lay.reach)],
-                )
-            )
-        return pieces
+        value = value.reshape(lay.reach, lay.slots * BLOCK, width)
+        return lax.all_to_all(value, "reach", 0, 0, tiled=True).reshape(shape)
 
     next_day = [(d, d + 1) for d in range(day_total - 1)]
     last_day = [(d + 1, d) for d in range(day_total - 1)]
-    received_a = jnp.concatenate(ring(sent_a, False), axis=0)
+    received_a = ring(sent_a)
     prior_inputs = lax.ppermute(prior, "day", next_day)
-    received_b = ring(sent_b, False)
+    received_b = ring(sent_b)
     shared = (prior_inputs, pack, pack_other)
     own_a, day_a, home_a, *grads = attend(
         lay, 0, tab, in_blocks, up_blocks, received_a, *shared, None
     )
-    received_b, grads = lax.optimization_barrier((received_b, grads))
-    received_b = jnp.concatenate(received_b, axis=0)
-    home_a = ring(home_a, True)
+    home_a = ring(home_a)
     day_a = lax.ppermute(day_a, "day", last_day)
     own_b, day_b, home_b, grad_mine, grad_other = attend(
         lay, 1, tab, in_blocks, up_blocks, received_b, *shared, grads
@@ -491,19 +516,18 @@
         (home_a, day_a, home_b, day_b, grad_other)
     )
     grad_swapped = exchanged(grad_other, "head", 1)
-    home_b = ring(home_b, True)
+    home_b = ring(home_b)
     day_b = lax.ppermute(day_b, "day", last_day)
     part, other, (home_b, day_b) = sum_gradients(grad_mine + grad_swapped, (home_b, day_b))
-    home_a, home_b = jnp.concatenate(home_a, axis=0), jnp.concatenate(home_b, axis=0)
     half_shape = jax.ShapeDtypeStruct((blocks_dev, BLOCK, half), F32)
     keep, give = pl.pallas_call(
         lambda *refs: fold_kernel(lay, *refs),
         out_shape=(half_shape, half_shape),
-        in_specs=[smem] + [in_vmem] * 6,
+        in_specs=[smem] * 2 + [in_vmem] * 6,
         out_specs=[in_vmem] * 2,
         compiler_params=pltpu.CompilerParams(vmem_limit_bytes=16 << 20),
         name="fold",
-    )(tab, own_a, own_b, day_a, day_b, home_a, home_b)
+    )(tab, homes, own_a, own_b, day_a, day_b, home_a, home_b)
     got = exchanged(give, "head", 1)
     back_blocks = pl.pallas_call(
         add_kernel,

time: 126 us -> 110 us (0.87)
  starting transfers between devices: 39.5 us -> 32.8 us
  Pallas kernels: 40.4 us -> 35.4 us
  local copies, waits for them, and re-layouts: 7.75 us -> 6.32 us
  other arithmetic: 1.63 us -> 0.3 us
    ppermute x12 -> x0, starting transfers between devices: 24.3 us -> none  [ring(): lax.ppermute(value[shift * lay.slots:(shift + 1) * lay.slots], 'reach', [...]
    all_to_all x0 -> x4, starting transfers between devices: none -> 19.5 us  [ring(): return lax.all_to_all(value, 'reach', 0, 0, tiled=True).reshape(shape)]
    ppermute x12 -> x0, waiting for transfers between devices: 9.08 us -> none  [ring(): lax.ppermute(value[shift * lay.slots:(shift + 1) * lay.slots], 'reach', [...]
    pallas_call x2, Pallas kernels: 32.5 us -> 25.1 us  [attend(): pl.pallas_call(lambda *refs: attention_kernel(lay, chunk, *refs), grid_sp...]
    all_to_all x0 -> x4, waiting for transfers between devices: none -> 6.85 us  [ring(): return lax.all_to_all(value, 'reach', 0, 0, tiled=True).reshape(shape)]
    ppermute x1, waiting for transfers between devices: 0.01 us -> 4.81 us  [on_device(): day_b = lax.ppermute(day_b, 'day', last_day)]
    ppermute x7, waiting for transfers between devices: 25.8 us -> 22.3 us  [exchanged(): lax.ppermute(value, axis, [(place, place ^ bit) for place in range(count)])]
    pallas_call x1 -> x2, Pallas kernels: 3.56 us -> 5.08 us  [the longest x1 2.9 us: on_device(): pl.pallas_call(lambda *refs: pick_kernel(lay, *refs), out_shape=(sent_sha...]
  transfers between devices with their start and end apart: 22 -> 14, of which waited for: 8 -> 7; matrix products, arithmetic and copies ran while one was open for 2% -> 0% of each run, Pallas kernels for 30% -> 27%
where the time goes in v6:
time: 110 us
  Pallas kernels  35.4 us (32%)
  waiting for transfers between devices  34 us (31%)
  starting transfers between devices  32.8 us (30%)
  local copies, waits for them, and re-layouts  6.32 us (6%)
    pallas_call x2, Pallas kernels, attend(): pl.pallas_call(lambda *refs: attention_kernel(lay, chunk, *refs), grid_sp...  25.1 us
    ppermute x7, waiting for transfers between devices, exchanged(): lax.ppermute(value, axis, [(place, place ^ bit) for place in range(count)])  22.3 us
    all_to_all x4, starting transfers between devices, ring(): return lax.all_to_all(value, 'reach', 0, 0, tiled=True).reshape(shape)  19.5 us
    ppermute x7, starting transfers between devices, exchanged(): lax.ppermute(value, axis, [(place, place ^ bit) for place in range(count)])  7.1 us
    all_to_all x4, waiting for transfers between devices, ring(): return lax.all_to_all(value, 'reach', 0, 0, tiled=True).reshape(shape)  6.85 us
    unnamed x43, local copies, waits for them, and re-layouts  6.32 us
    ppermute x1, waiting for transfers between devices, on_device(): day_b = lax.ppermute(day_b, 'day', last_day)  4.81 us
    ppermute x1, starting transfers between devices, on_device(): prior_inputs = lax.ppermute(prior, 'day', next_day)  3.56 us
  transfers between devices with their start and end apart: 14, of which 7 were waited for; matrix products, arithmetic and copies ran while one was open for 0% of the time, Pallas kernels for 27%

profile of v6, /device:TPU:0, one launch (start us, length us, event | category | flops | bytes accessed | tf_op | source)
XLA Modules:
  0.0 109.7 jit_solution(10503350207564740209)
XLA Ops:
  0.6 0.1 pad_add_fusion.refs_1_.refs_2_.where
  0.7 0.7 copy-done.6
  1.4 2.9 %pick.1 = (bf16[8,128,256]{2,1,0:T(8,128)(2,1)}, s32[128]{0:T(128)S(1)}) custom-call(s32[64]{0:T(128)S(1)} %copy-done.6, s32[4]{0:T(128)S(1)} %pad_add_fusion.refs_1_.refs_2_.where, bf16[16,128,256]{2,1,0:T(8,128)(2,1)} %bitcast.18), custom_call_target="tpu_custom_call" | custom-call | tf_op jit(solution)/shard_map/pick/pallas_call | solution.py:467
  4.3 6.3 %all-to-all-start = ((bf16[4,256,256]{2,1,0:T(8,128)(2,1)}), bf16[4,256,256]{2,1,0:T(8,128)(2,1)S(1)}, u32[]{:S(2)}, u32[]{:S(2)}) async-start(bf16[4,256,256]{2,1,0:T(8,128)(2,1)} %bitcast.6), calls=%async_computation | async-start | bytes 1048576 | tf_op jit(solution)/shard_map/all_to_all | solution.py:499
  10.6 0.6 copy-done.7
  11.3 2.2 %deal.1 = (bf16[8,128,256]{2,1,0:T(8,128)(2,1)}, bf16[8,128,256]{2,1,0:T(8,128)(2,1)S(1)}, s32[128]{0:T(128)S(1)}) custom-call(s32[64]{0:T(128)S(1)} %copy-done.6, s32[64]{0:T(128)S(1)} %copy-done.7, s32[4]{0:T(128)S(1)} %pad_add_fusion.refs_1_.refs_2_.where, s32[128]{0:T(128)S(1)} %get-tuple-element.34.refs_3_.refs_1_, bf16[16,128,256]{2,1,0:T(8,128)(2,1)S(1)} %bitcast.21), custom_call_target="tpu_custom_call" | custom-call | tf_op jit(solution)/shard_map/deal/pallas_call | solution.py:479
  13.5 0.0 copy-start.13
  13.5 3.6 %collective-permute-start = (bf16[8,128,256]{2,1,0:T(8,128)(2,1)S(1)}, bf16[8,128,256]{2,1,0:T(8,128)(2,1)S(1)}, u32[]{:S(2)}, u32[]{:S(2)}) collective-permute-start(bf16[8,128,256]{2,1,0:T(8,128)(2,1)S(1)} %get-tuple-element.37), channel_id=1, source_target_pairs={{0,2},{1,3},{4,6},{5,7},{8,10},{9,11},{12,14},{13,15},{16,18},{17,... | collective-permute-start | bytes 1572872 | tf_op jit(solution)/shard_map/ppermute | solution.py:504
  17.1 0.1 copy.15
  17.2 0.0 copy-start.14
  17.2 0.1 copy.13
  17.3 0.7 copy-done.14
  18.0 0.1 copy.14
  18.1 0.7 copy-done.15
  18.9 0.1 collective-permute-start.1
  19.0 6.1 %all-to-all-done = bf16[4,256,256]{2,1,0:T(8,128)(2,1)S(1)} async-done(((bf16[4,256,256]{2,1,0:T(8,128)(2,1)}), bf16[4,256,256]{2,1,0:T(8,128)(2,1)S(1)}, u32[]{:S(2)}, u32[]{:S(2)}) %all-to-all-start) | async-done | bytes 524320 | tf_op jit(solution)/shard_map/all_to_all | solution.py:499
  25.1 3.5 %all-to-all-start.1 = ((bf16[4,256,256]{2,1,0:T(8,128)(2,1)}), bf16[4,256,256]{2,1,0:T(8,128)(2,1)S(1)}, u32[]{:S(2)}, u32[]{:S(2)}) async-start(bf16[4,256,256]{2,1,0:T(8,128)(2,1)} %bitcast.11), calls=%async_computation.1 | async-start | bytes 1048576 | tf_op jit(solution)/shard_map/all_to_all | solution.py:499
  28.6 0.0 collective-permute-done.1.refs_6_
  28.6 0.0 copy-start.16
  28.6 0.7 copy-done.18
  29.3 0.2 copy-done.16
  29.5 12.4 %attention_0.1 = (f32[4,128,256]{2,1,0:T(8,128)}, bf16[4,128,256]{2,1,0:T(8,128)(2,1)}, bf16[8,128,256]{2,1,0:T(8,128)(2,1)}, f32[512,256]{1,0:T(8,128)}, f32[512,256]{1,0:T(8,128)}) custom-call(s32[128]{0:T(128)S(1)} %get-tuple-element.35.refs_0_, bf16[16,128,256]{2,1,0:T(8,128)(2,1)} %bitcast.19, bf16[16,128,256]{2,1,0:T(8,128)(2,1)} %bitcast.32, ...), custom_call_target="tpu_custom_call" | custom-call | flops 6375342080 | bytes 5242880 | tf_op jit(solution)/shard_map/attention_0/pallas_call | solution.py:363
  41.8 0.7 all-to-all-done.1
  42.6 4.5 %all-to-all-start.2 = ((bf16[4,256,256]{2,1,0:T(8,128)(2,1)}), bf16[4,256,256]{2,1,0:T(8,128)(2,1)S(1)}, u32[]{:S(2)}, u32[]{:S(2)}) async-start(bf16[4,256,256]{2,1,0:T(8,128)(2,1)} %bitcast.28), calls=%async_computation.2 | async-start | bytes 1048576 | tf_op jit(solution)/shard_map/all_to_all | solution.py:499
  47.1 1.3 %collective-permute-start.2 = (bf16[4,128,256]{2,1,0:T(8,128)(2,1)S(1)}, bf16[4,128,256]{2,1,0:T(8,128)(2,1)S(1)}, u32[]{:S(2)}, u32[]{:S(2)}) collective-permute-start(bf16[4,128,256]{2,1,0:T(8,128)(2,1)S(1)} %copy-done.19), channel_id=1, source_target_pairs={{2,0},{3,1},{6,4},{7,5},{10,8},{11,9},{14,12},{15,13},{18,16},{19,... | collective-permute-start | bytes 786440 | tf_op jit(solution)/shard_map/ppermute | solution.py:511
  48.3 12.7 %attention_1.1 = (f32[4,128,256]{2,1,0:T(8,128)}, bf16[4,128,256]{2,1,0:T(8,128)(2,1)}, bf16[8,128,256]{2,1,0:T(8,128)(2,1)}, f32[512,256]{1,0:T(8,128)}, f32[512,256]{1,0:T(8,128)}) custom-call(s32[128]{0:T(128)S(1)} %get-tuple-element.35.refs_0_, bf16[16,128,256]{2,1,0:T(8,128)(2,1)} %bitcast.20, bf16[16,128,256]{2,1,0:T(8,128)(2,1)} %bitcast.33, ...), custom_call_target="tpu_custom_call" | custom-call | flops 6375342080 | bytes 5242880 | tf_op jit(solution)/shard_map/attention_1/pallas_call | solution.py:363
  61.1 0.1 collective-permute-start.3
  61.2 5.2 %all-to-all-start.3 = ((bf16[4,256,256]{2,1,0:T(8,128)(2,1)}), bf16[4,256,256]{2,1,0:T(8,128)(2,1)S(1)}, u32[]{:S(2)}, u32[]{:S(2)}) async-start(bf16[4,256,256]{2,1,0:T(8,128)(2,1)} %bitcast.27), calls=%async_computation.3 | async-start | bytes 1048576 | tf_op jit(solution)/shard_map/all_to_all | solution.py:499
  66.4 0.1 add.13
  66.5 2.7 %collective-permute-start.4 = (bf16[256,256]{1,0:T(8,128)(2,1)S(1)}, bf16[256,256]{1,0:T(8,128)(2,1)S(1)}, u32[]{:S(2)}, u32[]{:S(2)}) collective-permute-start(bf16[256,256]{1,0:T(8,128)(2,1)S(1)} %select_convert_fusion), channel_id=1, source_target_pairs={{0,2},{2,0},{1,3},{3,1},{4,6},{6,4},{5,7},{7,5},{8,10},{10,8},{9,1... | collective-permute-start | bytes 393224 | tf_op jit(solution)/shard_map/ppermute | solution.py:402
  69.3 3.9 %collective-permute-done.4 = bf16[256,256]{1,0:T(8,128)(2,1)S(1)} collective-permute-done((bf16[256,256]{1,0:T(8,128)(2,1)S(1)}, bf16[256,256]{1,0:T(8,128)(2,1)S(1)}, u32[]{:S(2)}, u32[]{:S(2)}) %collective-permute-start.4) | collective-permute-done | bytes 131104 | tf_op jit(solution)/shard_map/ppermute | solution.py:402
  73.1 0.1 add_convert_fusion
  73.2 1.8 %collective-permute-start.5 = (bf16[256,256]{1,0:T(8,128)(2,1)S(1)}, bf16[256,256]{1,0:T(8,128)(2,1)S(1)}, u32[]{:S(2)}, u32[]{:S(2)}) collective-permute-start(bf16[256,256]{1,0:T(8,128)(2,1)S(1)} %add_convert_fusion), channel_id=1, source_target_pairs={{0,4},{4,0},{8,12},{12,8},{1,5},{5,1},{9,13},{13,9},{2,6},{6,2},{1... | collective-permute-start | bytes 393224 | tf_op jit(solution)/shard_map/ppermute | solution.py:402
  75.0 1.3 %collective-permute-start.6 = (bf16[4,128,256]{2,1,0:T(8,128)(2,1)S(1)}, bf16[4,128,256]{2,1,0:T(8,128)(2,1)S(1)}, u32[]{:S(2)}, u32[]{:S(2)}) collective-permute-start(bf16[4,128,256]{2,1,0:T(8,128)(2,1)S(1)} %copy-done.17), channel_id=1, source_target_pairs={{2,0},{3,1},{6,4},{7,5},{10,8},{11,9},{14,12},{15,13},{18,16},{19,... | collective-permute-start | bytes 786440 | tf_op jit(solution)/shard_map/ppermute | solution.py:520
  76.3 3.0 %collective-permute-done.5 = bf16[256,256]{1,0:T(8,128)(2,1)S(1)} collective-permute-done((bf16[256,256]{1,0:T(8,128)(2,1)S(1)}, bf16[256,256]{1,0:T(8,128)(2,1)S(1)}, u32[]{:S(2)}, u32[]{:S(2)}) %collective-permute-start.5) | collective-permute-done | bytes 131104 | tf_op jit(solution)/shard_map/ppermute | solution.py:402
  79.3 4.8 %collective-permute-done.6.refs_5_ = bf16[4,128,256]{2,1,0:T(8,128)(2,1)S(1)} collective-permute-done((bf16[4,128,256]{2,1,0:T(8,128)(2,1)S(1)}, bf16[4,128,256]{2,1,0:T(8,128)(2,1)S(1)}, u32[]{:S(2)}, u32[]{:S(2)}) %collective-permute-start.6) | collective-permute-done | bytes 262176 | tf_op jit(solution)/shard_map/ppermute | solution.py:520
  84.2 0.7 copy-done.3
  84.9 0.0 copy-start.4
  84.9 0.9 copy-done.4
  85.8 2.6 %fold.1 = (f32[16,128,128]{2,1,0:T(8,128)S(1)}, f32[16,128,128]{2,1,0:T(8,128)}) custom-call(s32[128]{0:T(128)S(1)} %get-tuple-element.35.refs_0_, s32[128]{0:T(128)S(1)} %get-tuple-element.34.refs_3_.refs_1_, f32[4,128,256]{2,1,0:T(8,128)S(1)} %copy-done.1, f32[4,128,256]{2,1,0:T(8,128)S(1)} %copy-done.2, ...), custom_call_target="tpu_custom_call" | custom-call | tf_op jit(solution)/shard_map/fold/pallas_call | solution.py:523
  88.4 2.4 %collective-permute-start.8 = (bf16[256,256]{1,0:T(8,128)(2,1)S(1)}, bf16[256,256]{1,0:T(8,128)(2,1)S(1)}, u32[]{:S(2)}, u32[]{:S(2)}) collective-permute-start(bf16[256,256]{1,0:T(8,128)(2,1)S(1)} %convert_add_fusion.1), channel_id=1, source_target_pairs={{0,8},{4,12},{8,0},{12,4},{1,9},{5,13},{9,1},{13,5},{2,10},{6,14},... | collective-permute-start | bytes 393224 | tf_op jit(solution)/shard_map/ppermute | solution.py:402
  90.7 7.3 %collective-permute-done.8 = bf16[256,256]{1,0:T(8,128)(2,1)S(1)} collective-permute-done((bf16[256,256]{1,0:T(8,128)(2,1)S(1)}, bf16[256,256]{1,0:T(8,128)(2,1)S(1)}, u32[]{:S(2)}, u32[]{:S(2)}) %collective-permute-start.8) | collective-permute-done | bytes 131104 | tf_op jit(solution)/shard_map/ppermute | solution.py:402
  98.0 0.0 copy-start.8
  98.0 0.1 collective-permute-start.9
  98.1 8.2 %collective-permute-done.9.other = f32[256,256]{1,0:T(8,128)S(1)} collective-permute-done((f32[256,256]{1,0:T(8,128)S(1)}, f32[256,256]{1,0:T(8,128)S(1)}, u32[]{:S(2)}, u32[]{:S(2)}) %collective-permute-start.9) | collective-permute-done | bytes 262176 | tf_op jit(solution)/shard_map/ppermute | solution.py:402
  106.3 0.7 copy-done.10
  107.0 1.9 %split.1 = (f32[256,128]{1,0:T(8,128)}, f32[256,128]{1,0:T(8,128)}, f32[256,128]{1,0:T(8,128)}, f32[128,256]{1,0:T(8,128)}) custom-call(s32[4]{0:T(128)} %copy-done.5, f32[256,256]{1,0:T(8,128)} %copy-done.8, f32[256,256]{1,0:T(8,128)} %copy-done.10), custom_call_target="tpu_custom_call" | custom-call | tf_op jit(solution)/shard_map/split/pallas_call | solution.py:540
  108.9 0.9 add.26
  (37 shorter events, 0.2 us)
Async XLA Ops:
  0.7 9.9 %copy-start.5 = (s32[4]{0:T(128)}, s32[4]{0:T(128)S(1)}, u32[]{:S(2)}) copy-start(s32[4]{0:T(128)S(1)} %pad_add_fusion.refs_1_.refs_2_.where) | copy-start | bytes 52
  0.7 0.7 copy-start.6
  1.4 9.2 %copy-start = (bf16[1,2048,256]{2,1,0:T(8,128)(2,1)S(1)}, bf16[1,2048,256]{2,1,0:T(8,128)(2,1)}, u32[]{:S(2)}) copy-start(bf16[1,2048,256]{2,1,0:T(8,128)(2,1)} %param.8) | copy-start | bytes 3145732
  4.3 20.8 %all-to-all-start = ((bf16[4,256,256]{2,1,0:T(8,128)(2,1)}), bf16[4,256,256]{2,1,0:T(8,128)(2,1)S(1)}, u32[]{:S(2)}, u32[]{:S(2)}) async-start(bf16[4,256,256]{2,1,0:T(8,128)(2,1)} %bitcast.6), calls=%async_computation | async-start | bytes 1048576 | tf_op jit(solution)/shard_map/all_to_all | solution.py:499
  10.6 0.7 copy-start.7
  11.3 5.8 %copy-start.12 = (bf16[256,128]{1,0:T(8,128)(2,1)S(1)}, bf16[256,128]{1,0:T(8,128)(2,1)}, u32[]{:S(2)}) copy-start(bf16[256,128]{1,0:T(8,128)(2,1)} %param.10) | copy-start | bytes 196612
  13.5 3.7 %copy-start.13 = (bf16[256,128]{1,0:T(8,128)(2,1)S(1)}, bf16[256,128]{1,0:T(8,128)(2,1)}, u32[]{:S(2)}) copy-start(bf16[256,128]{1,0:T(8,128)(2,1)} %param.11) | copy-start | bytes 196612
  13.5 15.1 %collective-permute-start = (bf16[8,128,256]{2,1,0:T(8,128)(2,1)S(1)}, bf16[8,128,256]{2,1,0:T(8,128)(2,1)S(1)}, u32[]{:S(2)}, u32[]{:S(2)}) collective-permute-start(bf16[8,128,256]{2,1,0:T(8,128)(2,1)S(1)} %get-tuple-element.37), channel_id=1, source_target_pairs={{0,2},{1,3},{4,6},{5,7},{8,10},{9,11},{12,14},{13,15},{16,18},{17,... | collective-permute-start | bytes 1572872 | tf_op jit(solution)/shard_map/ppermute | solution.py:504
  17.2 0.8 copy-start.14
  18.0 0.8 copy-start.15
  18.9 6.2 %copy-start.11 = (bf16[512,256]{1,0:T(8,128)(2,1)}, bf16[512,256]{1,0:T(8,128)(2,1)S(1)}, u32[]{:S(2)}) copy-start(bf16[512,256]{1,0:T(8,128)(2,1)S(1)} %pad_maximum_fusion.refs_5_) | copy-start | bytes 786436
  18.9 9.7 %collective-permute-start.1 = (bf16[512,256]{1,0:T(8,128)(2,1)S(1)}, bf16[512,256]{1,0:T(8,128)(2,1)S(1)}, u32[]{:S(2)}, u32[]{:S(2)}) collective-permute-start(bf16[512,256]{1,0:T(8,128)(2,1)S(1)} %pad_maximum_fusion.refs_5_), channel_id=1, source_target_pairs={{0,1},{1,0},{2,3},{3,2},{4,5},{5,4},{6,7},{7,6},{8,9},{9,8},{10,11... | collective-permute-start | bytes 786440 | tf_op jit(solution)/shard_map/ppermute | solution.py:402
  25.1 17.4 %all-to-all-start.1 = ((bf16[4,256,256]{2,1,0:T(8,128)(2,1)}), bf16[4,256,256]{2,1,0:T(8,128)(2,1)S(1)}, u32[]{:S(2)}, u32[]{:S(2)}) async-start(bf16[4,256,256]{2,1,0:T(8,128)(2,1)} %bitcast.11), calls=%async_computation.1 | async-start | bytes 1048576 | tf_op jit(solution)/shard_map/all_to_all | solution.py:499
  28.6 0.7 copy-start.18
  28.6 0.9 copy-start.16
  42.5 4.5 %copy-start.19 = (bf16[4,128,256]{2,1,0:T(8,128)(2,1)S(1)}, bf16[4,128,256]{2,1,0:T(8,128)(2,1)}, u32[]{:S(2)}) copy-start(bf16[4,128,256]{2,1,0:T(8,128)(2,1)} %get-tuple-element.44) | copy-start | bytes 786436
  42.6 18.5 %all-to-all-start.2 = ((bf16[4,256,256]{2,1,0:T(8,128)(2,1)}), bf16[4,256,256]{2,1,0:T(8,128)(2,1)S(1)}, u32[]{:S(2)}, u32[]{:S(2)}) async-start(bf16[4,256,256]{2,1,0:T(8,128)(2,1)} %bitcast.28), calls=%async_computation.2 | async-start | bytes 1048576 | tf_op jit(solution)/shard_map/all_to_all | solution.py:499
  47.1 14.0 %collective-permute-start.2 = (bf16[4,128,256]{2,1,0:T(8,128)(2,1)S(1)}, bf16[4,128,256]{2,1,0:T(8,128)(2,1)S(1)}, u32[]{:S(2)}, u32[]{:S(2)}) collective-permute-start(bf16[4,128,256]{2,1,0:T(8,128)(2,1)S(1)} %copy-done.19), channel_id=1, source_target_pairs={{2,0},{3,1},{6,4},{7,5},{10,8},{11,9},{14,12},{15,13},{18,16},{19,... | collective-permute-start | bytes 786440 | tf_op jit(solution)/shard_map/ppermute | solution.py:511
  61.1 5.3 %collective-permute-start.3 = (f32[512,256]{1,0:T(8,128)}, f32[512,256]{1,0:T(8,128)S(1)}, u32[]{:S(2)}, u32[]{:S(2)}) collective-permute-start(f32[512,256]{1,0:T(8,128)} %get-tuple-element.50), channel_id=1, source_target_pairs={{0,1},{1,0},{2,3},{3,2},{4,5},{5,4},{6,7},{7,6},{8,9},{9,8},{10,11... | collective-permute-start | bytes 1572872 | tf_op jit(solution)/shard_map/ppermute | solution.py:402
  61.1 5.3 %copy-start.9 = (f32[512,256]{1,0:T(8,128)S(1)}, f32[512,256]{1,0:T(8,128)}, u32[]{:S(2)}) copy-start(f32[512,256]{1,0:T(8,128)} %get-tuple-element.49) | copy-start | bytes 1572868
  61.2 23.7 %all-to-all-start.3 = ((bf16[4,256,256]{2,1,0:T(8,128)(2,1)}), bf16[4,256,256]{2,1,0:T(8,128)(2,1)S(1)}, u32[]{:S(2)}, u32[]{:S(2)}) async-start(bf16[4,256,256]{2,1,0:T(8,128)(2,1)} %bitcast.27), calls=%async_computation.3 | async-start | bytes 1048576 | tf_op jit(solution)/shard_map/all_to_all | solution.py:499
  66.5 8.5 %copy-start.17 = (bf16[4,128,256]{2,1,0:T(8,128)(2,1)S(1)}, bf16[4,128,256]{2,1,0:T(8,128)(2,1)}, u32[]{:S(2)}) copy-start(bf16[4,128,256]{2,1,0:T(8,128)(2,1)} %get-tuple-element.52) | copy-start | bytes 786436
  66.5 18.4 %copy-start.2 = (f32[4,128,256]{2,1,0:T(8,128)S(1)}, f32[4,128,256]{2,1,0:T(8,128)}, u32[]{:S(2)}) copy-start(f32[4,128,256]{2,1,0:T(8,128)} %get-tuple-element.42.refs_3_) | copy-start | bytes 1572868
  66.5 18.3 %copy-start.1 = (f32[4,128,256]{2,1,0:T(8,128)S(1)}, f32[4,128,256]{2,1,0:T(8,128)}, u32[]{:S(2)}) copy-start(f32[4,128,256]{2,1,0:T(8,128)} %get-tuple-element.38.refs_2_) | copy-start | bytes 1572868
  66.5 6.6 %collective-permute-start.4 = (bf16[256,256]{1,0:T(8,128)(2,1)S(1)}, bf16[256,256]{1,0:T(8,128)(2,1)S(1)}, u32[]{:S(2)}, u32[]{:S(2)}) collective-permute-start(bf16[256,256]{1,0:T(8,128)(2,1)S(1)} %select_convert_fusion), channel_id=1, source_target_pairs={{0,2},{2,0},{1,3},{3,1},{4,6},{6,4},{5,7},{7,5},{8,10},{10,8},{9,1... | collective-permute-start | bytes 393224 | tf_op jit(solution)/shard_map/ppermute | solution.py:402
  73.2 6.1 %collective-permute-start.5 = (bf16[256,256]{1,0:T(8,128)(2,1)S(1)}, bf16[256,256]{1,0:T(8,128)(2,1)S(1)}, u32[]{:S(2)}, u32[]{:S(2)}) collective-permute-start(bf16[256,256]{1,0:T(8,128)(2,1)S(1)} %add_convert_fusion), channel_id=1, source_target_pairs={{0,4},{4,0},{8,12},{12,8},{1,5},{5,1},{9,13},{13,9},{2,6},{6,2},{1... | collective-permute-start | bytes 393224 | tf_op jit(solution)/shard_map/ppermute | solution.py:402
  75.0 9.2 %collective-permute-start.6 = (bf16[4,128,256]{2,1,0:T(8,128)(2,1)S(1)}, bf16[4,128,256]{2,1,0:T(8,128)(2,1)S(1)}, u32[]{:S(2)}, u32[]{:S(2)}) collective-permute-start(bf16[4,128,256]{2,1,0:T(8,128)(2,1)S(1)} %copy-done.17), channel_id=1, source_target_pairs={{2,0},{3,1},{6,4},{7,5},{10,8},{11,9},{14,12},{15,13},{18,16},{19,... | collective-permute-start | bytes 786440 | tf_op jit(solution)/shard_map/ppermute | solution.py:520
  84.2 0.7 copy-start.3
  84.9 1.0 copy-start.4
  88.4 20.5 %collective-permute-start.7 = (f32[16,128,128]{2,1,0:T(8,128)}, f32[16,128,128]{2,1,0:T(8,128)S(1)}, u32[]{:S(2)}, u32[]{:S(2)}) collective-permute-start(f32[16,128,128]{2,1,0:T(8,128)} %get-tuple-element.57), channel_id=1, source_target_pairs={{0,1},{1,0},{2,3},{3,2},{4,5},{5,4},{6,7},{7,6},{8,9},{9,8},{10,11... | collective-permute-start | bytes 3145736 | tf_op jit(solution)/shard_map/ppermute | solution.py:402
  88.4 9.6 %collective-permute-start.8 = (bf16[256,256]{1,0:T(8,128)(2,1)S(1)}, bf16[256,256]{1,0:T(8,128)(2,1)S(1)}, u32[]{:S(2)}, u32[]{:S(2)}) collective-permute-start(bf16[256,256]{1,0:T(8,128)(2,1)S(1)} %convert_add_fusion.1), channel_id=1, source_target_pairs={{0,8},{4,12},{8,0},{12,4},{1,9},{5,13},{9,1},{13,5},{2,10},{6,14},... | collective-permute-start | bytes 393224 | tf_op jit(solution)/shard_map/ppermute | solution.py:402
  98.0 8.3 %copy-start.8 = (f32[256,256]{1,0:T(8,128)}, f32[256,256]{1,0:T(8,128)S(1)}, u32[]{:S(2)}) copy-start(f32[256,256]{1,0:T(8,128)S(1)} %convert_add_fusion.part) | copy-start | bytes 786436
  98.0 8.2 %collective-permute-start.9 = (f32[256,256]{1,0:T(8,128)S(1)}, f32[256,256]{1,0:T(8,128)S(1)}, u32[]{:S(2)}, u32[]{:S(2)}) collective-permute-start(f32[256,256]{1,0:T(8,128)S(1)} %convert_add_fusion.part), channel_id=1, source_target_pairs={{0,2},{2,0},{1,3},{3,1},{4,6},{6,4},{5,7},{7,5},{8,10},{10,8},{9,1... | collective-permute-start | bytes 786440 | tf_op jit(solution)/shard_map/ppermute | solution.py:402
  106.3 0.7 copy-start.10

commit v7 on v6

--- a/solution.py
+++ b/solution.py
@@ -407,7 +407,7 @@
     return low.astype(F32) + exchanged(low, axis, bit).astype(F32)
 
 
-def sum_gradients(total, settled):
+def sum_gradients(total, home_b, fold):
     half = total.shape[0] // 2
     first = lax.rem(lax.axis_index("day"), 2) == 0
     kept = jnp.where(first, total[:half], total[half:])
@@ -421,15 +421,17 @@
     while bit < lax.axis_size("reach"):
         part = summed_over(part, "reach", bit)
         if bit == 1:
-            part, *settled = lax.optimization_barrier((part, *settled))
+            part, home_b = lax.optimization_barrier((part, home_b))
         bit *= 2
-    return part, exchanged(part, "day", 1), settled
+    part, folded = lax.optimization_barrier((part.astype(BF16), fold(home_b)))
+    return part, exchanged(part, "day", 1), folded
 
 
 def split_kernel(where, part, other, query_out, key_out, value_out, output_out):
     first = lax.rem(where[3], 2) == 0
-    upper = jnp.where(first, part[...], other[...])
-    lower = jnp.where(first, other[...], part[...])
+    mine, theirs = part[...].astype(F32), other[...].astype(F32)
+    upper = jnp.where(first, mine, theirs)
+    lower = jnp.where(first, theirs, mine)
     key_out[...] = upper[:, :GROUP]
     value_out[...] = upper[:, GROUP:]
     query_out[...] = lower[:GROUP].T
@@ -518,16 +520,19 @@
     grad_swapped = exchanged(grad_other, "head", 1)
     home_b = ring(home_b)
     day_b = lax.ppermute(day_b, "day", last_day)
-    part, other, (home_b, day_b) = sum_gradients(grad_mine + grad_swapped, (home_b, day_b))
     half_shape = jax.ShapeDtypeStruct((blocks_dev, BLOCK, half), F32)
-    keep, give = pl.pallas_call(
-        lambda *refs: fold_kernel(lay, *refs),
-        out_shape=(half_shape, half_shape),
-        in_specs=[smem] * 2 + [in_vmem] * 6,
-        out_specs=[in_vmem] * 2,
-        compiler_params=pltpu.CompilerParams(vmem_limit_bytes=16 << 20),
-        name="fold",
-    )(tab, homes, own_a, own_b, day_a, day_b, home_a, home_b)
+
+    def fold(home_b):
+        return pl.pallas_call(
+            lambda *refs: fold_kernel(lay, *refs),
+            out_shape=(half_shape, half_shape),
+            in_specs=[smem] * 2 + [in_vmem] * 6,
+            out_specs=[in_vmem] * 2,
+            compiler_params=pltpu.CompilerParams(vmem_limit_bytes=16 << 20),
+            name="fold",
+        )(tab, homes, own_a, own_b, day_a, day_b, home_a, home_b)
+
+    part, other, (keep, give) = sum_gradients(grad_mine + grad_swapped, home_b, fold)
     got = exchanged(give, "head", 1)
     back_blocks = pl.pallas_call(
         add_kernel,

time: 110 us -> 100 us (0.909)
  waiting for transfers between devices: 34 us -> 21.9 us
  starting transfers between devices: 32.8 us -> 34.8 us
    ppermute x7, waiting for transfers between devices: 22.3 us -> 11.9 us  [exchanged(): lax.ppermute(value, axis, [(place, place ^ bit) for place in range(count)])]
    ppermute x1, waiting for transfers between devices: 4.81 us -> 0.97 us  [on_device(): day_b = lax.ppermute(day_b, 'day', last_day)]
    all_to_all x4, waiting for transfers between devices: 6.85 us -> 9.03 us  [ring(): return lax.all_to_all(value, 'reach', 0, 0, tiled=True).reshape(shape)]
    ppermute x7, starting transfers between devices: 7.1 us -> 9.11 us  [exchanged(): lax.ppermute(value, axis, [(place, place ^ bit) for place in range(count)])]
  transfers between devices with their start and end apart: 14 -> 14, of which waited for: 7 -> 8; matrix products, arithmetic and copies ran while one was open for 0% -> 1% of each run, Pallas kernels for 27% -> 32%
where the time goes in v7:
time: 100 us; the launch traced here: 99.6 us
  Pallas kernels  35.4 us (35%)
  starting transfers between devices  34.8 us (35%)
  waiting for transfers between devices  21.9 us (22%)
  local copies, waits for them, and re-layouts  6.28 us (6%)
    pallas_call x2, Pallas kernels, attend(): pl.pallas_call(lambda *refs: attention_kernel(lay, chunk, *refs), grid_sp...  25.1 us
    all_to_all x4, starting transfers between devices, ring(): return lax.all_to_all(value, 'reach', 0, 0, tiled=True).reshape(shape)  19.5 us
    ppermute x7, waiting for transfers between devices, exchanged(): lax.ppermute(value, axis, [(place, place ^ bit) for place in range(count)])  11.9 us
    ppermute x7, starting transfers between devices, exchanged(): lax.ppermute(value, axis, [(place, place ^ bit) for place in range(count)])  9.11 us
    all_to_all x4, waiting for transfers between devices, ring(): return lax.all_to_all(value, 'reach', 0, 0, tiled=True).reshape(shape)  9.03 us
    unnamed x43, local copies, waits for them, and re-layouts  6.28 us
    ppermute x1, starting transfers between devices, on_device(): prior_inputs = lax.ppermute(prior, 'day', next_day)  3.56 us
    pallas_call x1, Pallas kernels, on_device(): pl.pallas_call(lambda *refs: pick_kernel(lay, *refs), out_shape=(sent_sha...  2.9 us
  transfers between devices with their start and end apart: 14, of which 8 were waited for; matrix products, arithmetic and copies ran while one was open for 1% of the time, Pallas kernels for 32%

profile of v7, /device:TPU:0, one launch (start us, length us, event | category | flops | bytes accessed | tf_op | source)
XLA Modules:
  0.0 99.6 jit_solution(12715115365634963413)
XLA Ops:
  0.6 0.1 pad_add_fusion.refs_1_.refs_2_.where
  0.7 0.7 copy-done.6
  1.4 2.9 %pick.1 = (bf16[8,128,256]{2,1,0:T(8,128)(2,1)}, s32[128]{0:T(128)S(1)}) custom-call(s32[64]{0:T(128)S(1)} %copy-done.6, s32[4]{0:T(128)S(1)} %pad_add_fusion.refs_1_.refs_2_.where, bf16[16,128,256]{2,1,0:T(8,128)(2,1)} %bitcast.18), custom_call_target="tpu_custom_call" | custom-call | tf_op jit(solution)/shard_map/pick/pallas_call | solution.py:469
  4.3 6.3 %all-to-all-start.1 = ((bf16[4,256,256]{2,1,0:T(8,128)(2,1)}), bf16[4,256,256]{2,1,0:T(8,128)(2,1)S(1)}, u32[]{:S(2)}, u32[]{:S(2)}) async-start(bf16[4,256,256]{2,1,0:T(8,128)(2,1)} %bitcast.11), calls=%async_computation.1 | async-start | bytes 1048576 | tf_op jit(solution)/shard_map/all_to_all | solution.py:501
  10.6 0.6 copy-done.7
  11.3 2.2 %deal.1 = (bf16[8,128,256]{2,1,0:T(8,128)(2,1)}, bf16[8,128,256]{2,1,0:T(8,128)(2,1)S(1)}, s32[128]{0:T(128)S(1)}) custom-call(s32[64]{0:T(128)S(1)} %copy-done.6, s32[64]{0:T(128)S(1)} %copy-done.7, s32[4]{0:T(128)S(1)} %pad_add_fusion.refs_1_.refs_2_.where, s32[128]{0:T(128)S(1)} %get-tuple-element.36.refs_3_.refs_1_, bf16[16,128,256]{2,1,0:T(8,128)(2,1)S(1)} %bitcast.21), custom_call_target="tpu_custom_call" | custom-call | tf_op jit(solution)/shard_map/deal/pallas_call | solution.py:481
  13.5 0.0 copy-start.13
  13.5 3.6 %collective-permute-start = (bf16[8,128,256]{2,1,0:T(8,128)(2,1)S(1)}, bf16[8,128,256]{2,1,0:T(8,128)(2,1)S(1)}, u32[]{:S(2)}, u32[]{:S(2)}) collective-permute-start(bf16[8,128,256]{2,1,0:T(8,128)(2,1)S(1)} %get-tuple-element.39), channel_id=1, source_target_pairs={{0,2},{1,3},{4,6},{5,7},{8,10},{9,11},{12,14},{13,15},{16,18},{17,... | collective-permute-start | bytes 1572872 | tf_op jit(solution)/shard_map/ppermute | solution.py:506
  17.1 0.1 copy.15
  17.2 0.0 copy-start.14
  17.2 0.1 copy.13
  17.3 0.7 copy-done.14
  18.0 0.1 copy.14
  18.1 0.7 copy-done.15
  18.9 0.1 collective-permute-start.1
  19.0 6.1 %all-to-all-done.1 = bf16[4,256,256]{2,1,0:T(8,128)(2,1)S(1)} async-done(((bf16[4,256,256]{2,1,0:T(8,128)(2,1)}), bf16[4,256,256]{2,1,0:T(8,128)(2,1)S(1)}, u32[]{:S(2)}, u32[]{:S(2)}) %all-to-all-start.1) | async-done | bytes 524320 | tf_op jit(solution)/shard_map/all_to_all | solution.py:501
  25.1 3.5 %all-to-all-start = ((bf16[4,256,256]{2,1,0:T(8,128)(2,1)}), bf16[4,256,256]{2,1,0:T(8,128)(2,1)S(1)}, u32[]{:S(2)}, u32[]{:S(2)}) async-start(bf16[4,256,256]{2,1,0:T(8,128)(2,1)} %bitcast.6), calls=%async_computation | async-start | bytes 1048576 | tf_op jit(solution)/shard_map/all_to_all | solution.py:501
  28.6 0.0 copy-start.16
  28.6 0.7 copy-done.18
  29.3 0.2 copy-done.16
  29.5 12.4 %attention_0.1 = (f32[4,128,256]{2,1,0:T(8,128)}, bf16[4,128,256]{2,1,0:T(8,128)(2,1)}, bf16[8,128,256]{2,1,0:T(8,128)(2,1)}, f32[512,256]{1,0:T(8,128)}, f32[512,256]{1,0:T(8,128)}) custom-call(s32[128]{0:T(128)S(1)} %get-tuple-element.37.refs_0_, bf16[16,128,256]{2,1,0:T(8,128)(2,1)} %bitcast.19, bf16[16,128,256]{2,1,0:T(8,128)(2,1)} %bitcast.32, ...), custom_call_target="tpu_custom_call" | custom-call | flops 6375342080 | bytes 5242880 | tf_op jit(solution)/shard_map/attention_0/pallas_call | solution.py:363
  41.8 0.7 all-to-all-done
  42.6 4.5 %all-to-all-start.2 = ((bf16[4,256,256]{2,1,0:T(8,128)(2,1)}), bf16[4,256,256]{2,1,0:T(8,128)(2,1)S(1)}, u32[]{:S(2)}, u32[]{:S(2)}) async-start(bf16[4,256,256]{2,1,0:T(8,128)(2,1)} %bitcast.28), calls=%async_computation.2 | async-start | bytes 1048576 | tf_op jit(solution)/shard_map/all_to_all | solution.py:501
  47.1 1.3 %collective-permute-start.2 = (bf16[4,128,256]{2,1,0:T(8,128)(2,1)S(1)}, bf16[4,128,256]{2,1,0:T(8,128)(2,1)S(1)}, u32[]{:S(2)}, u32[]{:S(2)}) collective-permute-start(bf16[4,128,256]{2,1,0:T(8,128)(2,1)S(1)} %copy-done.19), channel_id=1, source_target_pairs={{2,0},{3,1},{6,4},{7,5},{10,8},{11,9},{14,12},{15,13},{18,16},{19,... | collective-permute-start | bytes 786440 | tf_op jit(solution)/shard_map/ppermute | solution.py:513
  48.3 12.7 %attention_1.1 = (f32[4,128,256]{2,1,0:T(8,128)}, bf16[4,128,256]{2,1,0:T(8,128)(2,1)}, bf16[8,128,256]{2,1,0:T(8,128)(2,1)}, f32[512,256]{1,0:T(8,128)}, f32[512,256]{1,0:T(8,128)}) custom-call(s32[128]{0:T(128)S(1)} %get-tuple-element.37.refs_0_, bf16[16,128,256]{2,1,0:T(8,128)(2,1)} %bitcast.20, bf16[16,128,256]{2,1,0:T(8,128)(2,1)} %bitcast.33, ...), custom_call_target="tpu_custom_call" | custom-call | flops 6375342080 | bytes 5242880 | tf_op jit(solution)/shard_map/attention_1/pallas_call | solution.py:363
  61.1 0.1 collective-permute-start.3
  61.2 5.2 %all-to-all-start.3 = ((bf16[4,256,256]{2,1,0:T(8,128)(2,1)}), bf16[4,256,256]{2,1,0:T(8,128)(2,1)S(1)}, u32[]{:S(2)}, u32[]{:S(2)}) async-start(bf16[4,256,256]{2,1,0:T(8,128)(2,1)} %bitcast.27), calls=%async_computation.3 | async-start | bytes 1048576 | tf_op jit(solution)/shard_map/all_to_all | solution.py:501
  66.4 0.1 add.13
  66.5 2.7 %collective-permute-start.4 = (bf16[256,256]{1,0:T(8,128)(2,1)S(1)}, bf16[256,256]{1,0:T(8,128)(2,1)S(1)}, u32[]{:S(2)}, u32[]{:S(2)}) collective-permute-start(bf16[256,256]{1,0:T(8,128)(2,1)S(1)} %select_convert_fusion), channel_id=1, source_target_pairs={{0,2},{2,0},{1,3},{3,1},{4,6},{6,4},{5,7},{7,5},{8,10},{10,8},{9,1... | collective-permute-start | bytes 393224 | tf_op jit(solution)/shard_map/ppermute | solution.py:402
  69.3 3.9 %collective-permute-done.4 = bf16[256,256]{1,0:T(8,128)(2,1)S(1)} collective-permute-done((bf16[256,256]{1,0:T(8,128)(2,1)S(1)}, bf16[256,256]{1,0:T(8,128)(2,1)S(1)}, u32[]{:S(2)}, u32[]{:S(2)}) %collective-permute-start.4) | collective-permute-done | bytes 131104 | tf_op jit(solution)/shard_map/ppermute | solution.py:402
  73.1 0.1 add_convert_fusion.1
  73.2 1.8 %collective-permute-start.5 = (bf16[256,256]{1,0:T(8,128)(2,1)S(1)}, bf16[256,256]{1,0:T(8,128)(2,1)S(1)}, u32[]{:S(2)}, u32[]{:S(2)}) collective-permute-start(bf16[256,256]{1,0:T(8,128)(2,1)S(1)} %add_convert_fusion.1), channel_id=1, source_target_pairs={{0,4},{4,0},{8,12},{12,8},{1,5},{5,1},{9,13},{13,9},{2,6},{6,2},{1... | collective-permute-start | bytes 393224 | tf_op jit(solution)/shard_map/ppermute | solution.py:402
  75.0 1.3 %collective-permute-start.7 = (bf16[4,128,256]{2,1,0:T(8,128)(2,1)S(1)}, bf16[4,128,256]{2,1,0:T(8,128)(2,1)S(1)}, u32[]{:S(2)}, u32[]{:S(2)}) collective-permute-start(bf16[4,128,256]{2,1,0:T(8,128)(2,1)S(1)} %copy-done.17), channel_id=1, source_target_pairs={{2,0},{3,1},{6,4},{7,5},{10,8},{11,9},{14,12},{15,13},{18,16},{19,... | collective-permute-start | bytes 786440 | tf_op jit(solution)/shard_map/ppermute | solution.py:522
  76.3 3.0 %collective-permute-done.5 = bf16[256,256]{1,0:T(8,128)(2,1)S(1)} collective-permute-done((bf16[256,256]{1,0:T(8,128)(2,1)S(1)}, bf16[256,256]{1,0:T(8,128)(2,1)S(1)}, u32[]{:S(2)}, u32[]{:S(2)}) %collective-permute-start.5) | collective-permute-done | bytes 131104 | tf_op jit(solution)/shard_map/ppermute | solution.py:402
  79.4 2.2 %all-to-all-done.3 = bf16[4,256,256]{2,1,0:T(8,128)(2,1)S(1)} async-done(((bf16[4,256,256]{2,1,0:T(8,128)(2,1)}), bf16[4,256,256]{2,1,0:T(8,128)(2,1)S(1)}, u32[]{:S(2)}, u32[]{:S(2)}) %all-to-all-start.3) | async-done | bytes 524320 | tf_op jit(solution)/shard_map/all_to_all | solution.py:501
  81.5 1.7 %collective-permute-start.6 = (bf16[256,256]{1,0:T(8,128)(2,1)S(1)}, bf16[256,256]{1,0:T(8,128)(2,1)S(1)}, u32[]{:S(2)}, u32[]{:S(2)}) collective-permute-start(bf16[256,256]{1,0:T(8,128)(2,1)S(1)} %convert_add_fusion), channel_id=1, source_target_pairs={{0,8},{4,12},{8,0},{12,4},{1,9},{5,13},{9,1},{13,5},{2,10},{6,14},... | collective-permute-start | bytes 393224 | tf_op jit(solution)/shard_map/ppermute | solution.py:402
  83.2 1.0 collective-permute-done.7.refs_5_
  84.2 0.7 copy-done.3
  84.9 0.9 copy-done.4
  85.8 2.6 %fold.1 = (f32[16,128,128]{2,1,0:T(8,128)S(1)}, f32[16,128,128]{2,1,0:T(8,128)}) custom-call(s32[128]{0:T(128)S(1)} %get-tuple-element.37.refs_0_, s32[128]{0:T(128)S(1)} %get-tuple-element.36.refs_3_.refs_1_, f32[4,128,256]{2,1,0:T(8,128)S(1)} %copy-done.1, f32[4,128,256]{2,1,0:T(8,128)S(1)} %copy-done.2, ...), custom_call_target="tpu_custom_call" | custom-call | tf_op jit(solution)/shard_map/fold/pallas_call | solution.py:526
  88.4 0.9 collective-permute-done.6
  89.3 0.0 copy-start.8
  89.4 0.1 collective-permute-start.8
  89.4 2.7 %collective-permute-start.9 = (bf16[256,256]{1,0:T(8,128)(2,1)S(1)}, bf16[256,256]{1,0:T(8,128)(2,1)S(1)}, u32[]{:S(2)}, u32[]{:S(2)}) collective-permute-start(bf16[256,256]{1,0:T(8,128)(2,1)S(1)} %add_convert_fusion.part), channel_id=1, source_target_pairs={{0,2},{2,0},{1,3},{3,1},{4,6},{6,4},{5,7},{7,5},{8,10},{10,8},{9,1... | collective-permute-start | bytes 393224 | tf_op jit(solution)/shard_map/ppermute | solution.py:402
  92.1 4.1 %collective-permute-done.9.other = bf16[256,256]{1,0:T(8,128)(2,1)S(1)} collective-permute-done((bf16[256,256]{1,0:T(8,128)(2,1)S(1)}, bf16[256,256]{1,0:T(8,128)(2,1)S(1)}, u32[]{:S(2)}, u32[]{:S(2)}) %collective-permute-start.9) | collective-permute-done | bytes 131104 | tf_op jit(solution)/shard_map/ppermute | solution.py:402
  96.2 0.7 copy-done.11
  96.9 1.8 %split.1 = (f32[256,128]{1,0:T(8,128)}, f32[256,128]{1,0:T(8,128)}, f32[256,128]{1,0:T(8,128)}, f32[128,256]{1,0:T(8,128)}) custom-call(s32[4]{0:T(128)} %copy-done.5, bf16[256,256]{1,0:T(8,128)(2,1)} %copy-done.8, bf16[256,256]{1,0:T(8,128)(2,1)} %copy-done.11), custom_call_target="tpu_custom_call" | custom-call | tf_op jit(solution)/shard_map/split/pallas_call | solution.py:545
  98.7 0.9 add.26
  (37 shorter events, 0.2 us)
Async XLA Ops:
  0.7 9.9 %copy-start.5 = (s32[4]{0:T(128)}, s32[4]{0:T(128)S(1)}, u32[]{:S(2)}) copy-start(s32[4]{0:T(128)S(1)} %pad_add_fusion.refs_1_.refs_2_.where) | copy-start | bytes 52
  0.7 0.7 copy-start.6
  1.4 9.2 %copy-start = (bf16[1,2048,256]{2,1,0:T(8,128)(2,1)S(1)}, bf16[1,2048,256]{2,1,0:T(8,128)(2,1)}, u32[]{:S(2)}) copy-start(bf16[1,2048,256]{2,1,0:T(8,128)(2,1)} %param.8) | copy-start | bytes 3145732
  4.3 20.8 %all-to-all-start.1 = ((bf16[4,256,256]{2,1,0:T(8,128)(2,1)}), bf16[4,256,256]{2,1,0:T(8,128)(2,1)S(1)}, u32[]{:S(2)}, u32[]{:S(2)}) async-start(bf16[4,256,256]{2,1,0:T(8,128)(2,1)} %bitcast.11), calls=%async_computation.1 | async-start | bytes 1048576 | tf_op jit(solution)/shard_map/all_to_all | solution.py:501
  10.6 0.7 copy-start.7
  11.3 5.8 %copy-start.12 = (bf16[256,128]{1,0:T(8,128)(2,1)S(1)}, bf16[256,128]{1,0:T(8,128)(2,1)}, u32[]{:S(2)}) copy-start(bf16[256,128]{1,0:T(8,128)(2,1)} %param.10) | copy-start | bytes 196612
  13.5 3.7 %copy-start.13 = (bf16[256,128]{1,0:T(8,128)(2,1)S(1)}, bf16[256,128]{1,0:T(8,128)(2,1)}, u32[]{:S(2)}) copy-start(bf16[256,128]{1,0:T(8,128)(2,1)} %param.11) | copy-start | bytes 196612
  13.5 15.1 %collective-permute-start = (bf16[8,128,256]{2,1,0:T(8,128)(2,1)S(1)}, bf16[8,128,256]{2,1,0:T(8,128)(2,1)S(1)}, u32[]{:S(2)}, u32[]{:S(2)}) collective-permute-start(bf16[8,128,256]{2,1,0:T(8,128)(2,1)S(1)} %get-tuple-element.39), channel_id=1, source_target_pairs={{0,2},{1,3},{4,6},{5,7},{8,10},{9,11},{12,14},{13,15},{16,18},{17,... | collective-permute-start | bytes 1572872 | tf_op jit(solution)/shard_map/ppermute | solution.py:506
  17.2 0.8 copy-start.14
  18.0 0.8 copy-start.15
  18.9 6.2 %copy-start.10 = (bf16[512,256]{1,0:T(8,128)(2,1)}, bf16[512,256]{1,0:T(8,128)(2,1)S(1)}, u32[]{:S(2)}) copy-start(bf16[512,256]{1,0:T(8,128)(2,1)S(1)} %pad_maximum_fusion.refs_5_) | copy-start | bytes 786436
  18.9 9.7 %collective-permute-start.1 = (bf16[512,256]{1,0:T(8,128)(2,1)S(1)}, bf16[512,256]{1,0:T(8,128)(2,1)S(1)}, u32[]{:S(2)}, u32[]{:S(2)}) collective-permute-start(bf16[512,256]{1,0:T(8,128)(2,1)S(1)} %pad_maximum_fusion.refs_5_), channel_id=1, source_target_pairs={{0,1},{1,0},{2,3},{3,2},{4,5},{5,4},{6,7},{7,6},{8,9},{9,8},{10,11... | collective-permute-start | bytes 786440 | tf_op jit(solution)/shard_map/ppermute | solution.py:402
  25.1 17.4 %all-to-all-start = ((bf16[4,256,256]{2,1,0:T(8,128)(2,1)}), bf16[4,256,256]{2,1,0:T(8,128)(2,1)S(1)}, u32[]{:S(2)}, u32[]{:S(2)}) async-start(bf16[4,256,256]{2,1,0:T(8,128)(2,1)} %bitcast.6), calls=%async_computation | async-start | bytes 1048576 | tf_op jit(solution)/shard_map/all_to_all | solution.py:501
  28.6 0.7 copy-start.18
  28.6 0.9 copy-start.16
  42.5 4.5 %copy-start.19 = (bf16[4,128,256]{2,1,0:T(8,128)(2,1)S(1)}, bf16[4,128,256]{2,1,0:T(8,128)(2,1)}, u32[]{:S(2)}) copy-start(bf16[4,128,256]{2,1,0:T(8,128)(2,1)} %get-tuple-element.45) | copy-start | bytes 786436
  42.6 18.5 %all-to-all-start.2 = ((bf16[4,256,256]{2,1,0:T(8,128)(2,1)}), bf16[4,256,256]{2,1,0:T(8,128)(2,1)S(1)}, u32[]{:S(2)}, u32[]{:S(2)}) async-start(bf16[4,256,256]{2,1,0:T(8,128)(2,1)} %bitcast.28), calls=%async_computation.2 | async-start | bytes 1048576 | tf_op jit(solution)/shard_map/all_to_all | solution.py:501
  47.1 14.0 %collective-permute-start.2 = (bf16[4,128,256]{2,1,0:T(8,128)(2,1)S(1)}, bf16[4,128,256]{2,1,0:T(8,128)(2,1)S(1)}, u32[]{:S(2)}, u32[]{:S(2)}) collective-permute-start(bf16[4,128,256]{2,1,0:T(8,128)(2,1)S(1)} %copy-done.19), channel_id=1, source_target_pairs={{2,0},{3,1},{6,4},{7,5},{10,8},{11,9},{14,12},{15,13},{18,16},{19,... | collective-permute-start | bytes 786440 | tf_op jit(solution)/shard_map/ppermute | solution.py:513
  61.1 5.3 %collective-permute-start.3 = (f32[512,256]{1,0:T(8,128)}, f32[512,256]{1,0:T(8,128)S(1)}, u32[]{:S(2)}, u32[]{:S(2)}) collective-permute-start(f32[512,256]{1,0:T(8,128)} %get-tuple-element.49), channel_id=1, source_target_pairs={{0,1},{1,0},{2,3},{3,2},{4,5},{5,4},{6,7},{7,6},{8,9},{9,8},{10,11... | collective-permute-start | bytes 1572872 | tf_op jit(solution)/shard_map/ppermute | solution.py:402
  61.1 5.3 %copy-start.9 = (f32[512,256]{1,0:T(8,128)S(1)}, f32[512,256]{1,0:T(8,128)}, u32[]{:S(2)}) copy-start(f32[512,256]{1,0:T(8,128)} %get-tuple-element.43) | copy-start | bytes 1572868
  61.2 20.4 %all-to-all-start.3 = ((bf16[4,256,256]{2,1,0:T(8,128)(2,1)}), bf16[4,256,256]{2,1,0:T(8,128)(2,1)S(1)}, u32[]{:S(2)}, u32[]{:S(2)}) async-start(bf16[4,256,256]{2,1,0:T(8,128)(2,1)} %bitcast.27), calls=%async_computation.3 | async-start | bytes 1048576 | tf_op jit(solution)/shard_map/all_to_all | solution.py:501
  66.5 8.5 %copy-start.17 = (bf16[4,128,256]{2,1,0:T(8,128)(2,1)S(1)}, bf16[4,128,256]{2,1,0:T(8,128)(2,1)}, u32[]{:S(2)}) copy-start(bf16[4,128,256]{2,1,0:T(8,128)(2,1)} %get-tuple-element.55) | copy-start | bytes 786436
  66.5 18.4 %copy-start.2 = (f32[4,128,256]{2,1,0:T(8,128)S(1)}, f32[4,128,256]{2,1,0:T(8,128)}, u32[]{:S(2)}) copy-start(f32[4,128,256]{2,1,0:T(8,128)} %get-tuple-element.53.refs_3_) | copy-start | bytes 1572868
  66.5 18.3 %copy-start.1 = (f32[4,128,256]{2,1,0:T(8,128)S(1)}, f32[4,128,256]{2,1,0:T(8,128)}, u32[]{:S(2)}) copy-start(f32[4,128,256]{2,1,0:T(8,128)} %get-tuple-element.52.refs_2_) | copy-start | bytes 1572868
  66.5 6.6 %collective-permute-start.4 = (bf16[256,256]{1,0:T(8,128)(2,1)S(1)}, bf16[256,256]{1,0:T(8,128)(2,1)S(1)}, u32[]{:S(2)}, u32[]{:S(2)}) collective-permute-start(bf16[256,256]{1,0:T(8,128)(2,1)S(1)} %select_convert_fusion), channel_id=1, source_target_pairs={{0,2},{2,0},{1,3},{3,1},{4,6},{6,4},{5,7},{7,5},{8,10},{10,8},{9,1... | collective-permute-start | bytes 393224 | tf_op jit(solution)/shard_map/ppermute | solution.py:402
  73.2 6.1 %collective-permute-start.5 = (bf16[256,256]{1,0:T(8,128)(2,1)S(1)}, bf16[256,256]{1,0:T(8,128)(2,1)S(1)}, u32[]{:S(2)}, u32[]{:S(2)}) collective-permute-start(bf16[256,256]{1,0:T(8,128)(2,1)S(1)} %add_convert_fusion.1), channel_id=1, source_target_pairs={{0,4},{4,0},{8,12},{12,8},{1,5},{5,1},{9,13},{13,9},{2,6},{6,2},{1... | collective-permute-start | bytes 393224 | tf_op jit(solution)/shard_map/ppermute | solution.py:402
  75.0 9.2 %collective-permute-start.7 = (bf16[4,128,256]{2,1,0:T(8,128)(2,1)S(1)}, bf16[4,128,256]{2,1,0:T(8,128)(2,1)S(1)}, u32[]{:S(2)}, u32[]{:S(2)}) collective-permute-start(bf16[4,128,256]{2,1,0:T(8,128)(2,1)S(1)} %copy-done.17), channel_id=1, source_target_pairs={{2,0},{3,1},{6,4},{7,5},{10,8},{11,9},{14,12},{15,13},{18,16},{19,... | collective-permute-start | bytes 786440 | tf_op jit(solution)/shard_map/ppermute | solution.py:522
  81.5 7.8 %collective-permute-start.6 = (bf16[256,256]{1,0:T(8,128)(2,1)S(1)}, bf16[256,256]{1,0:T(8,128)(2,1)S(1)}, u32[]{:S(2)}, u32[]{:S(2)}) collective-permute-start(bf16[256,256]{1,0:T(8,128)(2,1)S(1)} %convert_add_fusion), channel_id=1, source_target_pairs={{0,8},{4,12},{8,0},{12,4},{1,9},{5,13},{9,1},{13,5},{2,10},{6,14},... | collective-permute-start | bytes 393224 | tf_op jit(solution)/shard_map/ppermute | solution.py:402
  84.2 0.7 copy-start.3
  84.9 1.0 copy-start.4
  89.3 6.9 %copy-start.8 = (bf16[256,256]{1,0:T(8,128)(2,1)}, bf16[256,256]{1,0:T(8,128)(2,1)S(1)}, u32[]{:S(2)}) copy-start(bf16[256,256]{1,0:T(8,128)(2,1)S(1)} %add_convert_fusion.part) | copy-start | bytes 393220
  89.4 9.4 %collective-permute-start.8 = (f32[16,128,128]{2,1,0:T(8,128)}, f32[16,128,128]{2,1,0:T(8,128)S(1)}, u32[]{:S(2)}, u32[]{:S(2)}) collective-permute-start(f32[16,128,128]{2,1,0:T(8,128)} %get-tuple-element.61), channel_id=1, source_target_pairs={{0,1},{1,0},{2,3},{3,2},{4,5},{5,4},{6,7},{7,6},{8,9},{9,8},{10,11... | collective-permute-start | bytes 3145736 | tf_op jit(solution)/shard_map/ppermute | solution.py:402
  89.4 6.8 %collective-permute-start.9 = (bf16[256,256]{1,0:T(8,128)(2,1)S(1)}, bf16[256,256]{1,0:T(8,128)(2,1)S(1)}, u32[]{:S(2)}, u32[]{:S(2)}) collective-permute-start(bf16[256,256]{1,0:T(8,128)(2,1)S(1)} %add_convert_fusion.part), channel_id=1, source_target_pairs={{0,2},{2,0},{1,3},{3,1},{4,6},{6,4},{5,7},{7,5},{8,10},{10,8},{9,1... | collective-permute-start | bytes 393224 | tf_op jit(solution)/shard_map/ppermute | solution.py:402
  96.2 0.7 copy-start.11

commit v8 on v7

--- a/solution.py
+++ b/solution.py
@@ -407,12 +407,14 @@
     return low.astype(F32) + exchanged(low, axis, bit).astype(F32)
 
 
-def sum_gradients(total, home_b, fold):
+def sum_gradients(total, home_b, ring, fold):
     half = total.shape[0] // 2
     first = lax.rem(lax.axis_index("day"), 2) == 0
     kept = jnp.where(first, total[:half], total[half:])
     given = jnp.where(first, total[half:], total[:half])
-    part = kept.astype(BF16).astype(F32) + exchanged(given.astype(BF16), "day", 1).astype(F32)
+    given, home_b = lax.optimization_barrier((given.astype(BF16), home_b))
+    home_b = ring(home_b)
+    part = kept.astype(BF16).astype(F32) + exchanged(given, "day", 1).astype(F32)
     bit = 2
     while bit < lax.axis_size("day"):
         part = summed_over(part, "day", bit)
@@ -420,11 +422,11 @@
     bit = 1
     while bit < lax.axis_size("reach"):
         part = summed_over(part, "reach", bit)
-        if bit == 1:
-            part, home_b = lax.optimization_barrier((part, home_b))
         bit *= 2
-    part, folded = lax.optimization_barrier((part.astype(BF16), fold(home_b)))
-    return part, exchanged(part, "day", 1), folded
+    part = part.astype(BF16)
+    keep, give = fold(home_b)
+    other, give = lax.optimization_barrier((exchanged(part, "day", 1), give))
+    return part, other, keep, give
 
 
 def split_kernel(where, part, other, query_out, key_out, value_out, output_out):
@@ -518,7 +520,6 @@
         (home_a, day_a, home_b, day_b, grad_other)
     )
     grad_swapped = exchanged(grad_other, "head", 1)
-    home_b = ring(home_b)
     day_b = lax.ppermute(day_b, "day", last_day)
     half_shape = jax.ShapeDtypeStruct((blocks_dev, BLOCK, half), F32)
 
@@ -532,7 +533,9 @@
             name="fold",
         )(tab, homes, own_a, own_b, day_a, day_b, home_a, home_b)
 
-    part, other, (keep, give) = sum_gradients(grad_mine + grad_swapped, home_b, fold)
+    part, other, keep, give = sum_gradients(
+        grad_mine + grad_swapped, home_b, ring, fold
+    )
     got = exchanged(give, "head", 1)
     back_blocks = pl.pallas_call(
         add_kernel,

time: 100 us -> 107 us (1.070)
  waiting for transfers between devices: 21.9 us -> 29.2 us
  starting transfers between devices: 34.8 us -> 33.6 us
    ppermute x7, waiting for transfers between devices: 11.9 us -> 22.3 us  [exchanged(): lax.ppermute(value, axis, [(place, place ^ bit) for place in range(count)])]
    all_to_all x4, waiting for transfers between devices: 9.03 us -> 6.87 us  [ring(): return lax.all_to_all(value, 'reach', 0, 0, tiled=True).reshape(shape)]
    all_to_all x4, starting transfers between devices: 19.5 us -> 18.1 us  [ring(): return lax.all_to_all(value, 'reach', 0, 0, tiled=True).reshape(shape)]
    unnamed x43 -> x39, local copies, waits for them, and re-layouts: 6.28 us -> 5.61 us
  transfers between devices with their start and end apart: 14 -> 14, of which waited for: 8 -> 6; matrix products, arithmetic and copies ran while one was open for 1% -> 0% of each run, Pallas kernels for 32% -> 30%
where the time goes in v8:
time: 107 us; the launch traced here: 106 us
  Pallas kernels  35.4 us (33%)
  starting transfers between devices  33.6 us (31%)
  waiting for transfers between devices  29.2 us (27%)
  local copies, waits for them, and re-layouts  5.61 us (5%)
  other arithmetic  1.36 us (1%)
    pallas_call x2, Pallas kernels, attend(): pl.pallas_call(lambda *refs: attention_kernel(lay, chunk, *refs), grid_sp...  25.1 us
    ppermute x7, waiting for transfers between devices, exchanged(): lax.ppermute(value, axis, [(place, place ^ bit) for place in range(count)])  22.3 us
    all_to_all x4, starting transfers between devices, ring(): return lax.all_to_all(value, 'reach', 0, 0, tiled=True).reshape(shape)  18.1 us
    ppermute x7, starting transfers between devices, exchanged(): lax.ppermute(value, axis, [(place, place ^ bit) for place in range(count)])  9.43 us
    all_to_all x4, waiting for transfers between devices, ring(): return lax.all_to_all(value, 'reach', 0, 0, tiled=True).reshape(shape)  6.87 us
    unnamed x39, local copies, waits for them, and re-layouts  5.61 us
    ppermute x1, starting transfers between devices, on_device(): prior_inputs = lax.ppermute(prior, 'day', next_day)  3.56 us
    pallas_call x1, Pallas kernels, on_device(): pl.pallas_call(lambda *refs: pick_kernel(lay, *refs), out_shape=(sent_sha...  2.9 us
  transfers between devices with their start and end apart: 14, of which 6 were waited for; matrix products, arithmetic and copies ran while one was open for 0% of the time, Pallas kernels for 30%

profile of v8, /device:TPU:0, one launch (start us, length us, event | category | flops | bytes accessed | tf_op | source)
XLA Modules:
  0.0 106.1 jit_solution(18154910638785709334)
XLA Ops:
  0.6 0.1 pad_add_fusion.refs_1_.refs_2_.where
  0.7 0.7 copy-done.6
  1.4 2.9 %pick.1 = (bf16[8,128,256]{2,1,0:T(8,128)(2,1)}, s32[128]{0:T(128)S(1)}) custom-call(s32[64]{0:T(128)S(1)} %copy-done.6, s32[4]{0:T(128)S(1)} %pad_add_fusion.refs_1_.refs_2_.where, bf16[16,128,256]{2,1,0:T(8,128)(2,1)} %bitcast.18), custom_call_target="tpu_custom_call" | custom-call | tf_op jit(solution)/shard_map/pick/pallas_call | solution.py:471
  4.3 6.3 %all-to-all-start = ((bf16[4,256,256]{2,1,0:T(8,128)(2,1)}), bf16[4,256,256]{2,1,0:T(8,128)(2,1)S(1)}, u32[]{:S(2)}, u32[]{:S(2)}) async-start(bf16[4,256,256]{2,1,0:T(8,128)(2,1)} %bitcast.6), calls=%async_computation | async-start | bytes 1048576 | tf_op jit(solution)/shard_map/all_to_all | solution.py:503
  10.6 0.6 copy-done.7
  11.3 2.2 %deal.1 = (bf16[8,128,256]{2,1,0:T(8,128)(2,1)}, bf16[8,128,256]{2,1,0:T(8,128)(2,1)S(1)}, s32[128]{0:T(128)S(1)}) custom-call(s32[64]{0:T(128)S(1)} %copy-done.6, s32[64]{0:T(128)S(1)} %copy-done.7, s32[4]{0:T(128)S(1)} %pad_add_fusion.refs_1_.refs_2_.where, s32[128]{0:T(128)S(1)} %get-tuple-element.35.refs_3_.refs_1_, bf16[16,128,256]{2,1,0:T(8,128)(2,1)S(1)} %bitcast.21), custom_call_target="tpu_custom_call" | custom-call | tf_op jit(solution)/shard_map/deal/pallas_call | solution.py:483
  13.5 0.0 copy-start.11
  13.5 3.6 %collective-permute-start = (bf16[8,128,256]{2,1,0:T(8,128)(2,1)S(1)}, bf16[8,128,256]{2,1,0:T(8,128)(2,1)S(1)}, u32[]{:S(2)}, u32[]{:S(2)}) collective-permute-start(bf16[8,128,256]{2,1,0:T(8,128)(2,1)S(1)} %get-tuple-element.38), channel_id=1, source_target_pairs={{0,2},{1,3},{4,6},{5,7},{8,10},{9,11},{12,14},{13,15},{16,18},{17,... | collective-permute-start | bytes 1572872 | tf_op jit(solution)/shard_map/ppermute | solution.py:508
  17.1 0.1 copy.15
  17.2 0.0 copy-start.12
  17.2 0.1 copy.13
  17.3 0.7 copy-done.12
  18.0 0.1 copy.14
  18.1 0.7 copy-done.13
  18.9 0.1 collective-permute-start.1
  19.0 6.1 %all-to-all-done = bf16[4,256,256]{2,1,0:T(8,128)(2,1)S(1)} async-done(((bf16[4,256,256]{2,1,0:T(8,128)(2,1)}), bf16[4,256,256]{2,1,0:T(8,128)(2,1)S(1)}, u32[]{:S(2)}, u32[]{:S(2)}) %all-to-all-start) | async-done | bytes 524320 | tf_op jit(solution)/shard_map/all_to_all | solution.py:503
  25.1 3.5 %all-to-all-start.1 = ((bf16[4,256,256]{2,1,0:T(8,128)(2,1)}), bf16[4,256,256]{2,1,0:T(8,128)(2,1)S(1)}, u32[]{:S(2)}, u32[]{:S(2)}) async-start(bf16[4,256,256]{2,1,0:T(8,128)(2,1)} %bitcast.11), calls=%async_computation.1 | async-start | bytes 1048576 | tf_op jit(solution)/shard_map/all_to_all | solution.py:503
  28.6 0.0 collective-permute-done.refs_4_
  28.6 0.0 copy-start.14
  28.6 0.7 copy-done.16
  29.3 0.2 copy-done.14
  29.5 12.3 %attention_0.1 = (f32[4,128,256]{2,1,0:T(8,128)}, bf16[4,128,256]{2,1,0:T(8,128)(2,1)}, bf16[8,128,256]{2,1,0:T(8,128)(2,1)}, f32[512,256]{1,0:T(8,128)}, f32[512,256]{1,0:T(8,128)}) custom-call(s32[128]{0:T(128)S(1)} %get-tuple-element.36.refs_0_, bf16[16,128,256]{2,1,0:T(8,128)(2,1)} %bitcast.19, bf16[16,128,256]{2,1,0:T(8,128)(2,1)} %bitcast.31, ...), custom_call_target="tpu_custom_call" | custom-call | flops 6375342080 | bytes 5242880 | tf_op jit(solution)/shard_map/attention_0/pallas_call | solution.py:363
  41.8 0.7 all-to-all-done.1
  42.6 4.5 %all-to-all-start.2 = ((bf16[4,256,256]{2,1,0:T(8,128)(2,1)}), bf16[4,256,256]{2,1,0:T(8,128)(2,1)S(1)}, u32[]{:S(2)}, u32[]{:S(2)}) async-start(bf16[4,256,256]{2,1,0:T(8,128)(2,1)} %bitcast.27), calls=%async_computation.2 | async-start | bytes 1048576 | tf_op jit(solution)/shard_map/all_to_all | solution.py:503
  47.0 1.3 %collective-permute-start.2 = (bf16[4,128,256]{2,1,0:T(8,128)(2,1)S(1)}, bf16[4,128,256]{2,1,0:T(8,128)(2,1)S(1)}, u32[]{:S(2)}, u32[]{:S(2)}) collective-permute-start(bf16[4,128,256]{2,1,0:T(8,128)(2,1)S(1)} %copy-done.17), channel_id=1, source_target_pairs={{2,0},{3,1},{6,4},{7,5},{10,8},{11,9},{14,12},{15,13},{18,16},{19,... | collective-permute-start | bytes 786440 | tf_op jit(solution)/shard_map/ppermute | solution.py:515
  48.3 12.7 %attention_1.1 = (f32[4,128,256]{2,1,0:T(8,128)}, bf16[4,128,256]{2,1,0:T(8,128)(2,1)}, bf16[8,128,256]{2,1,0:T(8,128)(2,1)}, f32[512,256]{1,0:T(8,128)}, f32[512,256]{1,0:T(8,128)}) custom-call(s32[128]{0:T(128)S(1)} %get-tuple-element.36.refs_0_, bf16[16,128,256]{2,1,0:T(8,128)(2,1)} %bitcast.20, bf16[16,128,256]{2,1,0:T(8,128)(2,1)} %bitcast.32, ...), custom_call_target="tpu_custom_call" | custom-call | flops 6375342080 | bytes 5242880 | tf_op jit(solution)/shard_map/attention_1/pallas_call | solution.py:363
  61.1 0.0 all-to-all-done.2
  61.1 0.1 collective-permute-start.4
  61.2 2.1 %collective-permute-done.4 = f32[512,256]{1,0:T(8,128)S(1)} collective-permute-done((f32[512,256]{1,0:T(8,128)}, f32[512,256]{1,0:T(8,128)S(1)}, u32[]{:S(2)}, u32[]{:S(2)}) %collective-permute-start.4) | collective-permute-done | bytes 524320 | tf_op jit(solution)/shard_map/ppermute | solution.py:402
  63.3 1.1 %add.13 = bf16[512,256]{1,0:T(8,128)(2,1)S(1)} add(f32[512,256]{1,0:T(8,128)} %get-tuple-element.52, f32[512,256]{1,0:T(8,128)S(1)} %collective-permute-done.4) | non-fusion elementwise | flops 131072 | bytes 1310720 | tf_op jit(solution)/shard_map/add | solution.py:537
  64.4 2.7 %collective-permute-start.5 = (bf16[256,256]{1,0:T(8,128)(2,1)S(1)}, bf16[256,256]{1,0:T(8,128)(2,1)S(1)}, u32[]{:S(2)}, u32[]{:S(2)}) collective-permute-start(bf16[256,256]{1,0:T(8,128)(2,1)S(1)} %select_convert_fusion.1), channel_id=1, source_target_pairs={{0,2},{2,0},{1,3},{3,1},{4,6},{6,4},{5,7},{7,5},{8,10},{10,8},{9,1... | collective-permute-start | bytes 393224 | tf_op jit(solution)/shard_map/ppermute | solution.py:402
  67.2 3.8 %collective-permute-done.5 = bf16[256,256]{1,0:T(8,128)(2,1)S(1)} collective-permute-done((bf16[256,256]{1,0:T(8,128)(2,1)S(1)}, bf16[256,256]{1,0:T(8,128)(2,1)S(1)}, u32[]{:S(2)}, u32[]{:S(2)}) %collective-permute-start.5) | collective-permute-done | bytes 131104 | tf_op jit(solution)/shard_map/ppermute | solution.py:402
  71.0 0.1 add_convert_fusion.2
  71.0 2.1 %collective-permute-start.6 = (bf16[256,256]{1,0:T(8,128)(2,1)S(1)}, bf16[256,256]{1,0:T(8,128)(2,1)S(1)}, u32[]{:S(2)}, u32[]{:S(2)}) collective-permute-start(bf16[256,256]{1,0:T(8,128)(2,1)S(1)} %add_convert_fusion.2), channel_id=1, source_target_pairs={{0,4},{4,0},{8,12},{12,8},{1,5},{5,1},{9,13},{13,9},{2,6},{6,2},{1... | collective-permute-start | bytes 393224 | tf_op jit(solution)/shard_map/ppermute | solution.py:402
  73.1 3.8 %all-to-all-start.3 = ((bf16[4,256,256]{2,1,0:T(8,128)(2,1)}), bf16[4,256,256]{2,1,0:T(8,128)(2,1)S(1)}, u32[]{:S(2)}, u32[]{:S(2)}) async-start(bf16[4,256,256]{2,1,0:T(8,128)(2,1)} %bitcast.15), calls=%async_computation.3 | async-start | bytes 1048576 | tf_op jit(solution)/shard_map/all_to_all | solution.py:503
  76.9 0.0 collective-permute-done.6
  76.9 3.0 %collective-permute-start.7 = (bf16[256,256]{1,0:T(8,128)(2,1)S(1)}, bf16[256,256]{1,0:T(8,128)(2,1)S(1)}, u32[]{:S(2)}, u32[]{:S(2)}) collective-permute-start(bf16[256,256]{1,0:T(8,128)(2,1)S(1)} %add_convert_fusion.1), channel_id=1, source_target_pairs={{0,8},{4,12},{8,0},{12,4},{1,9},{5,13},{9,1},{13,5},{2,10},{6,14},... | collective-permute-start | bytes 393224 | tf_op jit(solution)/shard_map/ppermute | solution.py:402
  79.9 1.3 %collective-permute-start.3 = (bf16[4,128,256]{2,1,0:T(8,128)(2,1)S(1)}, bf16[4,128,256]{2,1,0:T(8,128)(2,1)S(1)}, u32[]{:S(2)}, u32[]{:S(2)}) collective-permute-start(bf16[4,128,256]{2,1,0:T(8,128)(2,1)S(1)} %copy-done.15), channel_id=1, source_target_pairs={{2,0},{3,1},{6,4},{7,5},{10,8},{11,9},{14,12},{15,13},{18,16},{19,... | collective-permute-start | bytes 786440 | tf_op jit(solution)/shard_map/ppermute | solution.py:523
  81.2 15.4 %collective-permute-done.7 = bf16[256,256]{1,0:T(8,128)(2,1)S(1)} collective-permute-done((bf16[256,256]{1,0:T(8,128)(2,1)S(1)}, bf16[256,256]{1,0:T(8,128)(2,1)S(1)}, u32[]{:S(2)}, u32[]{:S(2)}) %collective-permute-start.7) | collective-permute-done | bytes 131104 | tf_op jit(solution)/shard_map/ppermute | solution.py:402
  96.6 1.5 %collective-permute-start.8 = (bf16[256,256]{1,0:T(8,128)(2,1)S(1)}, bf16[256,256]{1,0:T(8,128)(2,1)}, u32[]{:S(2)}, u32[]{:S(2)}) collective-permute-start(bf16[256,256]{1,0:T(8,128)(2,1)S(1)} %add_convert_fusion.part), channel_id=1, source_target_pairs={{0,2},{2,0},{1,3},{3,1},{4,6},{6,4},{5,7},{7,5},{8,10},{10,8},{9,1... | collective-permute-start | bytes 393224 | tf_op jit(solution)/shard_map/ppermute | solution.py:402
  98.1 0.0 collective-permute-done.3.refs_5_
  98.1 0.7 copy-done.3
  98.8 0.0 copy-start.4
  98.8 0.9 copy-done.4
  99.8 2.5 %fold.1 = (f32[16,128,128]{2,1,0:T(8,128)S(1)}, f32[16,128,128]{2,1,0:T(8,128)}) custom-call(s32[128]{0:T(128)S(1)} %get-tuple-element.36.refs_0_, s32[128]{0:T(128)S(1)} %get-tuple-element.35.refs_3_.refs_1_, f32[4,128,256]{2,1,0:T(8,128)S(1)} %copy-done.1, f32[4,128,256]{2,1,0:T(8,128)S(1)} %copy-done.2, ...), custom_call_target="tpu_custom_call" | custom-call | tf_op jit(solution)/shard_map/fold/pallas_call | solution.py:527
  102.3 1.8 %split.1 = (f32[256,128]{1,0:T(8,128)}, f32[256,128]{1,0:T(8,128)}, f32[256,128]{1,0:T(8,128)}, f32[128,256]{1,0:T(8,128)}) custom-call(s32[4]{0:T(128)} %copy-done.5, bf16[256,256]{1,0:T(8,128)(2,1)} %copy-done.8, bf16[256,256]{1,0:T(8,128)(2,1)} %collective-permute-done.8.other), custom_call_target="tpu_custom_call" | custom-call | tf_op jit(solution)/shard_map/split/pallas_call | solution.py:548
  104.2 1.0 collective-permute-done.9.got
  105.2 0.9 add.26
  (33 shorter events, 0.2 us)
Async XLA Ops:
  0.7 9.9 %copy-start.5 = (s32[4]{0:T(128)}, s32[4]{0:T(128)S(1)}, u32[]{:S(2)}) copy-start(s32[4]{0:T(128)S(1)} %pad_add_fusion.refs_1_.refs_2_.where) | copy-start | bytes 52
  0.7 0.7 copy-start.6
  1.4 9.2 %copy-start = (bf16[1,2048,256]{2,1,0:T(8,128)(2,1)S(1)}, bf16[1,2048,256]{2,1,0:T(8,128)(2,1)}, u32[]{:S(2)}) copy-start(bf16[1,2048,256]{2,1,0:T(8,128)(2,1)} %param.8) | copy-start | bytes 3145732
  4.3 20.8 %all-to-all-start = ((bf16[4,256,256]{2,1,0:T(8,128)(2,1)}), bf16[4,256,256]{2,1,0:T(8,128)(2,1)S(1)}, u32[]{:S(2)}, u32[]{:S(2)}) async-start(bf16[4,256,256]{2,1,0:T(8,128)(2,1)} %bitcast.6), calls=%async_computation | async-start | bytes 1048576 | tf_op jit(solution)/shard_map/all_to_all | solution.py:503
  10.6 0.7 copy-start.7
  11.3 5.8 %copy-start.10 = (bf16[256,128]{1,0:T(8,128)(2,1)S(1)}, bf16[256,128]{1,0:T(8,128)(2,1)}, u32[]{:S(2)}) copy-start(bf16[256,128]{1,0:T(8,128)(2,1)} %param.10) | copy-start | bytes 196612
  13.5 3.7 %copy-start.11 = (bf16[256,128]{1,0:T(8,128)(2,1)S(1)}, bf16[256,128]{1,0:T(8,128)(2,1)}, u32[]{:S(2)}) copy-start(bf16[256,128]{1,0:T(8,128)(2,1)} %param.11) | copy-start | bytes 196612
  13.5 15.1 %collective-permute-start = (bf16[8,128,256]{2,1,0:T(8,128)(2,1)S(1)}, bf16[8,128,256]{2,1,0:T(8,128)(2,1)S(1)}, u32[]{:S(2)}, u32[]{:S(2)}) collective-permute-start(bf16[8,128,256]{2,1,0:T(8,128)(2,1)S(1)} %get-tuple-element.38), channel_id=1, source_target_pairs={{0,2},{1,3},{4,6},{5,7},{8,10},{9,11},{12,14},{13,15},{16,18},{17,... | collective-permute-start | bytes 1572872 | tf_op jit(solution)/shard_map/ppermute | solution.py:508
  17.2 0.8 copy-start.12
  18.0 0.8 copy-start.13
  18.9 6.2 %copy-start.9 = (bf16[512,256]{1,0:T(8,128)(2,1)}, bf16[512,256]{1,0:T(8,128)(2,1)S(1)}, u32[]{:S(2)}) copy-start(bf16[512,256]{1,0:T(8,128)(2,1)S(1)} %pad_maximum_fusion.refs_5_) | copy-start | bytes 786436
  18.9 9.7 %collective-permute-start.1 = (bf16[512,256]{1,0:T(8,128)(2,1)S(1)}, bf16[512,256]{1,0:T(8,128)(2,1)S(1)}, u32[]{:S(2)}, u32[]{:S(2)}) collective-permute-start(bf16[512,256]{1,0:T(8,128)(2,1)S(1)} %pad_maximum_fusion.refs_5_), channel_id=1, source_target_pairs={{0,1},{1,0},{2,3},{3,2},{4,5},{5,4},{6,7},{7,6},{8,9},{9,8},{10,11... | collective-permute-start | bytes 786440 | tf_op jit(solution)/shard_map/ppermute | solution.py:402
  25.1 17.4 %all-to-all-start.1 = ((bf16[4,256,256]{2,1,0:T(8,128)(2,1)}), bf16[4,256,256]{2,1,0:T(8,128)(2,1)S(1)}, u32[]{:S(2)}, u32[]{:S(2)}) async-start(bf16[4,256,256]{2,1,0:T(8,128)(2,1)} %bitcast.11), calls=%async_computation.1 | async-start | bytes 1048576 | tf_op jit(solution)/shard_map/all_to_all | solution.py:503
  28.6 0.7 copy-start.16
  28.6 0.9 copy-start.14
  42.5 4.5 %copy-start.17 = (bf16[4,128,256]{2,1,0:T(8,128)(2,1)S(1)}, bf16[4,128,256]{2,1,0:T(8,128)(2,1)}, u32[]{:S(2)}) copy-start(bf16[4,128,256]{2,1,0:T(8,128)(2,1)} %get-tuple-element.45) | copy-start | bytes 786436
  42.6 18.5 %all-to-all-start.2 = ((bf16[4,256,256]{2,1,0:T(8,128)(2,1)}), bf16[4,256,256]{2,1,0:T(8,128)(2,1)S(1)}, u32[]{:S(2)}, u32[]{:S(2)}) async-start(bf16[4,256,256]{2,1,0:T(8,128)(2,1)} %bitcast.27), calls=%async_computation.2 | async-start | bytes 1048576 | tf_op jit(solution)/shard_map/all_to_all | solution.py:503
  47.0 14.0 %collective-permute-start.2 = (bf16[4,128,256]{2,1,0:T(8,128)(2,1)S(1)}, bf16[4,128,256]{2,1,0:T(8,128)(2,1)S(1)}, u32[]{:S(2)}, u32[]{:S(2)}) collective-permute-start(bf16[4,128,256]{2,1,0:T(8,128)(2,1)S(1)} %copy-done.17), channel_id=1, source_target_pairs={{2,0},{3,1},{6,4},{7,5},{10,8},{11,9},{14,12},{15,13},{18,16},{19,... | collective-permute-start | bytes 786440 | tf_op jit(solution)/shard_map/ppermute | solution.py:515
  61.1 2.2 %collective-permute-start.4 = (f32[512,256]{1,0:T(8,128)}, f32[512,256]{1,0:T(8,128)S(1)}, u32[]{:S(2)}, u32[]{:S(2)}) collective-permute-start(f32[512,256]{1,0:T(8,128)} %get-tuple-element.53), channel_id=1, source_target_pairs={{0,1},{1,0},{2,3},{3,2},{4,5},{5,4},{6,7},{7,6},{8,9},{9,8},{10,11... | collective-permute-start | bytes 1572872 | tf_op jit(solution)/shard_map/ppermute | solution.py:402
  64.4 6.5 %collective-permute-start.5 = (bf16[256,256]{1,0:T(8,128)(2,1)S(1)}, bf16[256,256]{1,0:T(8,128)(2,1)S(1)}, u32[]{:S(2)}, u32[]{:S(2)}) collective-permute-start(bf16[256,256]{1,0:T(8,128)(2,1)S(1)} %select_convert_fusion.1), channel_id=1, source_target_pairs={{0,2},{2,0},{1,3},{3,1},{4,6},{6,4},{5,7},{7,5},{8,10},{10,8},{9,1... | collective-permute-start | bytes 393224 | tf_op jit(solution)/shard_map/ppermute | solution.py:402
  71.0 5.8 %collective-permute-start.6 = (bf16[256,256]{1,0:T(8,128)(2,1)S(1)}, bf16[256,256]{1,0:T(8,128)(2,1)S(1)}, u32[]{:S(2)}, u32[]{:S(2)}) collective-permute-start(bf16[256,256]{1,0:T(8,128)(2,1)S(1)} %add_convert_fusion.2), channel_id=1, source_target_pairs={{0,4},{4,0},{8,12},{12,8},{1,5},{5,1},{9,13},{13,9},{2,6},{6,2},{1... | collective-permute-start | bytes 393224 | tf_op jit(solution)/shard_map/ppermute | solution.py:402
  73.1 6.8 %copy-start.15 = (bf16[4,128,256]{2,1,0:T(8,128)(2,1)S(1)}, bf16[4,128,256]{2,1,0:T(8,128)(2,1)}, u32[]{:S(2)}) copy-start(bf16[4,128,256]{2,1,0:T(8,128)(2,1)} %get-tuple-element.50) | copy-start | bytes 786436
  73.1 25.7 %copy-start.2 = (f32[4,128,256]{2,1,0:T(8,128)S(1)}, f32[4,128,256]{2,1,0:T(8,128)}, u32[]{:S(2)}) copy-start(f32[4,128,256]{2,1,0:T(8,128)} %get-tuple-element.43.refs_3_) | copy-start | bytes 1572868
  73.1 25.7 %all-to-all-start.3 = ((bf16[4,256,256]{2,1,0:T(8,128)(2,1)}), bf16[4,256,256]{2,1,0:T(8,128)(2,1)S(1)}, u32[]{:S(2)}, u32[]{:S(2)}) async-start(bf16[4,256,256]{2,1,0:T(8,128)(2,1)} %bitcast.15), calls=%async_computation.3 | async-start | bytes 1048576 | tf_op jit(solution)/shard_map/all_to_all | solution.py:503
  76.9 22.0 %copy-start.1 = (f32[4,128,256]{2,1,0:T(8,128)S(1)}, f32[4,128,256]{2,1,0:T(8,128)}, u32[]{:S(2)}) copy-start(f32[4,128,256]{2,1,0:T(8,128)} %get-tuple-element.39.refs_2_) | copy-start | bytes 1572868
  76.9 19.7 %collective-permute-start.7 = (bf16[256,256]{1,0:T(8,128)(2,1)S(1)}, bf16[256,256]{1,0:T(8,128)(2,1)S(1)}, u32[]{:S(2)}, u32[]{:S(2)}) collective-permute-start(bf16[256,256]{1,0:T(8,128)(2,1)S(1)} %add_convert_fusion.1), channel_id=1, source_target_pairs={{0,8},{4,12},{8,0},{12,4},{1,9},{5,13},{9,1},{13,5},{2,10},{6,14},... | collective-permute-start | bytes 393224 | tf_op jit(solution)/shard_map/ppermute | solution.py:402
  79.9 18.2 %collective-permute-start.3 = (bf16[4,128,256]{2,1,0:T(8,128)(2,1)S(1)}, bf16[4,128,256]{2,1,0:T(8,128)(2,1)S(1)}, u32[]{:S(2)}, u32[]{:S(2)}) collective-permute-start(bf16[4,128,256]{2,1,0:T(8,128)(2,1)S(1)} %copy-done.15), channel_id=1, source_target_pairs={{2,0},{3,1},{6,4},{7,5},{10,8},{11,9},{14,12},{15,13},{18,16},{19,... | collective-permute-start | bytes 786440 | tf_op jit(solution)/shard_map/ppermute | solution.py:523
  96.6 5.7 %copy-start.8 = (bf16[256,256]{1,0:T(8,128)(2,1)}, bf16[256,256]{1,0:T(8,128)(2,1)S(1)}, u32[]{:S(2)}) copy-start(bf16[256,256]{1,0:T(8,128)(2,1)S(1)} %add_convert_fusion.part) | copy-start | bytes 393220
  96.6 5.7 %collective-permute-start.8 = (bf16[256,256]{1,0:T(8,128)(2,1)S(1)}, bf16[256,256]{1,0:T(8,128)(2,1)}, u32[]{:S(2)}, u32[]{:S(2)}) collective-permute-start(bf16[256,256]{1,0:T(8,128)(2,1)S(1)} %add_convert_fusion.part), channel_id=1, source_target_pairs={{0,2},{2,0},{1,3},{3,1},{4,6},{6,4},{5,7},{7,5},{8,10},{10,8},{9,1... | collective-permute-start | bytes 393224 | tf_op jit(solution)/shard_map/ppermute | solution.py:402
  98.1 0.7 copy-start.3
  98.8 1.0 copy-start.4
  102.3 2.9 %collective-permute-start.9 = (f32[16,128,128]{2,1,0:T(8,128)}, f32[16,128,128]{2,1,0:T(8,128)S(1)}, u32[]{:S(2)}, u32[]{:S(2)}) collective-permute-start(f32[16,128,128]{2,1,0:T(8,128)} %get-tuple-element.59), channel_id=1, source_target_pairs={{0,1},{1,0},{2,3},{3,2},{4,5},{5,4},{6,7},{7,6},{8,9},{9,8},{10,11... | collective-permute-start | bytes 3145736 | tf_op jit(solution)/shard_map/ppermute | solution.py:402

commit v9 on v7

--- a/solution.py
+++ b/solution.py
@@ -34,69 +34,58 @@
         self.core = self.item_of + blocks_dev
         self.later_day = self.core + 1
         self.size = -(-(self.core + 2) // 128) * 128
+        self.spare = blocks_dev
         self.home_of = 0
-        self.chunk_of = blocks_dev
-        self.asker_of = 2 * blocks_dev
-        self.picks = 3 * blocks_dev
-        self.homes_size = -(-(self.picks + CHUNKS * self.places) // 128) * 128
-
-
-def pick_kernel(lay, partner, where, inputs, sent, homes, held, sem):
+        self.chunk_of = blocks_dev + 1
+        self.asker_of = 2 * (blocks_dev + 1)
+        self.picks = 3 * (blocks_dev + 1)
+        self.spare_pick = self.picks + CHUNKS * self.places
+        self.homes_size = -(-(self.spare_pick + 1) // 128) * 128
+
+
+def pick_kernel(lay, partner_hbm, inputs, sent, homes, partner, held, sems):
     bd, slots = lay.blocks, lay.slots
-    reach_pos, core = where[0], where[1]
-    copy = pltpu.make_async_copy(inputs, held, sem)
+    reach_pos, core = lax.axis_index("reach"), lax.axis_index("head")
+    table_copy = pltpu.make_async_copy(partner_hbm, partner, sems.at[0])
+    table_copy.start()
+    copy = pltpu.make_async_copy(inputs, held, sems.at[1])
     copy.start()
-
-    def clear_picks(index, carry):
-        homes[lay.picks + index] = 0
-        return carry
-
-    lax.fori_loop(0, CHUNKS * lay.places, clear_picks, 0, unroll=True)
+    for place in range(CHUNKS * lay.places):
+        homes[lay.picks + place] = 0
+    table_copy.wait()
 
     def one_reach(peer, carry):
-        def before(index, total):
-            source = lax.div(partner[peer * bd + index], bd)
-            return total + jnp.where(source < reach_pos, 1, 0)
-
-        base = lax.fori_loop(0, bd, before, jnp.int32(0), unroll=True)
-
-        def serve(index, rank):
-            wanted = partner[peer * bd + index]
-            hit = lax.div(wanted, bd) == reach_pos
-
-            @pl.when(hit)
-            def _():
-                place = base + rank
-                owner = lax.rem(place, CORES)
-                chunk = lax.rem(lax.div(place, CORES), CHUNKS)
-                slot = peer * slots + jnp.minimum(lax.div(rank, WORKERS), slots - 1)
-                local = lax.rem(wanted, bd)
-                homes[lay.home_of + local] = slot
-                homes[lay.chunk_of + local] = chunk
-                homes[lay.asker_of + local] = owner
-
-                @pl.when(owner == core)
-                def _():
-                    homes[lay.picks + chunk * lay.places + slot] = local
-
-            return rank + jnp.where(hit, 1, 0)
-
-        lax.fori_loop(0, bd, serve, jnp.int32(0))
+        base = jnp.int32(0)
+        wanted = []
+        for index in range(bd):
+            block = partner[peer * bd + index]
+            source = lax.div(block, bd)
+            base = base + jnp.where(source < reach_pos, 1, 0)
+            wanted.append((source == reach_pos, lax.rem(block, bd)))
+        rank = jnp.int32(0)
+        for hit, local in wanted:
+            place = base + rank
+            owner = lax.rem(place, CORES)
+            chunk = lax.rem(lax.div(place, CORES), CHUNKS)
+            slot = peer * slots + jnp.minimum(lax.div(rank, WORKERS), slots - 1)
+            target = jnp.where(hit, local, lay.spare)
+            homes[lay.home_of + target] = slot
+            homes[lay.chunk_of + target] = chunk
+            homes[lay.asker_of + target] = owner
+            pick = lay.picks + chunk * lay.places + slot
+            homes[jnp.where(hit & (owner == core), pick, lay.spare_pick)] = local
+            rank = rank + jnp.where(hit, 1, 0)
         return carry
 
     lax.fori_loop(0, lay.reach, one_reach, 0)
     copy.wait()
-
-    def pick(place, carry):
+    for place in range(lay.places):
         sent[place] = held[homes[lay.picks + place]]
-        return carry
-
-    lax.fori_loop(0, lay.places, pick, 0)
-
-
-def deal_kernel(lay, partner, counts, where, homes, inputs, sent, prior, tab, start, used):
+
+
+def deal_kernel(lay, partner, counts, homes, inputs, sent, prior, tab, start, used):
     bd, slots = lay.blocks, lay.slots
-    reach_pos, core = where[0], where[1]
+    reach_pos, core = lax.axis_index("reach"), lax.axis_index("head")
 
     def clear(index, carry):
         used[index] = 0
@@ -143,7 +132,7 @@
 
     lax.fori_loop(0, bd, assign, 0)
     tab[lay.core] = core
-    tab[lay.later_day] = where[2]
+    tab[lay.later_day] = jnp.where(lax.axis_index("day") > 0, 1, 0)
 
     def pick(place, carry):
         sent[place] = inputs[homes[lay.picks + lay.places + place]]
@@ -427,8 +416,8 @@
     return part, exchanged(part, "day", 1), folded
 
 
-def split_kernel(where, part, other, query_out, key_out, value_out, output_out):
-    first = lax.rem(where[3], 2) == 0
+def split_kernel(part, other, query_out, key_out, value_out, output_out):
+    first = lax.rem(lax.axis_index("day"), 2) == 0
     mine, theirs = part[...].astype(F32), other[...].astype(F32)
     upper = jnp.where(first, mine, theirs)
     lower = jnp.where(first, theirs, mine)
@@ -451,14 +440,6 @@
     half = width // 2
     in_blocks = inputs.reshape(blocks_dev, BLOCK, width)
     up_blocks = upstream.reshape(blocks_dev, BLOCK, width)
-    where = jnp.stack(
-        [
-            lax.axis_index("reach"),
-            lax.axis_index("head"),
-            (lax.axis_index("day") > 0).astype(jnp.int32),
-            lax.axis_index("day"),
-        ]
-    )
     pack = jnp.concatenate([key_weight.T, value_weight.T, query_weight.T, output_weight], axis=0)
     pack_other = exchanged(pack, "head", 1)
 
@@ -469,15 +450,19 @@
     sent_a, homes = pl.pallas_call(
         lambda *refs: pick_kernel(lay, *refs),
         out_shape=(sent_shape, jax.ShapeDtypeStruct((lay.homes_size,), jnp.int32)),
-        in_specs=[smem, smem, anywhere],
+        in_specs=[anywhere, anywhere],
         out_specs=(in_vmem, smem),
         scratch_shapes=[
+            pltpu.SMEM(partner.shape, jnp.int32),
             pltpu.VMEM((blocks_dev, BLOCK, width), BF16),
-            pltpu.SemaphoreType.DMA,
+            pltpu.SemaphoreType.DMA((2,)),
         ],
         compiler_params=pltpu.CompilerParams(vmem_limit_bytes=16 << 20),
         name="pick",
-    )(partner, where, pltpu.with_memory_space_constraint(in_blocks, pltpu.HBM))
+    )(
+        pltpu.with_memory_space_constraint(partner, pltpu.HBM),
+        pltpu.with_memory_space_constraint(in_blocks, pltpu.HBM),
+    )
     sent_b, prior, tab = pl.pallas_call(
         lambda *refs: deal_kernel(lay, *refs),
         out_shape=(
@@ -485,7 +470,7 @@
             jax.ShapeDtypeStruct((lay.items, BLOCK, width), BF16),
             jax.ShapeDtypeStruct((lay.size,), jnp.int32),
         ),
-        in_specs=[smem, smem, smem, smem, in_vmem],
+        in_specs=[smem, smem, smem, in_vmem],
         out_specs=(in_vmem, in_vmem, smem),
         scratch_shapes=[
             pltpu.SMEM((lay.reach,), jnp.int32),
@@ -493,7 +478,7 @@
         ],
         compiler_params=pltpu.CompilerParams(vmem_limit_bytes=16 << 20),
         name="deal",
-    )(partner, counts, where, homes, in_blocks)
+    )(partner, counts, homes, in_blocks)
 
     def ring(value):
         shape = value.shape
@@ -514,8 +499,8 @@
     own_b, day_b, home_b, grad_mine, grad_other = attend(
         lay, 1, tab, in_blocks, up_blocks, received_b, *shared, grads
     )
-    home_a, day_a, home_b, day_b, grad_other = lax.optimization_barrier(
-        (home_a, day_a, home_b, day_b, grad_other)
+    home_a, home_b, day_b, grad_other = lax.optimization_barrier(
+        (home_a, home_b, day_b, grad_other)
     )
     grad_swapped = exchanged(grad_other, "head", 1)
     home_b = ring(home_b)
@@ -542,6 +527,7 @@
         compiler_params=pltpu.CompilerParams(vmem_limit_bytes=16 << 20),
         name="add",
     )(keep, got)
+    back_blocks, other = lax.optimization_barrier((back_blocks, other))
     weight_grads = pl.pallas_call(
         split_kernel,
         out_shape=(
@@ -550,10 +536,9 @@
             jax.ShapeDtypeStruct((width, half), F32),
             jax.ShapeDtypeStruct((half, width), F32),
         ),
-        in_specs=[smem] + [in_vmem] * 2,
-        out_specs=[in_vmem] * 4,
+        grid=(1,),
         name="split",
-    )(where, part, other)
+    )(part, other)
 
     return (back_blocks.reshape(1, rows_dev, half), *weight_grads)
 

time: 100 us -> 96.8 us (0.968)
  waiting for transfers between devices: 21.9 us -> 26.2 us
  starting transfers between devices: 34.8 us -> 30.8 us
  local copies, waits for them, and re-layouts: 6.28 us -> 3.99 us
  Pallas kernels: 35.4 us -> 34.1 us
    ppermute x7, starting transfers between devices: 9.11 us -> 5.87 us  [exchanged(): lax.ppermute(value, axis, [(place, place ^ bit) for place in range(count)])]
    ppermute x1, waiting for transfers between devices: 0.97 us -> 3.35 us  [on_device(): day_b = lax.ppermute(day_b, 'day', last_day)]
    unnamed x43 -> x37, local copies, waits for them, and re-layouts: 6.28 us -> 3.99 us
    ppermute x1, waiting for transfers between devices: 0.01 us -> 2.01 us  [on_device(): day_a = lax.ppermute(day_a, 'day', last_day)]
    ppermute x7, waiting for transfers between devices: 11.9 us -> 10.6 us  [exchanged(): lax.ppermute(value, axis, [(place, place ^ bit) for place in range(count)])]
    all_to_all x4, waiting for transfers between devices: 9.03 us -> 10.2 us  [ring(): return lax.all_to_all(value, 'reach', 0, 0, tiled=True).reshape(shape)]
  transfers between devices with their start and end apart: 14 -> 14, of which waited for: 8 -> 10; matrix products, arithmetic and copies ran while one was open for 1% -> 1% of each run, Pallas kernels for 32% -> 31%
where the time goes in v9:
time: 96.8 us; the launch traced here: 96.2 us
  Pallas kernels  34.1 us (35%)
  starting transfers between devices  30.8 us (32%)
  waiting for transfers between devices  26.2 us (27%)
  local copies, waits for them, and re-layouts  3.99 us (4%)
    pallas_call x2, Pallas kernels, attend(): pl.pallas_call(lambda *refs: attention_kernel(lay, chunk, *refs), grid_sp...  25.1 us
    all_to_all x4, starting transfers between devices, ring(): return lax.all_to_all(value, 'reach', 0, 0, tiled=True).reshape(shape)  18.8 us
    ppermute x7, waiting for transfers between devices, exchanged(): lax.ppermute(value, axis, [(place, place ^ bit) for place in range(count)])  10.6 us
    all_to_all x4, waiting for transfers between devices, ring(): return lax.all_to_all(value, 'reach', 0, 0, tiled=True).reshape(shape)  10.2 us
    ppermute x7, starting transfers between devices, exchanged(): lax.ppermute(value, axis, [(place, place ^ bit) for place in range(count)])  5.87 us
    unnamed x37, local copies, waits for them, and re-layouts  3.99 us
    ppermute x1, starting transfers between devices, on_device(): prior_inputs = lax.ppermute(prior, 'day', next_day)  3.56 us
    ppermute x1, waiting for transfers between devices, on_device(): day_b = lax.ppermute(day_b, 'day', last_day)  3.35 us
  transfers between devices with their start and end apart: 14, of which 10 were waited for; matrix products, arithmetic and copies ran while one was open for 1% of the time, Pallas kernels for 31%

profile of v9, /device:TPU:0, one launch (start us, length us, event | category | flops | bytes accessed | tf_op | source)
XLA Modules:
  0.0 96.2 jit_solution(10228340776496674154)
XLA Ops:
  0.6 0.0 copy-start
  0.6 2.6 %pick.1 = (bf16[8,128,256]{2,1,0:T(8,128)(2,1)}, s32[128]{0:T(128)S(1)}) custom-call(s32[64]{0:T(128)} %refs_0_.3, bf16[16,128,256]{2,1,0:T(8,128)(2,1)} %bitcast.14), custom_call_target="tpu_custom_call" | custom-call | tf_op jit(solution)/shard_map/pick/pallas_call | solution.py:450
  3.3 6.3 %all-to-all-start.1 = ((bf16[4,256,256]{2,1,0:T(8,128)(2,1)}), bf16[4,256,256]{2,1,0:T(8,128)(2,1)S(1)}, u32[]{:S(2)}, u32[]{:S(2)}) async-start(bf16[4,256,256]{2,1,0:T(8,128)(2,1)} %bitcast.7), calls=%async_computation.1 | async-start | bytes 1048576 | tf_op jit(solution)/shard_map/all_to_all | solution.py:486
  9.6 0.6 copy-done.3
  10.2 0.0 copy-done.4
  10.3 2.2 %deal.1 = (bf16[8,128,256]{2,1,0:T(8,128)(2,1)}, bf16[8,128,256]{2,1,0:T(8,128)(2,1)S(1)}, s32[128]{0:T(128)S(1)}) custom-call(s32[64]{0:T(128)S(1)} %copy-done.3, s32[64]{0:T(128)S(1)} %copy-done.4, s32[128]{0:T(128)S(1)} %get-tuple-element.37.refs_2_.refs_1_, bf16[16,128,256]{2,1,0:T(8,128)(2,1)S(1)} %bitcast.17), custom_call_target="tpu_custom_call" | custom-call | tf_op jit(solution)/shard_map/deal/pallas_call | solution.py:466
  12.5 0.0 copy-start.10
  12.5 3.6 %collective-permute-start = (bf16[8,128,256]{2,1,0:T(8,128)(2,1)S(1)}, bf16[8,128,256]{2,1,0:T(8,128)(2,1)S(1)}, u32[]{:S(2)}, u32[]{:S(2)}) collective-permute-start(bf16[8,128,256]{2,1,0:T(8,128)(2,1)S(1)} %get-tuple-element.40), channel_id=1, source_target_pairs={{0,2},{1,3},{4,6},{5,7},{8,10},{9,11},{12,14},{13,15},{16,18},{17,... | collective-permute-start | bytes 1572872 | tf_op jit(solution)/shard_map/ppermute | solution.py:491
  16.0 0.1 copy.13
  16.2 0.0 copy-start.11
  16.2 0.1 copy.14
  16.3 0.7 copy-done.11
  17.0 0.1 copy.15
  17.1 0.7 copy-done.12
  17.9 0.1 collective-permute-start.1
  18.0 6.1 %all-to-all-done.1 = bf16[4,256,256]{2,1,0:T(8,128)(2,1)S(1)} async-done(((bf16[4,256,256]{2,1,0:T(8,128)(2,1)}), bf16[4,256,256]{2,1,0:T(8,128)(2,1)S(1)}, u32[]{:S(2)}, u32[]{:S(2)}) %all-to-all-start.1) | async-done | bytes 524320 | tf_op jit(solution)/shard_map/all_to_all | solution.py:486
  24.1 3.5 %all-to-all-start = ((bf16[4,256,256]{2,1,0:T(8,128)(2,1)}), bf16[4,256,256]{2,1,0:T(8,128)(2,1)S(1)}, u32[]{:S(2)}, u32[]{:S(2)}) async-start(bf16[4,256,256]{2,1,0:T(8,128)(2,1)} %bitcast.2), calls=%async_computation | async-start | bytes 1048576 | tf_op jit(solution)/shard_map/all_to_all | solution.py:486
  27.6 0.0 collective-permute-done.1.refs_6_
  27.6 0.0 copy-start.13
  27.6 0.7 copy-done.16
  28.3 0.2 copy-done.13
  28.4 12.4 %attention_0.1 = (f32[4,128,256]{2,1,0:T(8,128)}, bf16[4,128,256]{2,1,0:T(8,128)(2,1)}, bf16[8,128,256]{2,1,0:T(8,128)(2,1)}, f32[512,256]{1,0:T(8,128)}, f32[512,256]{1,0:T(8,128)}) custom-call(s32[128]{0:T(128)S(1)} %get-tuple-element.38.refs_0_, bf16[16,128,256]{2,1,0:T(8,128)(2,1)} %bitcast.15, bf16[16,128,256]{2,1,0:T(8,128)(2,1)} %bitcast.28, ...), custom_call_target="tpu_custom_call" | custom-call | flops 6375342080 | bytes 5242880 | tf_op jit(solution)/shard_map/attention_0/pallas_call | solution.py:352
  40.8 0.7 all-to-all-done
  41.5 4.4 %all-to-all-start.2 = ((bf16[4,256,256]{2,1,0:T(8,128)(2,1)}), bf16[4,256,256]{2,1,0:T(8,128)(2,1)S(1)}, u32[]{:S(2)}, u32[]{:S(2)}) async-start(bf16[4,256,256]{2,1,0:T(8,128)(2,1)} %bitcast.24), calls=%async_computation.2 | async-start | bytes 1048576 | tf_op jit(solution)/shard_map/all_to_all | solution.py:486
  45.9 12.7 %attention_1.1 = (f32[4,128,256]{2,1,0:T(8,128)}, bf16[4,128,256]{2,1,0:T(8,128)(2,1)}, bf16[8,128,256]{2,1,0:T(8,128)(2,1)}, f32[512,256]{1,0:T(8,128)}, f32[512,256]{1,0:T(8,128)}) custom-call(s32[128]{0:T(128)S(1)} %get-tuple-element.38.refs_0_, bf16[16,128,256]{2,1,0:T(8,128)(2,1)} %bitcast.16, bf16[16,128,256]{2,1,0:T(8,128)(2,1)} %bitcast.29, ...), custom_call_target="tpu_custom_call" | custom-call | flops 6375342080 | bytes 5242880 | tf_op jit(solution)/shard_map/attention_1/pallas_call | solution.py:352
  58.6 0.7 all-to-all-done.2
  59.3 0.0 collective-permute-start.2
  59.3 4.6 %all-to-all-start.3 = ((bf16[4,256,256]{2,1,0:T(8,128)(2,1)}), bf16[4,256,256]{2,1,0:T(8,128)(2,1)S(1)}, u32[]{:S(2)}, u32[]{:S(2)}) async-start(bf16[4,256,256]{2,1,0:T(8,128)(2,1)} %bitcast.23), calls=%async_computation.3 | async-start | bytes 1048576 | tf_op jit(solution)/shard_map/all_to_all | solution.py:486
  64.0 0.1 add.13
  64.1 1.5 %collective-permute-start.3 = (bf16[256,256]{1,0:T(8,128)(2,1)S(1)}, bf16[256,256]{1,0:T(8,128)(2,1)S(1)}, u32[]{:S(2)}, u32[]{:S(2)}) collective-permute-start(bf16[256,256]{1,0:T(8,128)(2,1)S(1)} %select_convert_fusion), channel_id=1, source_target_pairs={{0,2},{2,0},{1,3},{3,1},{4,6},{6,4},{5,7},{7,5},{8,10},{10,8},{9,1... | collective-permute-start | bytes 393224 | tf_op jit(solution)/shard_map/ppermute | solution.py:391
  65.6 4.1 %collective-permute-done.3 = bf16[256,256]{1,0:T(8,128)(2,1)S(1)} collective-permute-done((bf16[256,256]{1,0:T(8,128)(2,1)S(1)}, bf16[256,256]{1,0:T(8,128)(2,1)S(1)}, u32[]{:S(2)}, u32[]{:S(2)}) %collective-permute-start.3) | collective-permute-done | bytes 131104 | tf_op jit(solution)/shard_map/ppermute | solution.py:391
  69.7 0.1 add_convert_fusion.1
  69.8 1.8 %collective-permute-start.4 = (bf16[256,256]{1,0:T(8,128)(2,1)S(1)}, bf16[256,256]{1,0:T(8,128)(2,1)S(1)}, u32[]{:S(2)}, u32[]{:S(2)}) collective-permute-start(bf16[256,256]{1,0:T(8,128)(2,1)S(1)} %add_convert_fusion.1), channel_id=1, source_target_pairs={{0,4},{4,0},{8,12},{12,8},{1,5},{5,1},{9,13},{13,9},{2,6},{6,2},{1... | collective-permute-start | bytes 393224 | tf_op jit(solution)/shard_map/ppermute | solution.py:391
  71.6 1.3 %collective-permute-start.6 = (bf16[4,128,256]{2,1,0:T(8,128)(2,1)S(1)}, bf16[4,128,256]{2,1,0:T(8,128)(2,1)S(1)}, u32[]{:S(2)}, u32[]{:S(2)}) collective-permute-start(bf16[4,128,256]{2,1,0:T(8,128)(2,1)S(1)} %copy-done.14), channel_id=1, source_target_pairs={{2,0},{3,1},{6,4},{7,5},{10,8},{11,9},{14,12},{15,13},{18,16},{19,... | collective-permute-start | bytes 786440 | tf_op jit(solution)/shard_map/ppermute | solution.py:498
  72.9 1.3 %collective-permute-start.7 = (bf16[4,128,256]{2,1,0:T(8,128)(2,1)S(1)}, bf16[4,128,256]{2,1,0:T(8,128)(2,1)S(1)}, u32[]{:S(2)}, u32[]{:S(2)}) collective-permute-start(bf16[4,128,256]{2,1,0:T(8,128)(2,1)S(1)} %copy-done.15), channel_id=1, source_target_pairs={{2,0},{3,1},{6,4},{7,5},{10,8},{11,9},{14,12},{15,13},{18,16},{19,... | collective-permute-start | bytes 786440 | tf_op jit(solution)/shard_map/ppermute | solution.py:507
  74.2 2.2 %collective-permute-done.4 = bf16[256,256]{1,0:T(8,128)(2,1)S(1)} collective-permute-done((bf16[256,256]{1,0:T(8,128)(2,1)S(1)}, bf16[256,256]{1,0:T(8,128)(2,1)S(1)}, u32[]{:S(2)}, u32[]{:S(2)}) %collective-permute-start.4) | collective-permute-done | bytes 131104 | tf_op jit(solution)/shard_map/ppermute | solution.py:391
  76.4 2.6 %all-to-all-done.3 = bf16[4,256,256]{2,1,0:T(8,128)(2,1)S(1)} async-done(((bf16[4,256,256]{2,1,0:T(8,128)(2,1)}), bf16[4,256,256]{2,1,0:T(8,128)(2,1)S(1)}, u32[]{:S(2)}, u32[]{:S(2)}) %all-to-all-start.3) | async-done | bytes 524320 | tf_op jit(solution)/shard_map/all_to_all | solution.py:486
  79.1 1.7 %collective-permute-start.5 = (bf16[256,256]{1,0:T(8,128)(2,1)S(1)}, bf16[256,256]{1,0:T(8,128)(2,1)S(1)}, u32[]{:S(2)}, u32[]{:S(2)}) collective-permute-start(bf16[256,256]{1,0:T(8,128)(2,1)S(1)} %convert_add_fusion), channel_id=1, source_target_pairs={{0,8},{4,12},{8,0},{12,4},{1,9},{5,13},{9,1},{13,5},{2,10},{6,14},... | collective-permute-start | bytes 393224 | tf_op jit(solution)/shard_map/ppermute | solution.py:391
  80.7 2.0 %collective-permute-done.6.refs_4_ = bf16[4,128,256]{2,1,0:T(8,128)(2,1)S(1)} collective-permute-done((bf16[4,128,256]{2,1,0:T(8,128)(2,1)S(1)}, bf16[4,128,256]{2,1,0:T(8,128)(2,1)S(1)}, u32[]{:S(2)}, u32[]{:S(2)}) %collective-permute-start.6) | collective-permute-done | bytes 262176 | tf_op jit(solution)/shard_map/ppermute | solution.py:498
  82.7 3.4 %collective-permute-done.7.refs_5_ = bf16[4,128,256]{2,1,0:T(8,128)(2,1)S(1)} collective-permute-done((bf16[4,128,256]{2,1,0:T(8,128)(2,1)S(1)}, bf16[4,128,256]{2,1,0:T(8,128)(2,1)S(1)}, u32[]{:S(2)}, u32[]{:S(2)}) %collective-permute-start.7) | collective-permute-done | bytes 262176 | tf_op jit(solution)/shard_map/ppermute | solution.py:507
  86.1 1.6 %fold.1 = (f32[16,128,128]{2,1,0:T(8,128)S(1)}, f32[16,128,128]{2,1,0:T(8,128)S(1)}) custom-call(s32[128]{0:T(128)S(1)} %get-tuple-element.38.refs_0_, s32[128]{0:T(128)S(1)} %get-tuple-element.37.refs_2_.refs_1_, f32[4,128,256]{2,1,0:T(8,128)S(1)} %copy-done.1, f32[4,128,256]{2,1,0:T(8,128)S(1)} %copy-done.2, ...), custom_call_target="tpu_custom_call" | custom-call | tf_op jit(solution)/shard_map/fold/pallas_call | solution.py:511
  87.7 0.1 collective-permute-start.8
  87.8 0.7 collective-permute-start.9
  88.5 1.9 %collective-permute-done.8.got = f32[16,128,128]{2,1,0:T(8,128)S(1)} collective-permute-done((f32[16,128,128]{2,1,0:T(8,128)S(1)}, f32[16,128,128]{2,1,0:T(8,128)S(1)}, u32[]{:S(2)}, u32[]{:S(2)}) %collective-permute-start.8) | collective-permute-done | bytes 1048608 | tf_op jit(solution)/shard_map/ppermute | solution.py:391
  90.4 0.9 add.20
  91.3 2.4 %collective-permute-done.9.other = bf16[256,256]{1,0:T(8,128)(2,1)S(1)} collective-permute-done((bf16[256,256]{1,0:T(8,128)(2,1)S(1)}, bf16[256,256]{1,0:T(8,128)(2,1)S(1)}, u32[]{:S(2)}, u32[]{:S(2)}) %collective-permute-start.9) | collective-permute-done | bytes 131104 | tf_op jit(solution)/shard_map/ppermute | solution.py:391
  93.7 0.7 copy-done.8
  94.4 1.8 %split.1 = (f32[256,128]{1,0:T(8,128)}, f32[256,128]{1,0:T(8,128)}, f32[256,128]{1,0:T(8,128)}, f32[128,256]{1,0:T(8,128)}) custom-call(bf16[256,256]{1,0:T(8,128)(2,1)} %copy-done.5, bf16[256,256]{1,0:T(8,128)(2,1)} %copy-done.8), custom_call_target="tpu_custom_call" | custom-call | tf_op jit(solution)/shard_map/split/pallas_call | solution.py:531
  (30 shorter events, 0.2 us)
Async XLA Ops:
  0.6 9.0 %copy-start = (bf16[1,2048,256]{2,1,0:T(8,128)(2,1)S(1)}, bf16[1,2048,256]{2,1,0:T(8,128)(2,1)}, u32[]{:S(2)}) copy-start(bf16[1,2048,256]{2,1,0:T(8,128)(2,1)} %param.8) | copy-start | bytes 3145732
  3.3 20.8 %all-to-all-start.1 = ((bf16[4,256,256]{2,1,0:T(8,128)(2,1)}), bf16[4,256,256]{2,1,0:T(8,128)(2,1)S(1)}, u32[]{:S(2)}, u32[]{:S(2)}) async-start(bf16[4,256,256]{2,1,0:T(8,128)(2,1)} %bitcast.7), calls=%async_computation.1 | async-start | bytes 1048576 | tf_op jit(solution)/shard_map/all_to_all | solution.py:486
  9.6 0.7 copy-start.3
  9.6 0.7 copy-start.4
  10.3 5.8 %copy-start.9 = (bf16[256,128]{1,0:T(8,128)(2,1)S(1)}, bf16[256,128]{1,0:T(8,128)(2,1)}, u32[]{:S(2)}) copy-start(bf16[256,128]{1,0:T(8,128)(2,1)} %param.11) | copy-start | bytes 196612
  12.5 3.7 %copy-start.10 = (bf16[256,128]{1,0:T(8,128)(2,1)S(1)}, bf16[256,128]{1,0:T(8,128)(2,1)}, u32[]{:S(2)}) copy-start(bf16[256,128]{1,0:T(8,128)(2,1)} %param.12) | copy-start | bytes 196612
  12.5 15.1 %collective-permute-start = (bf16[8,128,256]{2,1,0:T(8,128)(2,1)S(1)}, bf16[8,128,256]{2,1,0:T(8,128)(2,1)S(1)}, u32[]{:S(2)}, u32[]{:S(2)}) collective-permute-start(bf16[8,128,256]{2,1,0:T(8,128)(2,1)S(1)} %get-tuple-element.40), channel_id=1, source_target_pairs={{0,2},{1,3},{4,6},{5,7},{8,10},{9,11},{12,14},{13,15},{16,18},{17,... | collective-permute-start | bytes 1572872 | tf_op jit(solution)/shard_map/ppermute | solution.py:491
  16.2 0.8 copy-start.11
  17.0 0.8 copy-start.12
  17.9 6.2 %copy-start.7 = (bf16[512,256]{1,0:T(8,128)(2,1)}, bf16[512,256]{1,0:T(8,128)(2,1)S(1)}, u32[]{:S(2)}) copy-start(bf16[512,256]{1,0:T(8,128)(2,1)S(1)} %pad_maximum_fusion.refs_5_) | copy-start | bytes 786436
  17.9 9.7 %collective-permute-start.1 = (bf16[512,256]{1,0:T(8,128)(2,1)S(1)}, bf16[512,256]{1,0:T(8,128)(2,1)S(1)}, u32[]{:S(2)}, u32[]{:S(2)}) collective-permute-start(bf16[512,256]{1,0:T(8,128)(2,1)S(1)} %pad_maximum_fusion.refs_5_), channel_id=1, source_target_pairs={{0,1},{1,0},{2,3},{3,2},{4,5},{5,4},{6,7},{7,6},{8,9},{9,8},{10,11... | collective-permute-start | bytes 786440 | tf_op jit(solution)/shard_map/ppermute | solution.py:391
  24.1 17.4 %all-to-all-start = ((bf16[4,256,256]{2,1,0:T(8,128)(2,1)}), bf16[4,256,256]{2,1,0:T(8,128)(2,1)S(1)}, u32[]{:S(2)}, u32[]{:S(2)}) async-start(bf16[4,256,256]{2,1,0:T(8,128)(2,1)} %bitcast.2), calls=%async_computation | async-start | bytes 1048576 | tf_op jit(solution)/shard_map/all_to_all | solution.py:486
  27.6 0.7 copy-start.16
  27.6 0.9 copy-start.13
  41.5 17.8 %all-to-all-start.2 = ((bf16[4,256,256]{2,1,0:T(8,128)(2,1)}), bf16[4,256,256]{2,1,0:T(8,128)(2,1)S(1)}, u32[]{:S(2)}, u32[]{:S(2)}) async-start(bf16[4,256,256]{2,1,0:T(8,128)(2,1)} %bitcast.24), calls=%async_computation.2 | async-start | bytes 1048576 | tf_op jit(solution)/shard_map/all_to_all | solution.py:486
  59.3 4.6 %collective-permute-start.2 = (f32[512,256]{1,0:T(8,128)}, f32[512,256]{1,0:T(8,128)S(1)}, u32[]{:S(2)}, u32[]{:S(2)}) collective-permute-start(f32[512,256]{1,0:T(8,128)} %get-tuple-element.49), channel_id=1, source_target_pairs={{0,1},{1,0},{2,3},{3,2},{4,5},{5,4},{6,7},{7,6},{8,9},{9,8},{10,11... | collective-permute-start | bytes 1572872 | tf_op jit(solution)/shard_map/ppermute | solution.py:391
  59.3 4.6 %copy-start.6 = (f32[512,256]{1,0:T(8,128)S(1)}, f32[512,256]{1,0:T(8,128)}, u32[]{:S(2)}) copy-start(f32[512,256]{1,0:T(8,128)} %get-tuple-element.44) | copy-start | bytes 1572868
  59.3 19.7 %all-to-all-start.3 = ((bf16[4,256,256]{2,1,0:T(8,128)(2,1)}), bf16[4,256,256]{2,1,0:T(8,128)(2,1)S(1)}, u32[]{:S(2)}, u32[]{:S(2)}) async-start(bf16[4,256,256]{2,1,0:T(8,128)(2,1)} %bitcast.23), calls=%async_computation.3 | async-start | bytes 1048576 | tf_op jit(solution)/shard_map/all_to_all | solution.py:486
  63.9 9.0 %copy-start.15 = (bf16[4,128,256]{2,1,0:T(8,128)(2,1)S(1)}, bf16[4,128,256]{2,1,0:T(8,128)(2,1)}, u32[]{:S(2)}) copy-start(bf16[4,128,256]{2,1,0:T(8,128)(2,1)} %get-tuple-element.55) | copy-start | bytes 786436
  64.0 7.6 %copy-start.14 = (bf16[4,128,256]{2,1,0:T(8,128)(2,1)S(1)}, bf16[4,128,256]{2,1,0:T(8,128)(2,1)}, u32[]{:S(2)}) copy-start(bf16[4,128,256]{2,1,0:T(8,128)(2,1)} %get-tuple-element.54) | copy-start | bytes 786436
  64.0 22.0 %copy-start.2 = (f32[4,128,256]{2,1,0:T(8,128)S(1)}, f32[4,128,256]{2,1,0:T(8,128)}, u32[]{:S(2)}) copy-start(f32[4,128,256]{2,1,0:T(8,128)} %get-tuple-element.53.refs_3_) | copy-start | bytes 1572868
  64.1 22.0 %copy-start.1 = (f32[4,128,256]{2,1,0:T(8,128)S(1)}, f32[4,128,256]{2,1,0:T(8,128)}, u32[]{:S(2)}) copy-start(f32[4,128,256]{2,1,0:T(8,128)} %get-tuple-element.52.refs_2_) | copy-start | bytes 1572868
  64.1 5.7 %collective-permute-start.3 = (bf16[256,256]{1,0:T(8,128)(2,1)S(1)}, bf16[256,256]{1,0:T(8,128)(2,1)S(1)}, u32[]{:S(2)}, u32[]{:S(2)}) collective-permute-start(bf16[256,256]{1,0:T(8,128)(2,1)S(1)} %select_convert_fusion), channel_id=1, source_target_pairs={{0,2},{2,0},{1,3},{3,1},{4,6},{6,4},{5,7},{7,5},{8,10},{10,8},{9,1... | collective-permute-start | bytes 393224 | tf_op jit(solution)/shard_map/ppermute | solution.py:391
  69.8 6.6 %collective-permute-start.4 = (bf16[256,256]{1,0:T(8,128)(2,1)S(1)}, bf16[256,256]{1,0:T(8,128)(2,1)S(1)}, u32[]{:S(2)}, u32[]{:S(2)}) collective-permute-start(bf16[256,256]{1,0:T(8,128)(2,1)S(1)} %add_convert_fusion.1), channel_id=1, source_target_pairs={{0,4},{4,0},{8,12},{12,8},{1,5},{5,1},{9,13},{13,9},{2,6},{6,2},{1... | collective-permute-start | bytes 393224 | tf_op jit(solution)/shard_map/ppermute | solution.py:391
  71.6 11.1 %collective-permute-start.6 = (bf16[4,128,256]{2,1,0:T(8,128)(2,1)S(1)}, bf16[4,128,256]{2,1,0:T(8,128)(2,1)S(1)}, u32[]{:S(2)}, u32[]{:S(2)}) collective-permute-start(bf16[4,128,256]{2,1,0:T(8,128)(2,1)S(1)} %copy-done.14), channel_id=1, source_target_pairs={{2,0},{3,1},{6,4},{7,5},{10,8},{11,9},{14,12},{15,13},{18,16},{19,... | collective-permute-start | bytes 786440 | tf_op jit(solution)/shard_map/ppermute | solution.py:498
  72.9 13.2 %collective-permute-start.7 = (bf16[4,128,256]{2,1,0:T(8,128)(2,1)S(1)}, bf16[4,128,256]{2,1,0:T(8,128)(2,1)S(1)}, u32[]{:S(2)}, u32[]{:S(2)}) collective-permute-start(bf16[4,128,256]{2,1,0:T(8,128)(2,1)S(1)} %copy-done.15), channel_id=1, source_target_pairs={{2,0},{3,1},{6,4},{7,5},{10,8},{11,9},{14,12},{15,13},{18,16},{19,... | collective-permute-start | bytes 786440 | tf_op jit(solution)/shard_map/ppermute | solution.py:507
  79.1 8.6 %collective-permute-start.5 = (bf16[256,256]{1,0:T(8,128)(2,1)S(1)}, bf16[256,256]{1,0:T(8,128)(2,1)S(1)}, u32[]{:S(2)}, u32[]{:S(2)}) collective-permute-start(bf16[256,256]{1,0:T(8,128)(2,1)S(1)} %convert_add_fusion), channel_id=1, source_target_pairs={{0,8},{4,12},{8,0},{12,4},{1,9},{5,13},{9,1},{13,5},{2,10},{6,14},... | collective-permute-start | bytes 393224 | tf_op jit(solution)/shard_map/ppermute | solution.py:391
  87.7 3.6 %copy-start.5 = (bf16[256,256]{1,0:T(8,128)(2,1)}, bf16[256,256]{1,0:T(8,128)(2,1)S(1)}, u32[]{:S(2)}) copy-start(bf16[256,256]{1,0:T(8,128)(2,1)S(1)} %add_convert_fusion.part) | copy-start | bytes 393220
  87.7 2.7 %collective-permute-start.8 = (f32[16,128,128]{2,1,0:T(8,128)S(1)}, f32[16,128,128]{2,1,0:T(8,128)S(1)}, u32[]{:S(2)}, u32[]{:S(2)}) collective-permute-start(f32[16,128,128]{2,1,0:T(8,128)S(1)} %get-tuple-element.61), channel_id=1, source_target_pairs={{0,1},{1,0},{2,3},{3,2},{4,5},{5,4},{6,7},{7,6},{8,9},{9,8},{10,11... | collective-permute-start | bytes 3145736 | tf_op jit(solution)/shard_map/ppermute | solution.py:391
  87.8 5.9 %collective-permute-start.9 = (bf16[256,256]{1,0:T(8,128)(2,1)S(1)}, bf16[256,256]{1,0:T(8,128)(2,1)S(1)}, u32[]{:S(2)}, u32[]{:S(2)}) collective-permute-start(bf16[256,256]{1,0:T(8,128)(2,1)S(1)} %add_convert_fusion.part), channel_id=1, source_target_pairs={{0,2},{2,0},{1,3},{3,1},{4,6},{6,4},{5,7},{7,5},{8,10},{10,8},{9,1... | collective-permute-start | bytes 393224 | tf_op jit(solution)/shard_map/ppermute | solution.py:391
  93.7 0.7 copy-start.8

commit v10 on v9

v10 whole, which is shorter than its diff:
```python
import jax
import jax.numpy as jnp
from jax import lax
from jax.experimental import pallas as pl
from jax.experimental.pallas import tpu as pltpu
from jax.sharding import PartitionSpec as P

HD = 32
BLOCK = 128
GROUP = 128
CORES = 2
F32 = jnp.float32
BF16 = jnp.bfloat16
PACK = 4
STEP_ITEMS = 4
LOG2E = 1.4426950408889634


class Layout:
    def __init__(self, blocks_dev, reach_total):
        self.blocks = blocks_dev
        self.items = blocks_dev // CORES
        self.reach = reach_total
        self.slots = max(1, 2 * blocks_dev // reach_total // CORES)
        self.places = reach_total * self.slots
        self.block_of = 0
        self.recv_of = self.items
        self.count_own = 2 * self.items
        self.count_partner = 3 * self.items
        self.owner_of = 4 * self.items
        self.item_of = self.owner_of + blocks_dev
        self.later_day = self.item_of + blocks_dev
        self.size = -(-(self.later_day + 1) // 128) * 128
        self.spare = blocks_dev
        self.home_of = 0
        self.asker_of = blocks_dev + 1
        self.picks = 2 * (blocks_dev + 1)
        self.spare_pick = self.picks + self.places
        self.homes_size = -(-(self.spare_pick + 1) // 128) * 128


def pick_kernel(lay, partner_hbm, inputs, sent, homes, partner, held, sems):
    bd, slots = lay.blocks, lay.slots
    reach_pos, core = lax.axis_index("reach"), lax.axis_index("head")
    table_copy = pltpu.make_async_copy(partner_hbm, partner, sems.at[0])
    table_copy.start()
    copy = pltpu.make_async_copy(inputs, held, sems.at[1])
    copy.start()
    for place in range(lay.places):
        homes[lay.picks + place] = 0
    table_copy.wait()

    def one_reach(peer, carry):
        base = jnp.int32(0)
        wanted = []
        for index in range(bd):
            block = partner[peer * bd + index]
            source = lax.div(block, bd)
            base = base + jnp.where(source < reach_pos, 1, 0)
            wanted.append((source == reach_pos, lax.rem(block, bd)))
        rank = jnp.int32(0)
        for hit, local in wanted:
            place = base + rank
            owner = lax.rem(place, CORES)
            slot = peer * slots + jnp.minimum(lax.div(rank, CORES), slots - 1)
            target = jnp.where(hit, local, lay.spare)
            homes[lay.home_of + target] = slot
            homes[lay.asker_of + target] = owner
            homes[jnp.where(hit & (owner == core), lay.picks + slot, lay.spare_pick)] = local
            rank = rank + jnp.where(hit, 1, 0)
        return carry

    lax.fori_loop(0, lay.reach, one_reach, 0)
    copy.wait()
    for place in range(lay.places):
        sent[place] = held[homes[lay.picks + place]]


def deal_kernel(lay, partner, counts, inputs, prior, tab, start, used):
    bd, slots = lay.blocks, lay.slots
    reach_pos, core = lax.axis_index("reach"), lax.axis_index("head")

    def clear(index, carry):
        used[index] = 0
        start[index] = 0
        return carry

    lax.fori_loop(0, lay.reach, clear, 0, unroll=True)

    def count(index, carry):
        source = lax.div(partner[reach_pos * bd + index], bd)
        start[source] = start[source] + 1
        return carry

    lax.fori_loop(0, bd, count, 0)

    def prefix(index, total):
        here = start[index]
        start[index] = total
        return total + here

    lax.fori_loop(0, lay.reach, prefix, jnp.int32(0))

    def assign(index, carry):
        wanted = partner[reach_pos * bd + index]
        source = lax.div(wanted, bd)
        rank = used[source]
        used[source] = rank + 1
        place = start[source] + rank
        owner = lax.rem(place, CORES)
        item = lax.div(place, CORES)
        slot = jnp.minimum(lax.div(rank, CORES), slots - 1)
        tab[lay.owner_of + index] = owner
        tab[lay.item_of + index] = item

        @pl.when(owner == core)
        def _():
            tab[lay.block_of + item] = index
            tab[lay.recv_of + item] = source * slots + slot
            tab[lay.count_own + item] = counts[reach_pos * bd + index]
            tab[lay.count_partner + item] = counts[wanted]

        return carry

    lax.fori_loop(0, bd, assign, 0)
    tab[lay.later_day] = jnp.where(lax.axis_index("day") > 0, 1, 0)

    def pick_prior(item, carry):
        prior[item] = inputs[tab[lay.block_of + item]]
        return carry

    lax.fori_loop(0, lay.items, pick_prior, 0)


def dot(left, right):
    return lax.dot_general(left, right, (((1,), (0,)), ((), ())), preferred_element_type=F32)


def dot_t(left, right):
    return lax.dot_general(left, right, (((1,), (1,)), ((), ())), preferred_element_type=F32)


def attention_kernel(lay, tab, *refs):
    step = pl.program_id(0)
    read, refs = refs[: 4 * STEP_ITEMS], refs[4 * STEP_ITEMS :]
    mine_ref, other_ref, *refs = refs
    own_out_ref, day_ref, home_ref, grad_mine_ref, grad_other_ref = refs
    factor = HD ** (-0.5)
    per_group = GROUP // HD // PACK

    @pl.when(step == 0)
    def _():
        grad_mine_ref[...] = jnp.zeros_like(grad_mine_ref)
        grad_other_ref[...] = jnp.zeros_like(grad_other_ref)

    rows = lax.broadcasted_iota(jnp.int32, (BLOCK, PACK * BLOCK), 0)
    lane_head = lax.broadcasted_iota(jnp.int32, (BLOCK, GROUP), 1) // HD
    query_t = jnp.concatenate([mine_ref[256:384, :], other_ref[256:384, :]], axis=0)
    output_w = jnp.concatenate([mine_ref[384:512, :], other_ref[384:512, :]], axis=0)

    class Item:
        pass

    def begin(place):
        it = Item()
        own_ref, up_ref, partner_ref, prior_ref = read[4 * place : 4 * place + 4]
        it.place = place
        item = step * STEP_ITEMS + place
        it.item = item
        it.own, it.up = own_ref[0], up_ref[0]
        it.inputs = jnp.concatenate([it.own, partner_ref[0], prior_ref[0]], axis=0)
        queries = dot_t(it.own, query_t)
        back_out = dot_t(it.up, output_w)
        count_own = tab[lay.count_own + item]
        it.counts = (count_own, tab[lay.count_partner + item], count_own * tab[lay.later_day])
        it.groups = []
        for group, weights_ref in enumerate((mine_ref, other_ref)):
            kv_t = weights_ref[0:256, :]
            kv = dot_t(it.inputs, kv_t).astype(BF16)
            lanes = slice(group * GROUP, (group + 1) * GROUP)
            it.groups.append((kv_t, kv, kv.T, queries[:, lanes], back_out[:, lanes]))
        it.outputs_t, it.back_query_t = [], []
        it.keys, it.values = ([], []), ([], [])
        return it

    def start(it, part):
        _, kv, _, group_queries, group_back = it.groups[part // per_group]
        heads = [part % per_group * PACK + h for h in range(PACK)]
        query_pack, back_pack = (
            jnp.concatenate(
                [jnp.where(lane_head == h, rows_of, 0.0) for h in heads], axis=0
            ).astype(BF16)
            for rows_of in (group_queries, group_back)
        )
        logits = dot_t(kv[:, :GROUP], query_pack)
        return it, part, query_pack, back_pack, logits, dot_t(kv[:, GROUP:], back_pack)

    def middle(it, part, query_pack, back_pack, logits, back_weights):
        logits = jnp.concatenate(
            [
                jnp.where(rows < count, logits[index * BLOCK : (index + 1) * BLOCK], -1e30)
                for index, count in enumerate(it.counts)
            ],
            axis=0,
        )
        highest = jnp.max(logits, axis=0, keepdims=True)
        raised = jnp.exp2((logits - highest) * (factor * LOG2E))
        scale = 1.0 / jnp.sum(raised, axis=0, keepdims=True)
        weights = raised * scale
        center = jnp.sum(weights * back_weights, axis=0, keepdims=True)
        back_logits = (weights * ((back_weights - center) * factor)).astype(BF16)
        return it, part, query_pack, back_pack, weights.astype(BF16), back_logits

    def finish(it, part, query_pack, back_pack, weights_low, back_logits):
        group = part // per_group
        kv_cols = it.groups[group][2]
        it.values[group].append(dot(weights_low, back_pack))
        it.keys[group].append(dot(back_logits, query_pack))
        size = PACK * HD
        first = part % per_group * size
        out_t = dot(kv_cols[GROUP + first : GROUP + first + size, :], weights_low)
        query_grad_t = dot(kv_cols[first : first + size, :], back_logits)
        for h in range(PACK):
            lanes = slice(h * BLOCK, (h + 1) * BLOCK)
            it.outputs_t.append(out_t[h * HD : (h + 1) * HD, lanes])
            it.back_query_t.append(query_grad_t[h * HD : (h + 1) * HD, lanes])

    def end(it):
        inputs_t = it.inputs.T
        back_inputs = None
        for group, grad_ref in enumerate((grad_mine_ref, grad_other_ref)):
            kv_t = it.groups[group][0]
            keys, values = it.keys[group], it.values[group]
            back_kv = jnp.concatenate(
                [sum(keys[1:], keys[0]), sum(values[1:], values[0])], axis=1
            ).astype(BF16)
            term = dot(back_kv, kv_t)
            back_inputs = term if back_inputs is None else back_inputs + term
            grad_ref[0:256, :] += dot(inputs_t, back_kv)
        outputs_t = jnp.concatenate(it.outputs_t, axis=0).astype(BF16)
        back_query_t = jnp.concatenate(it.back_query_t, axis=0).astype(BF16)
        query_grad = dot(back_query_t, it.own)
        output_grad = dot(outputs_t, it.up)
        grad_mine_ref[256:384, :] += query_grad[:GROUP]
        grad_other_ref[256:384, :] += query_grad[GROUP:]
        grad_mine_ref[384:512, :] += output_grad[:GROUP]
        grad_other_ref[384:512, :] += output_grad[GROUP:]
        own_out_ref[it.place] = back_inputs[:BLOCK] + dot(back_query_t.T, query_t)
        home_ref[tab[lay.recv_of + it.item]] = back_inputs[BLOCK : 2 * BLOCK].astype(BF16)
        day_ref[it.place] = back_inputs[2 * BLOCK :].astype(BF16)

    parts = 2 * per_group
    items = [begin(0)]
    started = start(items[0], 0)
    waiting = None
    ended = 0
    for index in range(STEP_ITEMS * parts):
        following = None
        if index + 1 < STEP_ITEMS * parts:
            place, part = divmod(index + 1, parts)
            if part == 0:
                items.append(begin(place))
            following = start(items[place], part)
        if waiting is not None:
            finish(*waiting)
            if waiting[1] == parts - 1:
                end(waiting[0])
        waiting = middle(*started)
        started = following
    finish(*waiting)
    end(waiting[0])


def fold_kernel(lay, tab, homes, own_terms, day_terms, home_terms, keep, give):
    core = lax.axis_index("head")
    half = keep.shape[2]

    def one(block, carry):
        item = tab[lay.item_of + block]
        mine = tab[lay.owner_of + block] == core
        asked = homes[lay.asker_of + block] == core
        own = own_terms[item] + day_terms[item].astype(F32)
        home = home_terms[homes[lay.home_of + block]].astype(F32)
        total = jnp.where(mine, own, 0.0) + jnp.where(asked, home, 0.0)
        low, high = total[:, :half], total[:, half:]
        keep[block] = jnp.where(core == 0, low, high)
        give[block] = jnp.where(core == 0, high, low)
        return carry

    lax.fori_loop(0, lay.blocks, one, 0)


def add_kernel(kept, got, out):
    out[...] = (kept[...] + got[...]).astype(BF16)


def attend(lay, tab, in_blocks, up_blocks, received, prior_inputs, pack, pack_other):
    width = in_blocks.shape[-1]

    def at_item(place):
        return lambda step, tab: (step * STEP_ITEMS + place, 0, 0)

    def at_block(place):
        return lambda step, tab: (tab[lay.block_of + step * STEP_ITEMS + place], 0, 0)

    def at_recv(place):
        return lambda step, tab: (tab[lay.recv_of + step * STEP_ITEMS + place], 0, 0)

    def at_step(step, tab):
        return (step, 0, 0)

    def fixed(step, tab):
        return (0, 0)

    full_block = (1, BLOCK, width)
    weights_block = (4 * GROUP, width)
    in_specs, operands = [], []
    for place in range(STEP_ITEMS):
        in_specs += [
            pl.BlockSpec(full_block, at_block(place)),
            pl.BlockSpec(full_block, at_block(place)),
            pl.BlockSpec(full_block, at_recv(place)),
            pl.BlockSpec(full_block, at_item(place)),
        ]
        operands += [in_blocks, up_blocks, received, prior_inputs]
    in_specs += [pl.BlockSpec(weights_block, fixed)] * 2
    operands += [pack, pack_other]
    pieces = lay.items
    flops = 2 * pieces * (23 * BLOCK * width * width + 24 * BLOCK * 3 * BLOCK * 512)
    return pl.pallas_call(
        lambda *refs: attention_kernel(lay, *refs),
        grid_spec=pltpu.PrefetchScalarGridSpec(
            num_scalar_prefetch=1,
            grid=(pieces // STEP_ITEMS,),
            in_specs=in_specs,
            out_specs=(
                pl.BlockSpec((STEP_ITEMS, BLOCK, width), at_step),
                pl.BlockSpec((STEP_ITEMS, BLOCK, width), at_step),
                pl.BlockSpec((lay.places, BLOCK, width), lambda step, tab: (0, 0, 0)),
                pl.BlockSpec(weights_block, fixed),
                pl.BlockSpec(weights_block, fixed),
            ),
        ),
        out_shape=(
            pltpu.HBM((pieces, BLOCK, width), F32),
            pltpu.HBM((pieces, BLOCK, width), BF16),
            pltpu.HBM((lay.places, BLOCK, width), BF16),
            pltpu.HBM(weights_block, F32),
            pltpu.HBM(weights_block, F32),
        ),
        compiler_params=pltpu.CompilerParams(vmem_limit_bytes=32 << 20),
        cost_estimate=pl.CostEstimate(
            flops=flops, bytes_accessed=9 << 20, transcendentals=pieces * 8 * BLOCK * 3 * BLOCK
        ),
        name="attention",
    )(
        tab,
        *[
            value
            if value is received
            else pltpu.with_memory_space_constraint(value, pltpu.HBM)
            for value in operands
        ],
    )


def exchanged(value, axis, bit):
    count = lax.axis_size(axis)
    return lax.ppermute(value, axis, [(place, place ^ bit) for place in range(count)])


def summed_over(value, axis, bit):
    low = value.astype(BF16)
    return low.astype(F32) + exchanged(low, axis, bit).astype(F32)


def sum_gradients(total):
    half = total.shape[0] // 2
    first = lax.rem(lax.axis_index("day"), 2) == 0
    kept = jnp.where(first, total[:half], total[half:])
    given = jnp.where(first, total[half:], total[:half])
    part = kept.astype(BF16).astype(F32) + exchanged(given.astype(BF16), "day", 1).astype(F32)
    bit = 2
    while bit < lax.axis_size("day"):
        part = summed_over(part, "day", bit)
        bit *= 2
    bit = 1
    while bit < lax.axis_size("reach"):
        part = summed_over(part, "reach", bit)
        bit *= 2
    part = part.astype(BF16)
    return part, exchanged(part, "day", 1)


def split_kernel(part, other, query_out, key_out, value_out, output_out):
    first = lax.rem(lax.axis_index("day"), 2) == 0
    mine, theirs = part[...].astype(F32), other[...].astype(F32)
    upper = jnp.where(first, mine, theirs)
    lower = jnp.where(first, theirs, mine)
    key_out[...] = upper[:, :GROUP]
    value_out[...] = upper[:, GROUP:]
    query_out[...] = lower[:GROUP].T
    output_out[...] = lower[GROUP:]


def on_device(
    inputs, upstream, query_weight, key_weight, value_weight, output_weight, partner, counts
):
    days_dev, rows_dev, width = inputs.shape
    assert days_dev == 1 and width == 2 * GROUP
    blocks_dev = rows_dev // BLOCK
    reach_total = lax.axis_size("reach")
    day_total = lax.axis_size("day")
    assert lax.axis_size("head") == CORES
    lay = Layout(blocks_dev, reach_total)
    half = width // 2
    in_blocks = inputs.reshape(blocks_dev, BLOCK, width)
    up_blocks = upstream.reshape(blocks_dev, BLOCK, width)
    pack = jnp.concatenate([key_weight.T, value_weight.T, query_weight.T, output_weight], axis=0)
    pack_other = exchanged(pack, "head", 1)

    smem = pl.BlockSpec(memory_space=pltpu.SMEM)
    in_vmem = pl.BlockSpec(memory_space=pltpu.VMEM)
    anywhere = pl.BlockSpec(memory_space=pl.ANY)
    sent_shape = jax.ShapeDtypeStruct((lay.places, BLOCK, width), BF16)
    sent, homes = pl.pallas_call(
        lambda *refs: pick_kernel(lay, *refs),
        out_shape=(sent_shape, jax.ShapeDtypeStruct((lay.homes_size,), jnp.int32)),
        in_specs=[anywhere, anywhere],
        out_specs=(in_vmem, smem),
        scratch_shapes=[
            pltpu.SMEM(partner.shape, jnp.int32),
            pltpu.VMEM((blocks_dev, BLOCK, width), BF16),
            pltpu.SemaphoreType.DMA((2,)),
        ],
        compiler_params=pltpu.CompilerParams(vmem_limit_bytes=16 << 20),
        name="pick",
    )(
        pltpu.with_memory_space_constraint(partner, pltpu.HBM),
        pltpu.with_memory_space_constraint(in_blocks, pltpu.HBM),
    )
    prior, tab = pl.pallas_call(
        lambda *refs: deal_kernel(lay, *refs),
        out_shape=(
            jax.ShapeDtypeStruct((lay.items, BLOCK, width), BF16),
            jax.ShapeDtypeStruct((lay.size,), jnp.int32),
        ),
        in_specs=[smem, smem, in_vmem],
        out_specs=(in_vmem, smem),
        scratch_shapes=[
            pltpu.SMEM((lay.reach,), jnp.int32),
            pltpu.SMEM((lay.reach,), jnp.int32),
        ],
        compiler_params=pltpu.CompilerParams(vmem_limit_bytes=16 << 20),
        name="deal",
    )(partner, counts, in_blocks)

    def ring(value):
        shape = value.shape
        value = value.reshape(lay.reach, lay.slots * BLOCK, width)
        return lax.all_to_all(value, "reach", 0, 0, tiled=True).reshape(shape)

    next_day = [(d, d + 1) for d in range(day_total - 1)]
    last_day = [(d + 1, d) for d in range(day_total - 1)]
    received = ring(sent)
    prior_inputs = lax.ppermute(prior, "day", next_day)
    own_terms, day_terms, home_terms, grad_mine, grad_other = attend(
        lay, tab, in_blocks, up_blocks, received, prior_inputs, pack, pack_other
    )
    home_terms = ring(home_terms)
    grad_swapped = exchanged(grad_other, "head", 1)
    day_terms = lax.ppermute(day_terms, "day", last_day)
    half_shape = jax.ShapeDtypeStruct((blocks_dev, BLOCK, half), F32)

    part, other = sum_gradients(grad_mine + grad_swapped)
    _, home_terms = lax.optimization_barrier((part, home_terms))
    keep, give = pl.pallas_call(
        lambda *refs: fold_kernel(lay, *refs),
        out_shape=(half_shape, half_shape),
        in_specs=[smem] * 2 + [in_vmem] * 3,
        out_specs=[in_vmem] * 2,
        compiler_params=pltpu.CompilerParams(vmem_limit_bytes=16 << 20),
        name="fold",
    )(tab, homes, own_terms, day_terms, home_terms)
    other, give = lax.optimization_barrier((other, give))
    got = exchanged(give, "head", 1)
    back_blocks = pl.pallas_call(
        add_kernel,
        out_shape=jax.ShapeDtypeStruct((blocks_dev, BLOCK, half), BF16),
        in_specs=[in_vmem] * 2,
        out_specs=in_vmem,
        compiler_params=pltpu.CompilerParams(vmem_limit_bytes=16 << 20),
        name="add",
    )(keep, got)
    weight_grads = pl.pallas_call(
        split_kernel,
        out_shape=(
            jax.ShapeDtypeStruct((width, half), F32),
            jax.ShapeDtypeStruct((width, half), F32),
            jax.ShapeDtypeStruct((width, half), F32),
            jax.ShapeDtypeStruct((half, width), F32),
        ),
        grid=(1,),
        name="split",
    )(part, other)

    return (back_blocks.reshape(1, rows_dev, half), *weight_grads)


def solution(mesh):
    placed = (
        P(("groups", "day"), "reach", None),
        P(("groups", "day"), "reach", None),
        P(None, "head"),
        P(None, "head"),
        P(None, "head"),
        P("head", None),
        P("groups"),
        P("groups"),
    )
    return jax.shard_map(
        on_device,
        mesh=mesh,
        in_specs=placed,
        out_specs=(
            P(("groups", "day"), "reach", "head"),
            P("groups", "head"),
            P("groups", "head"),
            P("groups", "head"),
            P(("groups", "head"), None),
        ),
        check_vma=False,
    )
```

time: 96.8 us -> 101 us (1.043)
  waiting for transfers between devices: 26.2 us -> 41.6 us
  starting transfers between devices: 30.8 us -> 24.7 us
  Pallas kernels: 34.1 us -> 28.9 us
    ppermute x7, waiting for transfers between devices: 10.6 us -> 24.7 us  [exchanged(): lax.ppermute(value, axis, [(place, place ^ bit) for place in range(count)])]
    all_to_all x4 -> x2, starting transfers between devices: 18.8 us -> 10.1 us  [ring(): return lax.all_to_all(value, 'reach', 0, 0, tiled=True).reshape(shape)]
    ppermute x1, waiting for transfers between devices: 0.01 us -> 7.4 us  [on_device(): prior_inputs = lax.ppermute(prior, 'day', next_day)]
    ppermute x2 -> x1, waiting for transfers between devices: 5.36 us -> 0.01 us  [on_device(): day_terms = lax.ppermute(day_terms, 'day', last_day)]
    pallas_call x4 -> x3, Pallas kernels: 28.8 us -> 23.7 us  [the longest x1 19.7 us: attend(): pl.pallas_call(lambda *refs: attention_kernel(lay, *refs), grid_spec=pltp...]
    ppermute x7, starting transfers between devices: 5.87 us -> 9.74 us  [exchanged(): lax.ppermute(value, axis, [(place, place ^ bit) for place in range(count)])]
    ppermute x2 -> x1, starting transfers between devices: 2.57 us -> 1.28 us  [on_device(): day_terms = lax.ppermute(day_terms, 'day', last_day)]
    all_to_all x4 -> x2, waiting for transfers between devices: 10.2 us -> 9.45 us  [ring(): return lax.all_to_all(value, 'reach', 0, 0, tiled=True).reshape(shape)]
  transfers between devices with their start and end apart: 14 -> 11, of which waited for: 10 -> 7; matrix products, arithmetic and copies ran while one was open for 1% -> 1% of each run, Pallas kernels for 31% -> 6%
where the time goes in v10:
time: 101 us
  waiting for transfers between devices  41.6 us (41%)
  Pallas kernels  28.9 us (29%)
  starting transfers between devices  24.7 us (24%)
  local copies, waits for them, and re-layouts  4.23 us (4%)
    ppermute x7, waiting for transfers between devices, exchanged(): lax.ppermute(value, axis, [(place, place ^ bit) for place in range(count)])  24.7 us
    pallas_call x1, Pallas kernels, attend(): pl.pallas_call(lambda *refs: attention_kernel(lay, *refs), grid_spec=pltp...  19.7 us
    all_to_all x2, starting transfers between devices, ring(): return lax.all_to_all(value, 'reach', 0, 0, tiled=True).reshape(shape)  10.1 us
    ppermute x7, starting transfers between devices, exchanged(): lax.ppermute(value, axis, [(place, place ^ bit) for place in range(count)])  9.74 us
    all_to_all x2, waiting for transfers between devices, ring(): return lax.all_to_all(value, 'reach', 0, 0, tiled=True).reshape(shape)  9.45 us
    ppermute x1, waiting for transfers between devices, on_device(): prior_inputs = lax.ppermute(prior, 'day', next_day)  7.4 us
    unnamed x37, local copies, waits for them, and re-layouts  4.23 us
    ppermute x1, starting transfers between devices, on_device(): prior_inputs = lax.ppermute(prior, 'day', next_day)  3.56 us
  transfers between devices with their start and end apart: 11, of which 7 were waited for; matrix products, arithmetic and copies ran while one was open for 1% of the time, Pallas kernels for 6%

profile of v10, /device:TPU:0, one launch (start us, length us, event | category | flops | bytes accessed | tf_op | source)
XLA Modules:
  0.0 100.5 jit_solution(12071113028949730949)
XLA Ops:
  0.6 2.5 %pick.1 = (bf16[16,128,256]{2,1,0:T(8,128)(2,1)}, s32[128]{0:T(128)S(1)}) custom-call(s32[64]{0:T(128)} %refs_0_.3, bf16[16,128,256]{2,1,0:T(8,128)(2,1)} %bitcast.11), custom_call_target="tpu_custom_call" | custom-call | tf_op jit(solution)/shard_map/pick/pallas_call | solution.py:426
  3.1 0.0 copy-start
  3.1 0.0 copy-start.4
  3.2 0.0 copy-start.5
  3.2 6.5 %all-to-all-start = ((bf16[4,512,256]{2,1,0:T(8,128)(2,1)}), bf16[4,512,256]{2,1,0:T(8,128)(2,1)S(1)}, u32[]{:S(2)}, u32[]{:S(2)}) async-start(bf16[4,512,256]{2,1,0:T(8,128)(2,1)} %bitcast.2), calls=%async_computation | async-start | bytes 2097152 | tf_op jit(solution)/shard_map/all_to_all | solution.py:461
  9.6 0.0 copy-done.4
  9.6 0.0 copy-start.10
  9.7 1.8 %deal.1 = (bf16[8,128,256]{2,1,0:T(8,128)(2,1)S(1)}, s32[128]{0:T(128)S(1)}) custom-call(s32[64]{0:T(128)S(1)} %copy-done.4, s32[64]{0:T(128)S(1)} %copy-done.5, bf16[16,128,256]{2,1,0:T(8,128)(2,1)S(1)} %bitcast.16), custom_call_target="tpu_custom_call" | custom-call | tf_op jit(solution)/shard_map/deal/pallas_call | solution.py:442
  11.5 0.0 copy-start.11
  11.5 3.6 %collective-permute-start = (bf16[8,128,256]{2,1,0:T(8,128)(2,1)S(1)}, bf16[8,128,256]{2,1,0:T(8,128)(2,1)S(1)}, u32[]{:S(2)}, u32[]{:S(2)}) collective-permute-start(bf16[8,128,256]{2,1,0:T(8,128)(2,1)S(1)} %get-tuple-element.26), channel_id=1, source_target_pairs={{0,2},{1,3},{4,6},{5,7},{8,10},{9,11},{12,14},{13,15},{16,18},{17,... | collective-permute-start | bytes 1572872 | tf_op jit(solution)/shard_map/ppermute | solution.py:466
  15.1 0.0 copy-done.10
  15.1 0.1 copy.15
  15.2 0.0 copy-start.12
  15.2 0.1 copy.14
  15.3 0.7 copy-done.12
  16.0 0.1 copy.13
  16.1 0.7 copy-done.13
  16.9 0.1 collective-permute-start.1
  17.0 1.5 %collective-permute-done.1.refs_18_ = bf16[512,256]{1,0:T(8,128)(2,1)S(1)} collective-permute-done((bf16[512,256]{1,0:T(8,128)(2,1)S(1)}, bf16[512,256]{1,0:T(8,128)(2,1)S(1)}, u32[]{:S(2)}, u32[]{:S(2)}) %collective-permute-start.1) | collective-permute-done | bytes 262176 | tf_op jit(solution)/shard_map/ppermute | solution.py:369
  18.5 7.4 %collective-permute-done.refs_4_.refs_8_.refs_12_.refs_16_ = bf16[8,128,256]{2,1,0:T(8,128)(2,1)S(1)} collective-permute-done((bf16[8,128,256]{2,1,0:T(8,128)(2,1)S(1)}, bf16[8,128,256]{2,1,0:T(8,128)(2,1)S(1)}, u32[]{:S(2)}, u32[]{:S(2)}) %collective-permute-start) | collective-permute-done | bytes 524320 | tf_op jit(solution)/shard_map/ppermute | solution.py:466
  25.9 9.4 %all-to-all-done = bf16[4,512,256]{2,1,0:T(8,128)(2,1)S(1)} async-done(((bf16[4,512,256]{2,1,0:T(8,128)(2,1)}), bf16[4,512,256]{2,1,0:T(8,128)(2,1)S(1)}, u32[]{:S(2)}, u32[]{:S(2)}) %all-to-all-start) | async-done | bytes 1048608 | tf_op jit(solution)/shard_map/all_to_all | solution.py:461
  35.4 0.0 copy-done.8
  35.4 19.7 %attention.1 = (f32[8,128,256]{2,1,0:T(8,128)}, bf16[8,128,256]{2,1,0:T(8,128)(2,1)}, bf16[16,128,256]{2,1,0:T(8,128)(2,1)}, f32[512,256]{1,0:T(8,128)}, f32[512,256]{1,0:T(8,128)}) custom-call(s32[128]{0:T(128)S(1)} %get-tuple-element.23.refs_0_, bf16[16,128,256]{2,1,0:T(8,128)(2,1)} %bitcast.12, bf16[16,128,256]{2,1,0:T(8,128)(2,1)} %bitcast.26, ...), custom_call_target="tpu_custom_call" | custom-call | flops 12750684160 | bytes 9437184 | tf_op jit(solution)/shard_map/attention/pallas_call | solution.py:330
  55.1 0.1 collective-permute-start.3
  55.1 0.0 copy-start.7
  55.2 3.7 %all-to-all-start.1 = ((bf16[4,512,256]{2,1,0:T(8,128)(2,1)}), bf16[4,512,256]{2,1,0:T(8,128)(2,1)S(1)}, u32[]{:S(2)}, u32[]{:S(2)}) async-start(bf16[4,512,256]{2,1,0:T(8,128)(2,1)} %bitcast.21), calls=%async_computation.1 | async-start | bytes 2097152 | tf_op jit(solution)/shard_map/all_to_all | solution.py:461
  58.8 0.0 collective-permute-done.3
  58.9 0.1 add.13
  59.0 1.6 %collective-permute-start.4 = (bf16[256,256]{1,0:T(8,128)(2,1)S(1)}, bf16[256,256]{1,0:T(8,128)(2,1)S(1)}, u32[]{:S(2)}, u32[]{:S(2)}) collective-permute-start(bf16[256,256]{1,0:T(8,128)(2,1)S(1)} %select_convert_fusion), channel_id=1, source_target_pairs={{0,2},{2,0},{1,3},{3,1},{4,6},{6,4},{5,7},{7,5},{8,10},{10,8},{9,1... | collective-permute-start | bytes 393224 | tf_op jit(solution)/shard_map/ppermute | solution.py:369
  60.5 4.4 %collective-permute-done.4 = bf16[256,256]{1,0:T(8,128)(2,1)S(1)} collective-permute-done((bf16[256,256]{1,0:T(8,128)(2,1)S(1)}, bf16[256,256]{1,0:T(8,128)(2,1)S(1)}, u32[]{:S(2)}, u32[]{:S(2)}) %collective-permute-start.4) | collective-permute-done | bytes 131104 | tf_op jit(solution)/shard_map/ppermute | solution.py:369
  64.9 0.1 add_convert_fusion.2
  65.0 1.7 %collective-permute-start.5 = (bf16[256,256]{1,0:T(8,128)(2,1)S(1)}, bf16[256,256]{1,0:T(8,128)(2,1)S(1)}, u32[]{:S(2)}, u32[]{:S(2)}) collective-permute-start(bf16[256,256]{1,0:T(8,128)(2,1)S(1)} %add_convert_fusion.2), channel_id=1, source_target_pairs={{0,4},{4,0},{8,12},{12,8},{1,5},{5,1},{9,13},{13,9},{2,6},{6,2},{1... | collective-permute-start | bytes 393224 | tf_op jit(solution)/shard_map/ppermute | solution.py:369
  66.7 1.3 %collective-permute-start.2 = (bf16[8,128,256]{2,1,0:T(8,128)(2,1)S(1)}, bf16[8,128,256]{2,1,0:T(8,128)(2,1)S(1)}, u32[]{:S(2)}, u32[]{:S(2)}) collective-permute-start(bf16[8,128,256]{2,1,0:T(8,128)(2,1)S(1)} %copy-done.14), channel_id=1, source_target_pairs={{2,0},{3,1},{6,4},{7,5},{10,8},{11,9},{14,12},{15,13},{18,16},{19,... | collective-permute-start | bytes 1572872 | tf_op jit(solution)/shard_map/ppermute | solution.py:472
  68.0 11.6 %collective-permute-done.5 = bf16[256,256]{1,0:T(8,128)(2,1)S(1)} collective-permute-done((bf16[256,256]{1,0:T(8,128)(2,1)S(1)}, bf16[256,256]{1,0:T(8,128)(2,1)S(1)}, u32[]{:S(2)}, u32[]{:S(2)}) %collective-permute-start.5) | collective-permute-done | bytes 131104 | tf_op jit(solution)/shard_map/ppermute | solution.py:369
  79.6 4.7 %collective-permute-start.6 = (bf16[256,256]{1,0:T(8,128)(2,1)S(1)}, bf16[256,256]{1,0:T(8,128)(2,1)S(1)}, u32[]{:S(2)}, u32[]{:S(2)}) collective-permute-start(bf16[256,256]{1,0:T(8,128)(2,1)S(1)} %add_convert_fusion.1), channel_id=1, source_target_pairs={{0,8},{4,12},{8,0},{12,4},{1,9},{5,13},{9,1},{13,5},{2,10},{6,14},... | collective-permute-start | bytes 393224 | tf_op jit(solution)/shard_map/ppermute | solution.py:369
  84.3 6.8 %collective-permute-done.6 = bf16[256,256]{1,0:T(8,128)(2,1)S(1)} collective-permute-done((bf16[256,256]{1,0:T(8,128)(2,1)S(1)}, bf16[256,256]{1,0:T(8,128)(2,1)S(1)}, u32[]{:S(2)}, u32[]{:S(2)}) %collective-permute-start.6) | collective-permute-done | bytes 131104 | tf_op jit(solution)/shard_map/ppermute | solution.py:369
  91.1 1.6 %collective-permute-start.7 = (bf16[256,256]{1,0:T(8,128)(2,1)S(1)}, bf16[256,256]{1,0:T(8,128)(2,1)S(1)}, u32[]{:S(2)}, u32[]{:S(2)}) collective-permute-start(bf16[256,256]{1,0:T(8,128)(2,1)S(1)} %add_convert_fusion.part), channel_id=1, source_target_pairs={{0,2},{2,0},{1,3},{3,1},{4,6},{6,4},{5,7},{7,5},{8,10},{10,8},{9,1... | collective-permute-start | bytes 393224 | tf_op jit(solution)/shard_map/ppermute | solution.py:369
  92.7 0.0 all-to-all-done.1
  92.7 0.0 collective-permute-done.2.refs_3_
  92.7 0.8 copy-done.2
  93.5 1.0 %copy-done.3 = bf16[8,128,256]{2,1,0:T(8,128)(2,1)S(1)} copy-done((bf16[8,128,256]{2,1,0:T(8,128)(2,1)S(1)}, bf16[8,128,256]{2,1,0:T(8,128)(2,1)}, u32[]{:S(2)}) %copy-start.3) | copy-done | bytes 524312
  94.5 2.2 %fold.1 = (f32[16,128,128]{2,1,0:T(8,128)S(1)}, f32[16,128,128]{2,1,0:T(8,128)}) custom-call(s32[128]{0:T(128)S(1)} %get-tuple-element.23.refs_0_, s32[128]{0:T(128)S(1)} %get-tuple-element.24.refs_1_, f32[8,128,256]{2,1,0:T(8,128)S(1)} %copy-done.1, bf16[8,128,256]{2,1,0:T(8,128)(2,1)S(1)} %copy-done.3, bf16[16,128,256]{2,1,0:T(8,128)(2,1)S(1)} %bitcast.10), custom_call_target="tpu_custom_call" | custom-call | tf_op jit(solution)/shard_map/fold/pallas_call | solution.py:477
  96.7 0.0 collective-permute-done.7.other
  96.7 0.1 collective-permute-start.8
  96.8 0.6 copy-done.9
  97.3 1.8 %split.1 = (f32[256,128]{1,0:T(8,128)}, f32[256,128]{1,0:T(8,128)}, f32[256,128]{1,0:T(8,128)}, f32[128,256]{1,0:T(8,128)}) custom-call(bf16[256,256]{1,0:T(8,128)(2,1)} %copy-done.6, bf16[256,256]{1,0:T(8,128)(2,1)} %copy-done.9), custom_call_target="tpu_custom_call" | custom-call | tf_op jit(solution)/shard_map/split/pallas_call | solution.py:495
  99.1 0.5 collective-permute-done.8.got
  99.6 0.9 add.20
  (23 shorter events, 0.1 us)
Async XLA Ops:
  3.1 6.5 %copy-start = (bf16[1,2048,256]{2,1,0:T(8,128)(2,1)S(1)}, bf16[1,2048,256]{2,1,0:T(8,128)(2,1)}, u32[]{:S(2)}) copy-start(bf16[1,2048,256]{2,1,0:T(8,128)(2,1)} %param.8) | copy-start | bytes 3145732
  3.1 6.5 %copy-start.4 = (s32[64]{0:T(128)S(1)}, s32[64]{0:T(128)}, u32[]{:S(2)}) copy-start(s32[64]{0:T(128)} %refs_0_.3) | copy-start | bytes 772
  3.2 6.5 %copy-start.5 = (s32[64]{0:T(128)S(1)}, s32[64]{0:T(128)}, u32[]{:S(2)}) copy-start(s32[64]{0:T(128)} %refs_1_.1) | copy-start | bytes 772
  3.2 32.2 %all-to-all-start = ((bf16[4,512,256]{2,1,0:T(8,128)(2,1)}), bf16[4,512,256]{2,1,0:T(8,128)(2,1)S(1)}, u32[]{:S(2)}, u32[]{:S(2)}) async-start(bf16[4,512,256]{2,1,0:T(8,128)(2,1)} %bitcast.2), calls=%async_computation | async-start | bytes 2097152 | tf_op jit(solution)/shard_map/all_to_all | solution.py:461
  9.6 5.4 %copy-start.10 = (bf16[256,128]{1,0:T(8,128)(2,1)S(1)}, bf16[256,128]{1,0:T(8,128)(2,1)}, u32[]{:S(2)}) copy-start(bf16[256,128]{1,0:T(8,128)(2,1)} %param.10) | copy-start | bytes 196612
  11.5 3.7 %copy-start.11 = (bf16[256,128]{1,0:T(8,128)(2,1)S(1)}, bf16[256,128]{1,0:T(8,128)(2,1)}, u32[]{:S(2)}) copy-start(bf16[256,128]{1,0:T(8,128)(2,1)} %param.12) | copy-start | bytes 196612
  11.5 14.4 %collective-permute-start = (bf16[8,128,256]{2,1,0:T(8,128)(2,1)S(1)}, bf16[8,128,256]{2,1,0:T(8,128)(2,1)S(1)}, u32[]{:S(2)}, u32[]{:S(2)}) collective-permute-start(bf16[8,128,256]{2,1,0:T(8,128)(2,1)S(1)} %get-tuple-element.26), channel_id=1, source_target_pairs={{0,2},{1,3},{4,6},{5,7},{8,10},{9,11},{12,14},{13,15},{16,18},{17,... | collective-permute-start | bytes 1572872 | tf_op jit(solution)/shard_map/ppermute | solution.py:466
  15.2 0.8 copy-start.12
  16.0 0.8 copy-start.13
  16.9 18.5 %copy-start.8 = (bf16[512,256]{1,0:T(8,128)(2,1)}, bf16[512,256]{1,0:T(8,128)(2,1)S(1)}, u32[]{:S(2)}) copy-start(bf16[512,256]{1,0:T(8,128)(2,1)S(1)} %pad_maximum_fusion.refs_17_) | copy-start | bytes 786436
  16.9 1.6 %collective-permute-start.1 = (bf16[512,256]{1,0:T(8,128)(2,1)S(1)}, bf16[512,256]{1,0:T(8,128)(2,1)S(1)}, u32[]{:S(2)}, u32[]{:S(2)}) collective-permute-start(bf16[512,256]{1,0:T(8,128)(2,1)S(1)} %pad_maximum_fusion.refs_17_), channel_id=1, source_target_pairs={{0,1},{1,0},{2,3},{3,2},{4,5},{5,4},{6,7},{7,6},{8,9},{9,8},{10,11... | collective-permute-start | bytes 786440 | tf_op jit(solution)/shard_map/ppermute | solution.py:369
  18.5 16.9 %copy-start.16 = (bf16[512,256]{1,0:T(8,128)(2,1)}, bf16[512,256]{1,0:T(8,128)(2,1)S(1)}, u32[]{:S(2)}) copy-start(bf16[512,256]{1,0:T(8,128)(2,1)S(1)} %collective-permute-done.1.refs_18_) | copy-start | bytes 786436
  25.9 9.5 %copy-start.15 = (bf16[8,128,256]{2,1,0:T(8,128)(2,1)}, bf16[8,128,256]{2,1,0:T(8,128)(2,1)S(1)}, u32[]{:S(2)}) copy-start(bf16[8,128,256]{2,1,0:T(8,128)(2,1)S(1)} %collective-permute-done.refs_4_.refs_8_.refs_12_.refs_16_) | copy-start | bytes 1572868
  55.1 3.8 %collective-permute-start.3 = (f32[512,256]{1,0:T(8,128)}, f32[512,256]{1,0:T(8,128)S(1)}, u32[]{:S(2)}, u32[]{:S(2)}) collective-permute-start(f32[512,256]{1,0:T(8,128)} %get-tuple-element.30), channel_id=1, source_target_pairs={{0,1},{1,0},{2,3},{3,2},{4,5},{5,4},{6,7},{7,6},{8,9},{9,8},{10,11... | collective-permute-start | bytes 1572872 | tf_op jit(solution)/shard_map/ppermute | solution.py:369
  55.1 3.7 %copy-start.7 = (f32[512,256]{1,0:T(8,128)S(1)}, f32[512,256]{1,0:T(8,128)}, u32[]{:S(2)}) copy-start(f32[512,256]{1,0:T(8,128)} %get-tuple-element.29) | copy-start | bytes 1572868
  55.2 37.5 %all-to-all-start.1 = ((bf16[4,512,256]{2,1,0:T(8,128)(2,1)}), bf16[4,512,256]{2,1,0:T(8,128)(2,1)S(1)}, u32[]{:S(2)}, u32[]{:S(2)}) async-start(bf16[4,512,256]{2,1,0:T(8,128)(2,1)} %bitcast.21), calls=%async_computation.1 | async-start | bytes 2097152 | tf_op jit(solution)/shard_map/all_to_all | solution.py:461
  58.9 7.9 %copy-start.14 = (bf16[8,128,256]{2,1,0:T(8,128)(2,1)S(1)}, bf16[8,128,256]{2,1,0:T(8,128)(2,1)}, u32[]{:S(2)}) copy-start(bf16[8,128,256]{2,1,0:T(8,128)(2,1)} %get-tuple-element.28) | copy-start | bytes 1572868
  58.9 34.5 %copy-start.1 = (f32[8,128,256]{2,1,0:T(8,128)S(1)}, f32[8,128,256]{2,1,0:T(8,128)}, u32[]{:S(2)}) copy-start(f32[8,128,256]{2,1,0:T(8,128)} %get-tuple-element.27.refs_2_) | copy-start | bytes 3145732
  59.0 5.9 %collective-permute-start.4 = (bf16[256,256]{1,0:T(8,128)(2,1)S(1)}, bf16[256,256]{1,0:T(8,128)(2,1)S(1)}, u32[]{:S(2)}, u32[]{:S(2)}) collective-permute-start(bf16[256,256]{1,0:T(8,128)(2,1)S(1)} %select_convert_fusion), channel_id=1, source_target_pairs={{0,2},{2,0},{1,3},{3,1},{4,6},{6,4},{5,7},{7,5},{8,10},{10,8},{9,1... | collective-permute-start | bytes 393224 | tf_op jit(solution)/shard_map/ppermute | solution.py:369
  65.0 14.6 %collective-permute-start.5 = (bf16[256,256]{1,0:T(8,128)(2,1)S(1)}, bf16[256,256]{1,0:T(8,128)(2,1)S(1)}, u32[]{:S(2)}, u32[]{:S(2)}) collective-permute-start(bf16[256,256]{1,0:T(8,128)(2,1)S(1)} %add_convert_fusion.2), channel_id=1, source_target_pairs={{0,4},{4,0},{8,12},{12,8},{1,5},{5,1},{9,13},{13,9},{2,6},{6,2},{1... | collective-permute-start | bytes 393224 | tf_op jit(solution)/shard_map/ppermute | solution.py:369
  66.7 25.9 %collective-permute-start.2 = (bf16[8,128,256]{2,1,0:T(8,128)(2,1)S(1)}, bf16[8,128,256]{2,1,0:T(8,128)(2,1)S(1)}, u32[]{:S(2)}, u32[]{:S(2)}) collective-permute-start(bf16[8,128,256]{2,1,0:T(8,128)(2,1)S(1)} %copy-done.14), channel_id=1, source_target_pairs={{2,0},{3,1},{6,4},{7,5},{10,8},{11,9},{14,12},{15,13},{18,16},{19,... | collective-permute-start | bytes 1572872 | tf_op jit(solution)/shard_map/ppermute | solution.py:472
  79.6 11.4 %collective-permute-start.6 = (bf16[256,256]{1,0:T(8,128)(2,1)S(1)}, bf16[256,256]{1,0:T(8,128)(2,1)S(1)}, u32[]{:S(2)}, u32[]{:S(2)}) collective-permute-start(bf16[256,256]{1,0:T(8,128)(2,1)S(1)} %add_convert_fusion.1), channel_id=1, source_target_pairs={{0,8},{4,12},{8,0},{12,4},{1,9},{5,13},{9,1},{13,5},{2,10},{6,14},... | collective-permute-start | bytes 393224 | tf_op jit(solution)/shard_map/ppermute | solution.py:369
  91.1 5.6 %copy-start.6 = (bf16[256,256]{1,0:T(8,128)(2,1)}, bf16[256,256]{1,0:T(8,128)(2,1)S(1)}, u32[]{:S(2)}) copy-start(bf16[256,256]{1,0:T(8,128)(2,1)S(1)} %add_convert_fusion.part) | copy-start | bytes 393220
  91.1 5.6 %collective-permute-start.7 = (bf16[256,256]{1,0:T(8,128)(2,1)S(1)}, bf16[256,256]{1,0:T(8,128)(2,1)S(1)}, u32[]{:S(2)}, u32[]{:S(2)}) collective-permute-start(bf16[256,256]{1,0:T(8,128)(2,1)S(1)} %add_convert_fusion.part), channel_id=1, source_target_pairs={{0,2},{2,0},{1,3},{3,1},{4,6},{6,4},{5,7},{7,5},{8,10},{10,8},{9,1... | collective-permute-start | bytes 393224 | tf_op jit(solution)/shard_map/ppermute | solution.py:369
  92.7 0.8 copy-start.2
  93.5 1.0 %copy-start.3 = (bf16[8,128,256]{2,1,0:T(8,128)(2,1)S(1)}, bf16[8,128,256]{2,1,0:T(8,128)(2,1)}, u32[]{:S(2)}) copy-start(bf16[8,128,256]{2,1,0:T(8,128)(2,1)} %copy-done.2) | copy-start | bytes 1572868
  96.7 0.7 copy-start.9
  96.7 2.9 %collective-permute-start.8 = (f32[16,128,128]{2,1,0:T(8,128)}, f32[16,128,128]{2,1,0:T(8,128)S(1)}, u32[]{:S(2)}, u32[]{:S(2)}) collective-permute-start(f32[16,128,128]{2,1,0:T(8,128)} %get-tuple-element.35), channel_id=1, source_target_pairs={{0,1},{1,0},{2,3},{3,2},{4,5},{5,4},{6,7},{7,6},{8,9},{9,8},{10,11... | collective-permute-start | bytes 3145736 | tf_op jit(solution)/shard_map/ppermute | solution.py:369

commit v11 on v10

--- a/solution.py
+++ b/solution.py
@@ -9,6 +9,8 @@
 BLOCK = 128
 GROUP = 128
 CORES = 2
+CHUNKS = 2
+WORKERS = CORES * CHUNKS
 F32 = jnp.float32
 BF16 = jnp.bfloat16
 PACK = 4
@@ -20,8 +22,9 @@
     def __init__(self, blocks_dev, reach_total):
         self.blocks = blocks_dev
         self.items = blocks_dev // CORES
+        self.chunk_items = self.items // CHUNKS
         self.reach = reach_total
-        self.slots = max(1, 2 * blocks_dev // reach_total // CORES)
+        self.slots = max(1, 2 * blocks_dev // reach_total // WORKERS)
         self.places = reach_total * self.slots
         self.block_of = 0
         self.recv_of = self.items
@@ -29,13 +32,15 @@
         self.count_partner = 3 * self.items
         self.owner_of = 4 * self.items
         self.item_of = self.owner_of + blocks_dev
-        self.later_day = self.item_of + blocks_dev
-        self.size = -(-(self.later_day + 1) // 128) * 128
+        self.core = self.item_of + blocks_dev
+        self.later_day = self.core + 1
+        self.size = -(-(self.core + 2) // 128) * 128
         self.spare = blocks_dev
         self.home_of = 0
-        self.asker_of = blocks_dev + 1
-        self.picks = 2 * (blocks_dev + 1)
-        self.spare_pick = self.picks + self.places
+        self.chunk_of = blocks_dev + 1
+        self.asker_of = 2 * (blocks_dev + 1)
+        self.picks = 3 * (blocks_dev + 1)
+        self.spare_pick = self.picks + CHUNKS * self.places
         self.homes_size = -(-(self.spare_pick + 1) // 128) * 128
 
 
@@ -46,7 +51,7 @@
     table_copy.start()
     copy = pltpu.make_async_copy(inputs, held, sems.at[1])
     copy.start()
-    for place in range(lay.places):
+    for place in range(CHUNKS * lay.places):
         homes[lay.picks + place] = 0
     table_copy.wait()
 
@@ -62,11 +67,14 @@
         for hit, local in wanted:
             place = base + rank
             owner = lax.rem(place, CORES)
-            slot = peer * slots + jnp.minimum(lax.div(rank, CORES), slots - 1)
+            chunk = lax.rem(lax.div(place, CORES), CHUNKS)
+            slot = peer * slots + jnp.minimum(lax.div(rank, WORKERS), slots - 1)
             target = jnp.where(hit, local, lay.spare)
             homes[lay.home_of + target] = slot
+            homes[lay.chunk_of + target] = chunk
             homes[lay.asker_of + target] = owner
-            homes[jnp.where(hit & (owner == core), lay.picks + slot, lay.spare_pick)] = local
+            pick = lay.picks + chunk * lay.places + slot
+            homes[jnp.where(hit & (owner == core), pick, lay.spare_pick)] = local
             rank = rank + jnp.where(hit, 1, 0)
         return carry
 
@@ -76,7 +84,7 @@
         sent[place] = held[homes[lay.picks + place]]
 
 
-def deal_kernel(lay, partner, counts, inputs, prior, tab, start, used):
+def deal_kernel(lay, partner, counts, homes, inputs, sent, prior, tab, start, used):
     bd, slots = lay.blocks, lay.slots
     reach_pos, core = lax.axis_index("reach"), lax.axis_index("head")
 
@@ -108,8 +116,9 @@
         used[source] = rank + 1
         place = start[source] + rank
         owner = lax.rem(place, CORES)
-        item = lax.div(place, CORES)
-        slot = jnp.minimum(lax.div(rank, CORES), slots - 1)
+        chunk = lax.rem(lax.div(place, CORES), CHUNKS)
+        item = chunk * lay.chunk_items + lax.div(place, WORKERS)
+        slot = jnp.minimum(lax.div(rank, WORKERS), slots - 1)
         tab[lay.owner_of + index] = owner
         tab[lay.item_of + index] = item
 
@@ -123,12 +132,18 @@
         return carry
 
     lax.fori_loop(0, bd, assign, 0)
+    tab[lay.core] = core
     tab[lay.later_day] = jnp.where(lax.axis_index("day") > 0, 1, 0)
+
+    def pick(place, carry):
+        sent[place] = inputs[homes[lay.picks + lay.places + place]]
+        return carry
 
     def pick_prior(item, carry):
         prior[item] = inputs[tab[lay.block_of + item]]
         return carry
 
+    lax.fori_loop(0, lay.places, pick, 0)
     lax.fori_loop(0, lay.items, pick_prior, 0)
 
 
@@ -140,18 +155,24 @@
     return lax.dot_general(left, right, (((1,), (1,)), ((), ())), preferred_element_type=F32)
 
 
-def attention_kernel(lay, tab, *refs):
+def attention_kernel(lay, chunk, tab, *refs):
     step = pl.program_id(0)
     read, refs = refs[: 4 * STEP_ITEMS], refs[4 * STEP_ITEMS :]
     mine_ref, other_ref, *refs = refs
+    if chunk:
+        start_mine_ref, start_other_ref, *refs = refs
     own_out_ref, day_ref, home_ref, grad_mine_ref, grad_other_ref = refs
     factor = HD ** (-0.5)
     per_group = GROUP // HD // PACK
 
     @pl.when(step == 0)
     def _():
-        grad_mine_ref[...] = jnp.zeros_like(grad_mine_ref)
-        grad_other_ref[...] = jnp.zeros_like(grad_other_ref)
+        if chunk:
+            grad_mine_ref[...] = start_mine_ref[...]
+            grad_other_ref[...] = start_other_ref[...]
+        else:
+            grad_mine_ref[...] = jnp.zeros_like(grad_mine_ref)
+            grad_other_ref[...] = jnp.zeros_like(grad_other_ref)
 
     rows = lax.broadcasted_iota(jnp.int32, (BLOCK, PACK * BLOCK), 0)
     lane_head = lax.broadcasted_iota(jnp.int32, (BLOCK, GROUP), 1) // HD
@@ -165,7 +186,7 @@
         it = Item()
         own_ref, up_ref, partner_ref, prior_ref = read[4 * place : 4 * place + 4]
         it.place = place
-        item = step * STEP_ITEMS + place
+        item = step * STEP_ITEMS + place + chunk * lay.chunk_items
         it.item = item
         it.own, it.up = own_ref[0], up_ref[0]
         it.inputs = jnp.concatenate([it.own, partner_ref[0], prior_ref[0]], axis=0)
@@ -271,16 +292,22 @@
     end(waiting[0])
 
 
-def fold_kernel(lay, tab, homes, own_terms, day_terms, home_terms, keep, give):
-    core = lax.axis_index("head")
+def fold_kernel(lay, tab, homes, own_a, own_b, day_a, day_b, home_a, home_b, keep, give):
+    core = tab[lay.core]
     half = keep.shape[2]
 
     def one(block, carry):
         item = tab[lay.item_of + block]
         mine = tab[lay.owner_of + block] == core
+        place = homes[lay.home_of + block]
         asked = homes[lay.asker_of + block] == core
-        own = own_terms[item] + day_terms[item].astype(F32)
-        home = home_terms[homes[lay.home_of + block]].astype(F32)
+        early = homes[lay.chunk_of + block] == 0
+        in_a = item < lay.chunk_items
+        item_a = jnp.minimum(item, lay.chunk_items - 1)
+        item_b = jnp.maximum(item - lay.chunk_items, 0)
+        own = jnp.where(in_a, own_a[item_a], own_b[item_b])
+        own += jnp.where(in_a, day_a[item_a].astype(F32), day_b[item_b].astype(F32))
+        home = jnp.where(early, home_a[place].astype(F32), home_b[place].astype(F32))
         total = jnp.where(mine, own, 0.0) + jnp.where(asked, home, 0.0)
         low, high = total[:, :half], total[:, half:]
         keep[block] = jnp.where(core == 0, low, high)
@@ -294,17 +321,18 @@
     out[...] = (kept[...] + got[...]).astype(BF16)
 
 
-def attend(lay, tab, in_blocks, up_blocks, received, prior_inputs, pack, pack_other):
+def attend(lay, chunk, tab, in_blocks, up_blocks, received, prior_inputs, pack, pack_other, carried):
     width = in_blocks.shape[-1]
+    offset = chunk * lay.chunk_items
 
     def at_item(place):
-        return lambda step, tab: (step * STEP_ITEMS + place, 0, 0)
+        return lambda step, tab: (offset + step * STEP_ITEMS + place, 0, 0)
 
     def at_block(place):
-        return lambda step, tab: (tab[lay.block_of + step * STEP_ITEMS + place], 0, 0)
+        return lambda step, tab: (tab[lay.block_of + offset + step * STEP_ITEMS + place], 0, 0)
 
     def at_recv(place):
-        return lambda step, tab: (tab[lay.recv_of + step * STEP_ITEMS + place], 0, 0)
+        return lambda step, tab: (tab[lay.recv_of + offset + step * STEP_ITEMS + place], 0, 0)
 
     def at_step(step, tab):
         return (step, 0, 0)
@@ -325,10 +353,13 @@
         operands += [in_blocks, up_blocks, received, prior_inputs]
     in_specs += [pl.BlockSpec(weights_block, fixed)] * 2
     operands += [pack, pack_other]
-    pieces = lay.items
+    if chunk:
+        in_specs += [pl.BlockSpec(weights_block, fixed)] * 2
+        operands += carried
+    pieces = lay.chunk_items
     flops = 2 * pieces * (23 * BLOCK * width * width + 24 * BLOCK * 3 * BLOCK * 512)
     return pl.pallas_call(
-        lambda *refs: attention_kernel(lay, *refs),
+        lambda *refs: attention_kernel(lay, chunk, *refs),
         grid_spec=pltpu.PrefetchScalarGridSpec(
             num_scalar_prefetch=1,
             grid=(pieces // STEP_ITEMS,),
@@ -350,9 +381,9 @@
         ),
         compiler_params=pltpu.CompilerParams(vmem_limit_bytes=32 << 20),
         cost_estimate=pl.CostEstimate(
-            flops=flops, bytes_accessed=9 << 20, transcendentals=pieces * 8 * BLOCK * 3 * BLOCK
+            flops=flops, bytes_accessed=5 << 20, transcendentals=pieces * 8 * BLOCK * 3 * BLOCK
         ),
-        name="attention",
+        name=f"attention_{chunk}",
     )(
         tab,
         *[
@@ -374,12 +405,14 @@
     return low.astype(F32) + exchanged(low, axis, bit).astype(F32)
 
 
-def sum_gradients(total):
+def sum_gradients(total, early, home_b, ring):
     half = total.shape[0] // 2
     first = lax.rem(lax.axis_index("day"), 2) == 0
     kept = jnp.where(first, total[:half], total[half:])
-    given = jnp.where(first, total[half:], total[:half])
-    part = kept.astype(BF16).astype(F32) + exchanged(given.astype(BF16), "day", 1).astype(F32)
+    given = jnp.where(first, total[half:], total[:half]).astype(BF16)
+    given, early, home_b = lax.optimization_barrier((given, early, home_b))
+    home_b = ring(home_b)
+    part = kept.astype(BF16).astype(F32) + exchanged(given, "day", 1).astype(F32)
     bit = 2
     while bit < lax.axis_size("day"):
         part = summed_over(part, "day", bit)
@@ -389,7 +422,8 @@
         part = summed_over(part, "reach", bit)
         bit *= 2
     part = part.astype(BF16)
-    return part, exchanged(part, "day", 1)
+    part, home_b = lax.optimization_barrier((part, home_b))
+    return part, exchanged(part, "day", 1), early, home_b
 
 
 def split_kernel(part, other, query_out, key_out, value_out, output_out):
@@ -423,7 +457,7 @@
     in_vmem = pl.BlockSpec(memory_space=pltpu.VMEM)
     anywhere = pl.BlockSpec(memory_space=pl.ANY)
     sent_shape = jax.ShapeDtypeStruct((lay.places, BLOCK, width), BF16)
-    sent, homes = pl.pallas_call(
+    sent_a, homes = pl.pallas_call(
         lambda *refs: pick_kernel(lay, *refs),
         out_shape=(sent_shape, jax.ShapeDtypeStruct((lay.homes_size,), jnp.int32)),
         in_specs=[anywhere, anywhere],
@@ -439,21 +473,22 @@
         pltpu.with_memory_space_constraint(partner, pltpu.HBM),
         pltpu.with_memory_space_constraint(in_blocks, pltpu.HBM),
     )
-    prior, tab = pl.pallas_call(
+    sent_b, prior, tab = pl.pallas_call(
         lambda *refs: deal_kernel(lay, *refs),
         out_shape=(
+            sent_shape,
             jax.ShapeDtypeStruct((lay.items, BLOCK, width), BF16),
             jax.ShapeDtypeStruct((lay.size,), jnp.int32),
         ),
-        in_specs=[smem, smem, in_vmem],
-        out_specs=(in_vmem, smem),
+        in_specs=[smem, smem, smem, in_vmem],
+        out_specs=(in_vmem, in_vmem, smem),
         scratch_shapes=[
             pltpu.SMEM((lay.reach,), jnp.int32),
             pltpu.SMEM((lay.reach,), jnp.int32),
         ],
         compiler_params=pltpu.CompilerParams(vmem_limit_bytes=16 << 20),
         name="deal",
-    )(partner, counts, in_blocks)
+    )(partner, counts, homes, in_blocks)
 
     def ring(value):
         shape = value.shape
@@ -462,26 +497,31 @@
 
     next_day = [(d, d + 1) for d in range(day_total - 1)]
     last_day = [(d + 1, d) for d in range(day_total - 1)]
-    received = ring(sent)
+    received_a = ring(sent_a)
     prior_inputs = lax.ppermute(prior, "day", next_day)
-    own_terms, day_terms, home_terms, grad_mine, grad_other = attend(
-        lay, tab, in_blocks, up_blocks, received, prior_inputs, pack, pack_other
+    received_b = ring(sent_b)
+    shared = (prior_inputs, pack, pack_other)
+    own_a, day_a, home_a, *grads = attend(
+        lay, 0, tab, in_blocks, up_blocks, received_a, *shared, None
     )
-    home_terms = ring(home_terms)
+    home_a = ring(home_a)
+    day_a = lax.ppermute(day_a, "day", last_day)
+    own_b, day_b, home_b, grad_mine, grad_other = attend(
+        lay, 1, tab, in_blocks, up_blocks, received_b, *shared, grads
+    )
     grad_swapped = exchanged(grad_other, "head", 1)
-    day_terms = lax.ppermute(day_terms, "day", last_day)
+    day_b = lax.ppermute(day_b, "day", last_day)
     half_shape = jax.ShapeDtypeStruct((blocks_dev, BLOCK, half), F32)
 
-    part, other = sum_gradients(grad_mine + grad_swapped)
-    _, home_terms = lax.optimization_barrier((part, home_terms))
+    part, other, home_a, home_b = sum_gradients(grad_mine + grad_swapped, home_a, home_b, ring)
     keep, give = pl.pallas_call(
         lambda *refs: fold_kernel(lay, *refs),
         out_shape=(half_shape, half_shape),
-        in_specs=[smem] * 2 + [in_vmem] * 3,
+        in_specs=[smem] * 2 + [in_vmem] * 6,
         out_specs=[in_vmem] * 2,
         compiler_params=pltpu.CompilerParams(vmem_limit_bytes=16 << 20),
         name="fold",
-    )(tab, homes, own_terms, day_terms, home_terms)
+    )(tab, homes, own_a, own_b, day_a, day_b, home_a, home_b)
     other, give = lax.optimization_barrier((other, give))
     got = exchanged(give, "head", 1)
     back_blocks = pl.pallas_call(

time: 101 us -> 107 us (1.059)
  waiting for transfers between devices: 41.6 us -> 33.2 us
  starting transfers between devices: 24.7 us -> 32.7 us
  Pallas kernels: 28.9 us -> 32.7 us
  local copies, waits for them, and re-layouts: 4.23 us -> 5.63 us
    ppermute x1 -> x2, waiting for transfers between devices: 0.01 us -> 9.69 us  [the longest x1 5.57 us: on_device(): day_b = lax.ppermute(day_b, 'day', last_day)]
    ppermute x7, waiting for transfers between devices: 24.7 us -> 15.5 us  [exchanged(): lax.ppermute(value, axis, [(place, place ^ bit) for place in range(count)])]
    all_to_all x2 -> x4, starting transfers between devices: 10.1 us -> 18.4 us  [ring(): return lax.all_to_all(value, 'reach', 0, 0, tiled=True).reshape(shape)]
    ppermute x1, waiting for transfers between devices: 7.4 us -> 0.01 us  [on_device(): prior_inputs = lax.ppermute(prior, 'day', next_day)]
    pallas_call x2 -> x3, Pallas kernels: 21.5 us -> 24.8 us  [the longest x2 22.7 us: attend(): pl.pallas_call(lambda *refs: attention_kernel(lay, chunk, *refs), grid_sp...]
    ppermute x7, starting transfers between devices: 9.74 us -> 8.17 us  [exchanged(): lax.ppermute(value, axis, [(place, place ^ bit) for place in range(count)])]
    all_to_all x2 -> x4, waiting for transfers between devices: 9.45 us -> 8 us  [ring(): return lax.all_to_all(value, 'reach', 0, 0, tiled=True).reshape(shape)]
    unnamed x37 -> x39, local copies, waits for them, and re-layouts: 4.23 us -> 5.63 us
  transfers between devices with their start and end apart: 11 -> 14, of which waited for: 7 -> 8; matrix products, arithmetic and copies ran while one was open for 1% -> 2% of each run, Pallas kernels for 6% -> 27%
where the time goes in v11:
time: 107 us; the launch traced here: 106 us
  waiting for transfers between devices  33.2 us (31%)
  Pallas kernels  32.7 us (31%)
  starting transfers between devices  32.7 us (31%)
  local copies, waits for them, and re-layouts  5.63 us (5%)
  other arithmetic  1.28 us (1%)
    pallas_call x2, Pallas kernels, attend(): pl.pallas_call(lambda *refs: attention_kernel(lay, chunk, *refs), grid_sp...  22.7 us
    all_to_all x4, starting transfers between devices, ring(): return lax.all_to_all(value, 'reach', 0, 0, tiled=True).reshape(shape)  18.4 us
    ppermute x7, waiting for transfers between devices, exchanged(): lax.ppermute(value, axis, [(place, place ^ bit) for place in range(count)])  15.5 us
    ppermute x7, starting transfers between devices, exchanged(): lax.ppermute(value, axis, [(place, place ^ bit) for place in range(count)])  8.17 us
    all_to_all x4, waiting for transfers between devices, ring(): return lax.all_to_all(value, 'reach', 0, 0, tiled=True).reshape(shape)  8 us
    unnamed x39, local copies, waits for them, and re-layouts  5.63 us
    ppermute x1, waiting for transfers between devices, on_device(): day_b = lax.ppermute(day_b, 'day', last_day)  5.57 us
    ppermute x1, waiting for transfers between devices, on_device(): day_a = lax.ppermute(day_a, 'day', last_day)  4.12 us
  transfers between devices with their start and end apart: 14, of which 8 were waited for; matrix products, arithmetic and copies ran while one was open for 2% of the time, Pallas kernels for 27%

profile of v11, /device:TPU:0, one launch (start us, length us, event | category | flops | bytes accessed | tf_op | source)
XLA Modules:
  0.0 106.5 jit_solution(17568846068540644633)
XLA Ops:
  0.6 0.0 copy-start
  0.6 2.6 %pick.1 = (bf16[8,128,256]{2,1,0:T(8,128)(2,1)}, s32[128]{0:T(128)S(1)}) custom-call(s32[64]{0:T(128)} %refs_0_.3, bf16[16,128,256]{2,1,0:T(8,128)(2,1)} %bitcast.14), custom_call_target="tpu_custom_call" | custom-call | tf_op jit(solution)/shard_map/pick/pallas_call | solution.py:460
  3.3 6.3 %all-to-all-start = ((bf16[4,256,256]{2,1,0:T(8,128)(2,1)}), bf16[4,256,256]{2,1,0:T(8,128)(2,1)S(1)}, u32[]{:S(2)}, u32[]{:S(2)}) async-start(bf16[4,256,256]{2,1,0:T(8,128)(2,1)} %bitcast.2), calls=%async_computation | async-start | bytes 1048576 | tf_op jit(solution)/shard_map/all_to_all | solution.py:496
  9.6 0.6 copy-done.5
  10.2 0.0 copy-done.6
  10.3 2.2 %deal.1 = (bf16[8,128,256]{2,1,0:T(8,128)(2,1)}, bf16[8,128,256]{2,1,0:T(8,128)(2,1)S(1)}, s32[128]{0:T(128)S(1)}) custom-call(s32[64]{0:T(128)S(1)} %copy-done.5, s32[64]{0:T(128)S(1)} %copy-done.6, s32[128]{0:T(128)S(1)} %get-tuple-element.33.refs_2_.refs_1_, bf16[16,128,256]{2,1,0:T(8,128)(2,1)S(1)} %bitcast.23), custom_call_target="tpu_custom_call" | custom-call | tf_op jit(solution)/shard_map/deal/pallas_call | solution.py:476
  12.5 0.0 copy-start.11
  12.5 3.6 %collective-permute-start = (bf16[8,128,256]{2,1,0:T(8,128)(2,1)S(1)}, bf16[8,128,256]{2,1,0:T(8,128)(2,1)S(1)}, u32[]{:S(2)}, u32[]{:S(2)}) collective-permute-start(bf16[8,128,256]{2,1,0:T(8,128)(2,1)S(1)} %get-tuple-element.36), channel_id=1, source_target_pairs={{0,2},{1,3},{4,6},{5,7},{8,10},{9,11},{12,14},{13,15},{16,18},{17,... | collective-permute-start | bytes 1572872 | tf_op jit(solution)/shard_map/ppermute | solution.py:501
  16.0 0.1 copy.13
  16.2 0.0 copy-start.12
  16.2 0.1 copy.14
  16.3 0.7 copy-done.12
  17.0 0.1 copy.15
  17.1 0.7 copy-done.13
  17.9 0.1 collective-permute-start.1
  18.0 6.1 %all-to-all-done = bf16[4,256,256]{2,1,0:T(8,128)(2,1)S(1)} async-done(((bf16[4,256,256]{2,1,0:T(8,128)(2,1)}), bf16[4,256,256]{2,1,0:T(8,128)(2,1)S(1)}, u32[]{:S(2)}, u32[]{:S(2)}) %all-to-all-start) | async-done | bytes 524320 | tf_op jit(solution)/shard_map/all_to_all | solution.py:496
  24.1 3.5 %all-to-all-start.1 = ((bf16[4,256,256]{2,1,0:T(8,128)(2,1)}), bf16[4,256,256]{2,1,0:T(8,128)(2,1)S(1)}, u32[]{:S(2)}, u32[]{:S(2)}) async-start(bf16[4,256,256]{2,1,0:T(8,128)(2,1)} %bitcast.7), calls=%async_computation.1 | async-start | bytes 1048576 | tf_op jit(solution)/shard_map/all_to_all | solution.py:496
  27.6 0.0 collective-permute-done.refs_4_.refs_8_.refs_12_.refs_16_
  27.6 0.0 copy-start.14
  27.6 0.7 copy-done.17
  28.3 0.2 copy-done.14
  28.4 11.2 %attention_0.1 = (f32[4,128,256]{2,1,0:T(8,128)}, bf16[4,128,256]{2,1,0:T(8,128)(2,1)}, bf16[8,128,256]{2,1,0:T(8,128)(2,1)}, f32[512,256]{1,0:T(8,128)}, f32[512,256]{1,0:T(8,128)}) custom-call(s32[128]{0:T(128)S(1)} %get-tuple-element.34.refs_0_, bf16[16,128,256]{2,1,0:T(8,128)(2,1)} %bitcast.15, bf16[16,128,256]{2,1,0:T(8,128)(2,1)} %bitcast.39, ...), custom_call_target="tpu_custom_call" | custom-call | flops 6375342080 | bytes 5242880 | tf_op jit(solution)/shard_map/attention_0/pallas_call | solution.py:361
  39.6 1.9 %all-to-all-done.1 = bf16[4,256,256]{2,1,0:T(8,128)(2,1)S(1)} async-done(((bf16[4,256,256]{2,1,0:T(8,128)(2,1)}), bf16[4,256,256]{2,1,0:T(8,128)(2,1)S(1)}, u32[]{:S(2)}, u32[]{:S(2)}) %all-to-all-start.1) | async-done | bytes 524320 | tf_op jit(solution)/shard_map/all_to_all | solution.py:496
  41.5 3.6 %all-to-all-start.2 = ((bf16[4,256,256]{2,1,0:T(8,128)(2,1)}), bf16[4,256,256]{2,1,0:T(8,128)(2,1)S(1)}, u32[]{:S(2)}, u32[]{:S(2)}) async-start(bf16[4,256,256]{2,1,0:T(8,128)(2,1)} %bitcast.35), calls=%async_computation.2 | async-start | bytes 1048576 | tf_op jit(solution)/shard_map/all_to_all | solution.py:496
  45.2 11.5 %attention_1.1 = (f32[4,128,256]{2,1,0:T(8,128)}, bf16[4,128,256]{2,1,0:T(8,128)(2,1)}, bf16[8,128,256]{2,1,0:T(8,128)(2,1)}, f32[512,256]{1,0:T(8,128)}, f32[512,256]{1,0:T(8,128)}) custom-call(s32[128]{0:T(128)S(1)} %get-tuple-element.34.refs_0_, bf16[16,128,256]{2,1,0:T(8,128)(2,1)} %bitcast.19, bf16[16,128,256]{2,1,0:T(8,128)(2,1)} %bitcast.43, ...), custom_call_target="tpu_custom_call" | custom-call | flops 6375342080 | bytes 5242880 | tf_op jit(solution)/shard_map/attention_1/pallas_call | solution.py:361
  56.6 0.0 collective-permute-start.4
  56.7 2.1 %collective-permute-done.4 = f32[512,256]{1,0:T(8,128)S(1)} collective-permute-done((f32[512,256]{1,0:T(8,128)}, f32[512,256]{1,0:T(8,128)S(1)}, u32[]{:S(2)}, u32[]{:S(2)}) %collective-permute-start.4) | collective-permute-done | bytes 524320 | tf_op jit(solution)/shard_map/ppermute | solution.py:400
  58.8 1.1 %add.13 = bf16[512,256]{1,0:T(8,128)(2,1)S(1)} add(f32[512,256]{1,0:T(8,128)} %get-tuple-element.44, f32[512,256]{1,0:T(8,128)S(1)} %collective-permute-done.4) | non-fusion elementwise | flops 131072 | bytes 1310720 | tf_op jit(solution)/shard_map/add | solution.py:516
  59.9 0.0 all-to-all-done.2
  59.9 1.6 %collective-permute-start.5 = (bf16[256,256]{1,0:T(8,128)(2,1)S(1)}, bf16[256,256]{1,0:T(8,128)(2,1)S(1)}, u32[]{:S(2)}, u32[]{:S(2)}) collective-permute-start(bf16[256,256]{1,0:T(8,128)(2,1)S(1)} %select_convert_fusion.1), channel_id=1, source_target_pairs={{0,2},{2,0},{1,3},{3,1},{4,6},{6,4},{5,7},{7,5},{8,10},{10,8},{9,1... | collective-permute-start | bytes 393224 | tf_op jit(solution)/shard_map/ppermute | solution.py:400
  61.5 5.0 %all-to-all-start.3 = ((bf16[4,256,256]{2,1,0:T(8,128)(2,1)}), bf16[4,256,256]{2,1,0:T(8,128)(2,1)S(1)}, u32[]{:S(2)}, u32[]{:S(2)}) async-start(bf16[4,256,256]{2,1,0:T(8,128)(2,1)} %bitcast.11), calls=%async_computation.3 | async-start | bytes 1048576 | tf_op jit(solution)/shard_map/all_to_all | solution.py:496
  66.5 0.1 add_convert_fusion.2
  66.6 2.1 %collective-permute-start.6 = (bf16[256,256]{1,0:T(8,128)(2,1)S(1)}, bf16[256,256]{1,0:T(8,128)(2,1)S(1)}, u32[]{:S(2)}, u32[]{:S(2)}) collective-permute-start(bf16[256,256]{1,0:T(8,128)(2,1)S(1)} %add_convert_fusion.2), channel_id=1, source_target_pairs={{0,4},{4,0},{8,12},{12,8},{1,5},{5,1},{9,13},{13,9},{2,6},{6,2},{1... | collective-permute-start | bytes 393224 | tf_op jit(solution)/shard_map/ppermute | solution.py:400
  68.6 10.1 %collective-permute-done.6 = bf16[256,256]{1,0:T(8,128)(2,1)S(1)} collective-permute-done((bf16[256,256]{1,0:T(8,128)(2,1)S(1)}, bf16[256,256]{1,0:T(8,128)(2,1)S(1)}, u32[]{:S(2)}, u32[]{:S(2)}) %collective-permute-start.6) | collective-permute-done | bytes 131104 | tf_op jit(solution)/shard_map/ppermute | solution.py:400
  78.8 3.8 %collective-permute-start.7 = (bf16[256,256]{1,0:T(8,128)(2,1)S(1)}, bf16[256,256]{1,0:T(8,128)(2,1)S(1)}, u32[]{:S(2)}, u32[]{:S(2)}) collective-permute-start(bf16[256,256]{1,0:T(8,128)(2,1)S(1)} %add_convert_fusion.1), channel_id=1, source_target_pairs={{0,8},{4,12},{8,0},{12,4},{1,9},{5,13},{9,1},{13,5},{2,10},{6,14},... | collective-permute-start | bytes 393224 | tf_op jit(solution)/shard_map/ppermute | solution.py:400
  82.6 1.3 %collective-permute-start.3 = (bf16[4,128,256]{2,1,0:T(8,128)(2,1)S(1)}, bf16[4,128,256]{2,1,0:T(8,128)(2,1)S(1)}, u32[]{:S(2)}, u32[]{:S(2)}) collective-permute-start(bf16[4,128,256]{2,1,0:T(8,128)(2,1)S(1)} %copy-done.16), channel_id=1, source_target_pairs={{2,0},{3,1},{6,4},{7,5},{10,8},{11,9},{14,12},{15,13},{18,16},{19,... | collective-permute-start | bytes 786440 | tf_op jit(solution)/shard_map/ppermute | solution.py:513
  83.9 1.3 %collective-permute-start.2 = (bf16[4,128,256]{2,1,0:T(8,128)(2,1)S(1)}, bf16[4,128,256]{2,1,0:T(8,128)(2,1)S(1)}, u32[]{:S(2)}, u32[]{:S(2)}) collective-permute-start(bf16[4,128,256]{2,1,0:T(8,128)(2,1)S(1)} %copy-done.15), channel_id=1, source_target_pairs={{2,0},{3,1},{6,4},{7,5},{10,8},{11,9},{14,12},{15,13},{18,16},{19,... | collective-permute-start | bytes 786440 | tf_op jit(solution)/shard_map/ppermute | solution.py:508
  85.2 2.3 %collective-permute-done.7 = bf16[256,256]{1,0:T(8,128)(2,1)S(1)} collective-permute-done((bf16[256,256]{1,0:T(8,128)(2,1)S(1)}, bf16[256,256]{1,0:T(8,128)(2,1)S(1)}, u32[]{:S(2)}, u32[]{:S(2)}) %collective-permute-start.7) | collective-permute-done | bytes 131104 | tf_op jit(solution)/shard_map/ppermute | solution.py:400
  87.5 0.6 collective-permute-start.8
  88.2 5.6 %collective-permute-done.3.refs_5_ = bf16[4,128,256]{2,1,0:T(8,128)(2,1)S(1)} collective-permute-done((bf16[4,128,256]{2,1,0:T(8,128)(2,1)S(1)}, bf16[4,128,256]{2,1,0:T(8,128)(2,1)S(1)}, u32[]{:S(2)}, u32[]{:S(2)}) %collective-permute-start.3) | collective-permute-done | bytes 262176 | tf_op jit(solution)/shard_map/ppermute | solution.py:513
  93.7 4.1 %collective-permute-done.2.refs_4_ = bf16[4,128,256]{2,1,0:T(8,128)(2,1)S(1)} collective-permute-done((bf16[4,128,256]{2,1,0:T(8,128)(2,1)S(1)}, bf16[4,128,256]{2,1,0:T(8,128)(2,1)S(1)}, u32[]{:S(2)}, u32[]{:S(2)}) %collective-permute-start.2) | collective-permute-done | bytes 262176 | tf_op jit(solution)/shard_map/ppermute | solution.py:508
  97.9 0.7 copy-done.3
  98.6 0.9 copy-done.4
  99.5 2.5 %fold.1 = (f32[16,128,128]{2,1,0:T(8,128)S(1)}, f32[16,128,128]{2,1,0:T(8,128)}) custom-call(s32[128]{0:T(128)S(1)} %get-tuple-element.34.refs_0_, s32[128]{0:T(128)S(1)} %get-tuple-element.33.refs_2_.refs_1_, f32[4,128,256]{2,1,0:T(8,128)S(1)} %copy-done.1, f32[4,128,256]{2,1,0:T(8,128)S(1)} %copy-done.2, bf16[4,128,256]{2,1,0:T(8,128)(2,1)S(1)} %copy-done.4, ...), custom_call_target="tpu_custom_call" | custom-call | tf_op jit(solution)/shard_map/fold/pallas_call | solution.py:517
  102.1 0.7 copy-done.9
  102.7 1.8 %split.1 = (f32[256,128]{1,0:T(8,128)}, f32[256,128]{1,0:T(8,128)}, f32[256,128]{1,0:T(8,128)}, f32[128,256]{1,0:T(8,128)}) custom-call(bf16[256,256]{1,0:T(8,128)(2,1)} %copy-done.7, bf16[256,256]{1,0:T(8,128)(2,1)} %copy-done.9), custom_call_target="tpu_custom_call" | custom-call | tf_op jit(solution)/shard_map/split/pallas_call | solution.py:535
  104.5 1.1 collective-permute-done.9.got
  105.6 0.9 add.20
  (32 shorter events, 0.2 us)
Async XLA Ops:
  0.6 9.0 %copy-start = (bf16[1,2048,256]{2,1,0:T(8,128)(2,1)S(1)}, bf16[1,2048,256]{2,1,0:T(8,128)(2,1)}, u32[]{:S(2)}) copy-start(bf16[1,2048,256]{2,1,0:T(8,128)(2,1)} %param.8) | copy-start | bytes 3145732
  3.3 20.8 %all-to-all-start = ((bf16[4,256,256]{2,1,0:T(8,128)(2,1)}), bf16[4,256,256]{2,1,0:T(8,128)(2,1)S(1)}, u32[]{:S(2)}, u32[]{:S(2)}) async-start(bf16[4,256,256]{2,1,0:T(8,128)(2,1)} %bitcast.2), calls=%async_computation | async-start | bytes 1048576 | tf_op jit(solution)/shard_map/all_to_all | solution.py:496
  9.6 0.7 copy-start.5
  9.6 0.7 copy-start.6
  10.3 5.8 %copy-start.10 = (bf16[256,128]{1,0:T(8,128)(2,1)S(1)}, bf16[256,128]{1,0:T(8,128)(2,1)}, u32[]{:S(2)}) copy-start(bf16[256,128]{1,0:T(8,128)(2,1)} %param.11) | copy-start | bytes 196612
  12.5 3.7 %copy-start.11 = (bf16[256,128]{1,0:T(8,128)(2,1)S(1)}, bf16[256,128]{1,0:T(8,128)(2,1)}, u32[]{:S(2)}) copy-start(bf16[256,128]{1,0:T(8,128)(2,1)} %param.12) | copy-start | bytes 196612
  12.5 15.1 %collective-permute-start = (bf16[8,128,256]{2,1,0:T(8,128)(2,1)S(1)}, bf16[8,128,256]{2,1,0:T(8,128)(2,1)S(1)}, u32[]{:S(2)}, u32[]{:S(2)}) collective-permute-start(bf16[8,128,256]{2,1,0:T(8,128)(2,1)S(1)} %get-tuple-element.36), channel_id=1, source_target_pairs={{0,2},{1,3},{4,6},{5,7},{8,10},{9,11},{12,14},{13,15},{16,18},{17,... | collective-permute-start | bytes 1572872 | tf_op jit(solution)/shard_map/ppermute | solution.py:501
  16.2 0.8 copy-start.12
  17.0 0.8 copy-start.13
  17.9 6.2 %copy-start.8 = (bf16[512,256]{1,0:T(8,128)(2,1)}, bf16[512,256]{1,0:T(8,128)(2,1)S(1)}, u32[]{:S(2)}) copy-start(bf16[512,256]{1,0:T(8,128)(2,1)S(1)} %pad_maximum_fusion.refs_17_) | copy-start | bytes 786436
  17.9 9.7 %collective-permute-start.1 = (bf16[512,256]{1,0:T(8,128)(2,1)S(1)}, bf16[512,256]{1,0:T(8,128)(2,1)S(1)}, u32[]{:S(2)}, u32[]{:S(2)}) collective-permute-start(bf16[512,256]{1,0:T(8,128)(2,1)S(1)} %pad_maximum_fusion.refs_17_), channel_id=1, source_target_pairs={{0,1},{1,0},{2,3},{3,2},{4,5},{5,4},{6,7},{7,6},{8,9},{9,8},{10,11... | collective-permute-start | bytes 786440 | tf_op jit(solution)/shard_map/ppermute | solution.py:400
  24.1 17.4 %all-to-all-start.1 = ((bf16[4,256,256]{2,1,0:T(8,128)(2,1)}), bf16[4,256,256]{2,1,0:T(8,128)(2,1)S(1)}, u32[]{:S(2)}, u32[]{:S(2)}) async-start(bf16[4,256,256]{2,1,0:T(8,128)(2,1)} %bitcast.7), calls=%async_computation.1 | async-start | bytes 1048576 | tf_op jit(solution)/shard_map/all_to_all | solution.py:496
  27.6 0.7 copy-start.17
  27.6 0.9 copy-start.14
  41.5 18.4 %all-to-all-start.2 = ((bf16[4,256,256]{2,1,0:T(8,128)(2,1)}), bf16[4,256,256]{2,1,0:T(8,128)(2,1)S(1)}, u32[]{:S(2)}, u32[]{:S(2)}) async-start(bf16[4,256,256]{2,1,0:T(8,128)(2,1)} %bitcast.35), calls=%async_computation.2 | async-start | bytes 1048576 | tf_op jit(solution)/shard_map/all_to_all | solution.py:496
  56.6 2.1 %collective-permute-start.4 = (f32[512,256]{1,0:T(8,128)}, f32[512,256]{1,0:T(8,128)S(1)}, u32[]{:S(2)}, u32[]{:S(2)}) collective-permute-start(f32[512,256]{1,0:T(8,128)} %get-tuple-element.45), channel_id=1, source_target_pairs={{0,1},{1,0},{2,3},{3,2},{4,5},{5,4},{6,7},{7,6},{8,9},{9,8},{10,11... | collective-permute-start | bytes 1572872 | tf_op jit(solution)/shard_map/ppermute | solution.py:400
  59.9 6.5 %collective-permute-start.5 = (bf16[256,256]{1,0:T(8,128)(2,1)S(1)}, bf16[256,256]{1,0:T(8,128)(2,1)S(1)}, u32[]{:S(2)}, u32[]{:S(2)}) collective-permute-start(bf16[256,256]{1,0:T(8,128)(2,1)S(1)} %select_convert_fusion.1), channel_id=1, source_target_pairs={{0,2},{2,0},{1,3},{3,1},{4,6},{6,4},{5,7},{7,5},{8,10},{10,8},{9,1... | collective-permute-start | bytes 393224 | tf_op jit(solution)/shard_map/ppermute | solution.py:400
  61.5 21.1 %copy-start.16 = (bf16[4,128,256]{2,1,0:T(8,128)(2,1)S(1)}, bf16[4,128,256]{2,1,0:T(8,128)(2,1)}, u32[]{:S(2)}) copy-start(bf16[4,128,256]{2,1,0:T(8,128)(2,1)} %get-tuple-element.43) | copy-start | bytes 786436
  61.5 26.0 %all-to-all-start.3 = ((bf16[4,256,256]{2,1,0:T(8,128)(2,1)}), bf16[4,256,256]{2,1,0:T(8,128)(2,1)S(1)}, u32[]{:S(2)}, u32[]{:S(2)}) async-start(bf16[4,256,256]{2,1,0:T(8,128)(2,1)} %bitcast.11), calls=%async_computation.3 | async-start | bytes 1048576 | tf_op jit(solution)/shard_map/all_to_all | solution.py:496
  66.5 17.4 %copy-start.15 = (bf16[4,128,256]{2,1,0:T(8,128)(2,1)S(1)}, bf16[4,128,256]{2,1,0:T(8,128)(2,1)}, u32[]{:S(2)}) copy-start(bf16[4,128,256]{2,1,0:T(8,128)(2,1)} %get-tuple-element.42) | copy-start | bytes 786436
  66.5 32.1 %copy-start.2 = (f32[4,128,256]{2,1,0:T(8,128)S(1)}, f32[4,128,256]{2,1,0:T(8,128)}, u32[]{:S(2)}) copy-start(f32[4,128,256]{2,1,0:T(8,128)} %get-tuple-element.41.refs_3_) | copy-start | bytes 1572868
  66.5 32.0 %copy-start.1 = (f32[4,128,256]{2,1,0:T(8,128)S(1)}, f32[4,128,256]{2,1,0:T(8,128)}, u32[]{:S(2)}) copy-start(f32[4,128,256]{2,1,0:T(8,128)} %get-tuple-element.37.refs_2_) | copy-start | bytes 1572868
  66.6 12.2 %collective-permute-start.6 = (bf16[256,256]{1,0:T(8,128)(2,1)S(1)}, bf16[256,256]{1,0:T(8,128)(2,1)S(1)}, u32[]{:S(2)}, u32[]{:S(2)}) collective-permute-start(bf16[256,256]{1,0:T(8,128)(2,1)S(1)} %add_convert_fusion.2), channel_id=1, source_target_pairs={{0,4},{4,0},{8,12},{12,8},{1,5},{5,1},{9,13},{13,9},{2,6},{6,2},{1... | collective-permute-start | bytes 393224 | tf_op jit(solution)/shard_map/ppermute | solution.py:400
  78.8 8.7 %collective-permute-start.7 = (bf16[256,256]{1,0:T(8,128)(2,1)S(1)}, bf16[256,256]{1,0:T(8,128)(2,1)S(1)}, u32[]{:S(2)}, u32[]{:S(2)}) collective-permute-start(bf16[256,256]{1,0:T(8,128)(2,1)S(1)} %add_convert_fusion.1), channel_id=1, source_target_pairs={{0,8},{4,12},{8,0},{12,4},{1,9},{5,13},{9,1},{13,5},{2,10},{6,14},... | collective-permute-start | bytes 393224 | tf_op jit(solution)/shard_map/ppermute | solution.py:400
  82.6 11.1 %collective-permute-start.3 = (bf16[4,128,256]{2,1,0:T(8,128)(2,1)S(1)}, bf16[4,128,256]{2,1,0:T(8,128)(2,1)S(1)}, u32[]{:S(2)}, u32[]{:S(2)}) collective-permute-start(bf16[4,128,256]{2,1,0:T(8,128)(2,1)S(1)} %copy-done.16), channel_id=1, source_target_pairs={{2,0},{3,1},{6,4},{7,5},{10,8},{11,9},{14,12},{15,13},{18,16},{19,... | collective-permute-start | bytes 786440 | tf_op jit(solution)/shard_map/ppermute | solution.py:513
  83.9 13.9 %collective-permute-start.2 = (bf16[4,128,256]{2,1,0:T(8,128)(2,1)S(1)}, bf16[4,128,256]{2,1,0:T(8,128)(2,1)S(1)}, u32[]{:S(2)}, u32[]{:S(2)}) collective-permute-start(bf16[4,128,256]{2,1,0:T(8,128)(2,1)S(1)} %copy-done.15), channel_id=1, source_target_pairs={{2,0},{3,1},{6,4},{7,5},{10,8},{11,9},{14,12},{15,13},{18,16},{19,... | collective-permute-start | bytes 786440 | tf_op jit(solution)/shard_map/ppermute | solution.py:508
  87.5 14.5 %copy-start.7 = (bf16[256,256]{1,0:T(8,128)(2,1)}, bf16[256,256]{1,0:T(8,128)(2,1)S(1)}, u32[]{:S(2)}) copy-start(bf16[256,256]{1,0:T(8,128)(2,1)S(1)} %add_convert_fusion.part) | copy-start | bytes 393220
  87.5 14.5 %collective-permute-start.8 = (bf16[256,256]{1,0:T(8,128)(2,1)S(1)}, bf16[256,256]{1,0:T(8,128)(2,1)S(1)}, u32[]{:S(2)}, u32[]{:S(2)}) collective-permute-start(bf16[256,256]{1,0:T(8,128)(2,1)S(1)} %add_convert_fusion.part), channel_id=1, source_target_pairs={{0,2},{2,0},{1,3},{3,1},{4,6},{6,4},{5,7},{7,5},{8,10},{10,8},{9,1... | collective-permute-start | bytes 393224 | tf_op jit(solution)/shard_map/ppermute | solution.py:400
  97.8 0.7 copy-start.3
  98.6 1.0 copy-start.4
  102.1 0.7 copy-start.9
  102.7 2.9 %collective-permute-start.9 = (f32[16,128,128]{2,1,0:T(8,128)}, f32[16,128,128]{2,1,0:T(8,128)S(1)}, u32[]{:S(2)}, u32[]{:S(2)}) collective-permute-start(f32[16,128,128]{2,1,0:T(8,128)} %get-tuple-element.55), channel_id=1, source_target_pairs={{0,1},{1,0},{2,3},{3,2},{4,5},{5,4},{6,7},{7,6},{8,9},{9,8},{10,11... | collective-permute-start | bytes 3145736 | tf_op jit(solution)/shard_map/ppermute | solution.py:400

commit v12 on v11

--- a/solution.py
+++ b/solution.py
@@ -405,36 +405,58 @@
     return low.astype(F32) + exchanged(low, axis, bit).astype(F32)
 
 
-def sum_gradients(total, early, home_b, ring):
-    half = total.shape[0] // 2
-    first = lax.rem(lax.axis_index("day"), 2) == 0
-    kept = jnp.where(first, total[:half], total[half:])
-    given = jnp.where(first, total[half:], total[:half]).astype(BF16)
-    given, early, home_b = lax.optimization_barrier((given, early, home_b))
-    home_b = ring(home_b)
-    part = kept.astype(BF16).astype(F32) + exchanged(given, "day", 1).astype(F32)
+def halved_over(value, axis):
+    half = value.shape[0] // 2
+    first = lax.rem(lax.axis_index(axis), 2) == 0
+    low = value.astype(BF16)
+    kept = jnp.where(first, low[:half], low[half:])
+    given = jnp.where(first, low[half:], low[:half])
+    return kept.astype(F32) + exchanged(given, axis, 1).astype(F32)
+
+
+def sum_gradients(total, home_b, fold):
+    part = halved_over(total, "day")
     bit = 2
     while bit < lax.axis_size("day"):
         part = summed_over(part, "day", bit)
         bit *= 2
-    bit = 1
+    part = halved_over(part, "reach")
+    part, home_b = lax.optimization_barrier((part, home_b))
+    bit = 2
     while bit < lax.axis_size("reach"):
         part = summed_over(part, "reach", bit)
         bit *= 2
-    part = part.astype(BF16)
-    part, home_b = lax.optimization_barrier((part, home_b))
-    return part, exchanged(part, "day", 1), early, home_b
-
-
-def split_kernel(part, other, query_out, key_out, value_out, output_out):
-    first = lax.rem(lax.axis_index("day"), 2) == 0
-    mine, theirs = part[...].astype(F32), other[...].astype(F32)
-    upper = jnp.where(first, mine, theirs)
-    lower = jnp.where(first, theirs, mine)
-    key_out[...] = upper[:, :GROUP]
-    value_out[...] = upper[:, GROUP:]
-    query_out[...] = lower[:GROUP].T
-    output_out[...] = lower[GROUP:]
+    part, folded = lax.optimization_barrier((part.astype(BF16), fold(home_b)))
+    days = lax.axis_size("day")
+    both = [
+        (reach * days + day, (reach ^ 1) * days + (day ^ 1))
+        for reach in range(lax.axis_size("reach"))
+        for day in range(days)
+    ]
+    quarters = (
+        part,
+        exchanged(part, "reach", 1),
+        exchanged(part, "day", 1),
+        lax.ppermute(part, ("reach", "day"), both),
+    )
+    return quarters, folded
+
+
+def split_kernel(mine, along_reach, along_day, along_both, query_out, key_out, value_out, output_out):
+    day_half = lax.rem(lax.axis_index("day"), 2) == 0
+    reach_half = lax.rem(lax.axis_index("reach"), 2) == 0
+
+    def quarter(by_day, by_reach):
+        near = jnp.where(reach_half == by_reach, mine[...], along_reach[...])
+        far = jnp.where(reach_half == by_reach, along_day[...], along_both[...])
+        return jnp.where(day_half == by_day, near, far).astype(F32)
+
+    for place, by_reach in enumerate((True, False)):
+        rows = quarter(True, by_reach)
+        key_out[place * GROUP : (place + 1) * GROUP] = rows[:, :GROUP]
+        value_out[place * GROUP : (place + 1) * GROUP] = rows[:, GROUP:]
+    query_out[...] = quarter(False, True).T
+    output_out[...] = quarter(False, False)
 
 
 def on_device(
@@ -510,19 +532,22 @@
         lay, 1, tab, in_blocks, up_blocks, received_b, *shared, grads
     )
     grad_swapped = exchanged(grad_other, "head", 1)
+    home_a, home_b, grad_swapped = lax.optimization_barrier((home_a, home_b, grad_swapped))
+    home_b = ring(home_b)
     day_b = lax.ppermute(day_b, "day", last_day)
     half_shape = jax.ShapeDtypeStruct((blocks_dev, BLOCK, half), F32)
 
-    part, other, home_a, home_b = sum_gradients(grad_mine + grad_swapped, home_a, home_b, ring)
-    keep, give = pl.pallas_call(
-        lambda *refs: fold_kernel(lay, *refs),
-        out_shape=(half_shape, half_shape),
-        in_specs=[smem] * 2 + [in_vmem] * 6,
-        out_specs=[in_vmem] * 2,
-        compiler_params=pltpu.CompilerParams(vmem_limit_bytes=16 << 20),
-        name="fold",
-    )(tab, homes, own_a, own_b, day_a, day_b, home_a, home_b)
-    other, give = lax.optimization_barrier((other, give))
+    def fold(home_b):
+        return pl.pallas_call(
+            lambda *refs: fold_kernel(lay, *refs),
+            out_shape=(half_shape, half_shape),
+            in_specs=[smem] * 2 + [in_vmem] * 6,
+            out_specs=[in_vmem] * 2,
+            compiler_params=pltpu.CompilerParams(vmem_limit_bytes=16 << 20),
+            name="fold",
+        )(tab, homes, own_a, own_b, day_a, day_b, home_a, home_b)
+
+    quarters, (keep, give) = sum_gradients(grad_mine + grad_swapped, home_b, fold)
     got = exchanged(give, "head", 1)
     back_blocks = pl.pallas_call(
         add_kernel,
@@ -532,6 +557,7 @@
         compiler_params=pltpu.CompilerParams(vmem_limit_bytes=16 << 20),
         name="add",
     )(keep, got)
+    back_blocks, quarters = lax.optimization_barrier((back_blocks, quarters))
     weight_grads = pl.pallas_call(
         split_kernel,
         out_shape=(
@@ -542,7 +568,7 @@
         ),
         grid=(1,),
         name="split",
-    )(part, other)
+    )(*quarters)
 
     return (back_blocks.reshape(1, rows_dev, half), *weight_grads)
 

time: 107 us -> 96.5 us (0.902)
  waiting for transfers between devices: 33.2 us -> 26 us
  local copies, waits for them, and re-layouts: 5.63 us -> 3.95 us
    ppermute x1, waiting for transfers between devices: 5.57 us -> 0.01 us  [on_device(): day_b = lax.ppermute(day_b, 'day', last_day)]
    ppermute x7 -> x8, waiting for transfers between devices: 15.5 us -> 10.3 us  [exchanged(): lax.ppermute(value, axis, [(place, place ^ bit) for place in range(count)])]
    all_to_all x4, waiting for transfers between devices: 8 us -> 12.5 us  [ring(): return lax.all_to_all(value, 'reach', 0, 0, tiled=True).reshape(shape)]
    ppermute x1, waiting for transfers between devices: 4.12 us -> 2.17 us  [on_device(): day_a = lax.ppermute(day_a, 'day', last_day)]
    unnamed x39, local copies, waits for them, and re-layouts: 5.63 us -> 3.95 us
    add x1, other arithmetic: 1.13 us -> 0.03 us  [halved_over(): return kept.astype(F32) + exchanged(given, axis, 1).astype(F32)]
    ppermute x7 -> x8, starting transfers between devices: 8.17 us -> 7.24 us  [exchanged(): lax.ppermute(value, axis, [(place, place ^ bit) for place in range(count)])]
  transfers between devices with their start and end apart: 14 -> 16, of which waited for: 8 -> 11; matrix products, arithmetic and copies ran while one was open for 2% -> 0% of each run, Pallas kernels for 27% -> 28%
where the time goes in v12:
time: 96.5 us; the launch traced here: 95.8 us
  starting transfers between devices  31.9 us (33%)
  Pallas kernels  31.7 us (33%)
  waiting for transfers between devices  26 us (27%)
  local copies, waits for them, and re-layouts  3.95 us (4%)
  other arithmetic  1.27 us (1%)
    pallas_call x2, Pallas kernels, attend(): pl.pallas_call(lambda *refs: attention_kernel(lay, chunk, *refs), grid_sp...  22.6 us
    all_to_all x4, starting transfers between devices, ring(): return lax.all_to_all(value, 'reach', 0, 0, tiled=True).reshape(shape)  18.3 us
    all_to_all x4, waiting for transfers between devices, ring(): return lax.all_to_all(value, 'reach', 0, 0, tiled=True).reshape(shape)  12.5 us
    ppermute x8, waiting for transfers between devices, exchanged(): lax.ppermute(value, axis, [(place, place ^ bit) for place in range(count)])  10.3 us
    ppermute x8, starting transfers between devices, exchanged(): lax.ppermute(value, axis, [(place, place ^ bit) for place in range(count)])  7.24 us
    unnamed x39, local copies, waits for them, and re-layouts  3.95 us
    ppermute x1, starting transfers between devices, on_device(): prior_inputs = lax.ppermute(prior, 'day', next_day)  3.56 us
    pallas_call x1, Pallas kernels, on_device(): pl.pallas_call(lambda *refs: pick_kernel(lay, *refs), out_shape=(sent_sha...  2.61 us
  transfers between devices with their start and end apart: 16, of which 11 were waited for; matrix products, arithmetic and copies ran while one was open for 0% of the time, Pallas kernels for 28%

profile of v12, /device:TPU:0, one launch (start us, length us, event | category | flops | bytes accessed | tf_op | source)
XLA Modules:
  0.0 95.8 jit_solution(8127208329885580496)
XLA Ops:
  0.6 0.0 copy-start
  0.6 2.6 %pick.1 = (bf16[8,128,256]{2,1,0:T(8,128)(2,1)}, s32[128]{0:T(128)S(1)}) custom-call(s32[64]{0:T(128)} %refs_0_.3, bf16[16,128,256]{2,1,0:T(8,128)(2,1)} %bitcast.14), custom_call_target="tpu_custom_call" | custom-call | tf_op jit(solution)/shard_map/pick/pallas_call | solution.py:482
  3.3 6.3 %all-to-all-start.1 = ((bf16[4,256,256]{2,1,0:T(8,128)(2,1)}), bf16[4,256,256]{2,1,0:T(8,128)(2,1)S(1)}, u32[]{:S(2)}, u32[]{:S(2)}) async-start(bf16[4,256,256]{2,1,0:T(8,128)(2,1)} %bitcast.7), calls=%async_computation.1 | async-start | bytes 1048576 | tf_op jit(solution)/shard_map/all_to_all | solution.py:518
  9.6 0.6 copy-done.3
  10.2 0.0 copy-done.4
  10.3 2.2 %deal.1 = (bf16[8,128,256]{2,1,0:T(8,128)(2,1)}, bf16[8,128,256]{2,1,0:T(8,128)(2,1)S(1)}, s32[128]{0:T(128)S(1)}) custom-call(s32[64]{0:T(128)S(1)} %copy-done.3, s32[64]{0:T(128)S(1)} %copy-done.4, s32[128]{0:T(128)S(1)} %get-tuple-element.39.refs_2_.refs_1_, bf16[16,128,256]{2,1,0:T(8,128)(2,1)S(1)} %bitcast.23), custom_call_target="tpu_custom_call" | custom-call | tf_op jit(solution)/shard_map/deal/pallas_call | solution.py:498
  12.5 0.0 copy-start.8
  12.5 3.6 %collective-permute-start = (bf16[8,128,256]{2,1,0:T(8,128)(2,1)S(1)}, bf16[8,128,256]{2,1,0:T(8,128)(2,1)S(1)}, u32[]{:S(2)}, u32[]{:S(2)}) collective-permute-start(bf16[8,128,256]{2,1,0:T(8,128)(2,1)S(1)} %get-tuple-element.42), channel_id=1, source_target_pairs={{0,2},{1,3},{4,6},{5,7},{8,10},{9,11},{12,14},{13,15},{16,18},{17,... | collective-permute-start | bytes 1572872 | tf_op jit(solution)/shard_map/ppermute | solution.py:523
  16.1 0.1 copy.13
  16.2 0.0 copy-start.9
  16.2 0.1 copy.14
  16.3 0.7 copy-done.9
  17.0 0.1 copy.15
  17.1 0.7 copy-done.13
  17.9 0.1 collective-permute-start.1
  18.0 6.1 %all-to-all-done.1 = bf16[4,256,256]{2,1,0:T(8,128)(2,1)S(1)} async-done(((bf16[4,256,256]{2,1,0:T(8,128)(2,1)}), bf16[4,256,256]{2,1,0:T(8,128)(2,1)S(1)}, u32[]{:S(2)}, u32[]{:S(2)}) %all-to-all-start.1) | async-done | bytes 524320 | tf_op jit(solution)/shard_map/all_to_all | solution.py:518
  24.1 3.5 %all-to-all-start = ((bf16[4,256,256]{2,1,0:T(8,128)(2,1)}), bf16[4,256,256]{2,1,0:T(8,128)(2,1)S(1)}, u32[]{:S(2)}, u32[]{:S(2)}) async-start(bf16[4,256,256]{2,1,0:T(8,128)(2,1)} %bitcast.2), calls=%async_computation | async-start | bytes 1048576 | tf_op jit(solution)/shard_map/all_to_all | solution.py:518
  27.6 0.7 copy-done.17
  28.3 0.2 copy-done.14
  28.4 11.2 %attention_0.1 = (f32[4,128,256]{2,1,0:T(8,128)}, bf16[4,128,256]{2,1,0:T(8,128)(2,1)}, bf16[8,128,256]{2,1,0:T(8,128)(2,1)}, f32[512,256]{1,0:T(8,128)}, f32[512,256]{1,0:T(8,128)}) custom-call(s32[128]{0:T(128)S(1)} %get-tuple-element.40.refs_0_, bf16[16,128,256]{2,1,0:T(8,128)(2,1)} %bitcast.15, bf16[16,128,256]{2,1,0:T(8,128)(2,1)} %bitcast.39, ...), custom_call_target="tpu_custom_call" | custom-call | flops 6375342080 | bytes 5242880 | tf_op jit(solution)/shard_map/attention_0/pallas_call | solution.py:361
  39.6 1.9 %all-to-all-done = bf16[4,256,256]{2,1,0:T(8,128)(2,1)S(1)} async-done(((bf16[4,256,256]{2,1,0:T(8,128)(2,1)}), bf16[4,256,256]{2,1,0:T(8,128)(2,1)S(1)}, u32[]{:S(2)}, u32[]{:S(2)}) %all-to-all-start) | async-done | bytes 524320 | tf_op jit(solution)/shard_map/all_to_all | solution.py:518
  41.5 3.6 %all-to-all-start.2 = ((bf16[4,256,256]{2,1,0:T(8,128)(2,1)}), bf16[4,256,256]{2,1,0:T(8,128)(2,1)S(1)}, u32[]{:S(2)}, u32[]{:S(2)}) async-start(bf16[4,256,256]{2,1,0:T(8,128)(2,1)} %bitcast.35), calls=%async_computation.2 | async-start | bytes 1048576 | tf_op jit(solution)/shard_map/all_to_all | solution.py:518
  45.2 11.5 %attention_1.1 = (f32[4,128,256]{2,1,0:T(8,128)}, bf16[4,128,256]{2,1,0:T(8,128)(2,1)}, bf16[8,128,256]{2,1,0:T(8,128)(2,1)}, f32[512,256]{1,0:T(8,128)}, f32[512,256]{1,0:T(8,128)}) custom-call(s32[128]{0:T(128)S(1)} %get-tuple-element.40.refs_0_, bf16[16,128,256]{2,1,0:T(8,128)(2,1)} %bitcast.19, bf16[16,128,256]{2,1,0:T(8,128)(2,1)} %bitcast.43, ...), custom_call_target="tpu_custom_call" | custom-call | flops 6375342080 | bytes 5242880 | tf_op jit(solution)/shard_map/attention_1/pallas_call | solution.py:361
  56.6 2.1 %collective-permute-done.2 = f32[512,256]{1,0:T(8,128)S(1)} collective-permute-done((f32[512,256]{1,0:T(8,128)}, f32[512,256]{1,0:T(8,128)S(1)}, u32[]{:S(2)}, u32[]{:S(2)}) %collective-permute-start.2) | collective-permute-done | bytes 524320 | tf_op jit(solution)/shard_map/ppermute | solution.py:400
  58.8 0.2 all-to-all-done.2
  58.9 1.1 %add_convert_fusion = bf16[512,256]{1,0:T(8,128)(2,1)S(1)} fusion(f32[512,256]{1,0:T(8,128)} %get-tuple-element.46, f32[512,256]{1,0:T(8,128)S(1)} %collective-permute-done.2), kind=kLoop, calls=%fused_computation | loop fusion | flops 262144 | bytes 1310720 | tf_op jit(solution)/shard_map/convert_element_type | solution.py:411
  60.1 1.6 %collective-permute-start.3 = (bf16[256,256]{1,0:T(8,128)(2,1)S(1)}, bf16[256,256]{1,0:T(8,128)(2,1)S(1)}, u32[]{:S(2)}, u32[]{:S(2)}) collective-permute-start(bf16[256,256]{1,0:T(8,128)(2,1)S(1)} %broadcast_select_fusion), channel_id=1, source_target_pairs={{0,2},{2,0},{1,3},{3,1},{4,6},{6,4},{5,7},{7,5},{8,10},{10,8},{9,1... | collective-permute-start | bytes 393224 | tf_op jit(solution)/shard_map/ppermute | solution.py:400
  61.7 4.8 %all-to-all-start.3 = ((bf16[4,256,256]{2,1,0:T(8,128)(2,1)}), bf16[4,256,256]{2,1,0:T(8,128)(2,1)S(1)}, u32[]{:S(2)}, u32[]{:S(2)}) async-start(bf16[4,256,256]{2,1,0:T(8,128)(2,1)} %bitcast.11), calls=%async_computation.3 | async-start | bytes 1048576 | tf_op jit(solution)/shard_map/all_to_all | solution.py:518
  66.5 0.1 add_convert_fusion.1
  66.5 2.1 %collective-permute-start.4 = (bf16[128,256]{1,0:T(8,128)(2,1)S(1)}, bf16[128,256]{1,0:T(8,128)(2,1)S(1)}, u32[]{:S(2)}, u32[]{:S(2)}) collective-permute-start(bf16[128,256]{1,0:T(8,128)(2,1)S(1)} %broadcast_select_fusion.1), channel_id=1, source_target_pairs={{0,4},{4,0},{8,12},{12,8},{1,5},{5,1},{9,13},{13,9},{2,6},{6,2},{1... | collective-permute-start | bytes 196616 | tf_op jit(solution)/shard_map/ppermute | solution.py:400
  68.6 1.3 %collective-permute-start.7 = (bf16[4,128,256]{2,1,0:T(8,128)(2,1)S(1)}, bf16[4,128,256]{2,1,0:T(8,128)(2,1)S(1)}, u32[]{:S(2)}, u32[]{:S(2)}) collective-permute-start(bf16[4,128,256]{2,1,0:T(8,128)(2,1)S(1)} %copy-done.16), channel_id=1, source_target_pairs={{2,0},{3,1},{6,4},{7,5},{10,8},{11,9},{14,12},{15,13},{18,16},{19,... | collective-permute-start | bytes 786440 | tf_op jit(solution)/shard_map/ppermute | solution.py:537
  69.9 1.3 %collective-permute-start.6 = (bf16[4,128,256]{2,1,0:T(8,128)(2,1)S(1)}, bf16[4,128,256]{2,1,0:T(8,128)(2,1)S(1)}, u32[]{:S(2)}, u32[]{:S(2)}) collective-permute-start(bf16[4,128,256]{2,1,0:T(8,128)(2,1)S(1)} %copy-done.15), channel_id=1, source_target_pairs={{2,0},{3,1},{6,4},{7,5},{10,8},{11,9},{14,12},{15,13},{18,16},{19,... | collective-permute-start | bytes 786440 | tf_op jit(solution)/shard_map/ppermute | solution.py:530
  71.2 5.3 %collective-permute-done.4 = bf16[128,256]{1,0:T(8,128)(2,1)S(1)} collective-permute-done((bf16[128,256]{1,0:T(8,128)(2,1)S(1)}, bf16[128,256]{1,0:T(8,128)(2,1)S(1)}, u32[]{:S(2)}, u32[]{:S(2)}) %collective-permute-start.4) | collective-permute-done | bytes 65568 | tf_op jit(solution)/shard_map/ppermute | solution.py:400
  76.6 4.4 %all-to-all-done.3 = bf16[4,256,256]{2,1,0:T(8,128)(2,1)S(1)} async-done(((bf16[4,256,256]{2,1,0:T(8,128)(2,1)}), bf16[4,256,256]{2,1,0:T(8,128)(2,1)S(1)}, u32[]{:S(2)}, u32[]{:S(2)}) %all-to-all-start.3) | async-done | bytes 524320 | tf_op jit(solution)/shard_map/all_to_all | solution.py:518
  81.0 0.2 collective-permute-start.5
  81.2 2.2 %collective-permute-done.6.refs_4_ = bf16[4,128,256]{2,1,0:T(8,128)(2,1)S(1)} collective-permute-done((bf16[4,128,256]{2,1,0:T(8,128)(2,1)S(1)}, bf16[4,128,256]{2,1,0:T(8,128)(2,1)S(1)}, u32[]{:S(2)}, u32[]{:S(2)}) %collective-permute-start.6) | collective-permute-done | bytes 262176 | tf_op jit(solution)/shard_map/ppermute | solution.py:530
  83.4 1.6 %fold.1 = (f32[16,128,128]{2,1,0:T(8,128)S(1)}, f32[16,128,128]{2,1,0:T(8,128)S(1)}) custom-call(s32[128]{0:T(128)S(1)} %get-tuple-element.40.refs_0_, s32[128]{0:T(128)S(1)} %get-tuple-element.39.refs_2_.refs_1_, f32[4,128,256]{2,1,0:T(8,128)S(1)} %copy-done.1, f32[4,128,256]{2,1,0:T(8,128)S(1)} %copy-done.2, ...), custom_call_target="tpu_custom_call" | custom-call | tf_op jit(solution)/shard_map/fold/pallas_call | solution.py:541
  84.9 1.2 %collective-permute-done.5 = bf16[128,256]{1,0:T(8,128)(2,1)S(1)} collective-permute-done((bf16[128,256]{1,0:T(8,128)(2,1)S(1)}, bf16[128,256]{1,0:T(8,128)(2,1)S(1)}, u32[]{:S(2)}, u32[]{:S(2)}) %collective-permute-start.5) | collective-permute-done | bytes 65568 | tf_op jit(solution)/shard_map/ppermute | solution.py:400
  86.2 0.1 collective-permute-start.8
  86.3 0.6 collective-permute-start.10
  86.9 0.3 collective-permute-start.11
  87.2 2.6 %collective-permute-start.9 = (bf16[128,256]{1,0:T(8,128)(2,1)S(1)}, bf16[128,256]{1,0:T(8,128)(2,1)S(1)}, u32[]{:S(2)}, u32[]{:S(2)}) collective-permute-start(bf16[128,256]{1,0:T(8,128)(2,1)S(1)} %add_convert_fusion.2.mine), channel_id=1, source_target_pairs={{0,4},{4,0},{8,12},{12,8},{1,5},{5,1},{9,13},{13,9},{2,6},{6,2},{1... | collective-permute-start | bytes 196616 | tf_op jit(solution)/shard_map/ppermute | solution.py:400
  89.8 0.9 add.21
  90.7 0.9 collective-permute-done.10.along_day
  91.6 1.0 %collective-permute-done.11.along_both = bf16[128,256]{1,0:T(8,128)(2,1)S(1)} collective-permute-done((bf16[128,256]{1,0:T(8,128)(2,1)S(1)}, bf16[128,256]{1,0:T(8,128)(2,1)S(1)}, u32[]{:S(2)}, u32[]{:S(2)}) %collective-permute-start.11) | collective-permute-done | bytes 65568 | tf_op jit(solution)/shard_map/ppermute | solution.py:440
  92.6 0.7 collective-permute-done.9.along_reach
  93.4 0.6 copy-done.12
  94.0 1.8 %split.1 = (f32[256,128]{1,0:T(8,128)}, f32[256,128]{1,0:T(8,128)}, f32[256,128]{1,0:T(8,128)}, f32[128,256]{1,0:T(8,128)}) custom-call(bf16[128,256]{1,0:T(8,128)(2,1)} %copy-done.6, bf16[128,256]{1,0:T(8,128)(2,1)} %copy-done.12, bf16[128,256]{1,0:T(8,128)(2,1)} %copy-done.10, bf16[128,256]{1,0:T(8,128)(2,1)} %copy-done.11), custom_call_target="tpu_custom_call" | custom-call | tf_op jit(solution)/shard_map/split/pallas_call | solution.py:561
  (37 shorter events, 0.2 us)
Async XLA Ops:
  0.6 9.0 %copy-start = (bf16[1,2048,256]{2,1,0:T(8,128)(2,1)S(1)}, bf16[1,2048,256]{2,1,0:T(8,128)(2,1)}, u32[]{:S(2)}) copy-start(bf16[1,2048,256]{2,1,0:T(8,128)(2,1)} %param.8) | copy-start | bytes 3145732
  3.3 20.8 %all-to-all-start.1 = ((bf16[4,256,256]{2,1,0:T(8,128)(2,1)}), bf16[4,256,256]{2,1,0:T(8,128)(2,1)S(1)}, u32[]{:S(2)}, u32[]{:S(2)}) async-start(bf16[4,256,256]{2,1,0:T(8,128)(2,1)} %bitcast.7), calls=%async_computation.1 | async-start | bytes 1048576 | tf_op jit(solution)/shard_map/all_to_all | solution.py:518
  9.6 0.7 copy-start.3
  9.6 0.7 copy-start.4
  10.3 5.8 %copy-start.7 = (bf16[256,128]{1,0:T(8,128)(2,1)S(1)}, bf16[256,128]{1,0:T(8,128)(2,1)}, u32[]{:S(2)}) copy-start(bf16[256,128]{1,0:T(8,128)(2,1)} %param.11) | copy-start | bytes 196612
  12.5 3.7 %copy-start.8 = (bf16[256,128]{1,0:T(8,128)(2,1)S(1)}, bf16[256,128]{1,0:T(8,128)(2,1)}, u32[]{:S(2)}) copy-start(bf16[256,128]{1,0:T(8,128)(2,1)} %param.12) | copy-start | bytes 196612
  12.5 15.1 %collective-permute-start = (bf16[8,128,256]{2,1,0:T(8,128)(2,1)S(1)}, bf16[8,128,256]{2,1,0:T(8,128)(2,1)S(1)}, u32[]{:S(2)}, u32[]{:S(2)}) collective-permute-start(bf16[8,128,256]{2,1,0:T(8,128)(2,1)S(1)} %get-tuple-element.42), channel_id=1, source_target_pairs={{0,2},{1,3},{4,6},{5,7},{8,10},{9,11},{12,14},{13,15},{16,18},{17,... | collective-permute-start | bytes 1572872 | tf_op jit(solution)/shard_map/ppermute | solution.py:523
  16.2 0.8 copy-start.9
  17.0 0.8 copy-start.13
  17.9 6.2 %copy-start.5 = (bf16[512,256]{1,0:T(8,128)(2,1)}, bf16[512,256]{1,0:T(8,128)(2,1)S(1)}, u32[]{:S(2)}) copy-start(bf16[512,256]{1,0:T(8,128)(2,1)S(1)} %pad_maximum_fusion.refs_17_) | copy-start | bytes 786436
  17.9 9.7 %collective-permute-start.1 = (bf16[512,256]{1,0:T(8,128)(2,1)S(1)}, bf16[512,256]{1,0:T(8,128)(2,1)S(1)}, u32[]{:S(2)}, u32[]{:S(2)}) collective-permute-start(bf16[512,256]{1,0:T(8,128)(2,1)S(1)} %pad_maximum_fusion.refs_17_), channel_id=1, source_target_pairs={{0,1},{1,0},{2,3},{3,2},{4,5},{5,4},{6,7},{7,6},{8,9},{9,8},{10,11... | collective-permute-start | bytes 786440 | tf_op jit(solution)/shard_map/ppermute | solution.py:400
  24.1 17.4 %all-to-all-start = ((bf16[4,256,256]{2,1,0:T(8,128)(2,1)}), bf16[4,256,256]{2,1,0:T(8,128)(2,1)S(1)}, u32[]{:S(2)}, u32[]{:S(2)}) async-start(bf16[4,256,256]{2,1,0:T(8,128)(2,1)} %bitcast.2), calls=%async_computation | async-start | bytes 1048576 | tf_op jit(solution)/shard_map/all_to_all | solution.py:518
  27.6 0.7 copy-start.17
  27.6 0.9 copy-start.14
  41.5 17.4 %all-to-all-start.2 = ((bf16[4,256,256]{2,1,0:T(8,128)(2,1)}), bf16[4,256,256]{2,1,0:T(8,128)(2,1)S(1)}, u32[]{:S(2)}, u32[]{:S(2)}) async-start(bf16[4,256,256]{2,1,0:T(8,128)(2,1)} %bitcast.35), calls=%async_computation.2 | async-start | bytes 1048576 | tf_op jit(solution)/shard_map/all_to_all | solution.py:518
  56.6 2.1 %collective-permute-start.2 = (f32[512,256]{1,0:T(8,128)}, f32[512,256]{1,0:T(8,128)S(1)}, u32[]{:S(2)}, u32[]{:S(2)}) collective-permute-start(f32[512,256]{1,0:T(8,128)} %get-tuple-element.49), channel_id=1, source_target_pairs={{0,1},{1,0},{2,3},{3,2},{4,5},{5,4},{6,7},{7,6},{8,9},{9,8},{10,11... | collective-permute-start | bytes 1572872 | tf_op jit(solution)/shard_map/ppermute | solution.py:400
  60.1 6.4 %collective-permute-start.3 = (bf16[256,256]{1,0:T(8,128)(2,1)S(1)}, bf16[256,256]{1,0:T(8,128)(2,1)S(1)}, u32[]{:S(2)}, u32[]{:S(2)}) collective-permute-start(bf16[256,256]{1,0:T(8,128)(2,1)S(1)} %broadcast_select_fusion), channel_id=1, source_target_pairs={{0,2},{2,0},{1,3},{3,1},{4,6},{6,4},{5,7},{7,5},{8,10},{10,8},{9,1... | collective-permute-start | bytes 393224 | tf_op jit(solution)/shard_map/ppermute | solution.py:400
  61.7 7.0 %copy-start.16 = (bf16[4,128,256]{2,1,0:T(8,128)(2,1)S(1)}, bf16[4,128,256]{2,1,0:T(8,128)(2,1)}, u32[]{:S(2)}) copy-start(bf16[4,128,256]{2,1,0:T(8,128)(2,1)} %get-tuple-element.56) | copy-start | bytes 786436
  61.7 8.3 %copy-start.15 = (bf16[4,128,256]{2,1,0:T(8,128)(2,1)S(1)}, bf16[4,128,256]{2,1,0:T(8,128)(2,1)}, u32[]{:S(2)}) copy-start(bf16[4,128,256]{2,1,0:T(8,128)(2,1)} %get-tuple-element.55) | copy-start | bytes 786436
  61.7 21.7 %copy-start.2 = (f32[4,128,256]{2,1,0:T(8,128)S(1)}, f32[4,128,256]{2,1,0:T(8,128)}, u32[]{:S(2)}) copy-start(f32[4,128,256]{2,1,0:T(8,128)} %get-tuple-element.54.refs_3_) | copy-start | bytes 1572868
  61.7 19.3 %all-to-all-start.3 = ((bf16[4,256,256]{2,1,0:T(8,128)(2,1)}), bf16[4,256,256]{2,1,0:T(8,128)(2,1)S(1)}, u32[]{:S(2)}, u32[]{:S(2)}) async-start(bf16[4,256,256]{2,1,0:T(8,128)(2,1)} %bitcast.11), calls=%async_computation.3 | async-start | bytes 1048576 | tf_op jit(solution)/shard_map/all_to_all | solution.py:518
  66.5 16.9 %copy-start.1 = (f32[4,128,256]{2,1,0:T(8,128)S(1)}, f32[4,128,256]{2,1,0:T(8,128)}, u32[]{:S(2)}) copy-start(f32[4,128,256]{2,1,0:T(8,128)} %get-tuple-element.53.refs_2_) | copy-start | bytes 1572868
  66.5 10.0 %collective-permute-start.4 = (bf16[128,256]{1,0:T(8,128)(2,1)S(1)}, bf16[128,256]{1,0:T(8,128)(2,1)S(1)}, u32[]{:S(2)}, u32[]{:S(2)}) collective-permute-start(bf16[128,256]{1,0:T(8,128)(2,1)S(1)} %broadcast_select_fusion.1), channel_id=1, source_target_pairs={{0,4},{4,0},{8,12},{12,8},{1,5},{5,1},{9,13},{13,9},{2,6},{6,2},{1... | collective-permute-start | bytes 196616 | tf_op jit(solution)/shard_map/ppermute | solution.py:400
  68.6 12.6 %collective-permute-start.7 = (bf16[4,128,256]{2,1,0:T(8,128)(2,1)S(1)}, bf16[4,128,256]{2,1,0:T(8,128)(2,1)S(1)}, u32[]{:S(2)}, u32[]{:S(2)}) collective-permute-start(bf16[4,128,256]{2,1,0:T(8,128)(2,1)S(1)} %copy-done.16), channel_id=1, source_target_pairs={{2,0},{3,1},{6,4},{7,5},{10,8},{11,9},{14,12},{15,13},{18,16},{19,... | collective-permute-start | bytes 786440 | tf_op jit(solution)/shard_map/ppermute | solution.py:537
  69.9 13.4 %collective-permute-start.6 = (bf16[4,128,256]{2,1,0:T(8,128)(2,1)S(1)}, bf16[4,128,256]{2,1,0:T(8,128)(2,1)S(1)}, u32[]{:S(2)}, u32[]{:S(2)}) collective-permute-start(bf16[4,128,256]{2,1,0:T(8,128)(2,1)S(1)} %copy-done.15), channel_id=1, source_target_pairs={{2,0},{3,1},{6,4},{7,5},{10,8},{11,9},{14,12},{15,13},{18,16},{19,... | collective-permute-start | bytes 786440 | tf_op jit(solution)/shard_map/ppermute | solution.py:530
  81.0 5.2 %collective-permute-start.5 = (bf16[128,256]{1,0:T(8,128)(2,1)S(1)}, bf16[128,256]{1,0:T(8,128)(2,1)S(1)}, u32[]{:S(2)}, u32[]{:S(2)}) collective-permute-start(bf16[128,256]{1,0:T(8,128)(2,1)S(1)} %convert_add_fusion), channel_id=1, source_target_pairs={{0,8},{4,12},{8,0},{12,4},{1,9},{5,13},{9,1},{13,5},{2,10},{6,14},... | collective-permute-start | bytes 196616 | tf_op jit(solution)/shard_map/ppermute | solution.py:400
  86.2 4.5 %copy-start.6 = (bf16[128,256]{1,0:T(8,128)(2,1)}, bf16[128,256]{1,0:T(8,128)(2,1)S(1)}, u32[]{:S(2)}) copy-start(bf16[128,256]{1,0:T(8,128)(2,1)S(1)} %add_convert_fusion.2.mine) | copy-start | bytes 196612
  86.2 3.6 %collective-permute-start.8 = (f32[16,128,128]{2,1,0:T(8,128)S(1)}, f32[16,128,128]{2,1,0:T(8,128)S(1)}, u32[]{:S(2)}, u32[]{:S(2)}) collective-permute-start(f32[16,128,128]{2,1,0:T(8,128)S(1)} %get-tuple-element.62), channel_id=1, source_target_pairs={{0,1},{1,0},{2,3},{3,2},{4,5},{5,4},{6,7},{7,6},{8,9},{9,8},{10,11... | collective-permute-start | bytes 3145736 | tf_op jit(solution)/shard_map/ppermute | solution.py:400
  86.3 5.4 %collective-permute-start.10 = (bf16[128,256]{1,0:T(8,128)(2,1)S(1)}, bf16[128,256]{1,0:T(8,128)(2,1)S(1)}, u32[]{:S(2)}, u32[]{:S(2)}) collective-permute-start(bf16[128,256]{1,0:T(8,128)(2,1)S(1)} %add_convert_fusion.2.mine), channel_id=1, source_target_pairs={{0,2},{2,0},{1,3},{3,1},{4,6},{6,4},{5,7},{7,5},{8,10},{10,8},{9,1... | collective-permute-start | bytes 196616 | tf_op jit(solution)/shard_map/ppermute | solution.py:400
  86.9 5.8 %collective-permute-start.11 = (bf16[128,256]{1,0:T(8,128)(2,1)S(1)}, bf16[128,256]{1,0:T(8,128)(2,1)S(1)}, u32[]{:S(2)}, u32[]{:S(2)}) collective-permute-start(bf16[128,256]{1,0:T(8,128)(2,1)S(1)} %add_convert_fusion.2.mine), channel_id=1, source_target_pairs={{0,6},{2,4},{4,2},{6,0},{8,14},{10,12},{12,10},{14,8},{1,7},{3,5},... | collective-permute-start | bytes 196616 | tf_op jit(solution)/shard_map/ppermute | solution.py:440
  87.2 6.2 %collective-permute-start.9 = (bf16[128,256]{1,0:T(8,128)(2,1)S(1)}, bf16[128,256]{1,0:T(8,128)(2,1)S(1)}, u32[]{:S(2)}, u32[]{:S(2)}) collective-permute-start(bf16[128,256]{1,0:T(8,128)(2,1)S(1)} %add_convert_fusion.2.mine), channel_id=1, source_target_pairs={{0,4},{4,0},{8,12},{12,8},{1,5},{5,1},{9,13},{13,9},{2,6},{6,2},{1... | collective-permute-start | bytes 196616 | tf_op jit(solution)/shard_map/ppermute | solution.py:400
  91.6 1.7 %copy-start.10 = (bf16[128,256]{1,0:T(8,128)(2,1)}, bf16[128,256]{1,0:T(8,128)(2,1)S(1)}, u32[]{:S(2)}) copy-start(bf16[128,256]{1,0:T(8,128)(2,1)S(1)} %collective-permute-done.10.along_day) | copy-start | bytes 196612
  92.6 0.7 copy-start.11
  93.4 0.6 copy-start.12

commit v13 on v12

--- a/solution.py
+++ b/solution.py
@@ -161,7 +161,9 @@
     mine_ref, other_ref, *refs = refs
     if chunk:
         start_mine_ref, start_other_ref, *refs = refs
-    own_out_ref, day_ref, home_ref, grad_mine_ref, grad_other_ref = refs
+        own_out_ref, day_ref, home_ref, *piece_refs, grad_mine_ref, grad_other_ref = refs
+    else:
+        own_out_ref, day_ref, home_ref, grad_mine_ref, grad_other_ref = refs
     factor = HD ** (-0.5)
     per_group = GROUP // HD // PACK
 
@@ -291,6 +293,16 @@
     finish(*waiting)
     end(waiting[0])
 
+    if chunk:
+        @pl.when(step == pl.num_programs(0) - 1)
+        def _():
+            first = lax.rem(lax.axis_index("day"), 2) == 0
+            for place, grad_ref in enumerate((grad_mine_ref, grad_other_ref)):
+                half = grad_ref.shape[0] // 2
+                low, high = grad_ref[:half], grad_ref[half:]
+                piece_refs[2 * place][...] = jnp.where(first, low, high).astype(BF16)
+                piece_refs[2 * place + 1][...] = jnp.where(first, high, low).astype(BF16)
+
 
 def fold_kernel(lay, tab, homes, own_a, own_b, day_a, day_b, home_a, home_b, keep, give):
     core = tab[lay.core]
@@ -357,6 +369,9 @@
         in_specs += [pl.BlockSpec(weights_block, fixed)] * 2
         operands += carried
     pieces = lay.chunk_items
+    grads = [pltpu.HBM(weights_block, F32)] * 2
+    if chunk:
+        grads = [jax.ShapeDtypeStruct((2 * GROUP, width), BF16)] * 4
     flops = 2 * pieces * (23 * BLOCK * width * width + 24 * BLOCK * 3 * BLOCK * 512)
     return pl.pallas_call(
         lambda *refs: attention_kernel(lay, chunk, *refs),
@@ -368,16 +383,15 @@
                 pl.BlockSpec((STEP_ITEMS, BLOCK, width), at_step),
                 pl.BlockSpec((STEP_ITEMS, BLOCK, width), at_step),
                 pl.BlockSpec((lay.places, BLOCK, width), lambda step, tab: (0, 0, 0)),
-                pl.BlockSpec(weights_block, fixed),
-                pl.BlockSpec(weights_block, fixed),
+                *[pl.BlockSpec(grad.shape, fixed) for grad in grads],
             ),
+            scratch_shapes=[pltpu.VMEM(weights_block, F32)] * (2 if chunk else 0),
         ),
         out_shape=(
             pltpu.HBM((pieces, BLOCK, width), F32),
             pltpu.HBM((pieces, BLOCK, width), BF16),
             pltpu.HBM((lay.places, BLOCK, width), BF16),
-            pltpu.HBM(weights_block, F32),
-            pltpu.HBM(weights_block, F32),
+            *grads,
         ),
         compiler_params=pltpu.CompilerParams(vmem_limit_bytes=32 << 20),
         cost_estimate=pl.CostEstimate(
@@ -405,39 +419,37 @@
     return low.astype(F32) + exchanged(low, axis, bit).astype(F32)
 
 
-def halved_over(value, axis):
-    half = value.shape[0] // 2
-    first = lax.rem(lax.axis_index(axis), 2) == 0
-    low = value.astype(BF16)
-    kept = jnp.where(first, low[:half], low[half:])
-    given = jnp.where(first, low[half:], low[:half])
-    return kept.astype(F32) + exchanged(given, axis, 1).astype(F32)
-
-
-def sum_gradients(total, home_b, fold):
-    part = halved_over(total, "day")
+def neighbours(axis, other):
+    size = lax.axis_size(other)
+    return [
+        (place * size + at, (place ^ 1) * size + (at ^ 1))
+        for place in range(lax.axis_size(axis))
+        for at in range(size)
+    ]
+
+
+def sum_gradients(part, home_b, fold):
     bit = 2
     while bit < lax.axis_size("day"):
         part = summed_over(part, "day", bit)
         bit *= 2
-    part = halved_over(part, "reach")
+    half = part.shape[0] // 2
+    first = lax.rem(lax.axis_index("reach"), 2) == 0
+    low = part.astype(BF16)
+    kept = jnp.where(first, low[:half], low[half:])
+    given = jnp.where(first, low[half:], low[:half])
+    part = kept.astype(F32) + exchanged(given, "reach", 1).astype(F32)
     part, home_b = lax.optimization_barrier((part, home_b))
     bit = 2
     while bit < lax.axis_size("reach"):
         part = summed_over(part, "reach", bit)
         bit *= 2
     part, folded = lax.optimization_barrier((part.astype(BF16), fold(home_b)))
-    days = lax.axis_size("day")
-    both = [
-        (reach * days + day, (reach ^ 1) * days + (day ^ 1))
-        for reach in range(lax.axis_size("reach"))
-        for day in range(days)
-    ]
     quarters = (
         part,
         exchanged(part, "reach", 1),
         exchanged(part, "day", 1),
-        lax.ppermute(part, ("reach", "day"), both),
+        lax.ppermute(part, ("reach", "day"), neighbours("reach", "day")),
     )
     return quarters, folded
 
@@ -528,11 +540,16 @@
     )
     home_a = ring(home_a)
     day_a = lax.ppermute(day_a, "day", last_day)
-    own_b, day_b, home_b, grad_mine, grad_other = attend(
+    own_b, day_b, home_b, kept, to_day, to_core, to_both = attend(
         lay, 1, tab, in_blocks, up_blocks, received_b, *shared, grads
     )
-    grad_swapped = exchanged(grad_other, "head", 1)
-    home_a, home_b, grad_swapped = lax.optimization_barrier((home_a, home_b, grad_swapped))
+    pieces = (
+        exchanged(to_day, "day", 1),
+        exchanged(to_core, "head", 1),
+        lax.ppermute(to_both, ("day", "head"), neighbours("day", "head")),
+    )
+    home_a, home_b, kept = lax.optimization_barrier((home_a, home_b, kept))
+    pieces = (kept, *pieces)
     home_b = ring(home_b)
     day_b = lax.ppermute(day_b, "day", last_day)
     half_shape = jax.ShapeDtypeStruct((blocks_dev, BLOCK, half), F32)
@@ -547,7 +564,9 @@
             name="fold",
         )(tab, homes, own_a, own_b, day_a, day_b, home_a, home_b)
 
-    quarters, (keep, give) = sum_gradients(grad_mine + grad_swapped, home_b, fold)
+    quarters, (keep, give) = sum_gradients(
+        sum(piece.astype(F32) for piece in pieces), home_b, fold
+    )
     got = exchanged(give, "head", 1)
     back_blocks = pl.pallas_call(
         add_kernel,
@@ -567,6 +586,7 @@
             jax.ShapeDtypeStruct((half, width), F32),
         ),
         grid=(1,),
+        compiler_params=pltpu.CompilerParams(vmem_limit_bytes=16 << 20),
         name="split",
     )(*quarters)
 

time: 96.5 us -> 91.7 us (0.950)
  waiting for transfers between devices: 26 us -> 24.2 us
  Pallas kernels: 31.7 us -> 30.4 us
  other arithmetic: 1.27 us -> 0.14 us
    ppermute x8, waiting for transfers between devices: 10.3 us -> 6.22 us  [exchanged(): lax.ppermute(value, axis, [(place, place ^ bit) for place in range(count)])]
    ppermute x1 -> x2, starting transfers between devices: 0.31 us -> 2.56 us  [the longest x1 1.92 us: sum_gradients(): lax.ppermute(part, ('reach', 'day'), neighbours('reach', 'day'))]
    ppermute x8, starting transfers between devices: 7.24 us -> 5.46 us  [exchanged(): lax.ppermute(value, axis, [(place, place ^ bit) for place in range(count)])]
    ppermute x1 -> x2, waiting for transfers between devices: 1.02 us -> 2.21 us  [the longest x1 2.09 us: sum_gradients(): lax.ppermute(part, ('reach', 'day'), neighbours('reach', 'day'))]
    convert_element_type x2 -> x1, other arithmetic: 1.18 us -> 0.07 us  [sum_gradients(): low = part.astype(BF16)]
    unnamed x39 -> x31, local copies, waits for them, and re-layouts: 3.95 us -> 3.32 us
  transfers between devices with their start and end apart: 16 -> 17, of which waited for: 11 -> 10; matrix products, arithmetic and copies ran while one was open for 0% -> 0% of each run, Pallas kernels for 28% -> 30%
where the time goes in v13:
time: 91.7 us; the launch traced here: 91.1 us
  starting transfers between devices  32.1 us (35%)
  Pallas kernels  30.4 us (33%)
  waiting for transfers between devices  24.2 us (26%)
  local copies, waits for them, and re-layouts  3.32 us (4%)
    pallas_call x2, Pallas kernels, attend(): pl.pallas_call(lambda *refs: attention_kernel(lay, chunk, *refs), grid_sp...  22.3 us
    all_to_all x4, starting transfers between devices, ring(): return lax.all_to_all(value, 'reach', 0, 0, tiled=True).reshape(shape)  18 us
    all_to_all x4, waiting for transfers between devices, ring(): return lax.all_to_all(value, 'reach', 0, 0, tiled=True).reshape(shape)  12.8 us
    ppermute x8, waiting for transfers between devices, exchanged(): lax.ppermute(value, axis, [(place, place ^ bit) for place in range(count)])  6.22 us
    ppermute x8, starting transfers between devices, exchanged(): lax.ppermute(value, axis, [(place, place ^ bit) for place in range(count)])  5.46 us
    ppermute x1, starting transfers between devices, on_device(): prior_inputs = lax.ppermute(prior, 'day', next_day)  3.56 us
    unnamed x31, local copies, waits for them, and re-layouts  3.32 us
    ppermute x1, waiting for transfers between devices, on_device(): day_a = lax.ppermute(day_a, 'day', last_day)  2.96 us
  transfers between devices with their start and end apart: 17, of which 10 were waited for; matrix products, arithmetic and copies ran while one was open for 0% of the time, Pallas kernels for 30%

profile of v13, /device:TPU:0, one launch (start us, length us, event | category | flops | bytes accessed | tf_op | source)
XLA Modules:
  0.0 91.1 jit_solution(15874383983840311457)
XLA Ops:
  0.6 0.0 copy-start
  0.6 2.6 %pick.1 = (bf16[8,128,256]{2,1,0:T(8,128)(2,1)}, s32[128]{0:T(128)S(1)}) custom-call(s32[64]{0:T(128)} %refs_0_.3, bf16[16,128,256]{2,1,0:T(8,128)(2,1)} %bitcast.14), custom_call_target="tpu_custom_call" | custom-call | tf_op jit(solution)/shard_map/pick/pallas_call | solution.py:494
  3.3 6.3 %all-to-all-start = ((bf16[4,256,256]{2,1,0:T(8,128)(2,1)}), bf16[4,256,256]{2,1,0:T(8,128)(2,1)S(1)}, u32[]{:S(2)}, u32[]{:S(2)}) async-start(bf16[4,256,256]{2,1,0:T(8,128)(2,1)} %bitcast.2), calls=%async_computation | async-start | bytes 1048576 | tf_op jit(solution)/shard_map/all_to_all | solution.py:530
  9.6 0.6 copy-done.3
  10.2 0.0 copy-done.4
  10.3 2.2 %deal.1 = (bf16[8,128,256]{2,1,0:T(8,128)(2,1)}, bf16[8,128,256]{2,1,0:T(8,128)(2,1)S(1)}, s32[128]{0:T(128)S(1)}) custom-call(s32[64]{0:T(128)S(1)} %copy-done.3, s32[64]{0:T(128)S(1)} %copy-done.4, s32[128]{0:T(128)S(1)} %get-tuple-element.41.refs_2_.refs_1_, bf16[16,128,256]{2,1,0:T(8,128)(2,1)S(1)} %bitcast.23), custom_call_target="tpu_custom_call" | custom-call | tf_op jit(solution)/shard_map/deal/pallas_call | solution.py:510
  12.5 0.0 copy-start.7
  12.5 3.6 %collective-permute-start = (bf16[8,128,256]{2,1,0:T(8,128)(2,1)S(1)}, bf16[8,128,256]{2,1,0:T(8,128)(2,1)S(1)}, u32[]{:S(2)}, u32[]{:S(2)}) collective-permute-start(bf16[8,128,256]{2,1,0:T(8,128)(2,1)S(1)} %get-tuple-element.44), channel_id=1, source_target_pairs={{0,2},{1,3},{4,6},{5,7},{8,10},{9,11},{12,14},{13,15},{16,18},{17,... | collective-permute-start | bytes 1572872 | tf_op jit(solution)/shard_map/ppermute | solution.py:535
  16.0 0.1 copy.13
  16.2 0.0 copy-start.8
  16.2 0.1 copy.14
  16.3 0.7 copy-done.8
  17.0 0.1 copy.15
  17.1 0.7 copy-done.9
  17.9 0.1 collective-permute-start.1
  18.0 6.1 %all-to-all-done = bf16[4,256,256]{2,1,0:T(8,128)(2,1)S(1)} async-done(((bf16[4,256,256]{2,1,0:T(8,128)(2,1)}), bf16[4,256,256]{2,1,0:T(8,128)(2,1)S(1)}, u32[]{:S(2)}, u32[]{:S(2)}) %all-to-all-start) | async-done | bytes 524320 | tf_op jit(solution)/shard_map/all_to_all | solution.py:530
  24.1 3.5 %all-to-all-start.2 = ((bf16[4,256,256]{2,1,0:T(8,128)(2,1)}), bf16[4,256,256]{2,1,0:T(8,128)(2,1)S(1)}, u32[]{:S(2)}, u32[]{:S(2)}) async-start(bf16[4,256,256]{2,1,0:T(8,128)(2,1)} %bitcast.9), calls=%async_computation.2 | async-start | bytes 1048576 | tf_op jit(solution)/shard_map/all_to_all | solution.py:530
  27.6 0.0 collective-permute-done.1.refs_18_
  27.6 0.0 copy-start.10
  27.6 0.7 copy-done.13
  28.3 0.2 copy-done.10
  28.4 11.2 %attention_0.1 = (f32[4,128,256]{2,1,0:T(8,128)}, bf16[4,128,256]{2,1,0:T(8,128)(2,1)}, bf16[8,128,256]{2,1,0:T(8,128)(2,1)}, f32[512,256]{1,0:T(8,128)}, f32[512,256]{1,0:T(8,128)}) custom-call(s32[128]{0:T(128)S(1)} %get-tuple-element.42.refs_0_, bf16[16,128,256]{2,1,0:T(8,128)(2,1)} %bitcast.15, bf16[16,128,256]{2,1,0:T(8,128)(2,1)} %bitcast.40, ...), custom_call_target="tpu_custom_call" | custom-call | flops 6375342080 | bytes 5242880 | tf_op jit(solution)/shard_map/attention_0/pallas_call | solution.py:376
  39.6 1.9 %all-to-all-done.2 = bf16[4,256,256]{2,1,0:T(8,128)(2,1)S(1)} async-done(((bf16[4,256,256]{2,1,0:T(8,128)(2,1)}), bf16[4,256,256]{2,1,0:T(8,128)(2,1)S(1)}, u32[]{:S(2)}, u32[]{:S(2)}) %all-to-all-start.2) | async-done | bytes 524320 | tf_op jit(solution)/shard_map/all_to_all | solution.py:530
  41.5 3.6 %all-to-all-start.1 = ((bf16[4,256,256]{2,1,0:T(8,128)(2,1)}), bf16[4,256,256]{2,1,0:T(8,128)(2,1)S(1)}, u32[]{:S(2)}, u32[]{:S(2)}) async-start(bf16[4,256,256]{2,1,0:T(8,128)(2,1)} %bitcast.36), calls=%async_computation.1 | async-start | bytes 1048576 | tf_op jit(solution)/shard_map/all_to_all | solution.py:530
  45.2 11.1 %attention_1.1 = (f32[4,128,256]{2,1,0:T(8,128)}, bf16[4,128,256]{2,1,0:T(8,128)(2,1)}, bf16[8,128,256]{2,1,0:T(8,128)(2,1)}, bf16[256,256]{1,0:T(8,128)(2,1)S(1...) custom-call(s32[128]{0:T(128)S(1)} %get-tuple-element.42.refs_0_, ...), custom_call_target="tpu_custom_call" | custom-call | flops 6375342080 | bytes 5242880 | tf_op jit(solution)/shard_map/attention_1/pallas_call | solution.py:376
  56.3 1.5 %collective-permute-start.2 = (bf16[256,256]{1,0:T(8,128)(2,1)S(1)}, bf16[256,256]{1,0:T(8,128)(2,1)S(1)}, u32[]{:S(2)}, u32[]{:S(2)}) collective-permute-start(bf16[256,256]{1,0:T(8,128)(2,1)S(1)} %get-tuple-element.52), channel_id=1, source_target_pairs={{0,2},{2,0},{1,3},{3,1},{4,6},{6,4},{5,7},{7,5},{8,10},{10,8},{9,1... | collective-permute-start | bytes 393224 | tf_op jit(solution)/shard_map/ppermute | solution.py:414
  57.8 0.6 collective-permute-start.4
  58.5 0.5 all-to-all-done.1
  58.9 4.5 %all-to-all-start.3 = ((bf16[4,256,256]{2,1,0:T(8,128)(2,1)}), bf16[4,256,256]{2,1,0:T(8,128)(2,1)S(1)}, u32[]{:S(2)}, u32[]{:S(2)}) async-start(bf16[4,256,256]{2,1,0:T(8,128)(2,1)} %bitcast.35), calls=%async_computation.3 | async-start | bytes 1048576 | tf_op jit(solution)/shard_map/all_to_all | solution.py:530
  63.5 0.1 collective-permute-done.4
  63.6 0.1 add_convert_fusion
  63.7 2.0 %collective-permute-start.5 = (bf16[128,256]{1,0:T(8,128)(2,1)S(1)}, bf16[128,256]{1,0:T(8,128)(2,1)S(1)}, u32[]{:S(2)}, u32[]{:S(2)}) collective-permute-start(bf16[128,256]{1,0:T(8,128)(2,1)S(1)} %broadcast_select_fusion), channel_id=1, source_target_pairs={{0,4},{4,0},{8,12},{12,8},{1,5},{5,1},{9,13},{13,9},{2,6},{6,2},{1... | collective-permute-start | bytes 196616 | tf_op jit(solution)/shard_map/ppermute | solution.py:414
  65.7 1.3 %collective-permute-start.8 = (bf16[4,128,256]{2,1,0:T(8,128)(2,1)S(1)}, bf16[4,128,256]{2,1,0:T(8,128)(2,1)S(1)}, u32[]{:S(2)}, u32[]{:S(2)}) collective-permute-start(bf16[4,128,256]{2,1,0:T(8,128)(2,1)S(1)} %copy-done.12), channel_id=1, source_target_pairs={{2,0},{3,1},{6,4},{7,5},{10,8},{11,9},{14,12},{15,13},{18,16},{19,... | collective-permute-start | bytes 786440 | tf_op jit(solution)/shard_map/ppermute | solution.py:554
  67.0 1.3 %collective-permute-start.7 = (bf16[4,128,256]{2,1,0:T(8,128)(2,1)S(1)}, bf16[4,128,256]{2,1,0:T(8,128)(2,1)S(1)}, u32[]{:S(2)}, u32[]{:S(2)}) collective-permute-start(bf16[4,128,256]{2,1,0:T(8,128)(2,1)S(1)} %copy-done.11), channel_id=1, source_target_pairs={{2,0},{3,1},{6,4},{7,5},{10,8},{11,9},{14,12},{15,13},{18,16},{19,... | collective-permute-start | bytes 786440 | tf_op jit(solution)/shard_map/ppermute | solution.py:542
  68.3 5.5 %collective-permute-done.5 = bf16[128,256]{1,0:T(8,128)(2,1)S(1)} collective-permute-done((bf16[128,256]{1,0:T(8,128)(2,1)S(1)}, bf16[128,256]{1,0:T(8,128)(2,1)S(1)}, u32[]{:S(2)}, u32[]{:S(2)}) %collective-permute-start.5) | collective-permute-done | bytes 65568 | tf_op jit(solution)/shard_map/ppermute | solution.py:414
  73.8 4.3 %all-to-all-done.3 = bf16[4,256,256]{2,1,0:T(8,128)(2,1)S(1)} async-done(((bf16[4,256,256]{2,1,0:T(8,128)(2,1)}), bf16[4,256,256]{2,1,0:T(8,128)(2,1)S(1)}, u32[]{:S(2)}, u32[]{:S(2)}) %all-to-all-start.3) | async-done | bytes 524320 | tf_op jit(solution)/shard_map/all_to_all | solution.py:530
  78.1 0.2 collective-permute-start.6
  78.3 3.0 %collective-permute-done.7.refs_4_ = bf16[4,128,256]{2,1,0:T(8,128)(2,1)S(1)} collective-permute-done((bf16[4,128,256]{2,1,0:T(8,128)(2,1)S(1)}, bf16[4,128,256]{2,1,0:T(8,128)(2,1)S(1)}, u32[]{:S(2)}, u32[]{:S(2)}) %collective-permute-start.7) | collective-permute-done | bytes 262176 | tf_op jit(solution)/shard_map/ppermute | solution.py:542
  81.3 1.6 %fold.1 = (f32[16,128,128]{2,1,0:T(8,128)S(1)}, f32[16,128,128]{2,1,0:T(8,128)S(1)}) custom-call(s32[128]{0:T(128)S(1)} %get-tuple-element.42.refs_0_, s32[128]{0:T(128)S(1)} %get-tuple-element.41.refs_2_.refs_1_, f32[4,128,256]{2,1,0:T(8,128)S(1)} %copy-done.1, f32[4,128,256]{2,1,0:T(8,128)S(1)} %copy-done.2, ...), custom_call_target="tpu_custom_call" | custom-call | tf_op jit(solution)/shard_map/fold/pallas_call | solution.py:558
  82.9 0.4 collective-permute-done.6
  83.3 0.1 collective-permute-start.9
  83.4 0.1 collective-permute-start.10
  83.5 1.6 %collective-permute-start.11 = (bf16[128,256]{1,0:T(8,128)(2,1)S(1)}, bf16[128,256]{1,0:T(8,128)(2,1)S(1)}, u32[]{:S(2)}, u32[]{:S(2)}) collective-permute-start(bf16[128,256]{1,0:T(8,128)(2,1)S(1)} %add_convert_fusion.1.mine), channel_id=1, source_target_pairs={{0,2},{2,0},{1,3},{3,1},{4,6},{6,4},{5,7},{7,5},{8,10},{10,8},{9,1... | collective-permute-start | bytes 196616 | tf_op jit(solution)/shard_map/ppermute | solution.py:414
  85.0 1.9 %collective-permute-start.12 = (bf16[128,256]{1,0:T(8,128)(2,1)S(1)}, bf16[128,256]{1,0:T(8,128)(2,1)S(1)}, u32[]{:S(2)}, u32[]{:S(2)}) collective-permute-start(bf16[128,256]{1,0:T(8,128)(2,1)S(1)} %add_convert_fusion.1.mine), channel_id=1, source_target_pairs={{0,6},{2,4},{4,2},{6,0},{8,14},{10,12},{12,10},{14,8},{1,7},{3,5},... | collective-permute-start | bytes 196616 | tf_op jit(solution)/shard_map/ppermute | solution.py:452
  86.9 0.9 add.26
  87.8 0.3 collective-permute-done.10.along_reach
  88.1 2.1 %collective-permute-done.12.along_both = bf16[128,256]{1,0:T(8,128)(2,1)S(1)} collective-permute-done((bf16[128,256]{1,0:T(8,128)(2,1)S(1)}, bf16[128,256]{1,0:T(8,128)(2,1)S(1)}, u32[]{:S(2)}, u32[]{:S(2)}) %collective-permute-start.12) | collective-permute-done | bytes 65568 | tf_op jit(solution)/shard_map/ppermute | solution.py:452
  90.2 0.8 split.1
  (29 shorter events, 0.1 us)
Async XLA Ops:
  0.6 9.0 %copy-start = (bf16[1,2048,256]{2,1,0:T(8,128)(2,1)S(1)}, bf16[1,2048,256]{2,1,0:T(8,128)(2,1)}, u32[]{:S(2)}) copy-start(bf16[1,2048,256]{2,1,0:T(8,128)(2,1)} %param.8) | copy-start | bytes 3145732
  3.3 20.8 %all-to-all-start = ((bf16[4,256,256]{2,1,0:T(8,128)(2,1)}), bf16[4,256,256]{2,1,0:T(8,128)(2,1)S(1)}, u32[]{:S(2)}, u32[]{:S(2)}) async-start(bf16[4,256,256]{2,1,0:T(8,128)(2,1)} %bitcast.2), calls=%async_computation | async-start | bytes 1048576 | tf_op jit(solution)/shard_map/all_to_all | solution.py:530
  9.6 0.7 copy-start.3
  9.6 0.7 copy-start.4
  10.3 5.8 %copy-start.6 = (bf16[256,128]{1,0:T(8,128)(2,1)S(1)}, bf16[256,128]{1,0:T(8,128)(2,1)}, u32[]{:S(2)}) copy-start(bf16[256,128]{1,0:T(8,128)(2,1)} %param.11) | copy-start | bytes 196612
  12.5 3.7 %copy-start.7 = (bf16[256,128]{1,0:T(8,128)(2,1)S(1)}, bf16[256,128]{1,0:T(8,128)(2,1)}, u32[]{:S(2)}) copy-start(bf16[256,128]{1,0:T(8,128)(2,1)} %param.12) | copy-start | bytes 196612
  12.5 15.1 %collective-permute-start = (bf16[8,128,256]{2,1,0:T(8,128)(2,1)S(1)}, bf16[8,128,256]{2,1,0:T(8,128)(2,1)S(1)}, u32[]{:S(2)}, u32[]{:S(2)}) collective-permute-start(bf16[8,128,256]{2,1,0:T(8,128)(2,1)S(1)} %get-tuple-element.44), channel_id=1, source_target_pairs={{0,2},{1,3},{4,6},{5,7},{8,10},{9,11},{12,14},{13,15},{16,18},{17,... | collective-permute-start | bytes 1572872 | tf_op jit(solution)/shard_map/ppermute | solution.py:535
  16.2 0.8 copy-start.8
  17.0 0.8 copy-start.9
  17.9 6.2 %copy-start.5 = (bf16[512,256]{1,0:T(8,128)(2,1)}, bf16[512,256]{1,0:T(8,128)(2,1)S(1)}, u32[]{:S(2)}) copy-start(bf16[512,256]{1,0:T(8,128)(2,1)S(1)} %pad_maximum_fusion.refs_17_) | copy-start | bytes 786436
  17.9 9.7 %collective-permute-start.1 = (bf16[512,256]{1,0:T(8,128)(2,1)S(1)}, bf16[512,256]{1,0:T(8,128)(2,1)S(1)}, u32[]{:S(2)}, u32[]{:S(2)}) collective-permute-start(bf16[512,256]{1,0:T(8,128)(2,1)S(1)} %pad_maximum_fusion.refs_17_), channel_id=1, source_target_pairs={{0,1},{1,0},{2,3},{3,2},{4,5},{5,4},{6,7},{7,6},{8,9},{9,8},{10,11... | collective-permute-start | bytes 786440 | tf_op jit(solution)/shard_map/ppermute | solution.py:414
  24.1 17.4 %all-to-all-start.2 = ((bf16[4,256,256]{2,1,0:T(8,128)(2,1)}), bf16[4,256,256]{2,1,0:T(8,128)(2,1)S(1)}, u32[]{:S(2)}, u32[]{:S(2)}) async-start(bf16[4,256,256]{2,1,0:T(8,128)(2,1)} %bitcast.9), calls=%async_computation.2 | async-start | bytes 1048576 | tf_op jit(solution)/shard_map/all_to_all | solution.py:530
  27.6 0.7 copy-start.13
  27.6 0.9 copy-start.10
  41.5 17.4 %all-to-all-start.1 = ((bf16[4,256,256]{2,1,0:T(8,128)(2,1)}), bf16[4,256,256]{2,1,0:T(8,128)(2,1)S(1)}, u32[]{:S(2)}, u32[]{:S(2)}) async-start(bf16[4,256,256]{2,1,0:T(8,128)(2,1)} %bitcast.36), calls=%async_computation.1 | async-start | bytes 1048576 | tf_op jit(solution)/shard_map/all_to_all | solution.py:530
  56.3 7.1 %collective-permute-start.2 = (bf16[256,256]{1,0:T(8,128)(2,1)S(1)}, bf16[256,256]{1,0:T(8,128)(2,1)S(1)}, u32[]{:S(2)}, u32[]{:S(2)}) collective-permute-start(bf16[256,256]{1,0:T(8,128)(2,1)S(1)} %get-tuple-element.52), channel_id=1, source_target_pairs={{0,2},{2,0},{1,3},{3,1},{4,6},{6,4},{5,7},{7,5},{8,10},{10,8},{9,1... | collective-permute-start | bytes 393224 | tf_op jit(solution)/shard_map/ppermute | solution.py:414
  57.8 5.7 %collective-permute-start.3 = (bf16[256,256]{1,0:T(8,128)(2,1)S(1)}, bf16[256,256]{1,0:T(8,128)(2,1)S(1)}, u32[]{:S(2)}, u32[]{:S(2)}) collective-permute-start(bf16[256,256]{1,0:T(8,128)(2,1)S(1)} %get-tuple-element.53), channel_id=1, source_target_pairs={{0,1},{1,0},{2,3},{3,2},{4,5},{5,4},{6,7},{7,6},{8,9},{9,8},{10,11... | collective-permute-start | bytes 393224 | tf_op jit(solution)/shard_map/ppermute | solution.py:414
  57.8 5.8 %collective-permute-start.4 = (bf16[256,256]{1,0:T(8,128)(2,1)S(1)}, bf16[256,256]{1,0:T(8,128)(2,1)S(1)}, u32[]{:S(2)}, u32[]{:S(2)}) collective-permute-start(bf16[256,256]{1,0:T(8,128)(2,1)S(1)} %get-tuple-element.54), channel_id=1, source_target_pairs={{0,3},{1,2},{2,1},{3,0},{4,7},{5,6},{6,5},{7,4},{8,11},{9,10},{10,... | collective-permute-start | bytes 393224 | tf_op jit(solution)/shard_map/ppermute | solution.py:549
  58.9 6.7 %copy-start.12 = (bf16[4,128,256]{2,1,0:T(8,128)(2,1)S(1)}, bf16[4,128,256]{2,1,0:T(8,128)(2,1)}, u32[]{:S(2)}) copy-start(bf16[4,128,256]{2,1,0:T(8,128)(2,1)} %get-tuple-element.60) | copy-start | bytes 786436
  58.9 8.0 %copy-start.11 = (bf16[4,128,256]{2,1,0:T(8,128)(2,1)S(1)}, bf16[4,128,256]{2,1,0:T(8,128)(2,1)}, u32[]{:S(2)}) copy-start(bf16[4,128,256]{2,1,0:T(8,128)(2,1)} %get-tuple-element.59) | copy-start | bytes 786436
  58.9 19.2 %all-to-all-start.3 = ((bf16[4,256,256]{2,1,0:T(8,128)(2,1)}), bf16[4,256,256]{2,1,0:T(8,128)(2,1)S(1)}, u32[]{:S(2)}, u32[]{:S(2)}) async-start(bf16[4,256,256]{2,1,0:T(8,128)(2,1)} %bitcast.35), calls=%async_computation.3 | async-start | bytes 1048576 | tf_op jit(solution)/shard_map/all_to_all | solution.py:530
  63.5 17.8 %copy-start.1 = (f32[4,128,256]{2,1,0:T(8,128)S(1)}, f32[4,128,256]{2,1,0:T(8,128)}, u32[]{:S(2)}) copy-start(f32[4,128,256]{2,1,0:T(8,128)} %get-tuple-element.57.refs_2_) | copy-start | bytes 1572868
  63.5 17.8 %copy-start.2 = (f32[4,128,256]{2,1,0:T(8,128)S(1)}, f32[4,128,256]{2,1,0:T(8,128)}, u32[]{:S(2)}) copy-start(f32[4,128,256]{2,1,0:T(8,128)} %get-tuple-element.58.refs_3_) | copy-start | bytes 1572868
  63.7 10.1 %collective-permute-start.5 = (bf16[128,256]{1,0:T(8,128)(2,1)S(1)}, bf16[128,256]{1,0:T(8,128)(2,1)S(1)}, u32[]{:S(2)}, u32[]{:S(2)}) collective-permute-start(bf16[128,256]{1,0:T(8,128)(2,1)S(1)} %broadcast_select_fusion), channel_id=1, source_target_pairs={{0,4},{4,0},{8,12},{12,8},{1,5},{5,1},{9,13},{13,9},{2,6},{6,2},{1... | collective-permute-start | bytes 196616 | tf_op jit(solution)/shard_map/ppermute | solution.py:414
  65.7 12.7 %collective-permute-start.8 = (bf16[4,128,256]{2,1,0:T(8,128)(2,1)S(1)}, bf16[4,128,256]{2,1,0:T(8,128)(2,1)S(1)}, u32[]{:S(2)}, u32[]{:S(2)}) collective-permute-start(bf16[4,128,256]{2,1,0:T(8,128)(2,1)S(1)} %copy-done.12), channel_id=1, source_target_pairs={{2,0},{3,1},{6,4},{7,5},{10,8},{11,9},{14,12},{15,13},{18,16},{19,... | collective-permute-start | bytes 786440 | tf_op jit(solution)/shard_map/ppermute | solution.py:554
  67.0 14.3 %collective-permute-start.7 = (bf16[4,128,256]{2,1,0:T(8,128)(2,1)S(1)}, bf16[4,128,256]{2,1,0:T(8,128)(2,1)S(1)}, u32[]{:S(2)}, u32[]{:S(2)}) collective-permute-start(bf16[4,128,256]{2,1,0:T(8,128)(2,1)S(1)} %copy-done.11), channel_id=1, source_target_pairs={{2,0},{3,1},{6,4},{7,5},{10,8},{11,9},{14,12},{15,13},{18,16},{19,... | collective-permute-start | bytes 786440 | tf_op jit(solution)/shard_map/ppermute | solution.py:542
  78.1 5.2 %collective-permute-start.6 = (bf16[128,256]{1,0:T(8,128)(2,1)S(1)}, bf16[128,256]{1,0:T(8,128)(2,1)S(1)}, u32[]{:S(2)}, u32[]{:S(2)}) collective-permute-start(bf16[128,256]{1,0:T(8,128)(2,1)S(1)} %convert_add_fusion), channel_id=1, source_target_pairs={{0,8},{4,12},{8,0},{12,4},{1,9},{5,13},{9,1},{13,5},{2,10},{6,14},... | collective-permute-start | bytes 196616 | tf_op jit(solution)/shard_map/ppermute | solution.py:414
  83.3 3.6 %collective-permute-start.9 = (f32[16,128,128]{2,1,0:T(8,128)S(1)}, f32[16,128,128]{2,1,0:T(8,128)S(1)}, u32[]{:S(2)}, u32[]{:S(2)}) collective-permute-start(f32[16,128,128]{2,1,0:T(8,128)S(1)} %get-tuple-element.66), channel_id=1, source_target_pairs={{0,1},{1,0},{2,3},{3,2},{4,5},{5,4},{6,7},{7,6},{8,9},{9,8},{10,11... | collective-permute-start | bytes 3145736 | tf_op jit(solution)/shard_map/ppermute | solution.py:414
  83.4 4.7 %collective-permute-start.10 = (bf16[128,256]{1,0:T(8,128)(2,1)S(1)}, bf16[128,256]{1,0:T(8,128)(2,1)S(1)}, u32[]{:S(2)}, u32[]{:S(2)}) collective-permute-start(bf16[128,256]{1,0:T(8,128)(2,1)S(1)} %add_convert_fusion.1.mine), channel_id=1, source_target_pairs={{0,4},{4,0},{8,12},{12,8},{1,5},{5,1},{9,13},{13,9},{2,6},{6,2},{1... | collective-permute-start | bytes 196616 | tf_op jit(solution)/shard_map/ppermute | solution.py:414
  83.5 4.7 %collective-permute-start.11 = (bf16[128,256]{1,0:T(8,128)(2,1)S(1)}, bf16[128,256]{1,0:T(8,128)(2,1)S(1)}, u32[]{:S(2)}, u32[]{:S(2)}) collective-permute-start(bf16[128,256]{1,0:T(8,128)(2,1)S(1)} %add_convert_fusion.1.mine), channel_id=1, source_target_pairs={{0,2},{2,0},{1,3},{3,1},{4,6},{6,4},{5,7},{7,5},{8,10},{10,8},{9,1... | collective-permute-start | bytes 196616 | tf_op jit(solution)/shard_map/ppermute | solution.py:414
  85.0 5.2 %collective-permute-start.12 = (bf16[128,256]{1,0:T(8,128)(2,1)S(1)}, bf16[128,256]{1,0:T(8,128)(2,1)S(1)}, u32[]{:S(2)}, u32[]{:S(2)}) collective-permute-start(bf16[128,256]{1,0:T(8,128)(2,1)S(1)} %add_convert_fusion.1.mine), channel_id=1, source_target_pairs={{0,6},{2,4},{4,2},{6,0},{8,14},{10,12},{12,10},{14,8},{1,7},{3,5},... | collective-permute-start | bytes 196616 | tf_op jit(solution)/shard_map/ppermute | solution.py:452

commit v14 on v13

--- a/solution.py
+++ b/solution.py
@@ -44,6 +44,18 @@
         self.homes_size = -(-(self.spare_pick + 1) // 128) * 128
 
 
+def quotient(value, count):
+    if count & (count - 1) == 0:
+        return lax.shift_right_logical(value, jnp.int32(count.bit_length() - 1))
+    return lax.div(value, count)
+
+
+def remainder(value, count):
+    if count & (count - 1) == 0:
+        return lax.bitwise_and(value, jnp.int32(count - 1))
+    return lax.rem(value, count)
+
+
 def pick_kernel(lay, partner_hbm, inputs, sent, homes, partner, held, sems):
     bd, slots = lay.blocks, lay.slots
     reach_pos, core = lax.axis_index("reach"), lax.axis_index("head")
@@ -60,15 +72,15 @@
         wanted = []
         for index in range(bd):
             block = partner[peer * bd + index]
-            source = lax.div(block, bd)
+            source = quotient(block, bd)
             base = base + jnp.where(source < reach_pos, 1, 0)
-            wanted.append((source == reach_pos, lax.rem(block, bd)))
+            wanted.append((source == reach_pos, remainder(block, bd)))
         rank = jnp.int32(0)
         for hit, local in wanted:
             place = base + rank
-            owner = lax.rem(place, CORES)
-            chunk = lax.rem(lax.div(place, CORES), CHUNKS)
-            slot = peer * slots + jnp.minimum(lax.div(rank, WORKERS), slots - 1)
+            owner = remainder(place, CORES)
+            chunk = remainder(quotient(place, CORES), CHUNKS)
+            slot = peer * slots + jnp.minimum(quotient(rank, WORKERS), slots - 1)
             target = jnp.where(hit, local, lay.spare)
             homes[lay.home_of + target] = slot
             homes[lay.chunk_of + target] = chunk
@@ -96,7 +108,7 @@
     lax.fori_loop(0, lay.reach, clear, 0, unroll=True)
 
     def count(index, carry):
-        source = lax.div(partner[reach_pos * bd + index], bd)
+        source = quotient(partner[reach_pos * bd + index], bd)
         start[source] = start[source] + 1
         return carry
 
@@ -111,14 +123,14 @@
 
     def assign(index, carry):
         wanted = partner[reach_pos * bd + index]
-        source = lax.div(wanted, bd)
+        source = quotient(wanted, bd)
         rank = used[source]
         used[source] = rank + 1
         place = start[source] + rank
-        owner = lax.rem(place, CORES)
-        chunk = lax.rem(lax.div(place, CORES), CHUNKS)
-        item = chunk * lay.chunk_items + lax.div(place, WORKERS)
-        slot = jnp.minimum(lax.div(rank, WORKERS), slots - 1)
+        owner = remainder(place, CORES)
+        chunk = remainder(quotient(place, CORES), CHUNKS)
+        item = chunk * lay.chunk_items + quotient(place, WORKERS)
+        slot = jnp.minimum(quotient(rank, WORKERS), slots - 1)
         tab[lay.owner_of + index] = owner
         tab[lay.item_of + index] = item
 
@@ -428,7 +440,7 @@
     ]
 
 
-def sum_gradients(part, home_b, fold):
+def sum_gradients(part, home_b, day_b, fold):
     bit = 2
     while bit < lax.axis_size("day"):
         part = summed_over(part, "day", bit)
@@ -439,19 +451,21 @@
     kept = jnp.where(first, low[:half], low[half:])
     given = jnp.where(first, low[half:], low[:half])
     part = kept.astype(F32) + exchanged(given, "reach", 1).astype(F32)
-    part, home_b = lax.optimization_barrier((part, home_b))
+    part, day_b = lax.optimization_barrier((part, day_b))
     bit = 2
     while bit < lax.axis_size("reach"):
         part = summed_over(part, "reach", bit)
         bit *= 2
-    part, folded = lax.optimization_barrier((part.astype(BF16), fold(home_b)))
+    part, home_b = lax.optimization_barrier((part.astype(BF16), home_b))
     quarters = (
         part,
         exchanged(part, "reach", 1),
         exchanged(part, "day", 1),
         lax.ppermute(part, ("reach", "day"), neighbours("reach", "day")),
     )
-    return quarters, folded
+    keep, give = fold(home_b, day_b)
+    quarters, give = lax.optimization_barrier((quarters, give))
+    return quarters, (keep, give)
 
 
 def split_kernel(mine, along_reach, along_day, along_both, query_out, key_out, value_out, output_out):
@@ -548,13 +562,13 @@
         exchanged(to_core, "head", 1),
         lax.ppermute(to_both, ("day", "head"), neighbours("day", "head")),
     )
-    home_a, home_b, kept = lax.optimization_barrier((home_a, home_b, kept))
+    home_a, day_a, home_b, kept = lax.optimization_barrier((home_a, day_a, home_b, kept))
     pieces = (kept, *pieces)
     home_b = ring(home_b)
     day_b = lax.ppermute(day_b, "day", last_day)
     half_shape = jax.ShapeDtypeStruct((blocks_dev, BLOCK, half), F32)
 
-    def fold(home_b):
+    def fold(home_b, day_b):
         return pl.pallas_call(
             lambda *refs: fold_kernel(lay, *refs),
             out_shape=(half_shape, half_shape),
@@ -565,7 +579,7 @@
         )(tab, homes, own_a, own_b, day_a, day_b, home_a, home_b)
 
     quarters, (keep, give) = sum_gradients(
-        sum(piece.astype(F32) for piece in pieces), home_b, fold
+        sum(piece.astype(F32) for piece in pieces), home_b, day_b, fold
     )
     got = exchanged(give, "head", 1)
     back_blocks = pl.pallas_call(
@@ -576,7 +590,6 @@
         compiler_params=pltpu.CompilerParams(vmem_limit_bytes=16 << 20),
         name="add",
     )(keep, got)
-    back_blocks, quarters = lax.optimization_barrier((back_blocks, quarters))
     weight_grads = pl.pallas_call(
         split_kernel,
         out_shape=(

time: 91.7 us -> 94.7 us (1.033)
  starting transfers between devices: 32.1 us -> 36.5 us
  waiting for transfers between devices: 24.2 us -> 23.2 us
    ppermute x8, starting transfers between devices: 5.46 us -> 11.4 us  [exchanged(): lax.ppermute(value, axis, [(place, place ^ bit) for place in range(count)])]
    ppermute x8, waiting for transfers between devices: 6.22 us -> 11.9 us  [exchanged(): lax.ppermute(value, axis, [(place, place ^ bit) for place in range(count)])]
    all_to_all x4, waiting for transfers between devices: 12.8 us -> 8.15 us  [ring(): return lax.all_to_all(value, 'reach', 0, 0, tiled=True).reshape(shape)]
    ppermute x1, waiting for transfers between devices: 2.96 us -> 0.01 us  [on_device(): day_a = lax.ppermute(day_a, 'day', last_day)]
    ppermute x1, starting transfers between devices: 1.92 us -> 0.08 us  [sum_gradients(): lax.ppermute(part, ('reach', 'day'), neighbours('reach', 'day'))]
    ppermute x1, waiting for transfers between devices: 0.01 us -> 1.49 us  [on_device(): day_b = lax.ppermute(day_b, 'day', last_day)]
  transfers between devices with their start and end apart: 17 -> 17, of which waited for: 10 -> 7; matrix products, arithmetic and copies ran while one was open for 0% -> 0% of each run, Pallas kernels for 30% -> 28%
where the time goes in v14:
time: 94.7 us; the launch traced here: 94.1 us
  starting transfers between devices  36.5 us (39%)
  Pallas kernels  30 us (32%)
  waiting for transfers between devices  23.2 us (24%)
  local copies, waits for them, and re-layouts  3.32 us (4%)
    pallas_call x2, Pallas kernels, attend(): pl.pallas_call(lambda *refs: attention_kernel(lay, chunk, *refs), grid_sp...  22.3 us
    all_to_all x4, starting transfers between devices, ring(): return lax.all_to_all(value, 'reach', 0, 0, tiled=True).reshape(shape)  18.6 us
    ppermute x8, waiting for transfers between devices, exchanged(): lax.ppermute(value, axis, [(place, place ^ bit) for place in range(count)])  11.9 us
    ppermute x8, starting transfers between devices, exchanged(): lax.ppermute(value, axis, [(place, place ^ bit) for place in range(count)])  11.4 us
    all_to_all x4, waiting for transfers between devices, ring(): return lax.all_to_all(value, 'reach', 0, 0, tiled=True).reshape(shape)  8.15 us
    ppermute x1, starting transfers between devices, on_device(): prior_inputs = lax.ppermute(prior, 'day', next_day)  3.56 us
    unnamed x31, local copies, waits for them, and re-layouts  3.32 us
    pallas_call x1, Pallas kernels, on_device(): pl.pallas_call(lambda *refs: pick_kernel(lay, *refs), out_shape=(sent_sha...  2.3 us
  transfers between devices with their start and end apart: 17, of which 7 were waited for; matrix products, arithmetic and copies ran while one was open for 0% of the time, Pallas kernels for 28%

profile of v14, /device:TPU:0, one launch (start us, length us, event | category | flops | bytes accessed | tf_op | source)
XLA Modules:
  0.0 94.1 jit_solution(13477819684234507357)
XLA Ops:
  0.6 0.0 copy-start
  0.6 2.3 %pick.1 = (bf16[8,128,256]{2,1,0:T(8,128)(2,1)}, s32[128]{0:T(128)S(1)}) custom-call(s32[64]{0:T(128)} %refs_0_.3, bf16[16,128,256]{2,1,0:T(8,128)(2,1)} %bitcast.14), custom_call_target="tpu_custom_call" | custom-call | tf_op jit(solution)/shard_map/pick/pallas_call | solution.py:508
  2.9 6.3 %all-to-all-start = ((bf16[4,256,256]{2,1,0:T(8,128)(2,1)}), bf16[4,256,256]{2,1,0:T(8,128)(2,1)S(1)}, u32[]{:S(2)}, u32[]{:S(2)}) async-start(bf16[4,256,256]{2,1,0:T(8,128)(2,1)} %bitcast.2), calls=%async_computation | async-start | bytes 1048576 | tf_op jit(solution)/shard_map/all_to_all | solution.py:544
  9.3 0.6 copy-done.3
  9.9 0.0 copy-done.4
  10.0 2.0 %deal.1 = (bf16[8,128,256]{2,1,0:T(8,128)(2,1)}, bf16[8,128,256]{2,1,0:T(8,128)(2,1)S(1)}, s32[128]{0:T(128)S(1)}) custom-call(s32[64]{0:T(128)S(1)} %copy-done.3, s32[64]{0:T(128)S(1)} %copy-done.4, s32[128]{0:T(128)S(1)} %get-tuple-element.41.refs_2_.refs_1_, bf16[16,128,256]{2,1,0:T(8,128)(2,1)S(1)} %bitcast.23), custom_call_target="tpu_custom_call" | custom-call | tf_op jit(solution)/shard_map/deal/pallas_call | solution.py:524
  12.0 0.0 copy-start.7
  12.0 3.6 %collective-permute-start = (bf16[8,128,256]{2,1,0:T(8,128)(2,1)S(1)}, bf16[8,128,256]{2,1,0:T(8,128)(2,1)S(1)}, u32[]{:S(2)}, u32[]{:S(2)}) collective-permute-start(bf16[8,128,256]{2,1,0:T(8,128)(2,1)S(1)} %get-tuple-element.44), channel_id=1, source_target_pairs={{0,2},{1,3},{4,6},{5,7},{8,10},{9,11},{12,14},{13,15},{16,18},{17,... | collective-permute-start | bytes 1572872 | tf_op jit(solution)/shard_map/ppermute | solution.py:549
  15.6 0.1 copy.13
  15.7 0.0 copy-start.8
  15.7 0.1 copy.14
  15.8 0.7 copy-done.8
  16.5 0.1 copy.15
  16.7 0.7 copy-done.9
  17.4 0.1 collective-permute-start.1
  17.5 6.3 %all-to-all-done = bf16[4,256,256]{2,1,0:T(8,128)(2,1)S(1)} async-done(((bf16[4,256,256]{2,1,0:T(8,128)(2,1)}), bf16[4,256,256]{2,1,0:T(8,128)(2,1)S(1)}, u32[]{:S(2)}, u32[]{:S(2)}) %all-to-all-start) | async-done | bytes 524320 | tf_op jit(solution)/shard_map/all_to_all | solution.py:544
  23.8 3.5 %all-to-all-start.1 = ((bf16[4,256,256]{2,1,0:T(8,128)(2,1)}), bf16[4,256,256]{2,1,0:T(8,128)(2,1)S(1)}, u32[]{:S(2)}, u32[]{:S(2)}) async-start(bf16[4,256,256]{2,1,0:T(8,128)(2,1)} %bitcast.7), calls=%async_computation.1 | async-start | bytes 1048576 | tf_op jit(solution)/shard_map/all_to_all | solution.py:544
  27.2 0.0 collective-permute-done.1.refs_18_
  27.3 0.0 collective-permute-done.refs_4_.refs_8_.refs_12_.refs_16_
  27.3 0.0 copy-start.10
  27.3 0.7 copy-done.13
  28.0 0.2 copy-done.10
  28.1 11.2 %attention_0.1 = (f32[4,128,256]{2,1,0:T(8,128)}, bf16[4,128,256]{2,1,0:T(8,128)(2,1)}, bf16[8,128,256]{2,1,0:T(8,128)(2,1)}, f32[512,256]{1,0:T(8,128)}, f32[512,256]{1,0:T(8,128)}) custom-call(s32[128]{0:T(128)S(1)} %get-tuple-element.42.refs_0_, bf16[16,128,256]{2,1,0:T(8,128)(2,1)} %bitcast.15, bf16[16,128,256]{2,1,0:T(8,128)(2,1)} %bitcast.40, ...), custom_call_target="tpu_custom_call" | custom-call | flops 6375342080 | bytes 5242880 | tf_op jit(solution)/shard_map/attention_0/pallas_call | solution.py:388
  39.3 1.9 %all-to-all-done.1 = bf16[4,256,256]{2,1,0:T(8,128)(2,1)S(1)} async-done(((bf16[4,256,256]{2,1,0:T(8,128)(2,1)}), bf16[4,256,256]{2,1,0:T(8,128)(2,1)S(1)}, u32[]{:S(2)}, u32[]{:S(2)}) %all-to-all-start.1) | async-done | bytes 524320 | tf_op jit(solution)/shard_map/all_to_all | solution.py:544
  41.2 3.6 %all-to-all-start.2 = ((bf16[4,256,256]{2,1,0:T(8,128)(2,1)}), bf16[4,256,256]{2,1,0:T(8,128)(2,1)S(1)}, u32[]{:S(2)}, u32[]{:S(2)}) async-start(bf16[4,256,256]{2,1,0:T(8,128)(2,1)} %bitcast.36), calls=%async_computation.2 | async-start | bytes 1048576 | tf_op jit(solution)/shard_map/all_to_all | solution.py:544
  44.8 1.5 %collective-permute-start.2 = (bf16[4,128,256]{2,1,0:T(8,128)(2,1)S(1)}, bf16[4,128,256]{2,1,0:T(8,128)(2,1)S(1)}, u32[]{:S(2)}, u32[]{:S(2)}) collective-permute-start(bf16[4,128,256]{2,1,0:T(8,128)(2,1)S(1)} %copy-done.12), channel_id=1, source_target_pairs={{2,0},{3,1},{6,4},{7,5},{10,8},{11,9},{14,12},{15,13},{18,16},{19,... | collective-permute-start | bytes 786440 | tf_op jit(solution)/shard_map/ppermute | solution.py:556
  46.3 11.1 %attention_1.1 = (f32[4,128,256]{2,1,0:T(8,128)}, bf16[4,128,256]{2,1,0:T(8,128)(2,1)}, bf16[8,128,256]{2,1,0:T(8,128)(2,1)}, bf16[256,256]{1,0:T(8,128)(2,1)S(1...) custom-call(s32[128]{0:T(128)S(1)} %get-tuple-element.42.refs_0_, ...), custom_call_target="tpu_custom_call" | custom-call | flops 6375342080 | bytes 5242880 | tf_op jit(solution)/shard_map/attention_1/pallas_call | solution.py:388
  57.5 2.7 %collective-permute-start.3 = (bf16[256,256]{1,0:T(8,128)(2,1)S(1)}, bf16[256,256]{1,0:T(8,128)(2,1)S(1)}, u32[]{:S(2)}, u32[]{:S(2)}) collective-permute-start(bf16[256,256]{1,0:T(8,128)(2,1)S(1)} %get-tuple-element.56), channel_id=1, source_target_pairs={{0,2},{2,0},{1,3},{3,1},{4,6},{6,4},{5,7},{7,5},{8,10},{10,8},{9,1... | collective-permute-start | bytes 393224 | tf_op jit(solution)/shard_map/ppermute | solution.py:426
  60.1 0.2 collective-permute-start.5
  60.3 0.0 collective-permute-done.2.refs_4_
  60.3 0.0 all-to-all-done.2
  60.3 5.2 %all-to-all-start.3 = ((bf16[4,256,256]{2,1,0:T(8,128)(2,1)}), bf16[4,256,256]{2,1,0:T(8,128)(2,1)S(1)}, u32[]{:S(2)}, u32[]{:S(2)}) async-start(bf16[4,256,256]{2,1,0:T(8,128)(2,1)} %bitcast.35), calls=%async_computation.3 | async-start | bytes 1048576 | tf_op jit(solution)/shard_map/all_to_all | solution.py:544
  65.5 0.0 collective-permute-done.3
  65.5 0.1 add_convert_fusion
  65.6 2.1 %collective-permute-start.6 = (bf16[128,256]{1,0:T(8,128)(2,1)S(1)}, bf16[128,256]{1,0:T(8,128)(2,1)S(1)}, u32[]{:S(2)}, u32[]{:S(2)}) collective-permute-start(bf16[128,256]{1,0:T(8,128)(2,1)S(1)} %broadcast_select_fusion), channel_id=1, source_target_pairs={{0,4},{4,0},{8,12},{12,8},{1,5},{5,1},{9,13},{13,9},{2,6},{6,2},{1... | collective-permute-start | bytes 196616 | tf_op jit(solution)/shard_map/ppermute | solution.py:426
  67.7 1.3 %collective-permute-start.7 = (bf16[4,128,256]{2,1,0:T(8,128)(2,1)S(1)}, bf16[4,128,256]{2,1,0:T(8,128)(2,1)S(1)}, u32[]{:S(2)}, u32[]{:S(2)}) collective-permute-start(bf16[4,128,256]{2,1,0:T(8,128)(2,1)S(1)} %copy-done.11), channel_id=1, source_target_pairs={{2,0},{3,1},{6,4},{7,5},{10,8},{11,9},{14,12},{15,13},{18,16},{19,... | collective-permute-start | bytes 786440 | tf_op jit(solution)/shard_map/ppermute | solution.py:568
  69.0 7.1 %collective-permute-done.6 = bf16[128,256]{1,0:T(8,128)(2,1)S(1)} collective-permute-done((bf16[128,256]{1,0:T(8,128)(2,1)S(1)}, bf16[128,256]{1,0:T(8,128)(2,1)S(1)}, u32[]{:S(2)}, u32[]{:S(2)}) %collective-permute-start.6) | collective-permute-done | bytes 65568 | tf_op jit(solution)/shard_map/ppermute | solution.py:426
  76.2 1.5 %collective-permute-done.7.refs_5_ = bf16[4,128,256]{2,1,0:T(8,128)(2,1)S(1)} collective-permute-done((bf16[4,128,256]{2,1,0:T(8,128)(2,1)S(1)}, bf16[4,128,256]{2,1,0:T(8,128)(2,1)S(1)}, u32[]{:S(2)}, u32[]{:S(2)}) %collective-permute-start.7) | collective-permute-done | bytes 262176 | tf_op jit(solution)/shard_map/ppermute | solution.py:568
  77.7 3.1 %collective-permute-start.8 = (bf16[128,256]{1,0:T(8,128)(2,1)S(1)}, bf16[128,256]{1,0:T(8,128)(2,1)S(1)}, u32[]{:S(2)}, u32[]{:S(2)}) collective-permute-start(bf16[128,256]{1,0:T(8,128)(2,1)S(1)} %convert_add_fusion), channel_id=1, source_target_pairs={{0,8},{4,12},{8,0},{12,4},{1,9},{5,13},{9,1},{13,5},{2,10},{6,14},... | collective-permute-start | bytes 196616 | tf_op jit(solution)/shard_map/ppermute | solution.py:426
  80.7 2.9 %collective-permute-done.8 = bf16[128,256]{1,0:T(8,128)(2,1)S(1)} collective-permute-done((bf16[128,256]{1,0:T(8,128)(2,1)S(1)}, bf16[128,256]{1,0:T(8,128)(2,1)S(1)}, u32[]{:S(2)}, u32[]{:S(2)}) %collective-permute-start.8) | collective-permute-done | bytes 65568 | tf_op jit(solution)/shard_map/ppermute | solution.py:426
  83.7 1.6 %collective-permute-start.10 = (bf16[128,256]{1,0:T(8,128)(2,1)S(1)}, bf16[128,256]{1,0:T(8,128)(2,1)S(1)}, u32[]{:S(2)}, u32[]{:S(2)}) collective-permute-start(bf16[128,256]{1,0:T(8,128)(2,1)S(1)} %add_convert_fusion.1.mine), channel_id=1, source_target_pairs={{0,2},{2,0},{1,3},{3,1},{4,6},{6,4},{5,7},{7,5},{8,10},{10,8},{9,1... | collective-permute-start | bytes 196616 | tf_op jit(solution)/shard_map/ppermute | solution.py:426
  85.4 0.1 collective-permute-start.11
  85.4 1.8 %collective-permute-start.9 = (bf16[128,256]{1,0:T(8,128)(2,1)S(1)}, bf16[128,256]{1,0:T(8,128)(2,1)S(1)}, u32[]{:S(2)}, u32[]{:S(2)}) collective-permute-start(bf16[128,256]{1,0:T(8,128)(2,1)S(1)} %add_convert_fusion.1.mine), channel_id=1, source_target_pairs={{0,4},{4,0},{8,12},{12,8},{1,5},{5,1},{9,13},{13,9},{2,6},{6,2},{1... | collective-permute-start | bytes 196616 | tf_op jit(solution)/shard_map/ppermute | solution.py:426
  87.3 1.6 %fold.1 = (f32[16,128,128]{2,1,0:T(8,128)S(1)}, f32[16,128,128]{2,1,0:T(8,128)S(1)}) custom-call(s32[128]{0:T(128)S(1)} %get-tuple-element.42.refs_0_, s32[128]{0:T(128)S(1)} %get-tuple-element.41.refs_2_.refs_1_, f32[4,128,256]{2,1,0:T(8,128)S(1)} %copy-done.1, f32[4,128,256]{2,1,0:T(8,128)S(1)} %copy-done.2, ...), custom_call_target="tpu_custom_call" | custom-call | tf_op jit(solution)/shard_map/fold/pallas_call | solution.py:572
  88.8 1.7 %collective-permute-done.11.along_both = bf16[128,256]{1,0:T(8,128)(2,1)S(1)} collective-permute-done((bf16[128,256]{1,0:T(8,128)(2,1)S(1)}, bf16[128,256]{1,0:T(8,128)(2,1)S(1)}, u32[]{:S(2)}, u32[]{:S(2)}) %collective-permute-start.11) | collective-permute-done | bytes 65568 | tf_op jit(solution)/shard_map/ppermute | solution.py:464
  90.5 0.9 split.1
  91.4 1.8 %collective-permute-done.12.got = f32[16,128,128]{2,1,0:T(8,128)S(1)} collective-permute-done((f32[16,128,128]{2,1,0:T(8,128)S(1)}, f32[16,128,128]{2,1,0:T(8,128)S(1)}, u32[]{:S(2)}, u32[]{:S(2)}) %collective-permute-start.12) | collective-permute-done | bytes 1048608 | tf_op jit(solution)/shard_map/ppermute | solution.py:426
  93.2 0.9 add.26
  (29 shorter events, 0.1 us)
Async XLA Ops:
  0.6 8.7 %copy-start = (bf16[1,2048,256]{2,1,0:T(8,128)(2,1)S(1)}, bf16[1,2048,256]{2,1,0:T(8,128)(2,1)}, u32[]{:S(2)}) copy-start(bf16[1,2048,256]{2,1,0:T(8,128)(2,1)} %param.8) | copy-start | bytes 3145732
  2.9 20.8 %all-to-all-start = ((bf16[4,256,256]{2,1,0:T(8,128)(2,1)}), bf16[4,256,256]{2,1,0:T(8,128)(2,1)S(1)}, u32[]{:S(2)}, u32[]{:S(2)}) async-start(bf16[4,256,256]{2,1,0:T(8,128)(2,1)} %bitcast.2), calls=%async_computation | async-start | bytes 1048576 | tf_op jit(solution)/shard_map/all_to_all | solution.py:544
  9.3 0.7 copy-start.3
  9.3 0.7 copy-start.4
  9.9 5.6 %copy-start.6 = (bf16[256,128]{1,0:T(8,128)(2,1)S(1)}, bf16[256,128]{1,0:T(8,128)(2,1)}, u32[]{:S(2)}) copy-start(bf16[256,128]{1,0:T(8,128)(2,1)} %param.11) | copy-start | bytes 196612
  12.0 3.7 %copy-start.7 = (bf16[256,128]{1,0:T(8,128)(2,1)S(1)}, bf16[256,128]{1,0:T(8,128)(2,1)}, u32[]{:S(2)}) copy-start(bf16[256,128]{1,0:T(8,128)(2,1)} %param.12) | copy-start | bytes 196612
  12.0 15.3 %collective-permute-start = (bf16[8,128,256]{2,1,0:T(8,128)(2,1)S(1)}, bf16[8,128,256]{2,1,0:T(8,128)(2,1)S(1)}, u32[]{:S(2)}, u32[]{:S(2)}) collective-permute-start(bf16[8,128,256]{2,1,0:T(8,128)(2,1)S(1)} %get-tuple-element.44), channel_id=1, source_target_pairs={{0,2},{1,3},{4,6},{5,7},{8,10},{9,11},{12,14},{13,15},{16,18},{17,... | collective-permute-start | bytes 1572872 | tf_op jit(solution)/shard_map/ppermute | solution.py:549
  15.7 0.8 copy-start.8
  16.5 0.8 copy-start.9
  17.4 6.4 %copy-start.5 = (bf16[512,256]{1,0:T(8,128)(2,1)}, bf16[512,256]{1,0:T(8,128)(2,1)S(1)}, u32[]{:S(2)}) copy-start(bf16[512,256]{1,0:T(8,128)(2,1)S(1)} %pad_maximum_fusion.refs_17_) | copy-start | bytes 786436
  17.4 9.8 %collective-permute-start.1 = (bf16[512,256]{1,0:T(8,128)(2,1)S(1)}, bf16[512,256]{1,0:T(8,128)(2,1)S(1)}, u32[]{:S(2)}, u32[]{:S(2)}) collective-permute-start(bf16[512,256]{1,0:T(8,128)(2,1)S(1)} %pad_maximum_fusion.refs_17_), channel_id=1, source_target_pairs={{0,1},{1,0},{2,3},{3,2},{4,5},{5,4},{6,7},{7,6},{8,9},{9,8},{10,11... | collective-permute-start | bytes 786440 | tf_op jit(solution)/shard_map/ppermute | solution.py:426
  23.8 17.4 %all-to-all-start.1 = ((bf16[4,256,256]{2,1,0:T(8,128)(2,1)}), bf16[4,256,256]{2,1,0:T(8,128)(2,1)S(1)}, u32[]{:S(2)}, u32[]{:S(2)}) async-start(bf16[4,256,256]{2,1,0:T(8,128)(2,1)} %bitcast.7), calls=%async_computation.1 | async-start | bytes 1048576 | tf_op jit(solution)/shard_map/all_to_all | solution.py:544
  27.3 0.7 copy-start.13
  27.3 0.9 copy-start.10
  41.2 3.6 %copy-start.12 = (bf16[4,128,256]{2,1,0:T(8,128)(2,1)S(1)}, bf16[4,128,256]{2,1,0:T(8,128)(2,1)}, u32[]{:S(2)}) copy-start(bf16[4,128,256]{2,1,0:T(8,128)(2,1)} %get-tuple-element.51) | copy-start | bytes 786436
  41.2 19.1 %all-to-all-start.2 = ((bf16[4,256,256]{2,1,0:T(8,128)(2,1)}), bf16[4,256,256]{2,1,0:T(8,128)(2,1)S(1)}, u32[]{:S(2)}, u32[]{:S(2)}) async-start(bf16[4,256,256]{2,1,0:T(8,128)(2,1)} %bitcast.36), calls=%async_computation.2 | async-start | bytes 1048576 | tf_op jit(solution)/shard_map/all_to_all | solution.py:544
  44.8 15.5 %collective-permute-start.2 = (bf16[4,128,256]{2,1,0:T(8,128)(2,1)S(1)}, bf16[4,128,256]{2,1,0:T(8,128)(2,1)S(1)}, u32[]{:S(2)}, u32[]{:S(2)}) collective-permute-start(bf16[4,128,256]{2,1,0:T(8,128)(2,1)S(1)} %copy-done.12), channel_id=1, source_target_pairs={{2,0},{3,1},{6,4},{7,5},{10,8},{11,9},{14,12},{15,13},{18,16},{19,... | collective-permute-start | bytes 786440 | tf_op jit(solution)/shard_map/ppermute | solution.py:556
  57.5 8.1 %collective-permute-start.3 = (bf16[256,256]{1,0:T(8,128)(2,1)S(1)}, bf16[256,256]{1,0:T(8,128)(2,1)S(1)}, u32[]{:S(2)}, u32[]{:S(2)}) collective-permute-start(bf16[256,256]{1,0:T(8,128)(2,1)S(1)} %get-tuple-element.56), channel_id=1, source_target_pairs={{0,2},{2,0},{1,3},{3,1},{4,6},{6,4},{5,7},{7,5},{8,10},{10,8},{9,1... | collective-permute-start | bytes 393224 | tf_op jit(solution)/shard_map/ppermute | solution.py:426
  60.1 5.4 %collective-permute-start.4 = (bf16[256,256]{1,0:T(8,128)(2,1)S(1)}, bf16[256,256]{1,0:T(8,128)(2,1)S(1)}, u32[]{:S(2)}, u32[]{:S(2)}) collective-permute-start(bf16[256,256]{1,0:T(8,128)(2,1)S(1)} %get-tuple-element.57), channel_id=1, source_target_pairs={{0,1},{1,0},{2,3},{3,2},{4,5},{5,4},{6,7},{7,6},{8,9},{9,8},{10,11... | collective-permute-start | bytes 393224 | tf_op jit(solution)/shard_map/ppermute | solution.py:426
  60.1 5.4 %collective-permute-start.5 = (bf16[256,256]{1,0:T(8,128)(2,1)S(1)}, bf16[256,256]{1,0:T(8,128)(2,1)S(1)}, u32[]{:S(2)}, u32[]{:S(2)}) collective-permute-start(bf16[256,256]{1,0:T(8,128)(2,1)S(1)} %get-tuple-element.58), channel_id=1, source_target_pairs={{0,3},{1,2},{2,1},{3,0},{4,7},{5,6},{6,5},{7,4},{8,11},{9,10},{10,... | collective-permute-start | bytes 393224 | tf_op jit(solution)/shard_map/ppermute | solution.py:563
  60.3 7.4 %copy-start.11 = (bf16[4,128,256]{2,1,0:T(8,128)(2,1)S(1)}, bf16[4,128,256]{2,1,0:T(8,128)(2,1)}, u32[]{:S(2)}) copy-start(bf16[4,128,256]{2,1,0:T(8,128)(2,1)} %get-tuple-element.59) | copy-start | bytes 786436
  60.3 23.4 %all-to-all-start.3 = ((bf16[4,256,256]{2,1,0:T(8,128)(2,1)}), bf16[4,256,256]{2,1,0:T(8,128)(2,1)S(1)}, u32[]{:S(2)}, u32[]{:S(2)}) async-start(bf16[4,256,256]{2,1,0:T(8,128)(2,1)} %bitcast.35), calls=%async_computation.3 | async-start | bytes 1048576 | tf_op jit(solution)/shard_map/all_to_all | solution.py:544
  65.5 21.8 %copy-start.1 = (f32[4,128,256]{2,1,0:T(8,128)S(1)}, f32[4,128,256]{2,1,0:T(8,128)}, u32[]{:S(2)}) copy-start(f32[4,128,256]{2,1,0:T(8,128)} %get-tuple-element.45.refs_2_) | copy-start | bytes 1572868
  65.5 21.8 %copy-start.2 = (f32[4,128,256]{2,1,0:T(8,128)S(1)}, f32[4,128,256]{2,1,0:T(8,128)}, u32[]{:S(2)}) copy-start(f32[4,128,256]{2,1,0:T(8,128)} %get-tuple-element.49.refs_3_) | copy-start | bytes 1572868
  65.6 10.5 %collective-permute-start.6 = (bf16[128,256]{1,0:T(8,128)(2,1)S(1)}, bf16[128,256]{1,0:T(8,128)(2,1)S(1)}, u32[]{:S(2)}, u32[]{:S(2)}) collective-permute-start(bf16[128,256]{1,0:T(8,128)(2,1)S(1)} %broadcast_select_fusion), channel_id=1, source_target_pairs={{0,4},{4,0},{8,12},{12,8},{1,5},{5,1},{9,13},{13,9},{2,6},{6,2},{1... | collective-permute-start | bytes 196616 | tf_op jit(solution)/shard_map/ppermute | solution.py:426
  67.7 9.9 %collective-permute-start.7 = (bf16[4,128,256]{2,1,0:T(8,128)(2,1)S(1)}, bf16[4,128,256]{2,1,0:T(8,128)(2,1)S(1)}, u32[]{:S(2)}, u32[]{:S(2)}) collective-permute-start(bf16[4,128,256]{2,1,0:T(8,128)(2,1)S(1)} %copy-done.11), channel_id=1, source_target_pairs={{2,0},{3,1},{6,4},{7,5},{10,8},{11,9},{14,12},{15,13},{18,16},{19,... | collective-permute-start | bytes 786440 | tf_op jit(solution)/shard_map/ppermute | solution.py:568
  77.7 6.0 %collective-permute-start.8 = (bf16[128,256]{1,0:T(8,128)(2,1)S(1)}, bf16[128,256]{1,0:T(8,128)(2,1)S(1)}, u32[]{:S(2)}, u32[]{:S(2)}) collective-permute-start(bf16[128,256]{1,0:T(8,128)(2,1)S(1)} %convert_add_fusion), channel_id=1, source_target_pairs={{0,8},{4,12},{8,0},{12,4},{1,9},{5,13},{9,1},{13,5},{2,10},{6,14},... | collective-permute-start | bytes 196616 | tf_op jit(solution)/shard_map/ppermute | solution.py:426
  83.7 5.1 %collective-permute-start.10 = (bf16[128,256]{1,0:T(8,128)(2,1)S(1)}, bf16[128,256]{1,0:T(8,128)(2,1)S(1)}, u32[]{:S(2)}, u32[]{:S(2)}) collective-permute-start(bf16[128,256]{1,0:T(8,128)(2,1)S(1)} %add_convert_fusion.1.mine), channel_id=1, source_target_pairs={{0,2},{2,0},{1,3},{3,1},{4,6},{6,4},{5,7},{7,5},{8,10},{10,8},{9,1... | collective-permute-start | bytes 196616 | tf_op jit(solution)/shard_map/ppermute | solution.py:426
  85.4 5.2 %collective-permute-start.11 = (bf16[128,256]{1,0:T(8,128)(2,1)S(1)}, bf16[128,256]{1,0:T(8,128)(2,1)S(1)}, u32[]{:S(2)}, u32[]{:S(2)}) collective-permute-start(bf16[128,256]{1,0:T(8,128)(2,1)S(1)} %add_convert_fusion.1.mine), channel_id=1, source_target_pairs={{0,6},{2,4},{4,2},{6,0},{8,14},{10,12},{12,10},{14,8},{1,7},{3,5},... | collective-permute-start | bytes 196616 | tf_op jit(solution)/shard_map/ppermute | solution.py:464
  85.4 5.1 %collective-permute-start.9 = (bf16[128,256]{1,0:T(8,128)(2,1)S(1)}, bf16[128,256]{1,0:T(8,128)(2,1)S(1)}, u32[]{:S(2)}, u32[]{:S(2)}) collective-permute-start(bf16[128,256]{1,0:T(8,128)(2,1)S(1)} %add_convert_fusion.1.mine), channel_id=1, source_target_pairs={{0,4},{4,0},{8,12},{12,8},{1,5},{5,1},{9,13},{13,9},{2,6},{6,2},{1... | collective-permute-start | bytes 196616 | tf_op jit(solution)/shard_map/ppermute | solution.py:426
  90.5 2.7 %collective-permute-start.12 = (f32[16,128,128]{2,1,0:T(8,128)S(1)}, f32[16,128,128]{2,1,0:T(8,128)S(1)}, u32[]{:S(2)}, u32[]{:S(2)}) collective-permute-start(f32[16,128,128]{2,1,0:T(8,128)S(1)} %get-tuple-element.68), channel_id=1, source_target_pairs={{0,1},{1,0},{2,3},{3,2},{4,5},{5,4},{6,7},{7,6},{8,9},{9,8},{10,11... | collective-permute-start | bytes 3145736 | tf_op jit(solution)/shard_map/ppermute | solution.py:426

commit v15 on v14

--- a/solution.py
+++ b/solution.py
@@ -440,7 +440,7 @@
     ]
 
 
-def sum_gradients(part, home_b, day_b, fold):
+def sum_gradients(part, home_b, fold):
     bit = 2
     while bit < lax.axis_size("day"):
         part = summed_over(part, "day", bit)
@@ -451,21 +451,19 @@
     kept = jnp.where(first, low[:half], low[half:])
     given = jnp.where(first, low[half:], low[:half])
     part = kept.astype(F32) + exchanged(given, "reach", 1).astype(F32)
-    part, day_b = lax.optimization_barrier((part, day_b))
+    part, home_b = lax.optimization_barrier((part, home_b))
     bit = 2
     while bit < lax.axis_size("reach"):
         part = summed_over(part, "reach", bit)
         bit *= 2
-    part, home_b = lax.optimization_barrier((part.astype(BF16), home_b))
+    part, folded = lax.optimization_barrier((part.astype(BF16), fold(home_b)))
     quarters = (
         part,
         exchanged(part, "reach", 1),
         exchanged(part, "day", 1),
         lax.ppermute(part, ("reach", "day"), neighbours("reach", "day")),
     )
-    keep, give = fold(home_b, day_b)
-    quarters, give = lax.optimization_barrier((quarters, give))
-    return quarters, (keep, give)
+    return quarters, folded
 
 
 def split_kernel(mine, along_reach, along_day, along_both, query_out, key_out, value_out, output_out):
@@ -562,13 +560,13 @@
         exchanged(to_core, "head", 1),
         lax.ppermute(to_both, ("day", "head"), neighbours("day", "head")),
     )
-    home_a, day_a, home_b, kept = lax.optimization_barrier((home_a, day_a, home_b, kept))
+    home_a, home_b, kept = lax.optimization_barrier((home_a, home_b, kept))
     pieces = (kept, *pieces)
     home_b = ring(home_b)
     day_b = lax.ppermute(day_b, "day", last_day)
     half_shape = jax.ShapeDtypeStruct((blocks_dev, BLOCK, half), F32)
 
-    def fold(home_b, day_b):
+    def fold(home_b):
         return pl.pallas_call(
             lambda *refs: fold_kernel(lay, *refs),
             out_shape=(half_shape, half_shape),
@@ -579,7 +577,7 @@
         )(tab, homes, own_a, own_b, day_a, day_b, home_a, home_b)
 
     quarters, (keep, give) = sum_gradients(
-        sum(piece.astype(F32) for piece in pieces), home_b, day_b, fold
+        sum(piece.astype(F32) for piece in pieces), home_b, fold
     )
     got = exchanged(give, "head", 1)
     back_blocks = pl.pallas_call(
@@ -590,6 +588,7 @@
         compiler_params=pltpu.CompilerParams(vmem_limit_bytes=16 << 20),
         name="add",
     )(keep, got)
+    back_blocks, quarters = lax.optimization_barrier((back_blocks, quarters))
     weight_grads = pl.pallas_call(
         split_kernel,
         out_shape=(

time: 94.7 us -> 91.4 us (0.965)
  starting transfers between devices: 36.5 us -> 32.1 us
  waiting for transfers between devices: 23.2 us -> 24.4 us
    ppermute x8, starting transfers between devices: 11.4 us -> 5.46 us  [exchanged(): lax.ppermute(value, axis, [(place, place ^ bit) for place in range(count)])]
    ppermute x8, waiting for transfers between devices: 11.9 us -> 6.21 us  [exchanged(): lax.ppermute(value, axis, [(place, place ^ bit) for place in range(count)])]
    all_to_all x4, waiting for transfers between devices: 8.15 us -> 13 us  [ring(): return lax.all_to_all(value, 'reach', 0, 0, tiled=True).reshape(shape)]
    ppermute x1, waiting for transfers between devices: 0.01 us -> 2.97 us  [on_device(): day_a = lax.ppermute(day_a, 'day', last_day)]
    ppermute x1, starting transfers between devices: 0.08 us -> 1.91 us  [sum_gradients(): lax.ppermute(part, ('reach', 'day'), neighbours('reach', 'day'))]
    ppermute x1, waiting for transfers between devices: 1.49 us -> 0.01 us  [on_device(): day_b = lax.ppermute(day_b, 'day', last_day)]
  transfers between devices with their start and end apart: 17 -> 17, of which waited for: 7 -> 10; matrix products, arithmetic and copies ran while one was open for 0% -> 0% of each run, Pallas kernels for 28% -> 30%
where the time goes in v15:
time: 91.4 us; the launch traced here: 90.8 us
  starting transfers between devices  32.1 us (35%)
  Pallas kernels  30 us (33%)
  waiting for transfers between devices  24.4 us (27%)
  local copies, waits for them, and re-layouts  3.32 us (4%)
    pallas_call x2, Pallas kernels, attend(): pl.pallas_call(lambda *refs: attention_kernel(lay, chunk, *refs), grid_sp...  22.3 us
    all_to_all x4, starting transfers between devices, ring(): return lax.all_to_all(value, 'reach', 0, 0, tiled=True).reshape(shape)  18 us
    all_to_all x4, waiting for transfers between devices, ring(): return lax.all_to_all(value, 'reach', 0, 0, tiled=True).reshape(shape)  13 us
    ppermute x8, waiting for transfers between devices, exchanged(): lax.ppermute(value, axis, [(place, place ^ bit) for place in range(count)])  6.21 us
    ppermute x8, starting transfers between devices, exchanged(): lax.ppermute(value, axis, [(place, place ^ bit) for place in range(count)])  5.46 us
    ppermute x1, starting transfers between devices, on_device(): prior_inputs = lax.ppermute(prior, 'day', next_day)  3.56 us
    unnamed x31, local copies, waits for them, and re-layouts  3.32 us
    ppermute x1, waiting for transfers between devices, on_device(): day_a = lax.ppermute(day_a, 'day', last_day)  2.97 us
  transfers between devices with their start and end apart: 17, of which 10 were waited for; matrix products, arithmetic and copies ran while one was open for 0% of the time, Pallas kernels for 30%

profile of v15, /device:TPU:0, one launch (start us, length us, event | category | flops | bytes accessed | tf_op | source)
XLA Modules:
  0.0 90.8 jit_solution(13332551799096461112)
XLA Ops:
  0.6 0.0 copy-start
  0.6 2.3 %pick.1 = (bf16[8,128,256]{2,1,0:T(8,128)(2,1)}, s32[128]{0:T(128)S(1)}) custom-call(s32[64]{0:T(128)} %refs_0_.3, bf16[16,128,256]{2,1,0:T(8,128)(2,1)} %bitcast.14), custom_call_target="tpu_custom_call" | custom-call | tf_op jit(solution)/shard_map/pick/pallas_call | solution.py:506
  2.9 6.3 %all-to-all-start = ((bf16[4,256,256]{2,1,0:T(8,128)(2,1)}), bf16[4,256,256]{2,1,0:T(8,128)(2,1)S(1)}, u32[]{:S(2)}, u32[]{:S(2)}) async-start(bf16[4,256,256]{2,1,0:T(8,128)(2,1)} %bitcast.2), calls=%async_computation | async-start | bytes 1048576 | tf_op jit(solution)/shard_map/all_to_all | solution.py:542
  9.3 0.6 copy-done.3
  9.9 0.0 copy-done.4
  10.0 2.0 %deal.1 = (bf16[8,128,256]{2,1,0:T(8,128)(2,1)}, bf16[8,128,256]{2,1,0:T(8,128)(2,1)S(1)}, s32[128]{0:T(128)S(1)}) custom-call(s32[64]{0:T(128)S(1)} %copy-done.3, s32[64]{0:T(128)S(1)} %copy-done.4, s32[128]{0:T(128)S(1)} %get-tuple-element.41.refs_2_.refs_1_, bf16[16,128,256]{2,1,0:T(8,128)(2,1)S(1)} %bitcast.23), custom_call_target="tpu_custom_call" | custom-call | tf_op jit(solution)/shard_map/deal/pallas_call | solution.py:522
  12.0 0.0 copy-start.7
  12.0 3.6 %collective-permute-start = (bf16[8,128,256]{2,1,0:T(8,128)(2,1)S(1)}, bf16[8,128,256]{2,1,0:T(8,128)(2,1)S(1)}, u32[]{:S(2)}, u32[]{:S(2)}) collective-permute-start(bf16[8,128,256]{2,1,0:T(8,128)(2,1)S(1)} %get-tuple-element.44), channel_id=1, source_target_pairs={{0,2},{1,3},{4,6},{5,7},{8,10},{9,11},{12,14},{13,15},{16,18},{17,... | collective-permute-start | bytes 1572872 | tf_op jit(solution)/shard_map/ppermute | solution.py:547
  15.6 0.1 copy.13
  15.7 0.0 copy-start.8
  15.7 0.1 copy.14
  15.8 0.7 copy-done.8
  16.5 0.1 copy.15
  16.7 0.7 copy-done.9
  17.4 0.1 collective-permute-start.1
  17.5 6.3 %all-to-all-done = bf16[4,256,256]{2,1,0:T(8,128)(2,1)S(1)} async-done(((bf16[4,256,256]{2,1,0:T(8,128)(2,1)}), bf16[4,256,256]{2,1,0:T(8,128)(2,1)S(1)}, u32[]{:S(2)}, u32[]{:S(2)}) %all-to-all-start) | async-done | bytes 524320 | tf_op jit(solution)/shard_map/all_to_all | solution.py:542
  23.8 3.5 %all-to-all-start.2 = ((bf16[4,256,256]{2,1,0:T(8,128)(2,1)}), bf16[4,256,256]{2,1,0:T(8,128)(2,1)S(1)}, u32[]{:S(2)}, u32[]{:S(2)}) async-start(bf16[4,256,256]{2,1,0:T(8,128)(2,1)} %bitcast.9), calls=%async_computation.2 | async-start | bytes 1048576 | tf_op jit(solution)/shard_map/all_to_all | solution.py:542
  27.2 0.0 collective-permute-done.1.refs_18_
  27.3 0.0 copy-start.10
  27.3 0.7 copy-done.13
  28.0 0.2 copy-done.10
  28.1 11.2 %attention_0.1 = (f32[4,128,256]{2,1,0:T(8,128)}, bf16[4,128,256]{2,1,0:T(8,128)(2,1)}, bf16[8,128,256]{2,1,0:T(8,128)(2,1)}, f32[512,256]{1,0:T(8,128)}, f32[512,256]{1,0:T(8,128)}) custom-call(s32[128]{0:T(128)S(1)} %get-tuple-element.42.refs_0_, bf16[16,128,256]{2,1,0:T(8,128)(2,1)} %bitcast.15, bf16[16,128,256]{2,1,0:T(8,128)(2,1)} %bitcast.40, ...), custom_call_target="tpu_custom_call" | custom-call | flops 6375342080 | bytes 5242880 | tf_op jit(solution)/shard_map/attention_0/pallas_call | solution.py:388
  39.3 1.9 %all-to-all-done.2 = bf16[4,256,256]{2,1,0:T(8,128)(2,1)S(1)} async-done(((bf16[4,256,256]{2,1,0:T(8,128)(2,1)}), bf16[4,256,256]{2,1,0:T(8,128)(2,1)S(1)}, u32[]{:S(2)}, u32[]{:S(2)}) %all-to-all-start.2) | async-done | bytes 524320 | tf_op jit(solution)/shard_map/all_to_all | solution.py:542
  41.2 3.6 %all-to-all-start.1 = ((bf16[4,256,256]{2,1,0:T(8,128)(2,1)}), bf16[4,256,256]{2,1,0:T(8,128)(2,1)S(1)}, u32[]{:S(2)}, u32[]{:S(2)}) async-start(bf16[4,256,256]{2,1,0:T(8,128)(2,1)} %bitcast.36), calls=%async_computation.1 | async-start | bytes 1048576 | tf_op jit(solution)/shard_map/all_to_all | solution.py:542
  44.9 11.1 %attention_1.1 = (f32[4,128,256]{2,1,0:T(8,128)}, bf16[4,128,256]{2,1,0:T(8,128)(2,1)}, bf16[8,128,256]{2,1,0:T(8,128)(2,1)}, bf16[256,256]{1,0:T(8,128)(2,1)S(1...) custom-call(s32[128]{0:T(128)S(1)} %get-tuple-element.42.refs_0_, ...), custom_call_target="tpu_custom_call" | custom-call | flops 6375342080 | bytes 5242880 | tf_op jit(solution)/shard_map/attention_1/pallas_call | solution.py:388
  56.0 1.5 %collective-permute-start.2 = (bf16[256,256]{1,0:T(8,128)(2,1)S(1)}, bf16[256,256]{1,0:T(8,128)(2,1)S(1)}, u32[]{:S(2)}, u32[]{:S(2)}) collective-permute-start(bf16[256,256]{1,0:T(8,128)(2,1)S(1)} %get-tuple-element.52), channel_id=1, source_target_pairs={{0,2},{2,0},{1,3},{3,1},{4,6},{6,4},{5,7},{7,5},{8,10},{10,8},{9,1... | collective-permute-start | bytes 393224 | tf_op jit(solution)/shard_map/ppermute | solution.py:426
  57.5 0.6 collective-permute-start.4
  58.2 0.5 all-to-all-done.1
  58.6 4.5 %all-to-all-start.3 = ((bf16[4,256,256]{2,1,0:T(8,128)(2,1)}), bf16[4,256,256]{2,1,0:T(8,128)(2,1)S(1)}, u32[]{:S(2)}, u32[]{:S(2)}) async-start(bf16[4,256,256]{2,1,0:T(8,128)(2,1)} %bitcast.35), calls=%async_computation.3 | async-start | bytes 1048576 | tf_op jit(solution)/shard_map/all_to_all | solution.py:542
  63.2 0.1 collective-permute-done.4
  63.3 0.1 add_convert_fusion
  63.4 2.0 %collective-permute-start.5 = (bf16[128,256]{1,0:T(8,128)(2,1)S(1)}, bf16[128,256]{1,0:T(8,128)(2,1)S(1)}, u32[]{:S(2)}, u32[]{:S(2)}) collective-permute-start(bf16[128,256]{1,0:T(8,128)(2,1)S(1)} %broadcast_select_fusion), channel_id=1, source_target_pairs={{0,4},{4,0},{8,12},{12,8},{1,5},{5,1},{9,13},{13,9},{2,6},{6,2},{1... | collective-permute-start | bytes 196616 | tf_op jit(solution)/shard_map/ppermute | solution.py:426
  65.4 1.3 %collective-permute-start.8 = (bf16[4,128,256]{2,1,0:T(8,128)(2,1)S(1)}, bf16[4,128,256]{2,1,0:T(8,128)(2,1)S(1)}, u32[]{:S(2)}, u32[]{:S(2)}) collective-permute-start(bf16[4,128,256]{2,1,0:T(8,128)(2,1)S(1)} %copy-done.12), channel_id=1, source_target_pairs={{2,0},{3,1},{6,4},{7,5},{10,8},{11,9},{14,12},{15,13},{18,16},{19,... | collective-permute-start | bytes 786440 | tf_op jit(solution)/shard_map/ppermute | solution.py:566
  66.7 1.3 %collective-permute-start.7 = (bf16[4,128,256]{2,1,0:T(8,128)(2,1)S(1)}, bf16[4,128,256]{2,1,0:T(8,128)(2,1)S(1)}, u32[]{:S(2)}, u32[]{:S(2)}) collective-permute-start(bf16[4,128,256]{2,1,0:T(8,128)(2,1)S(1)} %copy-done.11), channel_id=1, source_target_pairs={{2,0},{3,1},{6,4},{7,5},{10,8},{11,9},{14,12},{15,13},{18,16},{19,... | collective-permute-start | bytes 786440 | tf_op jit(solution)/shard_map/ppermute | solution.py:554
  68.0 5.5 %collective-permute-done.5 = bf16[128,256]{1,0:T(8,128)(2,1)S(1)} collective-permute-done((bf16[128,256]{1,0:T(8,128)(2,1)S(1)}, bf16[128,256]{1,0:T(8,128)(2,1)S(1)}, u32[]{:S(2)}, u32[]{:S(2)}) %collective-permute-start.5) | collective-permute-done | bytes 65568 | tf_op jit(solution)/shard_map/ppermute | solution.py:426
  73.5 4.3 %all-to-all-done.3 = bf16[4,256,256]{2,1,0:T(8,128)(2,1)S(1)} async-done(((bf16[4,256,256]{2,1,0:T(8,128)(2,1)}), bf16[4,256,256]{2,1,0:T(8,128)(2,1)S(1)}, u32[]{:S(2)}, u32[]{:S(2)}) %all-to-all-start.3) | async-done | bytes 524320 | tf_op jit(solution)/shard_map/all_to_all | solution.py:542
  77.8 0.2 collective-permute-start.6
  78.0 3.0 %collective-permute-done.7.refs_4_ = bf16[4,128,256]{2,1,0:T(8,128)(2,1)S(1)} collective-permute-done((bf16[4,128,256]{2,1,0:T(8,128)(2,1)S(1)}, bf16[4,128,256]{2,1,0:T(8,128)(2,1)S(1)}, u32[]{:S(2)}, u32[]{:S(2)}) %collective-permute-start.7) | collective-permute-done | bytes 262176 | tf_op jit(solution)/shard_map/ppermute | solution.py:554
  81.0 1.6 %fold.1 = (f32[16,128,128]{2,1,0:T(8,128)S(1)}, f32[16,128,128]{2,1,0:T(8,128)S(1)}) custom-call(s32[128]{0:T(128)S(1)} %get-tuple-element.42.refs_0_, s32[128]{0:T(128)S(1)} %get-tuple-element.41.refs_2_.refs_1_, f32[4,128,256]{2,1,0:T(8,128)S(1)} %copy-done.1, f32[4,128,256]{2,1,0:T(8,128)S(1)} %copy-done.2, ...), custom_call_target="tpu_custom_call" | custom-call | tf_op jit(solution)/shard_map/fold/pallas_call | solution.py:570
  82.6 0.4 collective-permute-done.6
  83.0 0.1 collective-permute-start.9
  83.1 0.1 collective-permute-start.10
  83.2 1.6 %collective-permute-start.11 = (bf16[128,256]{1,0:T(8,128)(2,1)S(1)}, bf16[128,256]{1,0:T(8,128)(2,1)S(1)}, u32[]{:S(2)}, u32[]{:S(2)}) collective-permute-start(bf16[128,256]{1,0:T(8,128)(2,1)S(1)} %add_convert_fusion.1.mine), channel_id=1, source_target_pairs={{0,2},{2,0},{1,3},{3,1},{4,6},{6,4},{5,7},{7,5},{8,10},{10,8},{9,1... | collective-permute-start | bytes 196616 | tf_op jit(solution)/shard_map/ppermute | solution.py:426
  84.7 1.9 %collective-permute-start.12 = (bf16[128,256]{1,0:T(8,128)(2,1)S(1)}, bf16[128,256]{1,0:T(8,128)(2,1)S(1)}, u32[]{:S(2)}, u32[]{:S(2)}) collective-permute-start(bf16[128,256]{1,0:T(8,128)(2,1)S(1)} %add_convert_fusion.1.mine), channel_id=1, source_target_pairs={{0,6},{2,4},{4,2},{6,0},{8,14},{10,12},{12,10},{14,8},{1,7},{3,5},... | collective-permute-start | bytes 196616 | tf_op jit(solution)/shard_map/ppermute | solution.py:464
  86.6 0.9 add.26
  87.5 0.3 collective-permute-done.10.along_reach
  87.8 2.1 %collective-permute-done.12.along_both = bf16[128,256]{1,0:T(8,128)(2,1)S(1)} collective-permute-done((bf16[128,256]{1,0:T(8,128)(2,1)S(1)}, bf16[128,256]{1,0:T(8,128)(2,1)S(1)}, u32[]{:S(2)}, u32[]{:S(2)}) %collective-permute-start.12) | collective-permute-done | bytes 65568 | tf_op jit(solution)/shard_map/ppermute | solution.py:464
  89.9 0.8 split.1
  (29 shorter events, 0.1 us)
Async XLA Ops:
  0.6 8.7 %copy-start = (bf16[1,2048,256]{2,1,0:T(8,128)(2,1)S(1)}, bf16[1,2048,256]{2,1,0:T(8,128)(2,1)}, u32[]{:S(2)}) copy-start(bf16[1,2048,256]{2,1,0:T(8,128)(2,1)} %param.8) | copy-start | bytes 3145732
  2.9 20.8 %all-to-all-start = ((bf16[4,256,256]{2,1,0:T(8,128)(2,1)}), bf16[4,256,256]{2,1,0:T(8,128)(2,1)S(1)}, u32[]{:S(2)}, u32[]{:S(2)}) async-start(bf16[4,256,256]{2,1,0:T(8,128)(2,1)} %bitcast.2), calls=%async_computation | async-start | bytes 1048576 | tf_op jit(solution)/shard_map/all_to_all | solution.py:542
  9.3 0.7 copy-start.3
  9.3 0.7 copy-start.4
  9.9 5.6 %copy-start.6 = (bf16[256,128]{1,0:T(8,128)(2,1)S(1)}, bf16[256,128]{1,0:T(8,128)(2,1)}, u32[]{:S(2)}) copy-start(bf16[256,128]{1,0:T(8,128)(2,1)} %param.11) | copy-start | bytes 196612
  12.0 3.7 %copy-start.7 = (bf16[256,128]{1,0:T(8,128)(2,1)S(1)}, bf16[256,128]{1,0:T(8,128)(2,1)}, u32[]{:S(2)}) copy-start(bf16[256,128]{1,0:T(8,128)(2,1)} %param.12) | copy-start | bytes 196612
  12.0 15.3 %collective-permute-start = (bf16[8,128,256]{2,1,0:T(8,128)(2,1)S(1)}, bf16[8,128,256]{2,1,0:T(8,128)(2,1)S(1)}, u32[]{:S(2)}, u32[]{:S(2)}) collective-permute-start(bf16[8,128,256]{2,1,0:T(8,128)(2,1)S(1)} %get-tuple-element.44), channel_id=1, source_target_pairs={{0,2},{1,3},{4,6},{5,7},{8,10},{9,11},{12,14},{13,15},{16,18},{17,... | collective-permute-start | bytes 1572872 | tf_op jit(solution)/shard_map/ppermute | solution.py:547
  15.7 0.8 copy-start.8
  16.5 0.8 copy-start.9
  17.4 6.4 %copy-start.5 = (bf16[512,256]{1,0:T(8,128)(2,1)}, bf16[512,256]{1,0:T(8,128)(2,1)S(1)}, u32[]{:S(2)}) copy-start(bf16[512,256]{1,0:T(8,128)(2,1)S(1)} %pad_maximum_fusion.refs_17_) | copy-start | bytes 786436
  17.4 9.8 %collective-permute-start.1 = (bf16[512,256]{1,0:T(8,128)(2,1)S(1)}, bf16[512,256]{1,0:T(8,128)(2,1)S(1)}, u32[]{:S(2)}, u32[]{:S(2)}) collective-permute-start(bf16[512,256]{1,0:T(8,128)(2,1)S(1)} %pad_maximum_fusion.refs_17_), channel_id=1, source_target_pairs={{0,1},{1,0},{2,3},{3,2},{4,5},{5,4},{6,7},{7,6},{8,9},{9,8},{10,11... | collective-permute-start | bytes 786440 | tf_op jit(solution)/shard_map/ppermute | solution.py:426
  23.8 17.4 %all-to-all-start.2 = ((bf16[4,256,256]{2,1,0:T(8,128)(2,1)}), bf16[4,256,256]{2,1,0:T(8,128)(2,1)S(1)}, u32[]{:S(2)}, u32[]{:S(2)}) async-start(bf16[4,256,256]{2,1,0:T(8,128)(2,1)} %bitcast.9), calls=%async_computation.2 | async-start | bytes 1048576 | tf_op jit(solution)/shard_map/all_to_all | solution.py:542
  27.3 0.7 copy-start.13
  27.3 0.9 copy-start.10
  41.2 17.4 %all-to-all-start.1 = ((bf16[4,256,256]{2,1,0:T(8,128)(2,1)}), bf16[4,256,256]{2,1,0:T(8,128)(2,1)S(1)}, u32[]{:S(2)}, u32[]{:S(2)}) async-start(bf16[4,256,256]{2,1,0:T(8,128)(2,1)} %bitcast.36), calls=%async_computation.1 | async-start | bytes 1048576 | tf_op jit(solution)/shard_map/all_to_all | solution.py:542
  56.0 7.1 %collective-permute-start.2 = (bf16[256,256]{1,0:T(8,128)(2,1)S(1)}, bf16[256,256]{1,0:T(8,128)(2,1)S(1)}, u32[]{:S(2)}, u32[]{:S(2)}) collective-permute-start(bf16[256,256]{1,0:T(8,128)(2,1)S(1)} %get-tuple-element.52), channel_id=1, source_target_pairs={{0,2},{2,0},{1,3},{3,1},{4,6},{6,4},{5,7},{7,5},{8,10},{10,8},{9,1... | collective-permute-start | bytes 393224 | tf_op jit(solution)/shard_map/ppermute | solution.py:426
  57.5 5.7 %collective-permute-start.3 = (bf16[256,256]{1,0:T(8,128)(2,1)S(1)}, bf16[256,256]{1,0:T(8,128)(2,1)S(1)}, u32[]{:S(2)}, u32[]{:S(2)}) collective-permute-start(bf16[256,256]{1,0:T(8,128)(2,1)S(1)} %get-tuple-element.53), channel_id=1, source_target_pairs={{0,1},{1,0},{2,3},{3,2},{4,5},{5,4},{6,7},{7,6},{8,9},{9,8},{10,11... | collective-permute-start | bytes 393224 | tf_op jit(solution)/shard_map/ppermute | solution.py:426
  57.5 5.8 %collective-permute-start.4 = (bf16[256,256]{1,0:T(8,128)(2,1)S(1)}, bf16[256,256]{1,0:T(8,128)(2,1)S(1)}, u32[]{:S(2)}, u32[]{:S(2)}) collective-permute-start(bf16[256,256]{1,0:T(8,128)(2,1)S(1)} %get-tuple-element.54), channel_id=1, source_target_pairs={{0,3},{1,2},{2,1},{3,0},{4,7},{5,6},{6,5},{7,4},{8,11},{9,10},{10,... | collective-permute-start | bytes 393224 | tf_op jit(solution)/shard_map/ppermute | solution.py:561
  58.6 6.7 %copy-start.12 = (bf16[4,128,256]{2,1,0:T(8,128)(2,1)S(1)}, bf16[4,128,256]{2,1,0:T(8,128)(2,1)}, u32[]{:S(2)}) copy-start(bf16[4,128,256]{2,1,0:T(8,128)(2,1)} %get-tuple-element.60) | copy-start | bytes 786436
  58.6 8.0 %copy-start.11 = (bf16[4,128,256]{2,1,0:T(8,128)(2,1)S(1)}, bf16[4,128,256]{2,1,0:T(8,128)(2,1)}, u32[]{:S(2)}) copy-start(bf16[4,128,256]{2,1,0:T(8,128)(2,1)} %get-tuple-element.59) | copy-start | bytes 786436
  58.6 19.2 %all-to-all-start.3 = ((bf16[4,256,256]{2,1,0:T(8,128)(2,1)}), bf16[4,256,256]{2,1,0:T(8,128)(2,1)S(1)}, u32[]{:S(2)}, u32[]{:S(2)}) async-start(bf16[4,256,256]{2,1,0:T(8,128)(2,1)} %bitcast.35), calls=%async_computation.3 | async-start | bytes 1048576 | tf_op jit(solution)/shard_map/all_to_all | solution.py:542
  63.1 17.8 %copy-start.1 = (f32[4,128,256]{2,1,0:T(8,128)S(1)}, f32[4,128,256]{2,1,0:T(8,128)}, u32[]{:S(2)}) copy-start(f32[4,128,256]{2,1,0:T(8,128)} %get-tuple-element.57.refs_2_) | copy-start | bytes 1572868
  63.1 17.8 %copy-start.2 = (f32[4,128,256]{2,1,0:T(8,128)S(1)}, f32[4,128,256]{2,1,0:T(8,128)}, u32[]{:S(2)}) copy-start(f32[4,128,256]{2,1,0:T(8,128)} %get-tuple-element.58.refs_3_) | copy-start | bytes 1572868
  63.4 10.1 %collective-permute-start.5 = (bf16[128,256]{1,0:T(8,128)(2,1)S(1)}, bf16[128,256]{1,0:T(8,128)(2,1)S(1)}, u32[]{:S(2)}, u32[]{:S(2)}) collective-permute-start(bf16[128,256]{1,0:T(8,128)(2,1)S(1)} %broadcast_select_fusion), channel_id=1, source_target_pairs={{0,4},{4,0},{8,12},{12,8},{1,5},{5,1},{9,13},{13,9},{2,6},{6,2},{1... | collective-permute-start | bytes 196616 | tf_op jit(solution)/shard_map/ppermute | solution.py:426
  65.4 12.7 %collective-permute-start.8 = (bf16[4,128,256]{2,1,0:T(8,128)(2,1)S(1)}, bf16[4,128,256]{2,1,0:T(8,128)(2,1)S(1)}, u32[]{:S(2)}, u32[]{:S(2)}) collective-permute-start(bf16[4,128,256]{2,1,0:T(8,128)(2,1)S(1)} %copy-done.12), channel_id=1, source_target_pairs={{2,0},{3,1},{6,4},{7,5},{10,8},{11,9},{14,12},{15,13},{18,16},{19,... | collective-permute-start | bytes 786440 | tf_op jit(solution)/shard_map/ppermute | solution.py:566
  66.7 14.3 %collective-permute-start.7 = (bf16[4,128,256]{2,1,0:T(8,128)(2,1)S(1)}, bf16[4,128,256]{2,1,0:T(8,128)(2,1)S(1)}, u32[]{:S(2)}, u32[]{:S(2)}) collective-permute-start(bf16[4,128,256]{2,1,0:T(8,128)(2,1)S(1)} %copy-done.11), channel_id=1, source_target_pairs={{2,0},{3,1},{6,4},{7,5},{10,8},{11,9},{14,12},{15,13},{18,16},{19,... | collective-permute-start | bytes 786440 | tf_op jit(solution)/shard_map/ppermute | solution.py:554
  77.8 5.2 %collective-permute-start.6 = (bf16[128,256]{1,0:T(8,128)(2,1)S(1)}, bf16[128,256]{1,0:T(8,128)(2,1)S(1)}, u32[]{:S(2)}, u32[]{:S(2)}) collective-permute-start(bf16[128,256]{1,0:T(8,128)(2,1)S(1)} %convert_add_fusion), channel_id=1, source_target_pairs={{0,8},{4,12},{8,0},{12,4},{1,9},{5,13},{9,1},{13,5},{2,10},{6,14},... | collective-permute-start | bytes 196616 | tf_op jit(solution)/shard_map/ppermute | solution.py:426
  83.0 3.6 %collective-permute-start.9 = (f32[16,128,128]{2,1,0:T(8,128)S(1)}, f32[16,128,128]{2,1,0:T(8,128)S(1)}, u32[]{:S(2)}, u32[]{:S(2)}) collective-permute-start(f32[16,128,128]{2,1,0:T(8,128)S(1)} %get-tuple-element.66), channel_id=1, source_target_pairs={{0,1},{1,0},{2,3},{3,2},{4,5},{5,4},{6,7},{7,6},{8,9},{9,8},{10,11... | collective-permute-start | bytes 3145736 | tf_op jit(solution)/shard_map/ppermute | solution.py:426
  83.1 4.7 %collective-permute-start.10 = (bf16[128,256]{1,0:T(8,128)(2,1)S(1)}, bf16[128,256]{1,0:T(8,128)(2,1)S(1)}, u32[]{:S(2)}, u32[]{:S(2)}) collective-permute-start(bf16[128,256]{1,0:T(8,128)(2,1)S(1)} %add_convert_fusion.1.mine), channel_id=1, source_target_pairs={{0,4},{4,0},{8,12},{12,8},{1,5},{5,1},{9,13},{13,9},{2,6},{6,2},{1... | collective-permute-start | bytes 196616 | tf_op jit(solution)/shard_map/ppermute | solution.py:426
  83.2 4.7 %collective-permute-start.11 = (bf16[128,256]{1,0:T(8,128)(2,1)S(1)}, bf16[128,256]{1,0:T(8,128)(2,1)S(1)}, u32[]{:S(2)}, u32[]{:S(2)}) collective-permute-start(bf16[128,256]{1,0:T(8,128)(2,1)S(1)} %add_convert_fusion.1.mine), channel_id=1, source_target_pairs={{0,2},{2,0},{1,3},{3,1},{4,6},{6,4},{5,7},{7,5},{8,10},{10,8},{9,1... | collective-permute-start | bytes 196616 | tf_op jit(solution)/shard_map/ppermute | solution.py:426
  84.7 5.2 %collective-permute-start.12 = (bf16[128,256]{1,0:T(8,128)(2,1)S(1)}, bf16[128,256]{1,0:T(8,128)(2,1)S(1)}, u32[]{:S(2)}, u32[]{:S(2)}) collective-permute-start(bf16[128,256]{1,0:T(8,128)(2,1)S(1)} %add_convert_fusion.1.mine), channel_id=1, source_target_pairs={{0,6},{2,4},{4,2},{6,0},{8,14},{10,12},{12,10},{14,8},{1,7},{3,5},... | collective-permute-start | bytes 196616 | tf_op jit(solution)/shard_map/ppermute | solution.py:464

commit v16 on v15

--- a/solution.py
+++ b/solution.py
@@ -580,6 +580,8 @@
         sum(piece.astype(F32) for piece in pieces), home_b, fold
     )
     got = exchanged(give, "head", 1)
+    got, along_both = lax.optimization_barrier((got, quarters[3]))
+    quarters = (*quarters[:3], along_both)
     back_blocks = pl.pallas_call(
         add_kernel,
         out_shape=jax.ShapeDtypeStruct((blocks_dev, BLOCK, half), BF16),

time: 91.4 us -> 91.8 us (level)
    ppermute x8, starting transfers between devices: 5.46 us -> 6.98 us  [exchanged(): lax.ppermute(value, axis, [(place, place ^ bit) for place in range(count)])]
    ppermute x1, starting transfers between devices: 1.91 us -> 0.4 us  [sum_gradients(): lax.ppermute(part, ('reach', 'day'), neighbours('reach', 'day'))]
  transfers between devices with their start and end apart: 17 -> 17, of which waited for: 10 -> 11; matrix products, arithmetic and copies ran while one was open for 0% -> 0% of each run, Pallas kernels for 30% -> 29%
where the time goes in v16:
time: 91.8 us; the launch traced here: 91.2 us
  starting transfers between devices  32.1 us (35%)
  Pallas kernels  30 us (33%)
  waiting for transfers between devices  24.8 us (27%)
  local copies, waits for them, and re-layouts  3.32 us (4%)
    pallas_call x2, Pallas kernels, attend(): pl.pallas_call(lambda *refs: attention_kernel(lay, chunk, *refs), grid_sp...  22.3 us
    all_to_all x4, starting transfers between devices, ring(): return lax.all_to_all(value, 'reach', 0, 0, tiled=True).reshape(shape)  18 us
    all_to_all x4, waiting for transfers between devices, ring(): return lax.all_to_all(value, 'reach', 0, 0, tiled=True).reshape(shape)  13 us
    ppermute x8, starting transfers between devices, exchanged(): lax.ppermute(value, axis, [(place, place ^ bit) for place in range(count)])  6.98 us
    ppermute x8, waiting for transfers between devices, exchanged(): lax.ppermute(value, axis, [(place, place ^ bit) for place in range(count)])  6.46 us
    ppermute x1, starting transfers between devices, on_device(): prior_inputs = lax.ppermute(prior, 'day', next_day)  3.56 us
    unnamed x31, local copies, waits for them, and re-layouts  3.32 us
    ppermute x1, waiting for transfers between devices, on_device(): day_a = lax.ppermute(day_a, 'day', last_day)  2.97 us
  transfers between devices with their start and end apart: 17, of which 11 were waited for; matrix products, arithmetic and copies ran while one was open for 0% of the time, Pallas kernels for 29%

profile of v16, /device:TPU:0, one launch (start us, length us, event | category | flops | bytes accessed | tf_op | source)
XLA Modules:
  0.0 91.2 jit_solution(4105376494109258172)
XLA Ops:
  0.6 0.0 copy-start
  0.6 2.3 %pick.1 = (bf16[8,128,256]{2,1,0:T(8,128)(2,1)}, s32[128]{0:T(128)S(1)}) custom-call(s32[64]{0:T(128)} %refs_0_.3, bf16[16,128,256]{2,1,0:T(8,128)(2,1)} %bitcast.14), custom_call_target="tpu_custom_call" | custom-call | tf_op jit(solution)/shard_map/pick/pallas_call | solution.py:506
  2.9 6.3 %all-to-all-start = ((bf16[4,256,256]{2,1,0:T(8,128)(2,1)}), bf16[4,256,256]{2,1,0:T(8,128)(2,1)S(1)}, u32[]{:S(2)}, u32[]{:S(2)}) async-start(bf16[4,256,256]{2,1,0:T(8,128)(2,1)} %bitcast.2), calls=%async_computation | async-start | bytes 1048576 | tf_op jit(solution)/shard_map/all_to_all | solution.py:542
  9.3 0.6 copy-done.3
  9.9 0.0 copy-done.4
  10.0 2.0 %deal.1 = (bf16[8,128,256]{2,1,0:T(8,128)(2,1)}, bf16[8,128,256]{2,1,0:T(8,128)(2,1)S(1)}, s32[128]{0:T(128)S(1)}) custom-call(s32[64]{0:T(128)S(1)} %copy-done.3, s32[64]{0:T(128)S(1)} %copy-done.4, s32[128]{0:T(128)S(1)} %get-tuple-element.43.refs_2_.refs_1_, bf16[16,128,256]{2,1,0:T(8,128)(2,1)S(1)} %bitcast.23), custom_call_target="tpu_custom_call" | custom-call | tf_op jit(solution)/shard_map/deal/pallas_call | solution.py:522
  12.0 0.0 copy-start.7
  12.0 3.6 %collective-permute-start = (bf16[8,128,256]{2,1,0:T(8,128)(2,1)S(1)}, bf16[8,128,256]{2,1,0:T(8,128)(2,1)S(1)}, u32[]{:S(2)}, u32[]{:S(2)}) collective-permute-start(bf16[8,128,256]{2,1,0:T(8,128)(2,1)S(1)} %get-tuple-element.46), channel_id=1, source_target_pairs={{0,2},{1,3},{4,6},{5,7},{8,10},{9,11},{12,14},{13,15},{16,18},{17,... | collective-permute-start | bytes 1572872 | tf_op jit(solution)/shard_map/ppermute | solution.py:547
  15.6 0.1 copy.13
  15.7 0.0 copy-start.8
  15.7 0.1 copy.14
  15.8 0.7 copy-done.8
  16.5 0.1 copy.15
  16.7 0.7 copy-done.9
  17.4 0.1 collective-permute-start.1
  17.5 6.3 %all-to-all-done = bf16[4,256,256]{2,1,0:T(8,128)(2,1)S(1)} async-done(((bf16[4,256,256]{2,1,0:T(8,128)(2,1)}), bf16[4,256,256]{2,1,0:T(8,128)(2,1)S(1)}, u32[]{:S(2)}, u32[]{:S(2)}) %all-to-all-start) | async-done | bytes 524320 | tf_op jit(solution)/shard_map/all_to_all | solution.py:542
  23.8 3.5 %all-to-all-start.2 = ((bf16[4,256,256]{2,1,0:T(8,128)(2,1)}), bf16[4,256,256]{2,1,0:T(8,128)(2,1)S(1)}, u32[]{:S(2)}, u32[]{:S(2)}) async-start(bf16[4,256,256]{2,1,0:T(8,128)(2,1)} %bitcast.9), calls=%async_computation.2 | async-start | bytes 1048576 | tf_op jit(solution)/shard_map/all_to_all | solution.py:542
  27.3 0.0 copy-start.10
  27.3 0.7 copy-done.13
  28.0 0.2 copy-done.10
  28.1 11.2 %attention_0.1 = (f32[4,128,256]{2,1,0:T(8,128)}, bf16[4,128,256]{2,1,0:T(8,128)(2,1)}, bf16[8,128,256]{2,1,0:T(8,128)(2,1)}, f32[512,256]{1,0:T(8,128)}, f32[512,256]{1,0:T(8,128)}) custom-call(s32[128]{0:T(128)S(1)} %get-tuple-element.44.refs_0_, bf16[16,128,256]{2,1,0:T(8,128)(2,1)} %bitcast.15, bf16[16,128,256]{2,1,0:T(8,128)(2,1)} %bitcast.40, ...), custom_call_target="tpu_custom_call" | custom-call | flops 6375342080 | bytes 5242880 | tf_op jit(solution)/shard_map/attention_0/pallas_call | solution.py:388
  39.3 1.9 %all-to-all-done.2 = bf16[4,256,256]{2,1,0:T(8,128)(2,1)S(1)} async-done(((bf16[4,256,256]{2,1,0:T(8,128)(2,1)}), bf16[4,256,256]{2,1,0:T(8,128)(2,1)S(1)}, u32[]{:S(2)}, u32[]{:S(2)}) %all-to-all-start.2) | async-done | bytes 524320 | tf_op jit(solution)/shard_map/all_to_all | solution.py:542
  41.2 3.6 %all-to-all-start.1 = ((bf16[4,256,256]{2,1,0:T(8,128)(2,1)}), bf16[4,256,256]{2,1,0:T(8,128)(2,1)S(1)}, u32[]{:S(2)}, u32[]{:S(2)}) async-start(bf16[4,256,256]{2,1,0:T(8,128)(2,1)} %bitcast.36), calls=%async_computation.1 | async-start | bytes 1048576 | tf_op jit(solution)/shard_map/all_to_all | solution.py:542
  44.9 11.1 %attention_1.1 = (f32[4,128,256]{2,1,0:T(8,128)}, bf16[4,128,256]{2,1,0:T(8,128)(2,1)}, bf16[8,128,256]{2,1,0:T(8,128)(2,1)}, bf16[256,256]{1,0:T(8,128)(2,1)S(1...) custom-call(s32[128]{0:T(128)S(1)} %get-tuple-element.44.refs_0_, ...), custom_call_target="tpu_custom_call" | custom-call | flops 6375342080 | bytes 5242880 | tf_op jit(solution)/shard_map/attention_1/pallas_call | solution.py:388
  56.0 1.5 %collective-permute-start.2 = (bf16[256,256]{1,0:T(8,128)(2,1)S(1)}, bf16[256,256]{1,0:T(8,128)(2,1)S(1)}, u32[]{:S(2)}, u32[]{:S(2)}) collective-permute-start(bf16[256,256]{1,0:T(8,128)(2,1)S(1)} %get-tuple-element.54), channel_id=1, source_target_pairs={{0,2},{2,0},{1,3},{3,1},{4,6},{6,4},{5,7},{7,5},{8,10},{10,8},{9,1... | collective-permute-start | bytes 393224 | tf_op jit(solution)/shard_map/ppermute | solution.py:426
  57.5 0.6 collective-permute-start.4
  58.2 0.5 all-to-all-done.1
  58.6 4.5 %all-to-all-start.3 = ((bf16[4,256,256]{2,1,0:T(8,128)(2,1)}), bf16[4,256,256]{2,1,0:T(8,128)(2,1)S(1)}, u32[]{:S(2)}, u32[]{:S(2)}) async-start(bf16[4,256,256]{2,1,0:T(8,128)(2,1)} %bitcast.35), calls=%async_computation.3 | async-start | bytes 1048576 | tf_op jit(solution)/shard_map/all_to_all | solution.py:542
  63.2 0.1 collective-permute-done.4
  63.3 0.1 add_convert_fusion
  63.4 2.0 %collective-permute-start.5 = (bf16[128,256]{1,0:T(8,128)(2,1)S(1)}, bf16[128,256]{1,0:T(8,128)(2,1)S(1)}, u32[]{:S(2)}, u32[]{:S(2)}) collective-permute-start(bf16[128,256]{1,0:T(8,128)(2,1)S(1)} %broadcast_select_fusion), channel_id=1, source_target_pairs={{0,4},{4,0},{8,12},{12,8},{1,5},{5,1},{9,13},{13,9},{2,6},{6,2},{1... | collective-permute-start | bytes 196616 | tf_op jit(solution)/shard_map/ppermute | solution.py:426
  65.4 1.3 %collective-permute-start.8 = (bf16[4,128,256]{2,1,0:T(8,128)(2,1)S(1)}, bf16[4,128,256]{2,1,0:T(8,128)(2,1)S(1)}, u32[]{:S(2)}, u32[]{:S(2)}) collective-permute-start(bf16[4,128,256]{2,1,0:T(8,128)(2,1)S(1)} %copy-done.12), channel_id=1, source_target_pairs={{2,0},{3,1},{6,4},{7,5},{10,8},{11,9},{14,12},{15,13},{18,16},{19,... | collective-permute-start | bytes 786440 | tf_op jit(solution)/shard_map/ppermute | solution.py:566
  66.7 1.3 %collective-permute-start.7 = (bf16[4,128,256]{2,1,0:T(8,128)(2,1)S(1)}, bf16[4,128,256]{2,1,0:T(8,128)(2,1)S(1)}, u32[]{:S(2)}, u32[]{:S(2)}) collective-permute-start(bf16[4,128,256]{2,1,0:T(8,128)(2,1)S(1)} %copy-done.11), channel_id=1, source_target_pairs={{2,0},{3,1},{6,4},{7,5},{10,8},{11,9},{14,12},{15,13},{18,16},{19,... | collective-permute-start | bytes 786440 | tf_op jit(solution)/shard_map/ppermute | solution.py:554
  68.0 5.5 %collective-permute-done.5 = bf16[128,256]{1,0:T(8,128)(2,1)S(1)} collective-permute-done((bf16[128,256]{1,0:T(8,128)(2,1)S(1)}, bf16[128,256]{1,0:T(8,128)(2,1)S(1)}, u32[]{:S(2)}, u32[]{:S(2)}) %collective-permute-start.5) | collective-permute-done | bytes 65568 | tf_op jit(solution)/shard_map/ppermute | solution.py:426
  73.5 4.3 %all-to-all-done.3 = bf16[4,256,256]{2,1,0:T(8,128)(2,1)S(1)} async-done(((bf16[4,256,256]{2,1,0:T(8,128)(2,1)}), bf16[4,256,256]{2,1,0:T(8,128)(2,1)S(1)}, u32[]{:S(2)}, u32[]{:S(2)}) %all-to-all-start.3) | async-done | bytes 524320 | tf_op jit(solution)/shard_map/all_to_all | solution.py:542
  77.8 0.2 collective-permute-start.6
  78.0 3.0 %collective-permute-done.7.refs_4_ = bf16[4,128,256]{2,1,0:T(8,128)(2,1)S(1)} collective-permute-done((bf16[4,128,256]{2,1,0:T(8,128)(2,1)S(1)}, bf16[4,128,256]{2,1,0:T(8,128)(2,1)S(1)}, u32[]{:S(2)}, u32[]{:S(2)}) %collective-permute-start.7) | collective-permute-done | bytes 262176 | tf_op jit(solution)/shard_map/ppermute | solution.py:554
  81.0 1.6 %fold.1 = (f32[16,128,128]{2,1,0:T(8,128)S(1)}, f32[16,128,128]{2,1,0:T(8,128)S(1)}) custom-call(s32[128]{0:T(128)S(1)} %get-tuple-element.44.refs_0_, s32[128]{0:T(128)S(1)} %get-tuple-element.43.refs_2_.refs_1_, f32[4,128,256]{2,1,0:T(8,128)S(1)} %copy-done.1, f32[4,128,256]{2,1,0:T(8,128)S(1)} %copy-done.2, ...), custom_call_target="tpu_custom_call" | custom-call | tf_op jit(solution)/shard_map/fold/pallas_call | solution.py:570
  82.6 0.4 collective-permute-done.6
  83.0 0.1 collective-permute-start.9
  83.1 0.4 collective-permute-start.10
  83.5 2.6 %collective-permute-start.11 = (bf16[128,256]{1,0:T(8,128)(2,1)S(1)}, bf16[128,256]{1,0:T(8,128)(2,1)S(1)}, u32[]{:S(2)}, u32[]{:S(2)}) collective-permute-start(bf16[128,256]{1,0:T(8,128)(2,1)S(1)} %add_convert_fusion.1.mine), channel_id=1, source_target_pairs={{0,4},{4,0},{8,12},{12,8},{1,5},{5,1},{9,13},{13,9},{2,6},{6,2},{1... | collective-permute-start | bytes 196616 | tf_op jit(solution)/shard_map/ppermute | solution.py:426
  86.1 0.5 collective-permute-start.12
  86.6 2.3 %collective-permute-done.10.along_both = bf16[128,256]{1,0:T(8,128)(2,1)S(1)} collective-permute-done((bf16[128,256]{1,0:T(8,128)(2,1)S(1)}, bf16[128,256]{1,0:T(8,128)(2,1)S(1)}, u32[]{:S(2)}, u32[]{:S(2)}) %collective-permute-start.10) | collective-permute-done | bytes 65568 | tf_op jit(solution)/shard_map/ppermute | solution.py:464
  88.9 0.9 add.26
  89.8 0.1 collective-permute-done.11.along_reach
  89.9 0.4 collective-permute-done.12.along_day
  90.4 0.8 split.1
  (29 shorter events, 0.1 us)
Async XLA Ops:
  0.6 8.7 %copy-start = (bf16[1,2048,256]{2,1,0:T(8,128)(2,1)S(1)}, bf16[1,2048,256]{2,1,0:T(8,128)(2,1)}, u32[]{:S(2)}) copy-start(bf16[1,2048,256]{2,1,0:T(8,128)(2,1)} %param.8) | copy-start | bytes 3145732
  2.9 20.8 %all-to-all-start = ((bf16[4,256,256]{2,1,0:T(8,128)(2,1)}), bf16[4,256,256]{2,1,0:T(8,128)(2,1)S(1)}, u32[]{:S(2)}, u32[]{:S(2)}) async-start(bf16[4,256,256]{2,1,0:T(8,128)(2,1)} %bitcast.2), calls=%async_computation | async-start | bytes 1048576 | tf_op jit(solution)/shard_map/all_to_all | solution.py:542
  9.3 0.7 copy-start.3
  9.3 0.7 copy-start.4
  9.9 5.6 %copy-start.6 = (bf16[256,128]{1,0:T(8,128)(2,1)S(1)}, bf16[256,128]{1,0:T(8,128)(2,1)}, u32[]{:S(2)}) copy-start(bf16[256,128]{1,0:T(8,128)(2,1)} %param.11) | copy-start | bytes 196612
  12.0 3.7 %copy-start.7 = (bf16[256,128]{1,0:T(8,128)(2,1)S(1)}, bf16[256,128]{1,0:T(8,128)(2,1)}, u32[]{:S(2)}) copy-start(bf16[256,128]{1,0:T(8,128)(2,1)} %param.12) | copy-start | bytes 196612
  12.0 15.3 %collective-permute-start = (bf16[8,128,256]{2,1,0:T(8,128)(2,1)S(1)}, bf16[8,128,256]{2,1,0:T(8,128)(2,1)S(1)}, u32[]{:S(2)}, u32[]{:S(2)}) collective-permute-start(bf16[8,128,256]{2,1,0:T(8,128)(2,1)S(1)} %get-tuple-element.46), channel_id=1, source_target_pairs={{0,2},{1,3},{4,6},{5,7},{8,10},{9,11},{12,14},{13,15},{16,18},{17,... | collective-permute-start | bytes 1572872 | tf_op jit(solution)/shard_map/ppermute | solution.py:547
  15.7 0.8 copy-start.8
  16.5 0.8 copy-start.9
  17.4 6.4 %copy-start.5 = (bf16[512,256]{1,0:T(8,128)(2,1)}, bf16[512,256]{1,0:T(8,128)(2,1)S(1)}, u32[]{:S(2)}) copy-start(bf16[512,256]{1,0:T(8,128)(2,1)S(1)} %pad_maximum_fusion.refs_17_) | copy-start | bytes 786436
  17.4 9.8 %collective-permute-start.1 = (bf16[512,256]{1,0:T(8,128)(2,1)S(1)}, bf16[512,256]{1,0:T(8,128)(2,1)S(1)}, u32[]{:S(2)}, u32[]{:S(2)}) collective-permute-start(bf16[512,256]{1,0:T(8,128)(2,1)S(1)} %pad_maximum_fusion.refs_17_), channel_id=1, source_target_pairs={{0,1},{1,0},{2,3},{3,2},{4,5},{5,4},{6,7},{7,6},{8,9},{9,8},{10,11... | collective-permute-start | bytes 786440 | tf_op jit(solution)/shard_map/ppermute | solution.py:426
  23.8 17.4 %all-to-all-start.2 = ((bf16[4,256,256]{2,1,0:T(8,128)(2,1)}), bf16[4,256,256]{2,1,0:T(8,128)(2,1)S(1)}, u32[]{:S(2)}, u32[]{:S(2)}) async-start(bf16[4,256,256]{2,1,0:T(8,128)(2,1)} %bitcast.9), calls=%async_computation.2 | async-start | bytes 1048576 | tf_op jit(solution)/shard_map/all_to_all | solution.py:542
  27.3 0.7 copy-start.13
  27.3 0.9 copy-start.10
  41.2 17.4 %all-to-all-start.1 = ((bf16[4,256,256]{2,1,0:T(8,128)(2,1)}), bf16[4,256,256]{2,1,0:T(8,128)(2,1)S(1)}, u32[]{:S(2)}, u32[]{:S(2)}) async-start(bf16[4,256,256]{2,1,0:T(8,128)(2,1)} %bitcast.36), calls=%async_computation.1 | async-start | bytes 1048576 | tf_op jit(solution)/shard_map/all_to_all | solution.py:542
  56.0 7.1 %collective-permute-start.2 = (bf16[256,256]{1,0:T(8,128)(2,1)S(1)}, bf16[256,256]{1,0:T(8,128)(2,1)S(1)}, u32[]{:S(2)}, u32[]{:S(2)}) collective-permute-start(bf16[256,256]{1,0:T(8,128)(2,1)S(1)} %get-tuple-element.54), channel_id=1, source_target_pairs={{0,2},{2,0},{1,3},{3,1},{4,6},{6,4},{5,7},{7,5},{8,10},{10,8},{9,1... | collective-permute-start | bytes 393224 | tf_op jit(solution)/shard_map/ppermute | solution.py:426
  57.5 5.7 %collective-permute-start.3 = (bf16[256,256]{1,0:T(8,128)(2,1)S(1)}, bf16[256,256]{1,0:T(8,128)(2,1)S(1)}, u32[]{:S(2)}, u32[]{:S(2)}) collective-permute-start(bf16[256,256]{1,0:T(8,128)(2,1)S(1)} %get-tuple-element.55), channel_id=1, source_target_pairs={{0,1},{1,0},{2,3},{3,2},{4,5},{5,4},{6,7},{7,6},{8,9},{9,8},{10,11... | collective-permute-start | bytes 393224 | tf_op jit(solution)/shard_map/ppermute | solution.py:426
  57.5 5.8 %collective-permute-start.4 = (bf16[256,256]{1,0:T(8,128)(2,1)S(1)}, bf16[256,256]{1,0:T(8,128)(2,1)S(1)}, u32[]{:S(2)}, u32[]{:S(2)}) collective-permute-start(bf16[256,256]{1,0:T(8,128)(2,1)S(1)} %get-tuple-element.56), channel_id=1, source_target_pairs={{0,3},{1,2},{2,1},{3,0},{4,7},{5,6},{6,5},{7,4},{8,11},{9,10},{10,... | collective-permute-start | bytes 393224 | tf_op jit(solution)/shard_map/ppermute | solution.py:561
  58.6 6.7 %copy-start.12 = (bf16[4,128,256]{2,1,0:T(8,128)(2,1)S(1)}, bf16[4,128,256]{2,1,0:T(8,128)(2,1)}, u32[]{:S(2)}) copy-start(bf16[4,128,256]{2,1,0:T(8,128)(2,1)} %get-tuple-element.62) | copy-start | bytes 786436
  58.6 8.0 %copy-start.11 = (bf16[4,128,256]{2,1,0:T(8,128)(2,1)S(1)}, bf16[4,128,256]{2,1,0:T(8,128)(2,1)}, u32[]{:S(2)}) copy-start(bf16[4,128,256]{2,1,0:T(8,128)(2,1)} %get-tuple-element.61) | copy-start | bytes 786436
  58.6 19.2 %all-to-all-start.3 = ((bf16[4,256,256]{2,1,0:T(8,128)(2,1)}), bf16[4,256,256]{2,1,0:T(8,128)(2,1)S(1)}, u32[]{:S(2)}, u32[]{:S(2)}) async-start(bf16[4,256,256]{2,1,0:T(8,128)(2,1)} %bitcast.35), calls=%async_computation.3 | async-start | bytes 1048576 | tf_op jit(solution)/shard_map/all_to_all | solution.py:542
  63.1 17.8 %copy-start.1 = (f32[4,128,256]{2,1,0:T(8,128)S(1)}, f32[4,128,256]{2,1,0:T(8,128)}, u32[]{:S(2)}) copy-start(f32[4,128,256]{2,1,0:T(8,128)} %get-tuple-element.59.refs_2_) | copy-start | bytes 1572868
  63.1 17.8 %copy-start.2 = (f32[4,128,256]{2,1,0:T(8,128)S(1)}, f32[4,128,256]{2,1,0:T(8,128)}, u32[]{:S(2)}) copy-start(f32[4,128,256]{2,1,0:T(8,128)} %get-tuple-element.60.refs_3_) | copy-start | bytes 1572868
  63.4 10.1 %collective-permute-start.5 = (bf16[128,256]{1,0:T(8,128)(2,1)S(1)}, bf16[128,256]{1,0:T(8,128)(2,1)S(1)}, u32[]{:S(2)}, u32[]{:S(2)}) collective-permute-start(bf16[128,256]{1,0:T(8,128)(2,1)S(1)} %broadcast_select_fusion), channel_id=1, source_target_pairs={{0,4},{4,0},{8,12},{12,8},{1,5},{5,1},{9,13},{13,9},{2,6},{6,2},{1... | collective-permute-start | bytes 196616 | tf_op jit(solution)/shard_map/ppermute | solution.py:426
  65.4 12.7 %collective-permute-start.8 = (bf16[4,128,256]{2,1,0:T(8,128)(2,1)S(1)}, bf16[4,128,256]{2,1,0:T(8,128)(2,1)S(1)}, u32[]{:S(2)}, u32[]{:S(2)}) collective-permute-start(bf16[4,128,256]{2,1,0:T(8,128)(2,1)S(1)} %copy-done.12), channel_id=1, source_target_pairs={{2,0},{3,1},{6,4},{7,5},{10,8},{11,9},{14,12},{15,13},{18,16},{19,... | collective-permute-start | bytes 786440 | tf_op jit(solution)/shard_map/ppermute | solution.py:566
  66.7 14.3 %collective-permute-start.7 = (bf16[4,128,256]{2,1,0:T(8,128)(2,1)S(1)}, bf16[4,128,256]{2,1,0:T(8,128)(2,1)S(1)}, u32[]{:S(2)}, u32[]{:S(2)}) collective-permute-start(bf16[4,128,256]{2,1,0:T(8,128)(2,1)S(1)} %copy-done.11), channel_id=1, source_target_pairs={{2,0},{3,1},{6,4},{7,5},{10,8},{11,9},{14,12},{15,13},{18,16},{19,... | collective-permute-start | bytes 786440 | tf_op jit(solution)/shard_map/ppermute | solution.py:554
  77.8 5.2 %collective-permute-start.6 = (bf16[128,256]{1,0:T(8,128)(2,1)S(1)}, bf16[128,256]{1,0:T(8,128)(2,1)S(1)}, u32[]{:S(2)}, u32[]{:S(2)}) collective-permute-start(bf16[128,256]{1,0:T(8,128)(2,1)S(1)} %convert_add_fusion), channel_id=1, source_target_pairs={{0,8},{4,12},{8,0},{12,4},{1,9},{5,13},{9,1},{13,5},{2,10},{6,14},... | collective-permute-start | bytes 196616 | tf_op jit(solution)/shard_map/ppermute | solution.py:426
  83.0 5.9 %collective-permute-start.9 = (f32[16,128,128]{2,1,0:T(8,128)S(1)}, f32[16,128,128]{2,1,0:T(8,128)S(1)}, u32[]{:S(2)}, u32[]{:S(2)}) collective-permute-start(f32[16,128,128]{2,1,0:T(8,128)S(1)} %get-tuple-element.68), channel_id=1, source_target_pairs={{0,1},{1,0},{2,3},{3,2},{4,5},{5,4},{6,7},{7,6},{8,9},{9,8},{10,11... | collective-permute-start | bytes 3145736 | tf_op jit(solution)/shard_map/ppermute | solution.py:426
  83.1 5.9 %collective-permute-start.10 = (bf16[128,256]{1,0:T(8,128)(2,1)S(1)}, bf16[128,256]{1,0:T(8,128)(2,1)S(1)}, u32[]{:S(2)}, u32[]{:S(2)}) collective-permute-start(bf16[128,256]{1,0:T(8,128)(2,1)S(1)} %add_convert_fusion.1.mine), channel_id=1, source_target_pairs={{0,6},{2,4},{4,2},{6,0},{8,14},{10,12},{12,10},{14,8},{1,7},{3,5},... | collective-permute-start | bytes 196616 | tf_op jit(solution)/shard_map/ppermute | solution.py:464
  83.5 6.4 %collective-permute-start.11 = (bf16[128,256]{1,0:T(8,128)(2,1)S(1)}, bf16[128,256]{1,0:T(8,128)(2,1)S(1)}, u32[]{:S(2)}, u32[]{:S(2)}) collective-permute-start(bf16[128,256]{1,0:T(8,128)(2,1)S(1)} %add_convert_fusion.1.mine), channel_id=1, source_target_pairs={{0,4},{4,0},{8,12},{12,8},{1,5},{5,1},{9,13},{13,9},{2,6},{6,2},{1... | collective-permute-start | bytes 196616 | tf_op jit(solution)/shard_map/ppermute | solution.py:426
  86.1 4.3 %collective-permute-start.12 = (bf16[128,256]{1,0:T(8,128)(2,1)S(1)}, bf16[128,256]{1,0:T(8,128)(2,1)S(1)}, u32[]{:S(2)}, u32[]{:S(2)}) collective-permute-start(bf16[128,256]{1,0:T(8,128)(2,1)S(1)} %add_convert_fusion.1.mine), channel_id=1, source_target_pairs={{0,2},{2,0},{1,3},{3,1},{4,6},{6,4},{5,7},{7,5},{8,10},{10,8},{9,1... | collective-permute-start | bytes 196616 | tf_op jit(solution)/shard_map/ppermute | solution.py:426
